TPU v7x, 256 devices: a whole 4x4x8 slice. The times are simulated.
256 devices in a mesh: section: 4 (over y_hi, core), fsdp: 16 (over z, y_lo), batch: 4 (over x).
Axes of the slice: x: 4, y: 4 (y_hi: 2, y_lo: 2; y = y_hi * 2 + y_lo), z: 8, core: 2. Of those that a mesh axis runs over, the one named last changes fastest.
Arguments:
- frames: bfloat16 [4, 64, 48, 1536], P(None, ('fsdp', 'batch')), may hold values from -6 to 6
- cotangent: bfloat16 [4, 64, 48, 1536], P(None, ('fsdp', 'batch')), may hold values from -6 to 6
- lengths: int32 [4, 64], P(None, ('fsdp', 'batch')), may hold values from 24 to 48
- w_in: bfloat16 [4, 1536, 3072], P('section', 'fsdp'), may hold values from -0.15625 to 0.15625
- w_out: bfloat16 [4, 1536, 1536], P('section', 'fsdp'), may hold values from -0.15625 to 0.15625
- gain_pre: float32 [4, 1536], P('section'), may hold values from 0.5 to 1.5
- gain_mid: float32 [4, 1536], P('section'), may hold values from 0.5 to 1.5
- w_depth: float32 [4, 31, 1536], P('section'), may hold values from -2 to 2
Outputs:
- input_grads: bfloat16 [4, 4, 64, 48, 1536], P('section', None, ('fsdp', 'batch'))
- grad_w_in: float32 [4, 1536, 3072], P('section', 'fsdp')
- grad_w_out: float32 [4, 1536, 1536], P('section', 'fsdp')
- grad_gain_pre: float32 [4, 1536], P('section')
- grad_gain_mid: float32 [4, 1536], P('section')
- grad_depth: float32 [4, 31, 1536], P('section')
Inputs may be any that keep to these rules, and one draw needn't show every extreme that they name: `lengths`: frames at or after an utterance's length are padding.
All inputs are finite; a program needn't handle non-finite values.
Results may differ from a plain program's by a relative error of at most 0.03.
Values may be sent and summed in bfloat16 or wider, within the bound.
No kernel may reach another device: no remote copies, remote signals or barrier semaphores. Data moves between devices by JAX's collectives and lax.ppermute only.
A program may use at most 128 MiB of HBM per device.

v0:
```python
import math

import jax
import jax.numpy as jnp
from jax import lax
from jax.sharding import PartitionSpec as P

epsilon = 1e-05


def from_behind(x, axis, by):
    peers = lax.axis_size(axis)
    pairs = [(i, i + by) for i in range(peers) if 0 <= i + by < peers]
    return lax.ppermute(x, axis, pairs)


def layer_norm(values):
    mean_value = jnp.mean(values, axis=-1, keepdims=True)
    centred = values - mean_value
    inv_scale = lax.rsqrt(jnp.mean(centred * centred, axis=-1, keepdims=True) + epsilon)
    return (centred * inv_scale, inv_scale)


def norm_grad(upstream, normed, inv_scale):
    return (
        upstream
        - jnp.mean(upstream, axis=-1, keepdims=True)
        - normed * jnp.mean(upstream * normed, axis=-1, keepdims=True)
    ) * inv_scale


def project(left, right):
    batch_rows, length, inner = left.shape
    flat = jnp.dot(
        left.reshape(batch_rows * length, inner), right, preferred_element_type=jnp.float32
    )
    return flat.reshape(batch_rows, length, right.shape[1])


def project_back(left, right):
    batch_rows, length, inner = left.shape
    flat = lax.dot_general(
        left.reshape(batch_rows * length, inner),
        right,
        (((1,), (1,)), ((), ())),
        preferred_element_type=jnp.float32,
    )
    return flat.reshape(batch_rows, length, right.shape[0])


def depthwise(values, taps):
    kernel = taps.shape[0]
    half = kernel // 2
    length = values.shape[1]
    padded = jnp.pad(values, ((0, 0), (half, half), (0, 0)))
    total = padded[:, 0:length, :] * taps[0]
    for offset in range(1, kernel):
        total = total + padded[:, offset : offset + length, :] * taps[offset]
    return total


def section_forward(frames, w_in, w_out, gain_a, gain_b, taps, padding):
    model_width = frames.shape[-1]
    source = frames.astype(jnp.float32)
    normed_in, inv_in = layer_norm(source)
    projected = (normed_in * gain_a).astype(jnp.bfloat16)
    both = project(projected, w_in)
    glu_value = both[..., :model_width]
    glu_gate = jax.nn.sigmoid(both[..., model_width:])
    gated = glu_value * glu_gate * padding
    conv_out = depthwise(gated, taps)
    normed_mid, inv_mid = layer_norm(conv_out)
    scaled_mid = normed_mid * gain_b
    swished = (scaled_mid * jax.nn.sigmoid(scaled_mid)).astype(jnp.bfloat16)
    result = (source + project(swished, w_out)).astype(jnp.bfloat16)
    return (
        result,
        (
            normed_in,
            inv_in,
            projected,
            glu_value,
            glu_gate,
            gated,
            normed_mid,
            inv_mid,
            scaled_mid,
            swished,
        ),
    )


def section_backward(upstream, w_in, w_out, gain_a, gain_b, taps, padding, saved):
    (
        normed_in,
        inv_in,
        projected,
        glu_value,
        glu_gate,
        gated,
        normed_mid,
        inv_mid,
        scaled_mid,
        swished,
    ) = saved
    kernel = taps.shape[0]
    half = kernel // 2
    length = upstream.shape[1]
    swish_grad = project_back(upstream, w_out)
    sigmoid_mid = jax.nn.sigmoid(scaled_mid)
    scaled_grad = swish_grad * (sigmoid_mid + scaled_mid * sigmoid_mid * (1.0 - sigmoid_mid))
    gain_b_grad = jnp.sum(scaled_grad * normed_mid, axis=(0, 1))
    conv_grad = norm_grad(scaled_grad * gain_b, normed_mid, inv_mid)
    padded_in = jnp.pad(gated, ((0, 0), (half, half), (0, 0)))
    taps_grad = jnp.stack(
        [
            jnp.sum(conv_grad * padded_in[:, offset : offset + length, :], axis=(0, 1))
            for offset in range(kernel)
        ]
    )
    padded_grad = jnp.pad(conv_grad, ((0, 0), (half, half), (0, 0)))
    gated_grad = padded_grad[:, 2 * half : 2 * half + length, :] * taps[0]
    for offset in range(1, kernel):
        gated_grad = (
            gated_grad
            + padded_grad[:, 2 * half - offset : 2 * half - offset + length, :] * taps[offset]
        )
    gated_grad = gated_grad * padding
    value_grad = gated_grad * glu_gate
    gate_grad = gated_grad * glu_value * glu_gate * (1.0 - glu_gate)
    proj_grad = jnp.concatenate([value_grad, gate_grad], axis=-1).astype(jnp.bfloat16)
    input_side = project_back(proj_grad, w_in)
    gain_a_grad = jnp.sum(input_side * normed_in, axis=(0, 1))
    input_grad = (
        upstream.astype(jnp.float32) + norm_grad(input_side * gain_a, normed_in, inv_in)
    ).astype(jnp.bfloat16)
    return (input_grad, proj_grad, (gain_a_grad, gain_b_grad, taps_grad))


def saved_zeros(micro_count, frames_len, model_width):
    wide = (micro_count, 1, frames_len, model_width)
    narrow = (micro_count, 1, frames_len, 1)
    return (
        jnp.zeros(wide, jnp.float32),
        jnp.zeros(narrow, jnp.float32),
        jnp.zeros(wide, jnp.bfloat16),
        jnp.zeros(wide, jnp.float32),
        jnp.zeros(wide, jnp.float32),
        jnp.zeros(wide, jnp.float32),
        jnp.zeros(wide, jnp.float32),
        jnp.zeros(narrow, jnp.float32),
        jnp.zeros(wide, jnp.float32),
        jnp.zeros(wide, jnp.bfloat16),
    )


def put_slot(buffers, values, micro_slot):
    return jax.tree.map(
        lambda buffer, value: lax.dynamic_update_index_in_dim(buffer, value, micro_slot, 0),
        buffers,
        values,
    )


def take_slot(buffers, micro_slot):
    return jax.tree.map(
        lambda buffer: lax.dynamic_index_in_dim(buffer, micro_slot, 0, keepdims=False), buffers
    )


def local(frames, cotangent, lengths, w_in, w_out, gain_pre, gain_mid, w_depth):
    section_count = lax.axis_size("section")
    section_index = lax.axis_index("section")
    micro_count = frames.shape[0]
    frames_len = frames.shape[2]
    model_width = frames.shape[3]
    moments = micro_count + section_count - 1
    scale = 1.0 / math.sqrt(
        micro_count * frames_len * lax.axis_size("fsdp") * lax.axis_size("batch")
    )
    w_in_full, w_out_full = (
        lax.all_gather(w_in[0], "fsdp", axis=0, tiled=True),
        lax.all_gather(w_out[0], "fsdp", axis=0, tiled=True),
    )
    gain_a = gain_pre[0]
    gain_b = gain_mid[0]
    taps = w_depth[0]
    positions = jnp.arange(frames_len, dtype=jnp.int32)

    def frame_padding(micro_slot):
        return (positions < lengths[micro_slot, 0]).astype(jnp.float32).reshape(1, frames_len, 1)

    stored = saved_zeros(micro_count, frames_len, model_width)
    blank = jnp.zeros((1, frames_len, model_width), jnp.bfloat16)
    outgoing = blank
    for moment in range(moments):
        if moment > 0:
            incoming = from_behind(outgoing, "section", 1)
        else:
            incoming = blank
        if moment < micro_count:
            section_input = jnp.where(section_index == 0, frames[moment], incoming)
        else:
            section_input = incoming
        micro_index = moment - section_index
        active = (micro_index >= 0) & (micro_index < micro_count)
        micro_slot = jnp.clip(micro_index, 0, micro_count - 1)

        def advance(operands, micro_slot=micro_slot):
            current, buffers = operands
            result, saved = section_forward(
                current, w_in_full, w_out_full, gain_a, gain_b, taps, frame_padding(micro_slot)
            )
            return (result, put_slot(buffers, saved, micro_slot))

        def bypass(operands):
            return (jnp.zeros_like(operands[0]), operands[1])

        outgoing, stored = lax.cond(active, advance, bypass, (section_input, stored))
    row_buffers = (
        jnp.zeros((micro_count, frames_len, model_width), jnp.bfloat16),
        jnp.zeros((micro_count, frames_len, 2 * model_width), jnp.bfloat16),
        jnp.zeros((micro_count, frames_len, model_width), jnp.bfloat16),
        jnp.zeros((micro_count, frames_len, model_width), jnp.bfloat16),
        jnp.zeros((micro_count, frames_len, model_width), jnp.bfloat16),
    )
    small_sums = (
        jnp.zeros((model_width,), jnp.float32),
        jnp.zeros((model_width,), jnp.float32),
        jnp.zeros(taps.shape, jnp.float32),
    )
    returning = blank
    for moment in range(moments):
        if moment > 0:
            incoming = from_behind(returning, "section", -1)
        else:
            incoming = blank
        if moment < micro_count:
            upstream = jnp.where(section_index == section_count - 1, cotangent[moment], incoming)
        else:
            upstream = incoming
        micro_index = moment - (section_count - 1 - section_index)
        active = (micro_index >= 0) & (micro_index < micro_count)
        micro_slot = jnp.clip(micro_index, 0, micro_count - 1)

        def retreat(operands, micro_slot=micro_slot):
            current, buffers, totals = operands
            padding = frame_padding(micro_slot)
            saved = take_slot(stored, micro_slot)
            input_grad, proj_grad, minor_grads = section_backward(
                current, w_in_full, w_out_full, gain_a, gain_b, taps, padding, saved
            )
            row_values = (saved[2][0], proj_grad[0], saved[9][0], current[0], input_grad[0])
            buffers = put_slot(buffers, row_values, micro_slot)
            totals = tuple((total + extra for total, extra in zip(totals, minor_grads)))
            return (input_grad, buffers, totals)

        def hold(operands):
            return (jnp.zeros_like(operands[0]), operands[1], operands[2])

        returning, row_buffers, small_sums = lax.cond(
            active, retreat, hold, (upstream, row_buffers, small_sums)
        )
    total_rows = micro_count * frames_len
    proj_rows = row_buffers[0].reshape(total_rows, model_width)
    grad_rows = row_buffers[1].reshape(total_rows, 2 * model_width)
    swish_rows = row_buffers[2].reshape(total_rows, model_width)
    upstream_rows = row_buffers[3].reshape(total_rows, model_width)
    term_in = lax.dot_general(
        proj_rows, grad_rows, (((0,), (0,)), ((), ())), preferred_element_type=jnp.float32
    )
    term_out = lax.dot_general(
        swish_rows, upstream_rows, (((0,), (0,)), ((), ())), preferred_element_type=jnp.float32
    )
    rounded_in = lax.optimization_barrier(term_in.astype(jnp.bfloat16)).astype(jnp.float32)
    rounded_out = lax.optimization_barrier(term_out.astype(jnp.bfloat16)).astype(jnp.float32)
    shares = (
        lax.psum_scatter(
            rounded_in.astype(jnp.bfloat16), "fsdp", scatter_dimension=0, tiled=True
        ).astype(jnp.float32),
        lax.psum_scatter(
            rounded_out.astype(jnp.bfloat16), "fsdp", scatter_dimension=0, tiled=True
        ).astype(jnp.float32),
    )
    grad_in, grad_out = (
        lax.psum(shares[0].astype(jnp.bfloat16), "batch").astype(jnp.float32),
        lax.psum(shares[1].astype(jnp.bfloat16), "batch").astype(jnp.float32),
    )
    small_total = lax.psum((small_sums[0], small_sums[1], small_sums[2]), ("fsdp", "batch"))
    input_grads = row_buffers[4].reshape(1, micro_count, 1, frames_len, model_width)
    return (
        input_grads,
        (scale * grad_in)[None],
        (scale * grad_out)[None],
        (scale * small_total[0])[None],
        (scale * small_total[1])[None],
        (scale * small_total[2])[None],
    )


def solution(mesh):
    in_specs = (
        P(None, ("fsdp", "batch"), None, None),
        P(None, ("fsdp", "batch"), None, None),
        P(None, ("fsdp", "batch")),
        P("section", "fsdp", None),
        P("section", "fsdp", None),
        P("section", None),
        P("section", None),
        P("section", None, None),
    )
    out_specs = (
        P("section", None, ("fsdp", "batch"), None, None),
        P("section", "fsdp", None),
        P("section", "fsdp", None),
        P("section", None),
        P("section", None),
        P("section", None, None),
    )
    return jax.shard_map(local, mesh=mesh, in_specs=in_specs, out_specs=out_specs, check_vma=False)
```

profile of v0, /device:TPU:8, one launch (start us, length us, event | category | flops | bytes accessed | tf_op | source)
XLA Modules:
  0.0 1690.2 jit_solution(3717509409260355188)
XLA Ops:
  9.7 112.4 %all-gather.5.cloned.1.call-done = bf16[1,1536,1536]{2,1,0:T(8,128)(2,1)} async-done(((bf16[1,96,1536]{2,1,0:T(8,128)(2,1)}), bf16[1,1536,1536]{2,1,0:T(8,128)(2,1)}) %all-gather.5.cloned.1.call-update) | async-done | bytes 4718608 | tf_op jit(solution)/shard_map/all_gather | solution.py:183
  122.1 204.6 %all-gather.7.cloned.1.call-done = bf16[1,1536,3072]{2,1,0:T(8,128)(2,1)} async-done(((bf16[1,96,3072]{2,1,0:T(8,128)(2,1)}), bf16[1,1536,3072]{2,1,0:T(8,128)(2,1)}) %all-gather.7.cloned.1.call-update) | async-done | bytes 9437200 | tf_op jit(solution)/shard_map/all_gather | solution.py:182
  327.4 25.8 %conditional.14 = (bf16[1,48,1536]{2,1,0:T(8,128)(2,1)}, f32[4,1,48,1536]{3,2,1,0:T(8,128)}, f32[4,1,48,1]{2,3,1,0:T(1,128)}, bf16[4,1,48,1536]{3,2,1,0:T(8,128)...) conditional(s32[]{:T(128)} %convert_element_type.332, ...), branch_computations={%region_0.1_spmd, %region_1.6_spmd} | conditional | flops 688103936 | bytes 49524732 | solution.py:219
  327.9 5.5 convolution_bitcast_fusion
  342.2 4.0 fusion.1
  346.5 1.3 broadcast.1484.clone.2
  353.3 1.3 collective-permute-start
  355.8 17.7 %conditional.15 = (bf16[1,48,1536]{2,1,0:T(8,128)(2,1)}, f32[4,1,48,1536]{3,2,1,0:T(8,128)}, f32[4,1,48,1]{2,3,1,0:T(1,128)}, bf16[4,1,48,1536]{3,2,1,0:T(8,128)...) conditional(s32[]{:T(128)} %convert_element_type.331, ...), branch_computations={%region_6.7_spmd, %region_7.12_spmd} | conditional | flops 687735232 | bytes 22092980 | solution.py:219
  357.8 5.5 convolution_bitcast_fusion.2
  369.5 4.0 fusion.76
  373.5 2.3 collective-permute-start.1
  376.9 17.2 %conditional.16 = (bf16[1,48,1536]{2,1,0:T(8,128)(2,1)}, f32[4,1,48,1536]{3,2,1,0:T(8,128)}, f32[4,1,48,1]{2,3,1,0:T(1,128)}, bf16[4,1,48,1536]{3,2,1,0:T(8,128)...) conditional(s32[]{:T(128)} %convert_element_type.330, ...), branch_computations={%region_12.13_spmd, %region_13.18_spmd} | conditional | flops 687735232 | bytes 21503128 | solution.py:219
  378.5 5.5 convolution_bitcast_fusion.4
  390.2 4.0 fusion.151
  394.1 3.1 collective-permute-start.2
  398.5 16.3 conditional.17
  399.8 5.5 convolution_bitcast_fusion.6
  411.5 3.3 fusion.226
  415.5 7.0 collective-permute-start.3
  424.1 22.3 %collective-permute-start.4 = (bf16[1,48,1536]{2,1,0:T(8,128)(2,1)S(1)}, bf16[1,48,1536]{2,1,0:T(8,128)(2,1)S(1)}, u32[]{:S(2)}, u32[]{:S(2)}) collective-permute-start(bf16[1,48,1536]{2,1,0:T(8,128)(2,1)S(1)} %get-tuple-element.1558), channel_id=1, source_target_pairs={{0,64},{64,128},{128,192},{1,65},{65,129},{129,193},{2,66},{66,130... | collective-permute-start | bytes 442376 | tf_op jit(solution)/shard_map/ppermute | solution.py:14
  447.4 6.9 collective-permute-start.5
  456.2 4.9 conditional.21
  461.1 1.3 collective-permute-start.6
  462.4 21.9 %collective-permute-done.6 = bf16[1,48,1536]{2,1,0:T(8,128)(2,1)S(1)} collective-permute-done((bf16[1,48,1536]{2,1,0:T(8,128)(2,1)S(1)}, bf16[1,48,1536]{2,1,0:T(8,128)(2,1)S(1)}, u32[]{:S(2)}, u32[]{:S(2)}) %collective-permute-start.6) | collective-permute-done | bytes 147488 | tf_op jit(solution)/shard_map/ppermute | solution.py:14
  485.8 1.3 collective-permute-start.7
  487.1 7.6 collective-permute-done.7
  496.2 5.8 collective-permute-start.8
  501.9 119.7 %collective-permute-done.8 = bf16[1,48,1536]{2,1,0:T(8,128)(2,1)S(1)} collective-permute-done((bf16[1,48,1536]{2,1,0:T(8,128)(2,1)}, bf16[1,48,1536]{2,1,0:T(8,128)(2,1)S(1)}, u32[]{:S(2)}, u32[]{:S(2)}) %collective-permute-start.8) | collective-permute-done | bytes 147488 | tf_op jit(solution)/shard_map/ppermute | solution.py:14
  622.2 40.0 %conditional.24 = (bf16[1,48,1536]{2,1,0:T(8,128)(2,1)}, bf16[4,48,1536]{2,1,0:T(8,128)(2,1)}, bf16[4,48,3072]{2,1,0:T(8,128)(2,1)}, bf16[4,48,1536]{2,1,0:T(8,1...) conditional(s32[]{:T(128)} %convert_element_type.322, ...), branch_computations={%region_159.160_spmd, %region_160.198_spmd} | conditional | flops 692822144 | bytes 26455680 | solution.py:261
  622.2 1.6 constant_dynamic-update-slice_fusion.21
  623.9 4.0 fusion.1104
  642.8 3.3 stack.575
  647.9 1.3 compare_convert_fusion.10
  651.9 6.8 fusion.1096
  658.7 1.8 constant_dynamic-update-slice_fusion.20
  660.5 1.7 bitcast_dynamic-update-slice_fusion.55
  663.5 6.8 collective-permute-done.9
  671.0 24.6 %conditional.25 = (bf16[1,48,1536]{2,1,0:T(8,128)(2,1)S(1)}, bf16[4,48,1536]{2,1,0:T(8,128)(2,1)}, bf16[4,48,3072]{2,1,0:T(8,128)(2,1)}, bf16[4,48,1536]{2,1,0:T...) conditional(s32[]{:T(128)} %convert_element_type.321, ...), branch_computations={%region_198.199_spmd, %region_199.237_spmd} | conditional | flops 692748416 | bytes 27118580 | solution.py:261
  671.2 4.0 fusion.1252
  681.2 1.4 compare_convert_fusion.11
  685.2 6.8 fusion.1244
  692.1 1.8 constant_dynamic-update-slice_fusion.22
  693.9 1.7 bitcast_dynamic-update-slice_fusion.57
  696.9 6.7 collective-permute-done.10
  704.2 24.7 %conditional.26 = (bf16[1,48,1536]{2,1,0:T(8,128)(2,1)S(1)}, bf16[4,48,1536]{2,1,0:T(8,128)(2,1)}, bf16[4,48,3072]{2,1,0:T(8,128)(2,1)}, bf16[4,48,1536]{2,1,0:T...) conditional(s32[]{:T(128)} %convert_element_type.320, ...), branch_computations={%region_237.238_spmd, %region_238.276_spmd} | conditional | flops 692748416 | bytes 27118580 | solution.py:261
  704.4 4.0 fusion.1400
  714.4 1.4 compare_convert_fusion.12
  718.5 6.8 fusion.1392
  725.4 1.8 constant_dynamic-update-slice_fusion.24
  727.1 1.7 bitcast_dynamic-update-slice_fusion.59
  730.2 6.6 collective-permute-done.11
  736.8 24.5 %conditional.27 = (bf16[4,48,1536]{2,1,0:T(8,128)(2,1)}, bf16[4,48,3072]{2,1,0:T(8,128)(2,1)}, bf16[4,48,1536]{2,1,0:T(8,128)(2,1)}, bf16[4,48,1536]{2,1,0:T(8,1...) conditional(s32[]{:T(128)} %convert_element_type.319, ...), branch_computations={%region_276.277_spmd, %region_277.315_spmd} | conditional | flops 692748416 | bytes 25938872 | solution.py:261
  737.1 4.0 fusion.1548
  746.6 6.8 fusion.1538
  753.4 1.8 fusion.1555
  759.6 1.7 bitcast_dynamic-update-slice_fusion.61
  761.3 5.0 bitcast_convert_fusion.1
  766.3 7.8 bitcast_convert_fusion
  774.7 100.5 %reduce-scatter.5.cloned.1.call-done = bf16[96,1536]{1,0:T(8,128)(2,1)} async-done(((bf16[1536,1536]{1,0:T(8,128)(2,1)}), bf16[96,1536]{1,0:T(8,128)(2,1)}) %reduce-scatter.5.cloned.1.call-update) | async-done | bytes 294928 | tf_op jit(solution)/shard_map/reduce_scatter | solution.py:281
  875.3 206.3 %reduce-scatter.3.cloned.1.call-done = bf16[96,3072]{1,0:T(8,128)(2,1)} async-done(((bf16[1536,3072]{1,0:T(8,128)(2,1)}), bf16[96,3072]{1,0:T(8,128)(2,1)}) %reduce-scatter.3.cloned.1.call-update) | async-done | bytes 589840 | tf_op jit(solution)/shard_map/reduce_scatter | solution.py:278
  1081.6 300.9 %all-reduce.21 = (f32[1536]{0:T(1024)S(1)}, f32[1536]{0:T(1024)S(1)}) all-reduce(f32[1536]{0:T(1024)S(1)} %get-tuple-element.1639, f32[1536]{0:T(1024)S(1)} %get-tuple-element.1640), channel_id=1, replica_groups=mesh['section'=4,'fsdp'=16,'batch'=4] {'fsdp','batch'}, use_global_device_ids=true, to_apply=%region_319.320 | all-reduce | flops 3072 | bytes 24576 | tf_op jit(solution)/shard_map/psum | solution.py:289
  1383.6 244.8 %all-reduce.26.cloned.1.call-done = f32[31,1536]{1,0:T(8,128)} async-done(((f32[31,1536]{1,0:T(8,128)}), f32[31,1536]{1,0:T(8,128)}) %all-reduce.26.cloned.1.call-update) | async-done | bytes 190480 | tf_op jit(solution)/shard_map/psum | solution.py:289
  1630.1 49.6 %all-reduce.28.cloned.1.call-done = (bf16[96,3072]{1,0:T(8,128)(2,1)}, bf16[96,1536]{1,0:T(8,128)(2,1)}) async-done(((bf16[96,3072]{1,0:T(8,128)(2,1)}, bf16[96,1536]{1,0:T(8,128)(2,1)}), (bf16[96,3072]{1,0:T(8,128)(2,1)}, bf16[96,1536]{1,0:T(8,128)(2,1)})) %all-reduce.28.cloned.1.call-update) | async-done | bytes 884752 | tf_op jit(solution)/shard_map/psum | solution.py:286
  1679.7 2.2 multiply_bitcast_fusion
  (405 shorter events, 114.6 us)
Async XLA Ops:
  7.2 319.6 %copy-start.13 = (bf16[4,1,48,1536]{3,2,1,0:T(8,128)(2,1)S(1)}, bf16[4,1,48,1536]{3,2,1,0:T(8,128)(2,1)}, u32[]{:S(2)}) copy-start(bf16[4,1,48,1536]{3,2,1,0:T(8,128)(2,1)} %param.36) | copy-start | bytes 1769476
  7.2 319.6 %copy-start.24 = (s32[4,1]{0,1:T(1,128)S(1)}, s32[4,1]{0,1:T(1,128)}, u32[]{:S(2)}) copy-start(s32[4,1]{0,1:T(1,128)} %param.38) | copy-start | bytes 52
  7.2 319.6 %copy-start.7 = (f32[1,1536]{1,0:T(1,128)S(1)}, f32[1,1536]{1,0:T(1,128)}, u32[]{:S(2)}) copy-start(f32[1,1536]{1,0:T(1,128)} %param.41) | copy-start | bytes 18436
  7.2 319.6 %copy-start.8 = (f32[1,1536]{1,0:T(1,128)S(1)}, f32[1,1536]{1,0:T(1,128)}, u32[]{:S(2)}) copy-start(f32[1,1536]{1,0:T(1,128)} %param.42) | copy-start | bytes 18436
  7.2 114.8 %all-gather.5.cloned.1.call-start = ((), (), s32[]{:S(2)}) async-start(), calls=%async_computation.5 | async-start | bytes 5013504 | tf_op jit(solution)/shard_map/all_gather | solution.py:183
  7.9 318.7 %all-gather.7.cloned.1.call-start = ((), (), s32[]{:S(2)}) async-start(), calls=%async_computation.6 | async-start | bytes 10027008 | tf_op jit(solution)/shard_map/all_gather | solution.py:182
  8.7 866.6 %reduce-scatter.5.cloned.1.call-start = ((), (), s32[]{:S(2)}) async-start(), calls=%async_computation.3 | async-start | bytes 5013504 | tf_op jit(solution)/shard_map/reduce_scatter | solution.py:281
  326.8 0.7 copy-start.5
  340.5 5.8 copy-start
  346.2 1.6 copy-start.18
  346.5 2.9 copy-start.2
  348.5 4.7 copy-start.1
  348.5 4.7 copy-start.19
  350.2 3.1 copy-start.3
  353.3 2.5 collective-permute-start
  355.8 0.7 copy-start.15
  373.5 3.5 collective-permute-start.1
  394.1 4.3 collective-permute-start.2
  414.8 0.7 copy-start.17
  415.5 8.2 collective-permute-start.3
  424.1 23.3 %collective-permute-start.4 = (bf16[1,48,1536]{2,1,0:T(8,128)(2,1)S(1)}, bf16[1,48,1536]{2,1,0:T(8,128)(2,1)S(1)}, u32[]{:S(2)}, u32[]{:S(2)}) collective-permute-start(bf16[1,48,1536]{2,1,0:T(8,128)(2,1)S(1)} %get-tuple-element.1558), channel_id=1, source_target_pairs={{0,64},{64,128},{128,192},{1,65},{65,129},{129,193},{2,66},{66,130... | collective-permute-start | bytes 442376 | tf_op jit(solution)/shard_map/ppermute | solution.py:14
  447.4 7.9 collective-permute-start.5
  455.3 0.9 copy-start.6
  455.3 29.6 %copy-start.20 = (f32[4,1,48,1]{2,3,1,0:T(1,128)}, f32[4,1,48,1]{2,3,1,0:T(1,128)S(1)}, u32[]{:S(2)}) copy-start(f32[4,1,48,1]{2,3,1,0:T(1,128)S(1)} %get-tuple-element.2820) | copy-start | bytes 2308
  461.1 23.2 %collective-permute-start.6 = (bf16[1,48,1536]{2,1,0:T(8,128)(2,1)S(1)}, bf16[1,48,1536]{2,1,0:T(8,128)(2,1)S(1)}, u32[]{:S(2)}, u32[]{:S(2)}) collective-permute-start(bf16[1,48,1536]{2,1,0:T(8,128)(2,1)S(1)} %get-tuple-element.1588), channel_id=1, source_target_pairs={{64,0},{128,64},{192,128},{65,1},{129,65},{193,129},{66,2},{130,66... | collective-permute-start | bytes 442376 | tf_op jit(solution)/shard_map/ppermute | solution.py:14
  485.8 8.9 collective-permute-start.7
  496.2 125.5 %collective-permute-start.8 = (bf16[1,48,1536]{2,1,0:T(8,128)(2,1)}, bf16[1,48,1536]{2,1,0:T(8,128)(2,1)S(1)}, u32[]{:S(2)}, u32[]{:S(2)}) collective-permute-start(bf16[1,48,1536]{2,1,0:T(8,128)(2,1)} %get-tuple-element.1606), channel_id=1, source_target_pairs={{64,0},{128,64},{192,128},{65,1},{129,65},{193,129},{66,2},{130,66... | collective-permute-start | bytes 442376 | tf_op jit(solution)/shard_map/ppermute | solution.py:14
  651.8 6.8 copy-start.23
  662.2 8.1 collective-permute-start.9
  671.1 4.1 copy-start.11
  678.9 1.6 copy-start.26
  685.2 6.9 copy-start.12
  695.6 8.0 collective-permute-start.10
  704.4 4.1 copy-start.9
  712.2 1.6 copy-start.27
  718.5 6.9 copy-start.10
  728.9 7.9 collective-permute-start.11
  741.1 2.3 copy-start.28
  761.3 5.0 copy-start.4
  766.3 315.2 %reduce-scatter.3.cloned.1.call-start = ((), (), s32[]{:S(2)}) async-start(), calls=%async_computation.2 | async-start | bytes 10027008 | tf_op jit(solution)/shard_map/reduce_scatter | solution.py:278
  774.1 854.3 %all-reduce.26.cloned.1.call-start = ((), (), s32[]{:S(2)}) async-start(), calls=%async_computation.4 | async-start | bytes 393216 | tf_op jit(solution)/shard_map/psum | solution.py:289
  774.7 905.0 %all-reduce.28.cloned.1.call-start = ((), (), s32[]{:S(2)}) async-start(), calls=%async_computation.7 | async-start | bytes 1769472 | tf_op jit(solution)/shard_map/psum | solution.py:286
  1679.7 2.3 copy-start.14
Sparse Core Ops, SparseCore 0:
  9.8 112.1 all-gather.4
  123.8 202.7 all-gather.6
  766.4 108.8 reduce-scatter.4
  877.7 203.8 reduce-scatter.2
  1084.6 543.7 all-reduce.25
  1630.8 48.9 all-reduce.27
where the time goes:
time: 1700 us; the launch traced here: 1690 us
  waiting for transfers between devices  1100 us (65%)
  blocking collectives  301 us (18%)
  matrix products  93.3 us (5%)
  other arithmetic  63.8 us (4%)
  local copies, waits for them, and re-layouts  62.4 us (4%)
  starting transfers between devices  55.3 us (3%)
    psum x1, blocking collectives, local(): lax.psum((small_sums[0], small_sums[1], small_sums[2]), ('fsdp', 'batch'))  301 us
    psum x1, waiting for transfers between devices, local(): lax.psum((small_sums[0], small_sums[1], small_sums[2]), ('fsdp', 'batch'))  245 us
    reduce_scatter x1, waiting for transfers between devices, local(): lax.psum_scatter(rounded_in.astype(jnp.bfloat16), 'fsdp', scatter_dimensi...  206 us
    all_gather x1, waiting for transfers between devices, local(): lax.all_gather(w_in[0], 'fsdp', axis=0, tiled=True)  205 us
    ppermute x12, waiting for transfers between devices, from_behind(): return lax.ppermute(x, axis, pairs)  176 us
    all_gather x1, waiting for transfers between devices, local(): lax.all_gather(w_out[0], 'fsdp', axis=0, tiled=True)  112 us
    reduce_scatter x1, waiting for transfers between devices, local(): lax.psum_scatter(rounded_out.astype(jnp.bfloat16), 'fsdp', scatter_dimens...  101 us
    ppermute x12, starting transfers between devices, from_behind(): return lax.ppermute(x, axis, pairs)  55.1 us
  transfers between devices with their start and end apart: 18, of which 18 were waited for; matrix products, arithmetic and copies ran while one was open for 1% of the time, Pallas kernels for 0%

commit v1 on v0

--- a/solution.py
+++ b/solution.py
@@ -6,12 +6,91 @@
 from jax.sharding import PartitionSpec as P
 
 epsilon = 1e-05
+PAIR = 2
 
 
 def from_behind(x, axis, by):
     peers = lax.axis_size(axis)
     pairs = [(i, i + by) for i in range(peers) if 0 <= i + by < peers]
     return lax.ppermute(x, axis, pairs)
+
+
+def rotate(x, axis, by):
+    peers = lax.axis_size(axis)
+    return lax.ppermute(x, axis, [(i, (i + by) % peers) for i in range(peers)])
+
+
+def swap_pair(x):
+    peers = lax.axis_size("fsdp")
+    return lax.ppermute(x, "fsdp", [(i, i ^ 1) for i in range(peers)])
+
+
+def ring_position():
+    index = lax.axis_index("fsdp")
+    return index // PAIR, index % PAIR
+
+
+def pick(stacked, index):
+    return lax.dynamic_index_in_dim(stacked, index, 0, keepdims=False)
+
+
+def gather_rows(shard):
+    ring = lax.axis_size("fsdp") // PAIR
+    half = ring // 2
+    at, side = ring_position()
+    other = swap_pair(shard)
+    pair = jnp.where(side == 0, jnp.stack([shard, other]), jnp.stack([other, shard]))
+    whole = jnp.zeros((ring,) + pair.shape, pair.dtype)
+
+    def put(whole, piece, offset):
+        return lax.dynamic_update_slice(whole, piece[None], ((at + offset) % ring, 0, 0, 0))
+
+    whole = put(whole, pair, 0)
+    up, down = pair, pair
+    for hop in range(1, half):
+        up = rotate(up, "fsdp", PAIR)
+        down = rotate(down, "fsdp", -PAIR)
+        whole = put(put(whole, up, ring - hop), down, hop)
+    far_up = rotate(up[0], "fsdp", PAIR)
+    far_down = rotate(down[1], "fsdp", -PAIR)
+    whole = put(whole, jnp.stack([far_up, far_down]), half)
+    return whole.reshape((ring * PAIR,) + shard.shape)
+
+
+def scatter_rows(terms):
+    ring = lax.axis_size("fsdp") // PAIR
+    half = ring // 2
+    at, side = ring_position()
+    pairs = terms.reshape((ring, PAIR) + terms.shape[1:])
+    far = pick(pairs, (at + half) % ring)
+    up = rotate(far[0], "fsdp", PAIR)
+    down = rotate(far[1], "fsdp", -PAIR)
+    for hop in range(half - 1, 0, -1):
+        mine_up = pick(pairs, (at + hop) % ring).astype(jnp.float32)
+        mine_down = pick(pairs, (at + ring - hop) % ring).astype(jnp.float32)
+        up = up.astype(jnp.float32)
+        down = down.astype(jnp.float32)
+        if hop == half - 1:
+            up = jnp.stack([mine_up[0] + up, mine_up[1]])
+            down = jnp.stack([mine_down[0], mine_down[1] + down])
+        else:
+            up = mine_up + up
+            down = mine_down + down
+        up = rotate(up.astype(terms.dtype), "fsdp", PAIR)
+        down = rotate(down.astype(terms.dtype), "fsdp", -PAIR)
+    total = pick(pairs, at).astype(jnp.float32) + up.astype(jnp.float32) + down.astype(jnp.float32)
+    mine = jnp.where(side == 0, total[0], total[1])
+    theirs = jnp.where(side == 0, total[1], total[0])
+    return mine + swap_pair(theirs.astype(terms.dtype)).astype(jnp.float32)
+
+
+def batch_copies(x):
+    return x, rotate(x, "batch", 1), rotate(x, "batch", 2), rotate(x, "batch", 3)
+
+
+def sum_batch(x):
+    own, left, far, right = (part.astype(jnp.float32) for part in batch_copies(x))
+    return (own + far) + (left + right)
 
 
 def layer_norm(values):
@@ -29,23 +108,14 @@
     ) * inv_scale
 
 
-def project(left, right):
-    batch_rows, length, inner = left.shape
-    flat = jnp.dot(
-        left.reshape(batch_rows * length, inner), right, preferred_element_type=jnp.float32
-    )
-    return flat.reshape(batch_rows, length, right.shape[1])
-
-
-def project_back(left, right):
-    batch_rows, length, inner = left.shape
-    flat = lax.dot_general(
-        left.reshape(batch_rows * length, inner),
-        right,
-        (((1,), (1,)), ((), ())),
-        preferred_element_type=jnp.float32,
-    )
-    return flat.reshape(batch_rows, length, right.shape[0])
+def rows_by(left, right):
+    return jnp.dot(left, right, preferred_element_type=jnp.float32)
+
+
+def rows_back(left, right):
+    return lax.dot_general(
+        left, right, (((1,), (1,)), ((), ())), preferred_element_type=jnp.float32
+    )
 
 
 def depthwise(values, taps):
@@ -60,19 +130,19 @@
 
 
 def section_forward(frames, w_in, w_out, gain_a, gain_b, taps, padding):
-    model_width = frames.shape[-1]
     source = frames.astype(jnp.float32)
     normed_in, inv_in = layer_norm(source)
     projected = (normed_in * gain_a).astype(jnp.bfloat16)
-    both = project(projected, w_in)
-    glu_value = both[..., :model_width]
-    glu_gate = jax.nn.sigmoid(both[..., model_width:])
+    parts = w_in.shape[0]
+    both = [rows_by(projected[0], w_in[part])[None] for part in range(parts)]
+    glu_value = jnp.concatenate(both[: parts // 2], axis=-1)
+    glu_gate = jax.nn.sigmoid(jnp.concatenate(both[parts // 2 :], axis=-1))
     gated = glu_value * glu_gate * padding
     conv_out = depthwise(gated, taps)
     normed_mid, inv_mid = layer_norm(conv_out)
     scaled_mid = normed_mid * gain_b
     swished = (scaled_mid * jax.nn.sigmoid(scaled_mid)).astype(jnp.bfloat16)
-    result = (source + project(swished, w_out)).astype(jnp.bfloat16)
+    result = (source + rows_by(swished[0], w_out)[None]).astype(jnp.bfloat16)
     return (
         result,
         (
@@ -106,7 +176,7 @@
     kernel = taps.shape[0]
     half = kernel // 2
     length = upstream.shape[1]
-    swish_grad = project_back(upstream, w_out)
+    swish_grad = rows_back(upstream[0], w_out)[None]
     sigmoid_mid = jax.nn.sigmoid(scaled_mid)
     scaled_grad = swish_grad * (sigmoid_mid + scaled_mid * sigmoid_mid * (1.0 - sigmoid_mid))
     gain_b_grad = jnp.sum(scaled_grad * normed_mid, axis=(0, 1))
@@ -129,7 +199,11 @@
     value_grad = gated_grad * glu_gate
     gate_grad = gated_grad * glu_value * glu_gate * (1.0 - glu_gate)
     proj_grad = jnp.concatenate([value_grad, gate_grad], axis=-1).astype(jnp.bfloat16)
-    input_side = project_back(proj_grad, w_in)
+    parts, unused, width = w_in.shape
+    input_side = sum(
+        rows_back(proj_grad[0, :, part * width : (part + 1) * width], w_in[part])
+        for part in range(parts)
+    )[None]
     gain_a_grad = jnp.sum(input_side * normed_in, axis=(0, 1))
     input_grad = (
         upstream.astype(jnp.float32) + norm_grad(input_side * gain_a, normed_in, inv_in)
@@ -166,6 +240,43 @@
     return jax.tree.map(
         lambda buffer: lax.dynamic_index_in_dim(buffer, micro_slot, 0, keepdims=False), buffers
     )
+
+
+def gather_weights(w_in, w_out):
+    quarters = lax.axis_size("batch")
+    width = w_in.shape[1] // quarters
+    mine = lax.dynamic_slice_in_dim(w_in, lax.axis_index("batch") * width, width, 1)
+    mine = gather_rows(mine)
+    mine = mine.reshape(-1, width)
+    w_in_full = lax.all_gather(mine, "batch", axis=0, tiled=False)
+    w_out_full = gather_rows(w_out).reshape(-1, w_out.shape[1])
+    return w_in_full, w_out_full
+
+
+def reduce_weights(term_in, term_out, small, scale):
+    quarters, depth, width = term_in.shape
+    fsdp = lax.axis_size("fsdp")
+    rows = depth // fsdp
+    small_rows = -(-small.shape[0] // fsdp)
+    small_pad = jnp.pad(small, ((0, small_rows * fsdp - small.shape[0]), (0, 0)))
+    extra = jnp.pad(
+        small_pad.reshape(fsdp, small_rows, depth).astype(jnp.bfloat16),
+        ((0, 0), (0, 16 - small_rows), (0, 0)),
+    )
+    out_terms = jnp.concatenate([term_out.reshape(fsdp, rows, depth), extra], axis=1)
+    in_quarter = lax.psum_scatter(term_in, "batch", scatter_dimension=0, tiled=False)
+    out_share = scatter_rows(out_terms)
+    out_sum = sum_batch(out_share.astype(jnp.bfloat16))
+    grad_out = scale * out_sum[:rows]
+    small_sum = gather_rows(scale * out_sum[rows : rows + small_rows])
+    small_sum = small_sum.reshape(fsdp * small_rows, depth)[: small.shape[0]]
+    in_share = scatter_rows(in_quarter.reshape(fsdp, rows, width)).astype(jnp.bfloat16)
+    copies = jnp.stack(batch_copies(in_share))
+    here = lax.axis_index("batch")
+    grad_in = jnp.concatenate(
+        [pick(copies, (here + quarters - part) % quarters) for part in range(quarters)], axis=1
+    )
+    return scale * grad_in.astype(jnp.float32), grad_out, small_sum
 
 
 def local(frames, cotangent, lengths, w_in, w_out, gain_pre, gain_mid, w_depth):
@@ -178,10 +289,7 @@
     scale = 1.0 / math.sqrt(
         micro_count * frames_len * lax.axis_size("fsdp") * lax.axis_size("batch")
     )
-    w_in_full, w_out_full = (
-        lax.all_gather(w_in[0], "fsdp", axis=0, tiled=True),
-        lax.all_gather(w_out[0], "fsdp", axis=0, tiled=True),
-    )
+    w_in_full, w_out_full = gather_weights(w_in[0], w_out[0])
     gain_a = gain_pre[0]
     gain_b = gain_mid[0]
     taps = w_depth[0]
@@ -262,39 +370,31 @@
             active, retreat, hold, (upstream, row_buffers, small_sums)
         )
     total_rows = micro_count * frames_len
+    parts, unused, width = w_in_full.shape
     proj_rows = row_buffers[0].reshape(total_rows, model_width)
     grad_rows = row_buffers[1].reshape(total_rows, 2 * model_width)
     swish_rows = row_buffers[2].reshape(total_rows, model_width)
     upstream_rows = row_buffers[3].reshape(total_rows, model_width)
-    term_in = lax.dot_general(
-        proj_rows, grad_rows, (((0,), (0,)), ((), ())), preferred_element_type=jnp.float32
-    )
-    term_out = lax.dot_general(
-        swish_rows, upstream_rows, (((0,), (0,)), ((), ())), preferred_element_type=jnp.float32
-    )
-    rounded_in = lax.optimization_barrier(term_in.astype(jnp.bfloat16)).astype(jnp.float32)
-    rounded_out = lax.optimization_barrier(term_out.astype(jnp.bfloat16)).astype(jnp.float32)
-    shares = (
-        lax.psum_scatter(
-            rounded_in.astype(jnp.bfloat16), "fsdp", scatter_dimension=0, tiled=True
-        ).astype(jnp.float32),
-        lax.psum_scatter(
-            rounded_out.astype(jnp.bfloat16), "fsdp", scatter_dimension=0, tiled=True
-        ).astype(jnp.float32),
-    )
-    grad_in, grad_out = (
-        lax.psum(shares[0].astype(jnp.bfloat16), "batch").astype(jnp.float32),
-        lax.psum(shares[1].astype(jnp.bfloat16), "batch").astype(jnp.float32),
-    )
-    small_total = lax.psum((small_sums[0], small_sums[1], small_sums[2]), ("fsdp", "batch"))
+
+    def term(left, right):
+        return lax.dot_general(
+            left, right, (((0,), (0,)), ((), ())), preferred_element_type=jnp.float32
+        ).astype(jnp.bfloat16)
+
+    term_in = jnp.stack(
+        [term(proj_rows, grad_rows[:, part * width : (part + 1) * width]) for part in range(parts)]
+    )
+    term_out = term(swish_rows, upstream_rows)
+    small = jnp.concatenate([small_sums[0][None], small_sums[1][None], small_sums[2]], axis=0)
+    grad_in, grad_out, small_total = reduce_weights(term_in, term_out, small, scale)
     input_grads = row_buffers[4].reshape(1, micro_count, 1, frames_len, model_width)
     return (
         input_grads,
-        (scale * grad_in)[None],
-        (scale * grad_out)[None],
-        (scale * small_total[0])[None],
-        (scale * small_total[1])[None],
-        (scale * small_total[2])[None],
+        grad_in[None],
+        grad_out[None],
+        small_total[0:1],
+        small_total[1:2],
+        small_total[2:][None],
     )
 
 

time: 1700 us -> 815 us (0.48)
  waiting for transfers between devices: 1100 us -> 381 us
  blocking collectives: 301 us -> 0 us
  starting transfers between devices: 55.3 us -> 143 us
  other arithmetic: 63.8 us -> 85.8 us
  matrix products: 93.3 us -> 115 us
    reduce_scatter x2 -> x1, waiting for transfers between devices: 307 us -> 0.02 us  [reduce_weights(): lax.psum_scatter(term_in, 'batch', scatter_dimension=0, tiled=False)]
    psum x1 -> x0, blocking collectives: 301 us -> none  [local(): lax.psum((small_sums[0], small_sums[1], small_sums[2]), ('fsdp', 'batch'))]
    psum x2 -> x0, waiting for transfers between devices: 294 us -> none  [the longest x1 245 us: local(): lax.psum((small_sums[0], small_sums[1], small_sums[2]), ('fsdp', 'batch'))]
    all_gather x2 -> x1, waiting for transfers between devices: 317 us -> 34.1 us  [gather_weights(): w_in_full = lax.all_gather(mine, 'batch', axis=0, tiled=False)]
    ppermute x0 -> x51, waiting for transfers between devices: none -> 165 us  [the longest x46 141 us: rotate(): return lax.ppermute(x, axis, [(i, (i + by) % peers) for i in range(peers)])]
    ppermute x0 -> x51, starting transfers between devices: none -> 84 us  [the longest x46 79.3 us: rotate(): return lax.ppermute(x, axis, [(i, (i + by) % peers) for i in range(peers)])]
    dot_general x18 -> x45, matrix products: 93.3 us -> 115 us  [the longest x20 52.2 us: rows_by(): return jnp.dot(left, right, preferred_element_type=jnp.float32)]
  transfers between devices with their start and end apart: 18 -> 65, of which waited for: 18 -> 47; matrix products, arithmetic and copies ran while one was open for 1% -> 3% of each run, Pallas kernels for 0% -> 0%
where the time goes in v1:
time: 815 us; the launch traced here: 803 us
  waiting for transfers between devices  381 us (47%)
  starting transfers between devices  143 us (18%)
  matrix products  115 us (14%)
  other arithmetic  85.8 us (11%)
  local copies, waits for them, and re-layouts  58.3 us (7%)
  between operations  15.4 us (2%)
    ppermute x12, waiting for transfers between devices, from_behind(): return lax.ppermute(x, axis, pairs)  182 us
    ppermute x46, waiting for transfers between devices, rotate(): return lax.ppermute(x, axis, [(i, (i + by) % peers) for i in range(peers)])  141 us
    ppermute x46, starting transfers between devices, rotate(): return lax.ppermute(x, axis, [(i, (i + by) % peers) for i in range(peers)])  79.3 us
    ppermute x12, starting transfers between devices, from_behind(): return lax.ppermute(x, axis, pairs)  58.6 us
    dot_general x20, matrix products, rows_by(): return jnp.dot(left, right, preferred_element_type=jnp.float32)  52.2 us
    dot_general x20, matrix products, rows_back(): lax.dot_general(left, right, (((1,), (1,)), ((), ())), preferred_element_...  52.2 us
    all_gather x1, waiting for transfers between devices, gather_weights(): w_in_full = lax.all_gather(mine, 'batch', axis=0, tiled=False)  34.1 us
    dynamic_update_slice x31, other arithmetic, put_slot(): lax.dynamic_update_index_in_dim(buffer, value, micro_slot, 0)  33.1 us
  transfers between devices with their start and end apart: 65, of which 47 were waited for; matrix products, arithmetic and copies ran while one was open for 3% of the time, Pallas kernels for 0%

profile of v1, /device:TPU:8, one launch (start us, length us, event | category | flops | bytes accessed | tf_op | source)
XLA Modules:
  0.0 803.3 jit_solution(14332291004361967542)
XLA Ops:
  10.5 3.4 collective-permute-done.9
  16.6 3.9 collective-permute-start.11
  20.8 6.1 collective-permute-done.10
  27.0 3.2 collective-permute-start.13
  31.2 4.4 collective-permute-done.12
  35.6 3.2 collective-permute-start.15
  38.9 4.6 collective-permute-done.14
  43.7 3.3 collective-permute-start.17
  52.1 6.3 collective-permute-done
  58.6 3.4 collective-permute-start.2
  65.6 7.3 collective-permute-done.1
  73.8 3.6 collective-permute-start.4
  78.2 10.2 %collective-permute-done.3 = bf16[2,96,1536]{2,1,0:T(8,128)(2,1)S(1)} collective-permute-done((bf16[2,96,1536]{2,1,0:T(8,128)(2,1)S(1)}, bf16[2,96,1536]{2,1,0:T(8,128)(2,1)S(1)}, u32[]{:S(2)}, u32[]{:S(2)}) %collective-permute-start.3) | collective-permute-done | bytes 589856 | tf_op jit(solution)/shard_map/ppermute | solution.py:20
  93.7 9.2 %collective-permute-done.5 = bf16[2,96,1536]{2,1,0:T(8,128)(2,1)S(1)} collective-permute-done((bf16[2,96,1536]{2,1,0:T(8,128)(2,1)S(1)}, bf16[2,96,1536]{2,1,0:T(8,128)(2,1)S(1)}, u32[]{:S(2)}, u32[]{:S(2)}) %collective-permute-start.5) | collective-permute-done | bytes 589856 | tf_op jit(solution)/shard_map/ppermute | solution.py:20
  112.5 34.1 %all-gather.2.cloned.1.call-done = bf16[4,1536,768]{2,1,0:T(8,128)(2,1)} async-done(((bf16[1,1536,768]{2,1,0:T(8,128)(2,1)}), bf16[4,1536,768]{2,1,0:T(8,128)(2,1)}) %all-gather.2.cloned.1.call-update) | async-done | bytes 9437200 | tf_op jit(solution)/shard_map/all_gather | solution.py:251
  146.8 32.9 %conditional.14 = (bf16[1,48,1536]{2,1,0:T(8,128)(2,1)}, f32[4,1,48,1536]{3,2,1,0:T(8,128)}, f32[4,1,48,1]{2,3,1,0:T(1,128)}, bf16[4,1,48,1536]{3,2,1,0:T(8,128)...) conditional(s32[]{:T(128)} %convert_element_type.518, ...), branch_computations={%region_0.1_spmd, %region_1.6_spmd} | conditional | flops 690020864 | bytes 52937868 | solution.py:327
  165.4 4.4 fusion.13
  182.1 24.5 %conditional.15 = (bf16[1,48,1536]{2,1,0:T(8,128)(2,1)}, f32[4,1,48,1536]{3,2,1,0:T(8,128)}, f32[4,1,48,1]{2,3,1,0:T(1,128)}, bf16[4,1,48,1536]{3,2,1,0:T(8,128)...) conditional(s32[]{:T(128)} %convert_element_type.517, ...), branch_computations={%region_6.7_spmd, %region_7.12_spmd} | conditional | flops 689578432 | bytes 25214604 | solution.py:327
  202.6 4.0 fusion.114
  210.1 24.1 %conditional.16 = (bf16[1,48,1536]{2,1,0:T(8,128)(2,1)}, f32[4,1,48,1536]{3,2,1,0:T(8,128)}, f32[4,1,48,1]{2,3,1,0:T(1,128)}, bf16[4,1,48,1536]{3,2,1,0:T(8,128)...) conditional(s32[]{:T(128)} %convert_element_type.516, ...), branch_computations={%region_12.13_spmd, %region_13.18_spmd} | conditional | flops 689578432 | bytes 25214604 | solution.py:327
  230.2 4.0 fusion.215
  234.2 3.2 collective-permute-start.20
  238.5 21.1 %conditional.17 = (bf16[1,48,1536]{2,1,0:T(8,128)(2,1)}, f32[4,1,48,1536]{3,2,1,0:T(8,128)}, f32[4,1,48,1]{2,3,1,0:T(1,128)}, bf16[4,1,48,1536]{3,2,1,0:T(8,128)...) conditional(s32[]{:T(128)} %convert_element_type.515, ...), branch_computations={%region_18.19_spmd, %region_19.24_spmd} | conditional | flops 689578432 | bytes 25212052 | solution.py:327
  255.6 4.0 fusion.316
  259.6 7.0 collective-permute-start.21
  268.5 26.4 %collective-permute-start.22 = (bf16[1,48,1536]{2,1,0:T(8,128)(2,1)}, bf16[1,48,1536]{2,1,0:T(8,128)(2,1)S(1)}, u32[]{:S(2)}, u32[]{:S(2)}) collective-permute-start(bf16[1,48,1536]{2,1,0:T(8,128)(2,1)} %get-tuple-element.1569), channel_id=1, source_target_pairs={{0,64},{64,128},{128,192},{1,65},{65,129},{129,193},{2,66},{66,130... | collective-permute-start | bytes 442376 | tf_op jit(solution)/shard_map/ppermute | solution.py:15
  297.0 7.0 collective-permute-start.23
  305.7 4.9 conditional.21
  312.0 26.0 %collective-permute-done.24 = bf16[1,48,1536]{2,1,0:T(8,128)(2,1)S(1)} collective-permute-done((bf16[1,48,1536]{2,1,0:T(8,128)(2,1)S(1)}, bf16[1,48,1536]{2,1,0:T(8,128)(2,1)S(1)}, u32[]{:S(2)}, u32[]{:S(2)}) %collective-permute-start.24) | collective-permute-done | bytes 147488 | tf_op jit(solution)/shard_map/ppermute | solution.py:15
  340.2 7.3 collective-permute-done.25
  348.6 4.9 collective-permute-start.26
  353.5 121.5 %collective-permute-done.26 = bf16[1,48,1536]{2,1,0:T(8,128)(2,1)S(1)} collective-permute-done((bf16[1,48,1536]{2,1,0:T(8,128)(2,1)S(1)}, bf16[1,48,1536]{2,1,0:T(8,128)(2,1)S(1)}, u32[]{:S(2)}, u32[]{:S(2)}) %collective-permute-start.26) | collective-permute-done | bytes 147488 | tf_op jit(solution)/shard_map/ppermute | solution.py:15
  475.5 32.4 %conditional.24 = (bf16[1,48,1536]{2,1,0:T(8,128)(2,1)S(1)}, bf16[4,48,1536]{2,1,0:T(8,128)(2,1)}, bf16[4,48,3072]{2,1,0:T(8,128)(2,1)}, bf16[4,48,1536]{2,1,0:T...) conditional(s32[]{:T(128)} %convert_element_type.508, ...), branch_computations={%region_159.160_spmd, %region_160.198_spmd} | conditional | flops 692453504 | bytes 28226496 | solution.py:369
  477.2 4.0 fusion.1351
  509.2 6.6 collective-permute-done.27
  516.3 27.0 %conditional.25 = (bf16[1,48,1536]{2,1,0:T(8,128)(2,1)}, bf16[4,48,1536]{2,1,0:T(8,128)(2,1)}, bf16[4,48,3072]{2,1,0:T(8,128)(2,1)}, bf16[4,48,1536]{2,1,0:T(8,1...) conditional(s32[]{:T(128)} %convert_element_type.507, ...), branch_computations={%region_198.199_spmd, %region_199.237_spmd} | conditional | flops 692379776 | bytes 28890100 | solution.py:369
  516.6 4.0 fusion.1515
  544.6 6.9 collective-permute-done.28
  552.0 27.0 %conditional.26 = (bf16[1,48,1536]{2,1,0:T(8,128)(2,1)}, bf16[4,48,1536]{2,1,0:T(8,128)(2,1)}, bf16[4,48,3072]{2,1,0:T(8,128)(2,1)}, bf16[4,48,1536]{2,1,0:T(8,1...) conditional(s32[]{:T(128)} %convert_element_type.506, ...), branch_computations={%region_237.238_spmd, %region_238.276_spmd} | conditional | flops 692379776 | bytes 28890100 | solution.py:369
  552.2 4.0 fusion.1679
  580.3 6.9 collective-permute-done.29
  587.1 22.9 %conditional.27 = (bf16[4,48,3072]{2,1,0:T(8,128)(2,1)}, bf16[4,48,1536]{2,1,0:T(8,128)(2,1)}, bf16[4,48,1536]{2,1,0:T(8,128)(2,1)}, f32[31,1536]{1,0:T(8,128)S(...) conditional(s32[]{:T(128)} %convert_element_type.505, ...), branch_computations={%region_276.277_spmd, %region_277.315_spmd} | conditional | flops 692379776 | bytes 65459064 | solution.py:369
  587.6 4.2 fusion.1843
  617.9 4.7 pad_maximum_fusion.7
  626.0 3.6 collective-permute-start.46
  629.6 4.7 collective-permute-done.46
  634.5 3.8 collective-permute-start.47
  641.2 7.8 collective-permute-done.47
  649.0 7.8 collective-permute-done.43
  660.5 8.9 %collective-permute-done.44 = bf16[2,112,1536]{2,1,0:T(8,128)(2,1)S(1)} collective-permute-done((bf16[2,112,1536]{2,1,0:T(8,128)(2,1)S(1)}, bf16[2,112,1536]{2,1,0:T(8,128)(2,1)S(1)}, u32[]{:S(2)}, u32[]{:S(2)}) %collective-permute-start.44) | collective-permute-done | bytes 688160 | tf_op jit(solution)/shard_map/ppermute | solution.py:20
  669.9 3.3 collective-permute-start.49
  673.2 8.8 %collective-permute-done.45 = bf16[2,112,1536]{2,1,0:T(8,128)(2,1)S(1)} collective-permute-done((bf16[2,112,1536]{2,1,0:T(8,128)(2,1)S(1)}, bf16[2,112,1536]{2,1,0:T(8,128)(2,1)S(1)}, u32[]{:S(2)}, u32[]{:S(2)}) %collective-permute-start.45) | collective-permute-done | bytes 688160 | tf_op jit(solution)/shard_map/ppermute | solution.py:20
  684.3 6.7 collective-permute-done.50
  697.5 10.0 %collective-permute-done.51 = bf16[112,1536]{1,0:T(8,128)(2,1)S(1)} collective-permute-done((bf16[112,1536]{1,0:T(8,128)(2,1)S(1)}, bf16[112,1536]{1,0:T(8,128)(2,1)S(1)}, u32[]{:S(2)}, u32[]{:S(2)}) %collective-permute-start.51) | collective-permute-done | bytes 344096 | tf_op jit(solution)/shard_map/ppermute | solution.py:20
  707.5 10.2 %collective-permute-done.52 = bf16[112,1536]{1,0:T(8,128)(2,1)S(1)} collective-permute-done((bf16[112,1536]{1,0:T(8,128)(2,1)S(1)}, bf16[112,1536]{1,0:T(8,128)(2,1)S(1)}, u32[]{:S(2)}, u32[]{:S(2)}) %collective-permute-start.52) | collective-permute-done | bytes 344096 | tf_op jit(solution)/shard_map/ppermute | solution.py:20
  740.8 4.7 collective-permute-done.30
  746.8 3.3 collective-permute-start.35
  750.1 5.2 collective-permute-done.31
  755.6 3.3 collective-permute-start.62
  758.9 5.4 collective-permute-done.32
  767.3 4.6 collective-permute-done.36
  771.9 3.3 collective-permute-start.37
  775.5 4.0 collective-permute-done.37
  781.3 4.6 collective-permute-done.38
  (683 shorter events, 303.8 us)
Async XLA Ops:
  7.2 139.5 %all-gather.2.cloned.1.call-start = ((), (), s32[]{:S(2)}) async-start(), calls=%async_computation.1 | async-start | bytes 11796480 | tf_op jit(solution)/shard_map/all_gather | solution.py:251
  8.3 5.7 collective-permute-start.9
  14.7 12.3 %collective-permute-start.10 = (bf16[2,96,768]{2,1,0:T(8,128)(2,1)}, bf16[2,96,768]{2,1,0:T(8,128)(2,1)}, u32[]{:S(2)}, u32[]{:S(2)}) collective-permute-start(bf16[2,96,768]{2,1,0:T(8,128)(2,1)} %maximum_select_fusion.3), channel_id=1, source_target_pairs={{0,8},{4,12},{8,16},{12,20},{16,24},{20,28},{24,32},{28,36},{32,40... | collective-permute-start | bytes 884744 | tf_op jit(solution)/shard_map/ppermute | solution.py:20
  16.6 10.4 %collective-permute-start.11 = (bf16[2,96,768]{2,1,0:T(8,128)(2,1)}, bf16[2,96,768]{2,1,0:T(8,128)(2,1)S(1)}, u32[]{:S(2)}, u32[]{:S(2)}) collective-permute-start(bf16[2,96,768]{2,1,0:T(8,128)(2,1)} %maximum_select_fusion.3), channel_id=1, source_target_pairs={{0,56},{4,60},{8,0},{12,4},{16,8},{20,12},{24,16},{28,20},{32,24},... | collective-permute-start | bytes 884744 | tf_op jit(solution)/shard_map/ppermute | solution.py:20
  27.0 8.7 %collective-permute-start.12 = (bf16[2,96,768]{2,1,0:T(8,128)(2,1)}, bf16[2,96,768]{2,1,0:T(8,128)(2,1)S(1)}, u32[]{:S(2)}, u32[]{:S(2)}) collective-permute-start(bf16[2,96,768]{2,1,0:T(8,128)(2,1)} %collective-permute-done.10), channel_id=1, source_target_pairs={{0,8},{4,12},{8,16},{12,20},{16,24},{20,28},{24,32},{28,36},{32,40... | collective-permute-start | bytes 884744 | tf_op jit(solution)/shard_map/ppermute | solution.py:20
  27.0 8.7 %collective-permute-start.13 = (bf16[2,96,768]{2,1,0:T(8,128)(2,1)S(1)}, bf16[2,96,768]{2,1,0:T(8,128)(2,1)S(1)}, u32[]{:S(2)}, u32[]{:S(2)}) collective-permute-start(bf16[2,96,768]{2,1,0:T(8,128)(2,1)S(1)} %collective-permute-done.11), channel_id=1, source_target_pairs={{0,56},{4,60},{8,0},{12,4},{16,8},{20,12},{24,16},{28,20},{32,24},... | collective-permute-start | bytes 884744 | tf_op jit(solution)/shard_map/ppermute | solution.py:20
  35.6 7.9 collective-permute-start.14
  35.6 8.0 %collective-permute-start.15 = (bf16[2,96,768]{2,1,0:T(8,128)(2,1)S(1)}, bf16[2,96,768]{2,1,0:T(8,128)(2,1)S(1)}, u32[]{:S(2)}, u32[]{:S(2)}) collective-permute-start(bf16[2,96,768]{2,1,0:T(8,128)(2,1)S(1)} %collective-permute-done.13), channel_id=1, source_target_pairs={{0,56},{4,60},{8,0},{12,4},{16,8},{20,12},{24,16},{28,20},{32,24},... | collective-permute-start | bytes 884744 | tf_op jit(solution)/shard_map/ppermute | solution.py:20
  43.6 6.4 collective-permute-start.16
  43.7 6.3 collective-permute-start.17
  51.5 684.6 %reduce-scatter.2.cloned.1.call-start = ((), (), s32[]{:S(2)}) async-start(), calls=%async_computation.2 | async-start | bytes 11796480 | tf_op jit(solution)/shard_map/reduce_scatter | solution.py:267
  51.5 6.8 collective-permute-start
  58.4 14.5 %collective-permute-start.1 = (bf16[2,96,1536]{2,1,0:T(8,128)(2,1)S(1)}, bf16[2,96,1536]{2,1,0:T(8,128)(2,1)S(1)}, u32[]{:S(2)}, u32[]{:S(2)}) collective-permute-start(bf16[2,96,1536]{2,1,0:T(8,128)(2,1)S(1)} %maximum_select_fusion.1), channel_id=1, source_target_pairs={{0,8},{4,12},{8,16},{12,20},{16,24},{20,28},{24,32},{28,36},{32,40... | collective-permute-start | bytes 1769480 | tf_op jit(solution)/shard_map/ppermute | solution.py:20
  58.6 15.3 %collective-permute-start.2 = (bf16[2,96,1536]{2,1,0:T(8,128)(2,1)S(1)}, bf16[2,96,1536]{2,1,0:T(8,128)(2,1)S(1)}, u32[]{:S(2)}, u32[]{:S(2)}) collective-permute-start(bf16[2,96,1536]{2,1,0:T(8,128)(2,1)S(1)} %maximum_select_fusion.1), channel_id=1, source_target_pairs={{0,56},{4,60},{8,0},{12,4},{16,8},{20,12},{24,16},{28,20},{32,24},... | collective-permute-start | bytes 1769480 | tf_op jit(solution)/shard_map/ppermute | solution.py:20
  73.0 15.4 %collective-permute-start.3 = (bf16[2,96,1536]{2,1,0:T(8,128)(2,1)S(1)}, bf16[2,96,1536]{2,1,0:T(8,128)(2,1)S(1)}, u32[]{:S(2)}, u32[]{:S(2)}) collective-permute-start(bf16[2,96,1536]{2,1,0:T(8,128)(2,1)S(1)} %collective-permute-done.1), channel_id=1, source_target_pairs={{0,8},{4,12},{8,16},{12,20},{16,24},{20,28},{24,32},{28,36},{32,40... | collective-permute-start | bytes 1769480 | tf_op jit(solution)/shard_map/ppermute | solution.py:20
  73.8 17.3 %collective-permute-start.4 = (bf16[2,96,1536]{2,1,0:T(8,128)(2,1)S(1)}, bf16[2,96,1536]{2,1,0:T(8,128)(2,1)S(1)}, u32[]{:S(2)}, u32[]{:S(2)}) collective-permute-start(bf16[2,96,1536]{2,1,0:T(8,128)(2,1)S(1)} %collective-permute-done.2), channel_id=1, source_target_pairs={{0,56},{4,60},{8,0},{12,4},{16,8},{20,12},{24,16},{28,20},{32,24},... | collective-permute-start | bytes 1769480 | tf_op jit(solution)/shard_map/ppermute | solution.py:20
  88.4 14.5 %collective-permute-start.5 = (bf16[2,96,1536]{2,1,0:T(8,128)(2,1)S(1)}, bf16[2,96,1536]{2,1,0:T(8,128)(2,1)S(1)}, u32[]{:S(2)}, u32[]{:S(2)}) collective-permute-start(bf16[2,96,1536]{2,1,0:T(8,128)(2,1)S(1)} %collective-permute-done.3), channel_id=1, source_target_pairs={{0,8},{4,12},{8,16},{12,20},{16,24},{20,28},{24,32},{28,36},{32,40... | collective-permute-start | bytes 1769480 | tf_op jit(solution)/shard_map/ppermute | solution.py:20
  91.1 13.4 %collective-permute-start.6 = (bf16[2,96,1536]{2,1,0:T(8,128)(2,1)S(1)}, bf16[2,96,1536]{2,1,0:T(8,128)(2,1)S(1)}, u32[]{:S(2)}, u32[]{:S(2)}) collective-permute-start(bf16[2,96,1536]{2,1,0:T(8,128)(2,1)S(1)} %collective-permute-done.4), channel_id=1, source_target_pairs={{0,56},{4,60},{8,0},{12,4},{16,8},{20,12},{24,16},{28,20},{32,24},... | collective-permute-start | bytes 1769480 | tf_op jit(solution)/shard_map/ppermute | solution.py:20
  102.9 8.0 collective-permute-start.7
  104.6 7.1 collective-permute-start.8
  206.6 3.5 collective-permute-start.19
  234.2 4.3 collective-permute-start.20
  259.6 8.2 %collective-permute-start.21 = (bf16[1,48,1536]{2,1,0:T(8,128)(2,1)}, bf16[1,48,1536]{2,1,0:T(8,128)(2,1)S(1)}, u32[]{:S(2)}, u32[]{:S(2)}) collective-permute-start(bf16[1,48,1536]{2,1,0:T(8,128)(2,1)} %get-tuple-element.1558), channel_id=1, source_target_pairs={{0,64},{64,128},{128,192},{1,65},{65,129},{129,193},{2,66},{66,130... | collective-permute-start | bytes 442376 | tf_op jit(solution)/shard_map/ppermute | solution.py:15
  268.5 27.6 %collective-permute-start.22 = (bf16[1,48,1536]{2,1,0:T(8,128)(2,1)}, bf16[1,48,1536]{2,1,0:T(8,128)(2,1)S(1)}, u32[]{:S(2)}, u32[]{:S(2)}) collective-permute-start(bf16[1,48,1536]{2,1,0:T(8,128)(2,1)} %get-tuple-element.1569), channel_id=1, source_target_pairs={{0,64},{64,128},{128,192},{1,65},{65,129},{129,193},{2,66},{66,130... | collective-permute-start | bytes 442376 | tf_op jit(solution)/shard_map/ppermute | solution.py:15
  297.0 8.2 %collective-permute-start.23 = (bf16[1,48,1536]{2,1,0:T(8,128)(2,1)}, bf16[1,48,1536]{2,1,0:T(8,128)(2,1)S(1)}, u32[]{:S(2)}, u32[]{:S(2)}) collective-permute-start(bf16[1,48,1536]{2,1,0:T(8,128)(2,1)} %get-tuple-element.1580), channel_id=1, source_target_pairs={{0,64},{64,128},{128,192},{1,65},{65,129},{129,193},{2,66},{66,130... | collective-permute-start | bytes 442376 | tf_op jit(solution)/shard_map/ppermute | solution.py:15
  310.7 27.3 %collective-permute-start.24 = (bf16[1,48,1536]{2,1,0:T(8,128)(2,1)S(1)}, bf16[1,48,1536]{2,1,0:T(8,128)(2,1)S(1)}, u32[]{:S(2)}, u32[]{:S(2)}) collective-permute-start(bf16[1,48,1536]{2,1,0:T(8,128)(2,1)S(1)} %get-tuple-element.1599), channel_id=1, source_target_pairs={{64,0},{128,64},{192,128},{65,1},{129,65},{193,129},{66,2},{130,66... | collective-permute-start | bytes 442376 | tf_op jit(solution)/shard_map/ppermute | solution.py:15
  338.9 8.6 %collective-permute-start.25 = (bf16[1,48,1536]{2,1,0:T(8,128)(2,1)S(1)}, bf16[1,48,1536]{2,1,0:T(8,128)(2,1)S(1)}, u32[]{:S(2)}, u32[]{:S(2)}) collective-permute-start(bf16[1,48,1536]{2,1,0:T(8,128)(2,1)S(1)} %get-tuple-element.1608), channel_id=1, source_target_pairs={{64,0},{128,64},{192,128},{65,1},{129,65},{193,129},{66,2},{130,66... | collective-permute-start | bytes 442376 | tf_op jit(solution)/shard_map/ppermute | solution.py:15
  348.6 126.4 %collective-permute-start.26 = (bf16[1,48,1536]{2,1,0:T(8,128)(2,1)S(1)}, bf16[1,48,1536]{2,1,0:T(8,128)(2,1)S(1)}, u32[]{:S(2)}, u32[]{:S(2)}) collective-permute-start(bf16[1,48,1536]{2,1,0:T(8,128)(2,1)S(1)} %get-tuple-element.1617), channel_id=1, source_target_pairs={{64,0},{128,64},{192,128},{65,1},{129,65},{193,129},{66,2},{130,66... | collective-permute-start | bytes 442376 | tf_op jit(solution)/shard_map/ppermute | solution.py:15
  507.9 7.9 collective-permute-start.27
  543.3 8.2 %collective-permute-start.28 = (bf16[1,48,1536]{2,1,0:T(8,128)(2,1)}, bf16[1,48,1536]{2,1,0:T(8,128)(2,1)S(1)}, u32[]{:S(2)}, u32[]{:S(2)}) collective-permute-start(bf16[1,48,1536]{2,1,0:T(8,128)(2,1)} %get-tuple-element.1635), channel_id=1, source_target_pairs={{64,0},{128,64},{192,128},{65,1},{129,65},{193,129},{66,2},{130,66... | collective-permute-start | bytes 442376 | tf_op jit(solution)/shard_map/ppermute | solution.py:15
  579.0 8.2 %collective-permute-start.29 = (bf16[1,48,1536]{2,1,0:T(8,128)(2,1)}, bf16[1,48,1536]{2,1,0:T(8,128)(2,1)S(1)}, u32[]{:S(2)}, u32[]{:S(2)}) collective-permute-start(bf16[1,48,1536]{2,1,0:T(8,128)(2,1)} %get-tuple-element.1644), channel_id=1, source_target_pairs={{64,0},{128,64},{192,128},{65,1},{129,65},{193,129},{66,2},{130,66... | collective-permute-start | bytes 442376 | tf_op jit(solution)/shard_map/ppermute | solution.py:15
  626.0 8.3 %collective-permute-start.46 = (bf16[112,1536]{1,0:T(8,128)(2,1)S(1)}, bf16[112,1536]{1,0:T(8,128)(2,1)S(1)}, u32[]{:S(2)}, u32[]{:S(2)}) collective-permute-start(bf16[112,1536]{1,0:T(8,128)(2,1)S(1)} %get-tuple-element.2556), channel_id=1, source_target_pairs={{0,56},{4,60},{8,0},{12,4},{16,8},{20,12},{24,16},{28,20},{32,24},... | collective-permute-start | bytes 1032200 | tf_op jit(solution)/shard_map/ppermute | solution.py:20
  629.5 11.5 %collective-permute-start.42 = (bf16[112,1536]{1,0:T(8,128)(2,1)S(1)}, bf16[112,1536]{1,0:T(8,128)(2,1)S(1)}, u32[]{:S(2)}, u32[]{:S(2)}) collective-permute-start(bf16[112,1536]{1,0:T(8,128)(2,1)S(1)} %get-tuple-element.2555), channel_id=1, source_target_pairs={{0,8},{4,12},{8,16},{12,20},{16,24},{20,28},{24,32},{28,36},{32,40... | collective-permute-start | bytes 1032200 | tf_op jit(solution)/shard_map/ppermute | solution.py:20
  634.5 14.6 %collective-permute-start.47 = (bf16[2,112,1536]{2,1,0:T(8,128)(2,1)S(1)}, bf16[2,112,1536]{2,1,0:T(8,128)(2,1)S(1)}, u32[]{:S(2)}, u32[]{:S(2)}) collective-permute-start(bf16[2,112,1536]{2,1,0:T(8,128)(2,1)S(1)} %pad_maximum_fusion.9), channel_id=1, source_target_pairs={{0,56},{4,60},{8,0},{12,4},{16,8},{20,12},{24,16},{28,20},{32,24},... | collective-permute-start | bytes 2064392 | tf_op jit(solution)/shard_map/ppermute | solution.py:20
  641.2 15.7 %collective-permute-start.43 = (bf16[2,112,1536]{2,1,0:T(8,128)(2,1)S(1)}, bf16[2,112,1536]{2,1,0:T(8,128)(2,1)S(1)}, u32[]{:S(2)}, u32[]{:S(2)}) collective-permute-start(bf16[2,112,1536]{2,1,0:T(8,128)(2,1)S(1)} %pad_maximum_fusion.8), channel_id=1, source_target_pairs={{0,8},{4,12},{8,16},{12,20},{16,24},{20,28},{24,32},{28,36},{32,40... | collective-permute-start | bytes 2064392 | tf_op jit(solution)/shard_map/ppermute | solution.py:20
  657.2 12.2 %collective-permute-start.44 = (bf16[2,112,1536]{2,1,0:T(8,128)(2,1)S(1)}, bf16[2,112,1536]{2,1,0:T(8,128)(2,1)S(1)}, u32[]{:S(2)}, u32[]{:S(2)}) collective-permute-start(bf16[2,112,1536]{2,1,0:T(8,128)(2,1)S(1)} %get-tuple-element.2539), channel_id=1, source_target_pairs={{0,8},{4,12},{8,16},{12,20},{16,24},{20,28},{24,32},{28,36},{32,40... | collective-permute-start | bytes 2064392 | tf_op jit(solution)/shard_map/ppermute | solution.py:20
  657.3 12.1 %collective-permute-start.48 = (bf16[2,112,1536]{2,1,0:T(8,128)(2,1)S(1)}, bf16[2,112,1536]{2,1,0:T(8,128)(2,1)S(1)}, u32[]{:S(2)}, u32[]{:S(2)}) collective-permute-start(bf16[2,112,1536]{2,1,0:T(8,128)(2,1)S(1)} %get-tuple-element.2540), channel_id=1, source_target_pairs={{0,56},{4,60},{8,0},{12,4},{16,8},{20,12},{24,16},{28,20},{32,24},... | collective-permute-start | bytes 2064392 | tf_op jit(solution)/shard_map/ppermute | solution.py:20
  669.8 12.2 %collective-permute-start.45 = (bf16[2,112,1536]{2,1,0:T(8,128)(2,1)S(1)}, bf16[2,112,1536]{2,1,0:T(8,128)(2,1)S(1)}, u32[]{:S(2)}, u32[]{:S(2)}) collective-permute-start(bf16[2,112,1536]{2,1,0:T(8,128)(2,1)S(1)} %get-tuple-element.2537), channel_id=1, source_target_pairs={{0,8},{4,12},{8,16},{12,20},{16,24},{20,28},{24,32},{28,36},{32,40... | collective-permute-start | bytes 2064392 | tf_op jit(solution)/shard_map/ppermute | solution.py:20
  669.9 12.1 %collective-permute-start.49 = (bf16[2,112,1536]{2,1,0:T(8,128)(2,1)S(1)}, bf16[2,112,1536]{2,1,0:T(8,128)(2,1)}, u32[]{:S(2)}, u32[]{:S(2)}) collective-permute-start(bf16[2,112,1536]{2,1,0:T(8,128)(2,1)S(1)} %get-tuple-element.2538), channel_id=1, source_target_pairs={{0,56},{4,60},{8,0},{12,4},{16,8},{20,12},{24,16},{28,20},{32,24},... | collective-permute-start | bytes 2064392 | tf_op jit(solution)/shard_map/ppermute | solution.py:20
  683.6 7.3 collective-permute-start.50
  691.1 16.4 %collective-permute-start.51 = (bf16[112,1536]{1,0:T(8,128)(2,1)S(1)}, bf16[112,1536]{1,0:T(8,128)(2,1)S(1)}, u32[]{:S(2)}, u32[]{:S(2)}) collective-permute-start(bf16[112,1536]{1,0:T(8,128)(2,1)S(1)} %fusion.1873), channel_id=1, source_target_pairs={{0,2},{1,3},{2,0},{3,1},{4,6},{5,7},{6,4},{7,5},{8,10},{9,11},{10,... | collective-permute-start | bytes 1032200 | tf_op jit(solution)/shard_map/ppermute | solution.py:20
  694.3 23.4 %collective-permute-start.52 = (bf16[112,1536]{1,0:T(8,128)(2,1)S(1)}, bf16[112,1536]{1,0:T(8,128)(2,1)S(1)}, u32[]{:S(2)}, u32[]{:S(2)}) collective-permute-start(bf16[112,1536]{1,0:T(8,128)(2,1)S(1)} %fusion.1873), channel_id=1, source_target_pairs={{0,1},{1,2},{2,3},{3,0},{4,5},{5,6},{6,7},{7,4},{8,9},{9,10},{10,1... | collective-permute-start | bytes 1032200 | tf_op jit(solution)/shard_map/ppermute | solution.py:20
  694.3 23.4 %collective-permute-start.53 = (bf16[112,1536]{1,0:T(8,128)(2,1)S(1)}, bf16[112,1536]{1,0:T(8,128)(2,1)S(1)}, u32[]{:S(2)}, u32[]{:S(2)}) collective-permute-start(bf16[112,1536]{1,0:T(8,128)(2,1)S(1)} %fusion.1873), channel_id=1, source_target_pairs={{0,3},{1,0},{2,1},{3,2},{4,7},{5,4},{6,5},{7,6},{8,11},{9,8},{10,9... | collective-permute-start | bytes 1032200 | tf_op jit(solution)/shard_map/ppermute | solution.py:20
  717.8 3.9 collective-permute-start.54
  721.8 5.6 collective-permute-start.55
  723.3 4.3 collective-permute-start.56
  727.3 5.5 collective-permute-start.57
  727.6 5.3 collective-permute-start.58
  732.8 13.9 %collective-permute-start.59 = (f32[2,3,1536]{2,1,0:T(4,128)S(1)}, f32[2,3,1536]{2,1,0:T(4,128)S(1)}, u32[]{:S(2)}, u32[]{:S(2)}) collective-permute-start(f32[2,3,1536]{2,1,0:T(4,128)S(1)} %collective-permute-done.57), channel_id=1, source_target_pairs={{0,8},{4,12},{8,16},{12,20},{16,24},{20,28},{24,32},{28,36},{32,40... | collective-permute-start | bytes 110600 | tf_op jit(solution)/shard_map/ppermute | solution.py:20
  732.8 22.7 %collective-permute-start.60 = (f32[2,3,1536]{2,1,0:T(4,128)S(1)}, f32[2,3,1536]{2,1,0:T(4,128)S(1)}, u32[]{:S(2)}, u32[]{:S(2)}) collective-permute-start(f32[2,3,1536]{2,1,0:T(4,128)S(1)} %collective-permute-done.58), channel_id=1, source_target_pairs={{0,56},{4,60},{8,0},{12,4},{16,8},{20,12},{24,16},{28,20},{32,24},... | collective-permute-start | bytes 110600 | tf_op jit(solution)/shard_map/ppermute | solution.py:20
  737.4 8.1 %collective-permute-start.30 = (bf16[96,768]{1,0:T(8,128)(2,1)S(1)}, bf16[96,768]{1,0:T(8,128)(2,1)S(1)}, u32[]{:S(2)}, u32[]{:S(2)}) collective-permute-start(bf16[96,768]{1,0:T(8,128)(2,1)S(1)} %get-tuple-element.2548), channel_id=1, source_target_pairs={{0,8},{4,12},{8,16},{12,20},{16,24},{20,28},{24,32},{28,36},{32,40... | collective-permute-start | bytes 442376 | tf_op jit(solution)/shard_map/ppermute | solution.py:20
  737.5 8.0 collective-permute-start.34
  746.6 8.8 %collective-permute-start.31 = (bf16[2,96,768]{2,1,0:T(8,128)(2,1)S(1)}, bf16[2,96,768]{2,1,0:T(8,128)(2,1)S(1)}, u32[]{:S(2)}, u32[]{:S(2)}) collective-permute-start(bf16[2,96,768]{2,1,0:T(8,128)(2,1)S(1)} %pad_maximum_fusion.11), channel_id=1, source_target_pairs={{0,8},{4,12},{8,16},{12,20},{16,24},{20,28},{24,32},{28,36},{32,40... | collective-permute-start | bytes 884744 | tf_op jit(solution)/shard_map/ppermute | solution.py:20
  746.7 28.5 %collective-permute-start.61 = (f32[3,1536]{1,0:T(4,128)S(1)}, f32[3,1536]{1,0:T(4,128)S(1)}, u32[]{:S(2)}, u32[]{:S(2)}) collective-permute-start(f32[3,1536]{1,0:T(4,128)S(1)} %slice_bitcast_fusion.68), channel_id=1, source_target_pairs={{0,8},{4,12},{8,16},{12,20},{16,24},{20,28},{24,32},{28,36},{32,40... | collective-permute-start | bytes 55304 | tf_op jit(solution)/shard_map/ppermute | solution.py:20
  746.8 12.0 %collective-permute-start.35 = (bf16[2,96,768]{2,1,0:T(8,128)(2,1)S(1)}, bf16[2,96,768]{2,1,0:T(8,128)(2,1)S(1)}, u32[]{:S(2)}, u32[]{:S(2)}) collective-permute-start(bf16[2,96,768]{2,1,0:T(8,128)(2,1)S(1)} %pad_maximum_fusion.12), channel_id=1, source_target_pairs={{0,56},{4,60},{8,0},{12,4},{16,8},{20,12},{24,16},{28,20},{32,24},... | collective-permute-start | bytes 884744 | tf_op jit(solution)/shard_map/ppermute | solution.py:20
  755.5 8.8 %collective-permute-start.32 = (bf16[2,96,768]{2,1,0:T(8,128)(2,1)S(1)}, bf16[2,96,768]{2,1,0:T(8,128)(2,1)S(1)}, u32[]{:S(2)}, u32[]{:S(2)}) collective-permute-start(bf16[2,96,768]{2,1,0:T(8,128)(2,1)S(1)} %fusion.1879), channel_id=1, source_target_pairs={{0,8},{4,12},{8,16},{12,20},{16,24},{20,28},{24,32},{28,36},{32,40... | collective-permute-start | bytes 884744 | tf_op jit(solution)/shard_map/ppermute | solution.py:20
  755.6 19.7 %collective-permute-start.62 = (f32[3,1536]{1,0:T(4,128)S(1)}, f32[3,1536]{1,0:T(4,128)S(1)}, u32[]{:S(2)}, u32[]{:S(2)}) collective-permute-start(f32[3,1536]{1,0:T(4,128)S(1)} %slice_bitcast_fusion.67), channel_id=1, source_target_pairs={{0,56},{4,60},{8,0},{12,4},{16,8},{20,12},{24,16},{28,20},{32,24},... | collective-permute-start | bytes 55304 | tf_op jit(solution)/shard_map/ppermute | solution.py:20
  765.1 6.7 collective-permute-start.36
  767.1 8.3 %collective-permute-start.33 = (bf16[2,96,768]{2,1,0:T(8,128)(2,1)}, bf16[2,96,768]{2,1,0:T(8,128)(2,1)}, u32[]{:S(2)}, u32[]{:S(2)}) collective-permute-start(bf16[2,96,768]{2,1,0:T(8,128)(2,1)} %get-tuple-element.2544), channel_id=1, source_target_pairs={{0,8},{4,12},{8,16},{12,20},{16,24},{20,28},{24,32},{28,36},{32,40... | collective-permute-start | bytes 884744 | tf_op jit(solution)/shard_map/ppermute | solution.py:20
  771.9 7.5 collective-permute-start.37
  780.7 5.2 collective-permute-start.38
  785.9 6.4 collective-permute-start.39
  786.0 7.9 collective-permute-start.40
  789.2 5.6 collective-permute-start.41
  (68 other events, 496.7 us)
Sparse Core Ops, SparseCore 0:
  51.6 95.0 all-gather.1
  622.8 105.7 reduce-scatter.1

commit v2 on v1

v2 whole, which is shorter than its diff:
```python
import functools
import math

import jax
import jax.numpy as jnp
from jax import lax
from jax.experimental import pallas as pl
from jax.experimental.pallas import tpu as pltpu
from jax.sharding import PartitionSpec as P

epsilon = 1e-05
LANES = 128
SUBLANES = 8
MARGIN = 16
GAIN_A = 32
GAIN_B = 40
PARAM_ROWS = 48
VMEM_LIMIT = 64 * 1024 * 1024 - 64 * 1024
PAIR = 2


def rotate(x, axis, by):
    peers = lax.axis_size(axis)
    return lax.ppermute(x, axis, [(i, (i + by) % peers) for i in range(peers)])


def swap_pair(x):
    peers = lax.axis_size("fsdp")
    return lax.ppermute(x, "fsdp", [(i, i ^ 1) for i in range(peers)])


def ring_position():
    index = lax.axis_index("fsdp")
    return index // PAIR, index % PAIR


def pick(stacked, index):
    return lax.dynamic_index_in_dim(stacked, index, 0, keepdims=False)


def gather_rows(shard):
    ring = lax.axis_size("fsdp") // PAIR
    half = ring // 2
    at, side = ring_position()
    other = swap_pair(shard)
    pair = jnp.where(side == 0, jnp.stack([shard, other]), jnp.stack([other, shard]))
    whole = jnp.zeros((ring,) + pair.shape, pair.dtype)

    def put(whole, piece, offset):
        return lax.dynamic_update_slice(whole, piece[None], ((at + offset) % ring, 0, 0, 0))

    whole = put(whole, pair, 0)
    up, down = pair, pair
    for hop in range(1, half):
        up = rotate(up, "fsdp", PAIR)
        down = rotate(down, "fsdp", -PAIR)
        whole = put(put(whole, up, ring - hop), down, hop)
    far_up = rotate(up[0], "fsdp", PAIR)
    far_down = rotate(down[1], "fsdp", -PAIR)
    whole = put(whole, jnp.stack([far_up, far_down]), half)
    return whole.reshape((ring * PAIR,) + shard.shape)


def scatter_rows(terms):
    ring = lax.axis_size("fsdp") // PAIR
    half = ring // 2
    at, side = ring_position()
    pairs = terms.reshape((ring, PAIR) + terms.shape[1:])
    far = pick(pairs, (at + half) % ring)
    up = rotate(far[0], "fsdp", PAIR)
    down = rotate(far[1], "fsdp", -PAIR)
    for hop in range(half - 1, 0, -1):
        mine_up = pick(pairs, (at + hop) % ring).astype(jnp.float32)
        mine_down = pick(pairs, (at + ring - hop) % ring).astype(jnp.float32)
        up = up.astype(jnp.float32)
        down = down.astype(jnp.float32)
        if hop == half - 1:
            up = jnp.stack([mine_up[0] + up, mine_up[1]])
            down = jnp.stack([mine_down[0], mine_down[1] + down])
        else:
            up = mine_up + up
            down = mine_down + down
        up = rotate(up.astype(terms.dtype), "fsdp", PAIR)
        down = rotate(down.astype(terms.dtype), "fsdp", -PAIR)
    total = pick(pairs, at).astype(jnp.float32) + up.astype(jnp.float32) + down.astype(jnp.float32)
    mine = jnp.where(side == 0, total[0], total[1])
    theirs = jnp.where(side == 0, total[1], total[0])
    return mine + swap_pair(theirs.astype(terms.dtype)).astype(jnp.float32)


def batch_copies(x):
    return x, rotate(x, "batch", 1), rotate(x, "batch", 2), rotate(x, "batch", 3)


def sum_batch(x):
    own, left, far, right = (part.astype(jnp.float32) for part in batch_copies(x))
    return (own + far) + (left + right)


def layer_stats(values):
    mean_value = jnp.mean(values, axis=-1, keepdims=True)
    centred = values - mean_value
    inv_scale = lax.rsqrt(jnp.mean(centred * centred, axis=-1, keepdims=True) + epsilon)
    return centred * inv_scale, inv_scale


def norm_grad(upstream, normed, inv_scale):
    return (
        upstream
        - jnp.mean(upstream, axis=-1, keepdims=True)
        - normed * jnp.mean(upstream * normed, axis=-1, keepdims=True)
    ) * inv_scale


def rows_by(left, right):
    return jnp.dot(left, right, preferred_element_type=jnp.float32)


def rows_back(left, right):
    return lax.dot_general(
        left, right, (((1,), (1,)), ((), ())), preferred_element_type=jnp.float32
    )


def write_shifts(shifts, padded):
    span = shifts.shape[1]
    for by in range(SUBLANES):
        shifts[by] = padded[pl.ds(by, span), :]


def clear_margins(padded, length):
    zeros = jnp.zeros((MARGIN, padded.shape[1]), jnp.float32)
    padded[pl.ds(0, MARGIN), :] = zeros
    padded[pl.ds(MARGIN + length, MARGIN), :] = zeros


def each_lane_block(width, body):
    def step(block, carry):
        body(pl.ds(pl.multiple_of(block * LANES, LANES), LANES))
        return carry

    lax.fori_loop(0, width // LANES, step, 0)


def shifted(shifts, offset, length, lanes):
    start = offset // SUBLANES * SUBLANES
    return shifts[offset % SUBLANES, pl.ds(start, length), lanes]


def forward_kernel(
    info, incoming, frames, w_in, w_out, params, *refs, taps, length, width, aliased
):
    refs = refs[aliased:]
    outgoing, x_all, proj_all, swish_all, value_all, gate_all, mid_all, inv_all = refs[:8]
    (
        x_v, w_in_v, w_out_v, params_v, proj_v, swish_v, value_v, gate_v, mid_v, inv_v,
        padded, shifts, conv_v, out_v, in_sems, out_sems,
    ) = refs[8:]
    slot, active, first, valid = info[0], info[1], info[2], info[3]
    parts = w_in_v.shape[0]
    half = taps // 2

    @pl.when(active == 1)
    def run():
        x_copy = pltpu.make_async_copy(incoming, x_v, in_sems.at[0])
        frame_copy = pltpu.make_async_copy(frames.at[slot], x_v, in_sems.at[0])

        @pl.when(first == 1)
        def from_frames():
            frame_copy.start()

        @pl.when(first == 0)
        def from_neighbour():
            x_copy.start()

        params_copy = pltpu.make_async_copy(params, params_v, in_sems.at[1])
        params_copy.start()
        w_in_copies = [
            pltpu.make_async_copy(w_in.at[part], w_in_v.at[part], in_sems.at[2 + part])
            for part in range(parts)
        ]
        for copy in w_in_copies:
            copy.start()
        w_out_copy = pltpu.make_async_copy(w_out, w_out_v, in_sems.at[2 + parts])
        w_out_copy.start()
        saves = []

        def save(source, target):
            copy = pltpu.make_async_copy(source, target, out_sems.at[len(saves)])
            copy.start()
            saves.append(copy)

        clear_margins(padded, length)
        x_copy.wait()
        params_copy.wait()
        source = x_v[...].astype(jnp.float32)
        save(x_v, x_all.at[slot])
        normed_in, unused = layer_stats(source)
        proj_v[...] = (normed_in * params_v[pl.ds(GAIN_A, 1), :]).astype(jnp.bfloat16)
        save(proj_v, proj_all.at[slot])
        part_width = w_in_v.shape[2]
        for part in range(parts):
            w_in_copies[part].wait()
            out = rows_by(proj_v[...], w_in_v[part])
            place = part % (parts // 2)
            lanes = pl.ds(place * part_width, part_width)
            if part < parts // 2:
                value_v[:, lanes] = out
            else:
                gate_v[:, lanes] = jax.nn.sigmoid(out)
        save(value_v, value_all.at[slot])
        save(gate_v, gate_all.at[slot])
        rows = lax.broadcasted_iota(jnp.int32, (length, width), 0)
        mask = (rows < valid).astype(jnp.float32)
        padded[pl.ds(MARGIN, length), :] = value_v[...] * gate_v[...] * mask
        write_shifts(shifts, padded)

        def convolve(lanes):
            total = jnp.zeros((length, LANES), jnp.float32)
            for tap in range(taps):
                weight = params_v[pl.ds(tap, 1), lanes]
                total = total + shifted(shifts, tap + MARGIN - half, length, lanes) * weight
            conv_v[:, lanes] = total

        each_lane_block(width, convolve)
        normed_mid, inv_mid = layer_stats(conv_v[...])
        mid_v[...] = normed_mid
        inv_v[...] = jnp.broadcast_to(inv_mid, inv_v.shape)
        save(mid_v, mid_all.at[slot])
        save(inv_v, inv_all.at[slot])
        scaled_mid = normed_mid * params_v[pl.ds(GAIN_B, 1), :]
        swish_v[...] = (scaled_mid * jax.nn.sigmoid(scaled_mid)).astype(jnp.bfloat16)
        save(swish_v, swish_all.at[slot])
        w_out_copy.wait()
        source = x_v[...].astype(jnp.float32)
        out_v[...] = (source + rows_by(swish_v[...], w_out_v[...])).astype(jnp.bfloat16)
        save(out_v, outgoing)
        for copy in saves:
            copy.wait()


def backward_kernel(
    info, incoming, cotangent, w_in, w_out, params,
    x_all, value_all, gate_all, mid_all, inv_all, *refs, taps, length, width, aliased
):
    refs = refs[aliased:]
    outgoing, input_all, grad_all, up_all, small_all = refs[:5]
    (
        u_v, w_in_v, w_out_v, params_v, x_v, value_v, gate_v, mid_v, inv_v,
        padded, shifts, padded_grad, shifts_grad, conv_v, grad_v, small_v, out_v,
        in_sems, out_sems,
    ) = refs[5:]
    slot, active, first, valid = info[0], info[1], info[2], info[3]
    parts = w_in_v.shape[0]
    half = taps // 2

    @pl.when(active == 1)
    def run():
        u_copy = pltpu.make_async_copy(incoming, u_v, in_sems.at[0])
        given_copy = pltpu.make_async_copy(cotangent.at[slot], u_v, in_sems.at[0])

        @pl.when(first == 1)
        def from_cotangent():
            given_copy.start()

        @pl.when(first == 0)
        def from_neighbour():
            u_copy.start()

        w_out_copy = pltpu.make_async_copy(w_out, w_out_v, in_sems.at[1])
        w_out_copy.start()
        loads = []
        for number, (source, target) in enumerate((
            (params, params_v),
            (value_all.at[slot], value_v),
            (gate_all.at[slot], gate_v),
            (mid_all.at[slot], mid_v),
            (inv_all.at[slot], inv_v),
            (x_all.at[slot], x_v),
        )):
            copy = pltpu.make_async_copy(source, target, in_sems.at[2 + number])
            copy.start()
            loads.append(copy)
        w_in_copies = [
            pltpu.make_async_copy(w_in.at[part], w_in_v.at[part], in_sems.at[8 + part])
            for part in range(parts)
        ]
        for copy in w_in_copies:
            copy.start()
        saves = []

        def save(source, target):
            copy = pltpu.make_async_copy(source, target, out_sems.at[len(saves)])
            copy.start()
            saves.append(copy)

        clear_margins(padded, length)
        clear_margins(padded_grad, length)
        for copy in loads:
            copy.wait()
        rows = lax.broadcasted_iota(jnp.int32, (length, width), 0)
        mask = (rows < valid).astype(jnp.float32)
        padded[pl.ds(MARGIN, length), :] = value_v[...] * gate_v[...] * mask
        write_shifts(shifts, padded)
        u_copy.wait()
        save(u_v, up_all.at[slot])
        w_out_copy.wait()
        swish_grad = rows_back(u_v[...], w_out_v[...])
        normed_mid = mid_v[...]
        gain_b = params_v[pl.ds(GAIN_B, 1), :]
        scaled_mid = normed_mid * gain_b
        sigmoid_mid = jax.nn.sigmoid(scaled_mid)
        scaled_grad = swish_grad * (
            sigmoid_mid + scaled_mid * sigmoid_mid * (1.0 - sigmoid_mid)
        )
        small_v[pl.ds(GAIN_B, 1), :] = jnp.sum(scaled_grad * normed_mid, axis=0, keepdims=True)
        conv_grad = norm_grad(scaled_grad * gain_b, normed_mid, inv_v[:, :1])
        padded_grad[pl.ds(MARGIN, length), :] = conv_grad
        write_shifts(shifts_grad, padded_grad)

        def convolve(lanes):
            total = jnp.zeros((length, LANES), jnp.float32)
            for tap in range(taps):
                weight = params_v[pl.ds(tap, 1), lanes]
                total = total + shifted(shifts_grad, MARGIN + half - tap, length, lanes) * weight
            conv_v[:, lanes] = total

        each_lane_block(width, convolve)

        def correlate(lanes):
            given = padded_grad[pl.ds(MARGIN, length), lanes]
            for tap in range(taps):
                product = given * shifted(shifts, tap + MARGIN - half, length, lanes)
                small_v[pl.ds(tap, 1), lanes] = jnp.sum(product, axis=0, keepdims=True)

        each_lane_block(width, correlate)
        gated_grad = conv_v[...] * mask
        glu_gate = gate_v[...]
        grad_v[:, :width] = (gated_grad * glu_gate).astype(jnp.bfloat16)
        grad_v[:, width:] = (
            gated_grad * value_v[...] * glu_gate * (1.0 - glu_gate)
        ).astype(jnp.bfloat16)
        save(grad_v, grad_all.at[slot])
        part_width = w_in_v.shape[2]
        input_side = jnp.zeros((length, width), jnp.float32)
        for part in range(parts):
            w_in_copies[part].wait()
            lanes = pl.ds(part * part_width, part_width)
            input_side = input_side + rows_back(grad_v[:, lanes], w_in_v[part])
        normed_in, inv_in = layer_stats(x_v[...].astype(jnp.float32))
        small_v[pl.ds(GAIN_A, 1), :] = jnp.sum(input_side * normed_in, axis=0, keepdims=True)
        save(small_v, small_all.at[slot])
        gain_a = params_v[pl.ds(GAIN_A, 1), :]
        out_v[...] = (
            u_v[...].astype(jnp.float32) + norm_grad(input_side * gain_a, normed_in, inv_in)
        ).astype(jnp.bfloat16)
        save(out_v, outgoing)
        save(out_v, input_all.at[slot])
        for copy in saves:
            copy.wait()


def stage_call(kernel, scratch, info, inputs, out_shapes, buffers, taps, length, width, cost, sems):
    anywhere = pl.BlockSpec(memory_space=pl.ANY)
    aliases = {}
    operands = list(inputs)
    aliased = 0
    if buffers is not None:
        aliased = len(buffers)
        aliases = {1 + len(inputs) + number: 1 + number for number in range(aliased)}
        operands += list(buffers)
    in_sems, out_sems = sems
    return pl.pallas_call(
        functools.partial(kernel, taps=taps, length=length, width=width, aliased=aliased),
        grid_spec=pltpu.PrefetchScalarGridSpec(
            num_scalar_prefetch=1,
            grid=(),
            in_specs=[anywhere] * len(operands),
            out_specs=[anywhere] * len(out_shapes),
            scratch_shapes=list(scratch)
            + [pltpu.SemaphoreType.DMA((in_sems,)), pltpu.SemaphoreType.DMA((out_sems,))],
        ),
        out_shape=out_shapes,
        input_output_aliases=aliases,
        compiler_params=pltpu.CompilerParams(vmem_limit_bytes=VMEM_LIMIT),
        cost_estimate=cost,
    )(info, *operands)


def stage_cost(length, width):
    return pl.CostEstimate(
        flops=6 * length * width * width,
        transcendentals=2 * length * width,
        bytes_accessed=6 * width * width,
    )


def forward_stage(info, incoming, frames, w_in, w_out, params, buffers, taps):
    micro, length, width = frames.shape
    f32, bf16 = jnp.float32, jnp.bfloat16
    shape = jax.ShapeDtypeStruct
    outs = [shape((length, width), bf16)] + [
        shape((micro, length, width), dtype) for dtype in (bf16, bf16, bf16, f32, f32, f32)
    ] + [shape((micro, length, LANES), f32)]
    rows = functools.partial(pltpu.VMEM, (length, width))
    span = length + 2 * MARGIN
    scratch = [
        rows(bf16), pltpu.VMEM(w_in.shape, bf16), pltpu.VMEM(w_out.shape, bf16),
        pltpu.VMEM(params.shape, f32), rows(bf16), rows(bf16), rows(f32), rows(f32), rows(f32),
        pltpu.VMEM((length, LANES), f32), pltpu.VMEM((span, width), f32),
        pltpu.VMEM((SUBLANES, span - SUBLANES, width), f32), rows(f32), rows(bf16),
    ]
    return stage_call(
        forward_kernel, scratch, info, (incoming, frames, w_in, w_out, params), outs, buffers,
        taps, length, width, stage_cost(length, width), (3 + w_in.shape[0], 8),
    )


def backward_stage(info, incoming, cotangent, w_in, w_out, params, saved, buffers, taps):
    micro, length, width = cotangent.shape
    f32, bf16 = jnp.float32, jnp.bfloat16
    shape = jax.ShapeDtypeStruct
    outs = [
        shape((length, width), bf16), shape((micro, length, width), bf16),
        shape((micro, length, 2 * width), bf16), shape((micro, length, width), bf16),
        shape((micro,) + params.shape, f32),
    ]
    rows = functools.partial(pltpu.VMEM, (length, width))
    span = length + 2 * MARGIN
    lifted = pltpu.VMEM((SUBLANES, span - SUBLANES, width), f32)
    scratch = [
        rows(bf16), pltpu.VMEM(w_in.shape, bf16), pltpu.VMEM(w_out.shape, bf16),
        pltpu.VMEM(params.shape, f32), rows(bf16), rows(f32), rows(f32), rows(f32),
        pltpu.VMEM((length, LANES), f32), pltpu.VMEM((span, width), f32), lifted,
        pltpu.VMEM((span, width), f32), lifted, rows(f32),
        pltpu.VMEM((length, 2 * width), bf16), pltpu.VMEM(params.shape, f32), rows(bf16),
    ]
    return stage_call(
        backward_kernel, scratch, info, (incoming, cotangent, w_in, w_out, params) + tuple(saved),
        outs, buffers, taps, length, width, stage_cost(length, width), (8 + w_in.shape[0], 5),
    )


def gather_weights(w_in, w_out):
    quarters = lax.axis_size("batch")
    width = w_in.shape[1] // quarters
    mine = lax.dynamic_slice_in_dim(w_in, lax.axis_index("batch") * width, width, 1)
    mine = gather_rows(mine)
    mine = mine.reshape(-1, width)
    w_in_full = lax.all_gather(mine, "batch", axis=0, tiled=False)
    w_out_full = gather_rows(w_out).reshape(-1, w_out.shape[1])
    return w_in_full, w_out_full


def reduce_weights(term_in, term_out, small, scale):
    quarters, depth, width = term_in.shape
    fsdp = lax.axis_size("fsdp")
    rows = depth // fsdp
    small_rows = -(-small.shape[0] // fsdp)
    small_pad = jnp.pad(small, ((0, small_rows * fsdp - small.shape[0]), (0, 0)))
    extra = jnp.pad(
        small_pad.reshape(fsdp, small_rows, depth).astype(jnp.bfloat16),
        ((0, 0), (0, 16 - small_rows), (0, 0)),
    )
    out_terms = jnp.concatenate([term_out.reshape(fsdp, rows, depth), extra], axis=1)
    in_quarter = lax.psum_scatter(term_in, "batch", scatter_dimension=0, tiled=False)
    out_share = scatter_rows(out_terms)
    out_sum = sum_batch(out_share.astype(jnp.bfloat16))
    grad_out = scale * out_sum[:rows]
    small_sum = gather_rows(scale * out_sum[rows : rows + small_rows])
    small_sum = small_sum.reshape(fsdp * small_rows, depth)[: small.shape[0]]
    in_share = scatter_rows(in_quarter.reshape(fsdp, rows, width)).astype(jnp.bfloat16)
    copies = jnp.stack(batch_copies(in_share))
    here = lax.axis_index("batch")
    grad_in = jnp.concatenate(
        [pick(copies, (here + quarters - part) % quarters) for part in range(quarters)], axis=1
    )
    return scale * grad_in.astype(jnp.float32), grad_out, small_sum


def send_active(x, moment, senders, by):
    pairs = [(s, s + by) for s in senders if 0 <= s + by < lax.axis_size("section")]
    return lax.ppermute(x, "section", pairs)


def local(frames, cotangent, lengths, w_in, w_out, gain_pre, gain_mid, w_depth):
    sections = lax.axis_size("section")
    section_index = lax.axis_index("section")
    micro_count = frames.shape[0]
    frames_len = frames.shape[2]
    model_width = frames.shape[3]
    moments = micro_count + sections - 1
    scale = 1.0 / math.sqrt(
        micro_count * frames_len * lax.axis_size("fsdp") * lax.axis_size("batch")
    )
    w_in_full, w_out_full = gather_weights(w_in[0], w_out[0])
    taps = w_depth.shape[1]
    params = jnp.concatenate(
        [
            w_depth[0],
            jnp.zeros((GAIN_A - taps, model_width), jnp.float32),
            gain_pre,
            jnp.zeros((GAIN_B - GAIN_A - 1, model_width), jnp.float32),
            gain_mid,
            jnp.zeros((PARAM_ROWS - GAIN_B - 1, model_width), jnp.float32),
        ],
        axis=0,
    )
    frame_rows = frames.reshape(micro_count, frames_len, model_width)
    cotangent_rows = cotangent.reshape(micro_count, frames_len, model_width)

    def info_at(moment, place, first):
        micro_index = moment - place
        active = (micro_index >= 0) & (micro_index < micro_count)
        slot = jnp.clip(micro_index, 0, micro_count - 1)
        return jnp.stack(
            [slot, active.astype(jnp.int32), first.astype(jnp.int32), lengths[slot, 0]]
        ).astype(jnp.int32)

    def active_at(moment, flipped):
        places = [p for p in range(sections) if 0 <= moment - p < micro_count]
        return [sections - 1 - p for p in places] if flipped else places

    incoming = jnp.zeros((frames_len, model_width), jnp.bfloat16)
    saved = None
    for moment in range(moments):
        info = info_at(moment, section_index, section_index == 0)
        outgoing, *saved = forward_stage(
            info, incoming, frame_rows, w_in_full, w_out_full, params, saved, taps
        )
        if moment < moments - 1:
            incoming = send_active(outgoing, moment, active_at(moment, False), 1)
    x_all, proj_all, swish_all, value_all, gate_all, mid_all, inv_all = saved
    kept = (x_all, value_all, gate_all, mid_all, inv_all)
    place = sections - 1 - section_index
    grads = None
    for moment in range(moments):
        info = info_at(moment, place, place == 0)
        outgoing, *grads = backward_stage(
            info, incoming, cotangent_rows, w_in_full, w_out_full, params, kept, grads, taps
        )
        if moment < moments - 1:
            incoming = send_active(outgoing, moment, active_at(moment, True), -1)
    input_all, grad_all, up_all, small_all = grads
    total_rows = micro_count * frames_len
    parts, unused, width = w_in_full.shape
    proj_rows = proj_all.reshape(total_rows, model_width)
    grad_rows = grad_all.reshape(total_rows, 2 * model_width)
    swish_rows = swish_all.reshape(total_rows, model_width)
    upstream_rows = up_all.reshape(total_rows, model_width)

    def term(left, right):
        return lax.dot_general(
            left, right, (((0,), (0,)), ((), ())), preferred_element_type=jnp.float32
        ).astype(jnp.bfloat16)

    term_in = jnp.stack(
        [term(proj_rows, grad_rows[:, part * width : (part + 1) * width]) for part in range(parts)]
    )
    term_out = term(swish_rows, upstream_rows)
    small_rows = jnp.sum(small_all, axis=0)
    small = jnp.concatenate(
        [
            small_rows[GAIN_A : GAIN_A + 1],
            small_rows[GAIN_B : GAIN_B + 1],
            small_rows[:taps],
        ],
        axis=0,
    )
    grad_in, grad_out, small_total = reduce_weights(term_in, term_out, small, scale)
    input_grads = input_all.reshape(1, micro_count, 1, frames_len, model_width)
    return (
        input_grads,
        grad_in[None],
        grad_out[None],
        small_total[0:1],
        small_total[1:2],
        small_total[2:][None],
    )


def solution(mesh):
    in_specs = (
        P(None, ("fsdp", "batch"), None, None),
        P(None, ("fsdp", "batch"), None, None),
        P(None, ("fsdp", "batch")),
        P("section", "fsdp", None),
        P("section", "fsdp", None),
        P("section", None),
        P("section", None),
        P("section", None, None),
    )
    out_specs = (
        P("section", None, ("fsdp", "batch"), None, None),
        P("section", "fsdp", None),
        P("section", "fsdp", None),
        P("section", None),
        P("section", None),
        P("section", None, None),
    )
    return jax.shard_map(local, mesh=mesh, in_specs=in_specs, out_specs=out_specs, check_vma=False)
```

time: 815 us -> 576 us (0.71)
  matrix products: 115 us -> 6.02 us
  Pallas kernels: 0 us -> 86.8 us
  waiting for transfers between devices: 381 us -> 298 us
  other arithmetic: 85.8 us -> 32.4 us
  starting transfers between devices: 143 us -> 104 us
  local copies, waits for them, and re-layouts: 58.3 us -> 23 us
    dot_general x40 -> x0, matrix products: 104 us -> none  [the longest x20 52.2 us: rows_by(): return jnp.dot(left, right, preferred_element_type=jnp.float32)]
    ppermute x12, waiting for transfers between devices: 182 us -> 88.5 us  [send_active(): return lax.ppermute(x, 'section', pairs)]
    pallas_call x0 -> x14, Pallas kernels: none -> 86.8 us  [stage_call(): pl.pallas_call(functools.partial(kernel, taps=taps, length=length, width=...]
    ppermute x12, starting transfers between devices: 58.6 us -> 25.1 us  [send_active(): return lax.ppermute(x, 'section', pairs)]
    dynamic_update_slice x31 -> x0, other arithmetic: 33.1 us -> none  [put_slot(): lax.dynamic_update_index_in_dim(buffer, value, micro_slot, 0)]
    another operation x150 -> x1, local copies, waits for them, and re-layouts: 17.2 us -> 0.01 us
    reduce_sum x28 -> x1, other arithmetic: 14.7 us -> 0.06 us  [local(): small_rows = jnp.sum(small_all, axis=0)]
    ppermute x46, waiting for transfers between devices: 141 us -> 154 us  [rotate(): return lax.ppermute(x, axis, [(i, (i + by) % peers) for i in range(peers)])]
  transfers between devices with their start and end apart: 65 -> 65, of which waited for: 47 -> 40; matrix products, arithmetic and copies ran while one was open for 3% -> 8% of each run, Pallas kernels for 0% -> 0%
where the time goes in v2:
time: 576 us; the launch traced here: 566 us
  waiting for transfers between devices  298 us (52%)
  starting transfers between devices  104 us (18%)
  Pallas kernels  86.8 us (15%)
  other arithmetic  32.4 us (6%)
  local copies, waits for them, and re-layouts  23 us (4%)
  between operations  15.3 us (3%)
  matrix products  6.02 us (1%)
    ppermute x46, waiting for transfers between devices, rotate(): return lax.ppermute(x, axis, [(i, (i + by) % peers) for i in range(peers)])  154 us
    ppermute x12, waiting for transfers between devices, send_active(): return lax.ppermute(x, 'section', pairs)  88.5 us
    pallas_call x14, Pallas kernels, stage_call(): pl.pallas_call(functools.partial(kernel, taps=taps, length=length, width=...  86.8 us
    ppermute x46, starting transfers between devices, rotate(): return lax.ppermute(x, axis, [(i, (i + by) % peers) for i in range(peers)])  74.6 us
    all_gather x1, waiting for transfers between devices, gather_weights(): w_in_full = lax.all_gather(mine, 'batch', axis=0, tiled=False)  33.3 us
    ppermute x12, starting transfers between devices, send_active(): return lax.ppermute(x, 'section', pairs)  25.1 us
    ppermute x5, waiting for transfers between devices, swap_pair(): return lax.ppermute(x, 'fsdp', [(i, i ^ 1) for i in range(peers)])  22.5 us
    another operation x14, other arithmetic, info_at(): jnp.stack([slot, active.astype(jnp.int32), first.astype(jnp.int32), lengt...  17.3 us
  transfers between devices with their start and end apart: 65, of which 40 were waited for; matrix products, arithmetic and copies ran while one was open for 8% of the time, Pallas kernels for 0%

profile of v2, /device:TPU:8, one launch (start us, length us, event | category | flops | bytes accessed | tf_op | source)
XLA Modules:
  0.0 565.9 jit_solution(546016446977073389)
XLA Ops:
  8.1 2.3 collective-permute-start
  11.3 2.5 collective-permute-done
  15.9 4.0 collective-permute-start.2
  21.1 4.8 collective-permute-done.1
  25.9 3.2 collective-permute-start.4
  29.2 5.1 collective-permute-done.3
  34.4 3.2 collective-permute-start.6
  37.7 4.2 collective-permute-done.6
  41.9 3.8 collective-permute-start.8
  45.9 2.5 collective-permute-done.8
  48.4 3.8 collective-permute-done.7
  54.2 6.3 %collective-permute-done.9 = bf16[96,1536]{1,0:T(8,128)(2,1)S(1)} collective-permute-done((bf16[96,1536]{1,0:T(8,128)(2,1)S(1)}, bf16[96,1536]{1,0:T(8,128)(2,1)S(1)}, u32[]{:S(2)}, u32[]{:S(2)}) %collective-permute-start.9) | collective-permute-done | bytes 294944 | tf_op jit(solution)/shard_map/ppermute | solution.py:29
  60.7 3.2 collective-permute-start.11
  64.0 3.4 concatenate.67.params
  69.4 2.7 broadcast_in_dim.97
  74.0 3.5 collective-permute-start.13
  79.2 8.5 %collective-permute-done.12 = bf16[2,96,1536]{2,1,0:T(8,128)(2,1)S(1)} collective-permute-done((bf16[2,96,1536]{2,1,0:T(8,128)(2,1)S(1)}, bf16[2,96,1536]{2,1,0:T(8,128)(2,1)S(1)}, u32[]{:S(2)}, u32[]{:S(2)}) %collective-permute-start.12) | collective-permute-done | bytes 589856 | tf_op jit(solution)/shard_map/ppermute | solution.py:24
  88.0 3.7 collective-permute-start.15
  93.5 8.8 %collective-permute-done.15 = bf16[2,96,1536]{2,1,0:T(8,128)(2,1)S(1)} collective-permute-done((bf16[2,96,1536]{2,1,0:T(8,128)(2,1)S(1)}, bf16[2,96,1536]{2,1,0:T(8,128)(2,1)S(1)}, u32[]{:S(2)}, u32[]{:S(2)}) %collective-permute-start.15) | collective-permute-done | bytes 589856 | tf_op jit(solution)/shard_map/ppermute | solution.py:24
  102.3 3.8 collective-permute-start.17
  108.0 2.3 collective-permute-done.17
  110.3 3.8 collective-permute-done.16
  115.0 33.3 %all-gather.2.cloned.1.call-done.w_in = bf16[4,1536,768]{2,1,0:T(8,128)(2,1)} async-done(((bf16[1,1536,768]{2,1,0:T(8,128)(2,1)}), bf16[4,1536,768]{2,1,0:T(8,128)(2,1)}) %all-gather.2.cloned.1.call-update) | async-done | bytes 9437200 | tf_op jit(solution)/shard_map/all_gather | solution.py:450
  148.9 8.3 %shard_map.127 = (bf16[48,1536]{1,0:T(8,128)(2,1)}, bf16[4,48,1536]{2,1,0:T(8,128)(2,1)}, bf16[4,48,1536]{2,1,0:T(8,128)(2,1)}, bf16[4,48,1536]{2,1,0:T(8,128)(2...) custom-call(s32[4]{0:T(128)} %pad_add_fusion.12.info, ...), custom_call_target="tpu_custom_call" | custom-call | flops 679477248 | bytes 14155776 | tf_op jit(solution)/shard_map/pallas_call | solution.py:373
  160.5 8.3 %shard_map.128 = (bf16[48,1536]{1,0:T(8,128)(2,1)}, bf16[4,48,1536]{2,1,0:T(8,128)(2,1)}, bf16[4,48,1536]{2,1,0:T(8,128)(2,1)}, bf16[4,48,1536]{2,1,0:T(8,128)(2...) custom-call(s32[4]{0:T(128)} %pad_add_fusion.11.info, ...), custom_call_target="tpu_custom_call", output_to_operand_aliasing={{1}: (6, {}), {2}: (7, {}), {3}: (8, {}), {4}: (9, {}), {5}... | custom-call | flops 679477248 | bytes 14155776 | tf_op jit(solution)/shard_map/pallas_call | solution.py:373
  168.8 2.3 collective-permute-start.19
  172.2 8.3 %shard_map.129 = (bf16[48,1536]{1,0:T(8,128)(2,1)}, bf16[4,48,1536]{2,1,0:T(8,128)(2,1)}, bf16[4,48,1536]{2,1,0:T(8,128)(2,1)}, bf16[4,48,1536]{2,1,0:T(8,128)(2...) custom-call(s32[4]{0:T(128)} %pad_add_fusion.10.info, ...), custom_call_target="tpu_custom_call", output_to_operand_aliasing={{1}: (6, {}), {2}: (7, {}), {3}: (8, {}), {4}: (9, {}), {5}... | custom-call | flops 679477248 | bytes 14155776 | tf_op jit(solution)/shard_map/pallas_call | solution.py:373
  180.5 3.2 collective-permute-start.20
  184.8 8.7 %shard_map.130 = (bf16[48,1536]{1,0:T(8,128)(2,1)}, bf16[4,48,1536]{2,1,0:T(8,128)(2,1)}, bf16[4,48,1536]{2,1,0:T(8,128)(2,1)}, bf16[4,48,1536]{2,1,0:T(8,128)(2...) custom-call(s32[4]{0:T(128)} %pad_add_fusion.9.info, ...), custom_call_target="tpu_custom_call", output_to_operand_aliasing={{1}: (6, {}), {2}: (7, {}), {3}: (8, {}), {4}: (9, {}), {5}... | custom-call | flops 679477248 | bytes 14155776 | tf_op jit(solution)/shard_map/pallas_call | solution.py:373
  193.5 7.1 %collective-permute-start.21 = (bf16[48,1536]{1,0:T(8,128)(2,1)}, bf16[48,1536]{1,0:T(8,128)(2,1)}, u32[]{:S(2)}, u32[]{:S(2)}) collective-permute-start(bf16[48,1536]{1,0:T(8,128)(2,1)} %get-tuple-element.119), channel_id=1, source_target_pairs={{0,64},{64,128},{128,192},{1,65},{65,129},{129,193},{2,66},{66,130... | collective-permute-start | bytes 442376 | tf_op jit(solution)/shard_map/ppermute | solution.py:483
  221.0 72.0 %collective-permute-done.26.incoming = bf16[48,1536]{1,0:T(8,128)(2,1)} collective-permute-done((bf16[48,1536]{1,0:T(8,128)(2,1)}, bf16[48,1536]{1,0:T(8,128)(2,1)}, u32[]{:S(2)}, u32[]{:S(2)}) %collective-permute-start.26) | collective-permute-done | bytes 147488 | tf_op jit(solution)/shard_map/ppermute | solution.py:483
  293.0 12.1 %shard_map.137 = (bf16[48,1536]{1,0:T(8,128)(2,1)}, bf16[4,48,1536]{2,1,0:T(8,128)(2,1)}, bf16[4,48,3072]{2,1,0:T(8,128)(2,1)}, bf16[4,48,1536]{2,1,0:T(8,128)(2,1)}, f32[4,48,1536]{2,1,0:T(8,128)}) custom-call(s32[4]{0:T(128)} %pad_add_fusion.3.info, ...), custom_call_target="tpu_custom_call", output_to_operand_aliasing={{1}: (11, {}), {2}: (12, {}), {3}: (13, {}), {4}: (14, {})} | custom-call | flops 679477248 | bytes 14155776 | tf_op jit(solution)/shard_map/pallas_call | solution.py:373
  307.8 5.6 collective-permute-done.27.incoming
  313.4 11.9 %shard_map.138 = (bf16[48,1536]{1,0:T(8,128)(2,1)}, bf16[4,48,1536]{2,1,0:T(8,128)(2,1)}, bf16[4,48,3072]{2,1,0:T(8,128)(2,1)}, bf16[4,48,1536]{2,1,0:T(8,128)(2,1)}, f32[4,48,1536]{2,1,0:T(8,128)}) custom-call(s32[4]{0:T(128)} %pad_add_fusion.2.info, ...), custom_call_target="tpu_custom_call", output_to_operand_aliasing={{1}: (11, {}), {2}: (12, {}), {3}: (13, {}), {4}: (14, {})} | custom-call | flops 679477248 | bytes 14155776 | tf_op jit(solution)/shard_map/pallas_call | solution.py:373
  328.0 5.7 %collective-permute-done.28.incoming = bf16[48,1536]{1,0:T(8,128)(2,1)} collective-permute-done((bf16[48,1536]{1,0:T(8,128)(2,1)}, bf16[48,1536]{1,0:T(8,128)(2,1)}, u32[]{:S(2)}, u32[]{:S(2)}) %collective-permute-start.28) | collective-permute-done | bytes 147488 | tf_op jit(solution)/shard_map/ppermute | solution.py:483
  333.6 11.9 %shard_map.139 = (bf16[48,1536]{1,0:T(8,128)(2,1)}, bf16[4,48,1536]{2,1,0:T(8,128)(2,1)}, bf16[4,48,3072]{2,1,0:T(8,128)(2,1)}, bf16[4,48,1536]{2,1,0:T(8,128)(2,1)}, f32[4,48,1536]{2,1,0:T(8,128)}) custom-call(s32[4]{0:T(128)} %pad_add_fusion.1.info, ...), custom_call_target="tpu_custom_call", output_to_operand_aliasing={{1}: (11, {}), {2}: (12, {}), {3}: (13, {}), {4}: (14, {})} | custom-call | flops 679477248 | bytes 14155776 | tf_op jit(solution)/shard_map/pallas_call | solution.py:373
  348.1 5.2 collective-permute-done.29.incoming
  353.2 12.3 %shard_map.140 = (bf16[48,1536]{1,0:T(8,128)(2,1)}, bf16[4,48,1536]{2,1,0:T(8,128)(2,1)}, bf16[4,48,3072]{2,1,0:T(8,128)(2,1)}, bf16[4,48,1536]{2,1,0:T(8,128)(2,1)}, f32[4,48,1536]{2,1,0:T(8,128)}) custom-call(s32[4]{0:T(128)} %pad_add_fusion.info, ...), custom_call_target="tpu_custom_call", output_to_operand_aliasing={{1}: (11, {}), {2}: (12, {}), {3}: (13, {}), {4}: (14, {})} | custom-call | flops 679477248 | bytes 14155776 | tf_op jit(solution)/shard_map/pallas_call | solution.py:373
  370.2 4.7 pad_maximum_fusion
  382.7 8.8 %collective-permute-done.42 = bf16[112,1536]{1,0:T(8,128)(2,1)S(1)} collective-permute-done((bf16[112,1536]{1,0:T(8,128)(2,1)S(1)}, bf16[112,1536]{1,0:T(8,128)(2,1)S(1)}, u32[]{:S(2)}, u32[]{:S(2)}) %collective-permute-start.42) | collective-permute-done | bytes 344096 | tf_op jit(solution)/shard_map/ppermute | solution.py:24
  391.9 3.5 collective-permute-start.47
  395.4 15.8 %collective-permute-done.43 = bf16[2,112,1536]{2,1,0:T(8,128)(2,1)S(1)} collective-permute-done((bf16[2,112,1536]{2,1,0:T(8,128)(2,1)S(1)}, bf16[2,112,1536]{2,1,0:T(8,128)(2,1)S(1)}, u32[]{:S(2)}, u32[]{:S(2)}) %collective-permute-start.43) | collective-permute-done | bytes 688160 | tf_op jit(solution)/shard_map/ppermute | solution.py:24
  411.6 3.2 collective-permute-start.48
  414.8 14.9 %collective-permute-done.44 = bf16[2,112,1536]{2,1,0:T(8,128)(2,1)S(1)} collective-permute-done((bf16[2,112,1536]{2,1,0:T(8,128)(2,1)S(1)}, bf16[2,112,1536]{2,1,0:T(8,128)(2,1)S(1)}, u32[]{:S(2)}, u32[]{:S(2)}) %collective-permute-start.44) | collective-permute-done | bytes 688160 | tf_op jit(solution)/shard_map/ppermute | solution.py:24
  430.1 3.1 collective-permute-start.49
  433.2 8.5 %collective-permute-done.49 = bf16[2,112,1536]{2,1,0:T(8,128)(2,1)S(1)} collective-permute-done((bf16[2,112,1536]{2,1,0:T(8,128)(2,1)S(1)}, bf16[2,112,1536]{2,1,0:T(8,128)(2,1)S(1)}, u32[]{:S(2)}, u32[]{:S(2)}) %collective-permute-start.49) | collective-permute-done | bytes 688160 | tf_op jit(solution)/shard_map/ppermute | solution.py:24
  441.6 3.7 collective-permute-done.45
  447.3 6.7 %collective-permute-done.50 = bf16[112,1536]{1,0:T(8,128)(2,1)S(1)} collective-permute-done((bf16[112,1536]{1,0:T(8,128)(2,1)S(1)}, bf16[112,1536]{1,0:T(8,128)(2,1)S(1)}, u32[]{:S(2)}, u32[]{:S(2)}) %collective-permute-start.50) | collective-permute-done | bytes 344096 | tf_op jit(solution)/shard_map/ppermute | solution.py:29
  458.5 12.7 %collective-permute-done.53 = bf16[112,1536]{1,0:T(8,128)(2,1)S(1)} collective-permute-done((bf16[112,1536]{1,0:T(8,128)(2,1)S(1)}, bf16[112,1536]{1,0:T(8,128)(2,1)S(1)}, u32[]{:S(2)}, u32[]{:S(2)}) %collective-permute-start.53) | collective-permute-done | bytes 344096 | tf_op jit(solution)/shard_map/ppermute | solution.py:24
  471.2 3.0 collective-permute-done.52
  474.2 5.5 collective-permute-done.51
  481.4 2.4 collective-permute-done.54
  487.4 2.3 collective-permute-done.55
  489.7 3.4 collective-permute-start.58
  495.0 3.7 collective-permute-start.60
  500.3 3.2 collective-permute-start.34
  503.5 3.7 collective-permute-done.30
  508.6 3.1 collective-permute-start.62
  513.2 5.6 collective-permute-done.31
  521.4 5.6 collective-permute-done.32
  529.9 4.6 collective-permute-done.36
  536.1 5.4 collective-permute-done.37
  543.4 4.6 collective-permute-done.38
  553.2 2.8 collective-permute-done.40
  (212 shorter events, 100.6 us)
Async XLA Ops:
  7.2 141.1 %all-gather.2.cloned.1.call-start = ((), (), s32[]{:S(2)}) async-start(), calls=%async_computation.1 | async-start | bytes 11796480 | tf_op jit(solution)/shard_map/all_gather | solution.py:450
  8.1 5.7 %collective-permute-start = (bf16[96,768]{1,0:T(8,128)(2,1)S(1)}, bf16[96,768]{1,0:T(8,128)(2,1)S(1)}, u32[]{:S(2)}, u32[]{:S(2)}) collective-permute-start(bf16[96,768]{1,0:T(8,128)(2,1)S(1)} %fusion.61), channel_id=1, source_target_pairs={{0,4},{4,0},{8,12},{12,8},{16,20},{20,16},{24,28},{28,24},{32,36},... | collective-permute-start | bytes 442376 | tf_op jit(solution)/shard_map/ppermute | solution.py:29
  13.9 12.1 %collective-permute-start.1 = (bf16[2,96,768]{2,1,0:T(8,128)(2,1)S(1)}, bf16[2,96,768]{2,1,0:T(8,128)(2,1)S(1)}, u32[]{:S(2)}, u32[]{:S(2)}) collective-permute-start(bf16[2,96,768]{2,1,0:T(8,128)(2,1)S(1)} %maximum_select_fusion.3), channel_id=1, source_target_pairs={{0,8},{4,12},{8,16},{12,20},{16,24},{20,28},{24,32},{28,36},{32,40... | collective-permute-start | bytes 884744 | tf_op jit(solution)/shard_map/ppermute | solution.py:24
  15.9 10.1 %collective-permute-start.2 = (bf16[2,96,768]{2,1,0:T(8,128)(2,1)S(1)}, bf16[2,96,768]{2,1,0:T(8,128)(2,1)S(1)}, u32[]{:S(2)}, u32[]{:S(2)}) collective-permute-start(bf16[2,96,768]{2,1,0:T(8,128)(2,1)S(1)} %maximum_select_fusion.3), channel_id=1, source_target_pairs={{0,56},{4,60},{8,0},{12,4},{16,8},{20,12},{24,16},{28,20},{32,24},... | collective-permute-start | bytes 884744 | tf_op jit(solution)/shard_map/ppermute | solution.py:24
  25.9 8.4 %collective-permute-start.3 = (bf16[2,96,768]{2,1,0:T(8,128)(2,1)S(1)}, bf16[2,96,768]{2,1,0:T(8,128)(2,1)S(1)}, u32[]{:S(2)}, u32[]{:S(2)}) collective-permute-start(bf16[2,96,768]{2,1,0:T(8,128)(2,1)S(1)} %collective-permute-done.1), channel_id=1, source_target_pairs={{0,8},{4,12},{8,16},{12,20},{16,24},{20,28},{24,32},{28,36},{32,40... | collective-permute-start | bytes 884744 | tf_op jit(solution)/shard_map/ppermute | solution.py:24
  25.9 8.4 %collective-permute-start.4 = (bf16[2,96,768]{2,1,0:T(8,128)(2,1)S(1)}, bf16[2,96,768]{2,1,0:T(8,128)(2,1)S(1)}, u32[]{:S(2)}, u32[]{:S(2)}) collective-permute-start(bf16[2,96,768]{2,1,0:T(8,128)(2,1)S(1)} %collective-permute-done.2), channel_id=1, source_target_pairs={{0,56},{4,60},{8,0},{12,4},{16,8},{20,12},{24,16},{28,20},{32,24},... | collective-permute-start | bytes 884744 | tf_op jit(solution)/shard_map/ppermute | solution.py:24
  34.4 11.3 %collective-permute-start.5 = (bf16[2,96,768]{2,1,0:T(8,128)(2,1)S(1)}, bf16[2,96,768]{2,1,0:T(8,128)(2,1)S(1)}, u32[]{:S(2)}, u32[]{:S(2)}) collective-permute-start(bf16[2,96,768]{2,1,0:T(8,128)(2,1)S(1)} %collective-permute-done.3), channel_id=1, source_target_pairs={{0,8},{4,12},{8,16},{12,20},{16,24},{20,28},{24,32},{28,36},{32,40... | collective-permute-start | bytes 884744 | tf_op jit(solution)/shard_map/ppermute | solution.py:24
  34.4 7.5 %collective-permute-start.6 = (bf16[2,96,768]{2,1,0:T(8,128)(2,1)S(1)}, bf16[2,96,768]{2,1,0:T(8,128)(2,1)S(1)}, u32[]{:S(2)}, u32[]{:S(2)}) collective-permute-start(bf16[2,96,768]{2,1,0:T(8,128)(2,1)S(1)} %collective-permute-done.4), channel_id=1, source_target_pairs={{0,56},{4,60},{8,0},{12,4},{16,8},{20,12},{24,16},{28,20},{32,24},... | collective-permute-start | bytes 884744 | tf_op jit(solution)/shard_map/ppermute | solution.py:24
  41.9 6.5 %collective-permute-start.8 = (bf16[96,768]{1,0:T(8,128)(2,1)S(1)}, bf16[96,768]{1,0:T(8,128)(2,1)S(1)}, u32[]{:S(2)}, u32[]{:S(2)}) collective-permute-start(bf16[96,768]{1,0:T(8,128)(2,1)S(1)} %slice_bitcast_fusion.9), channel_id=1, source_target_pairs={{0,56},{4,60},{8,0},{12,4},{16,8},{20,12},{24,16},{28,20},{32,24},... | collective-permute-start | bytes 442376 | tf_op jit(solution)/shard_map/ppermute | solution.py:24
  45.7 6.4 %collective-permute-start.7 = (bf16[96,768]{1,0:T(8,128)(2,1)S(1)}, bf16[96,768]{1,0:T(8,128)(2,1)S(1)}, u32[]{:S(2)}, u32[]{:S(2)}) collective-permute-start(bf16[96,768]{1,0:T(8,128)(2,1)S(1)} %slice_bitcast_fusion.10), channel_id=1, source_target_pairs={{0,8},{4,12},{8,16},{12,20},{16,24},{20,28},{24,32},{28,36},{32,40... | collective-permute-start | bytes 442376 | tf_op jit(solution)/shard_map/ppermute | solution.py:24
  53.6 445.2 %reduce-scatter.2.cloned.1.call-start = ((), (), s32[]{:S(2)}) async-start(), calls=%async_computation.2 | async-start | bytes 11796480 | tf_op jit(solution)/shard_map/reduce_scatter | solution.py:466
  53.7 6.8 %collective-permute-start.9 = (bf16[96,1536]{1,0:T(8,128)(2,1)S(1)}, bf16[96,1536]{1,0:T(8,128)(2,1)S(1)}, u32[]{:S(2)}, u32[]{:S(2)}) collective-permute-start(bf16[96,1536]{1,0:T(8,128)(2,1)S(1)} %bitcast.289), channel_id=1, source_target_pairs={{0,4},{4,0},{8,12},{12,8},{16,20},{20,16},{24,28},{28,24},{32,36},... | collective-permute-start | bytes 884744 | tf_op jit(solution)/shard_map/ppermute | solution.py:29
  60.6 13.3 %collective-permute-start.10 = (bf16[2,96,1536]{2,1,0:T(8,128)(2,1)S(1)}, bf16[2,96,1536]{2,1,0:T(8,128)(2,1)S(1)}, u32[]{:S(2)}, u32[]{:S(2)}) collective-permute-start(bf16[2,96,1536]{2,1,0:T(8,128)(2,1)S(1)} %maximum_select_fusion.1), channel_id=1, source_target_pairs={{0,8},{4,12},{8,16},{12,20},{16,24},{20,28},{24,32},{28,36},{32,40... | collective-permute-start | bytes 1769480 | tf_op jit(solution)/shard_map/ppermute | solution.py:24
  60.7 13.3 %collective-permute-start.11 = (bf16[2,96,1536]{2,1,0:T(8,128)(2,1)S(1)}, bf16[2,96,1536]{2,1,0:T(8,128)(2,1)S(1)}, u32[]{:S(2)}, u32[]{:S(2)}) collective-permute-start(bf16[2,96,1536]{2,1,0:T(8,128)(2,1)S(1)} %maximum_select_fusion.1), channel_id=1, source_target_pairs={{0,56},{4,60},{8,0},{12,4},{16,8},{20,12},{24,16},{28,20},{32,24},... | collective-permute-start | bytes 1769480 | tf_op jit(solution)/shard_map/ppermute | solution.py:24
  74.0 13.8 %collective-permute-start.12 = (bf16[2,96,1536]{2,1,0:T(8,128)(2,1)S(1)}, bf16[2,96,1536]{2,1,0:T(8,128)(2,1)S(1)}, u32[]{:S(2)}, u32[]{:S(2)}) collective-permute-start(bf16[2,96,1536]{2,1,0:T(8,128)(2,1)S(1)} %collective-permute-done.10), channel_id=1, source_target_pairs={{0,8},{4,12},{8,16},{12,20},{16,24},{20,28},{24,32},{28,36},{32,40... | collective-permute-start | bytes 1769480 | tf_op jit(solution)/shard_map/ppermute | solution.py:24
  74.0 14.1 %collective-permute-start.13 = (bf16[2,96,1536]{2,1,0:T(8,128)(2,1)S(1)}, bf16[2,96,1536]{2,1,0:T(8,128)(2,1)S(1)}, u32[]{:S(2)}, u32[]{:S(2)}) collective-permute-start(bf16[2,96,1536]{2,1,0:T(8,128)(2,1)S(1)} %collective-permute-done.11), channel_id=1, source_target_pairs={{0,56},{4,60},{8,0},{12,4},{16,8},{20,12},{24,16},{28,20},{32,24},... | collective-permute-start | bytes 1769480 | tf_op jit(solution)/shard_map/ppermute | solution.py:24
  87.7 18.4 %collective-permute-start.14 = (bf16[2,96,1536]{2,1,0:T(8,128)(2,1)S(1)}, bf16[2,96,1536]{2,1,0:T(8,128)(2,1)S(1)}, u32[]{:S(2)}, u32[]{:S(2)}) collective-permute-start(bf16[2,96,1536]{2,1,0:T(8,128)(2,1)S(1)} %collective-permute-done.12), channel_id=1, source_target_pairs={{0,8},{4,12},{8,16},{12,20},{16,24},{20,28},{24,32},{28,36},{32,40... | collective-permute-start | bytes 1769480 | tf_op jit(solution)/shard_map/ppermute | solution.py:24
  88.0 14.3 %collective-permute-start.15 = (bf16[2,96,1536]{2,1,0:T(8,128)(2,1)S(1)}, bf16[2,96,1536]{2,1,0:T(8,128)(2,1)S(1)}, u32[]{:S(2)}, u32[]{:S(2)}) collective-permute-start(bf16[2,96,1536]{2,1,0:T(8,128)(2,1)S(1)} %collective-permute-done.13), channel_id=1, source_target_pairs={{0,56},{4,60},{8,0},{12,4},{16,8},{20,12},{24,16},{28,20},{32,24},... | collective-permute-start | bytes 1769480 | tf_op jit(solution)/shard_map/ppermute | solution.py:24
  102.3 8.0 %collective-permute-start.17 = (bf16[96,1536]{1,0:T(8,128)(2,1)S(1)}, bf16[96,1536]{1,0:T(8,128)(2,1)S(1)}, u32[]{:S(2)}, u32[]{:S(2)}) collective-permute-start(bf16[96,1536]{1,0:T(8,128)(2,1)S(1)} %slice_bitcast_fusion.6), channel_id=1, source_target_pairs={{0,56},{4,60},{8,0},{12,4},{16,8},{20,12},{24,16},{28,20},{32,24},... | collective-permute-start | bytes 884744 | tf_op jit(solution)/shard_map/ppermute | solution.py:24
  106.1 8.0 %collective-permute-start.16 = (bf16[96,1536]{1,0:T(8,128)(2,1)S(1)}, bf16[96,1536]{1,0:T(8,128)(2,1)S(1)}, u32[]{:S(2)}, u32[]{:S(2)}) collective-permute-start(bf16[96,1536]{1,0:T(8,128)(2,1)S(1)} %slice_bitcast_fusion.7), channel_id=1, source_target_pairs={{0,8},{4,12},{8,16},{12,20},{16,24},{20,28},{24,32},{28,36},{32,40... | collective-permute-start | bytes 884744 | tf_op jit(solution)/shard_map/ppermute | solution.py:24
  157.2 3.3 collective-permute-start.18
  168.8 3.4 collective-permute-start.19
  180.5 4.3 collective-permute-start.20
  193.5 8.4 %collective-permute-start.21 = (bf16[48,1536]{1,0:T(8,128)(2,1)}, bf16[48,1536]{1,0:T(8,128)(2,1)}, u32[]{:S(2)}, u32[]{:S(2)}) collective-permute-start(bf16[48,1536]{1,0:T(8,128)(2,1)} %get-tuple-element.119), channel_id=1, source_target_pairs={{0,64},{64,128},{128,192},{1,65},{65,129},{129,193},{2,66},{66,130... | collective-permute-start | bytes 442376 | tf_op jit(solution)/shard_map/ppermute | solution.py:483
  206.0 3.8 collective-permute-start.23
  211.7 2.6 collective-permute-start.24
  215.1 2.6 collective-permute-start.25
  218.5 74.5 %collective-permute-start.26 = (bf16[48,1536]{1,0:T(8,128)(2,1)}, bf16[48,1536]{1,0:T(8,128)(2,1)}, u32[]{:S(2)}, u32[]{:S(2)}) collective-permute-start(bf16[48,1536]{1,0:T(8,128)(2,1)} %get-tuple-element.158), channel_id=1, source_target_pairs={{192,128},{128,64},{64,0},{193,129},{129,65},{65,1},{194,130},{130... | collective-permute-start | bytes 442376 | tf_op jit(solution)/shard_map/ppermute | solution.py:483
  305.1 8.3 %collective-permute-start.27 = (bf16[48,1536]{1,0:T(8,128)(2,1)}, bf16[48,1536]{1,0:T(8,128)(2,1)}, u32[]{:S(2)}, u32[]{:S(2)}) collective-permute-start(bf16[48,1536]{1,0:T(8,128)(2,1)} %get-tuple-element.163), channel_id=1, source_target_pairs={{192,128},{128,64},{64,0},{193,129},{129,65},{65,1},{194,130},{130... | collective-permute-start | bytes 442376 | tf_op jit(solution)/shard_map/ppermute | solution.py:483
  325.4 8.3 %collective-permute-start.28 = (bf16[48,1536]{1,0:T(8,128)(2,1)}, bf16[48,1536]{1,0:T(8,128)(2,1)}, u32[]{:S(2)}, u32[]{:S(2)}) collective-permute-start(bf16[48,1536]{1,0:T(8,128)(2,1)} %get-tuple-element.168), channel_id=1, source_target_pairs={{128,64},{64,0},{129,65},{65,1},{130,66},{66,2},{131,67},{67,3},{1... | collective-permute-start | bytes 442376 | tf_op jit(solution)/shard_map/ppermute | solution.py:483
  345.6 7.7 %collective-permute-start.29 = (bf16[48,1536]{1,0:T(8,128)(2,1)}, bf16[48,1536]{1,0:T(8,128)(2,1)}, u32[]{:S(2)}, u32[]{:S(2)}) collective-permute-start(bf16[48,1536]{1,0:T(8,128)(2,1)} %get-tuple-element.173), channel_id=1, source_target_pairs={{64,0},{65,1},{66,2},{67,3},{68,4},{69,5},{70,6},{71,7},{72,8},{73... | collective-permute-start | bytes 442376 | tf_op jit(solution)/shard_map/ppermute | solution.py:483
  379.2 12.4 %collective-permute-start.42 = (bf16[112,1536]{1,0:T(8,128)(2,1)S(1)}, bf16[112,1536]{1,0:T(8,128)(2,1)S(1)}, u32[]{:S(2)}, u32[]{:S(2)}) collective-permute-start(bf16[112,1536]{1,0:T(8,128)(2,1)S(1)} %get-tuple-element.220), channel_id=1, source_target_pairs={{0,8},{4,12},{8,16},{12,20},{16,24},{20,28},{24,32},{28,36},{32,40... | collective-permute-start | bytes 1032200 | tf_op jit(solution)/shard_map/ppermute | solution.py:24
  380.8 11.0 %collective-permute-start.46 = (bf16[112,1536]{1,0:T(8,128)(2,1)S(1)}, bf16[112,1536]{1,0:T(8,128)(2,1)S(1)}, u32[]{:S(2)}, u32[]{:S(2)}) collective-permute-start(bf16[112,1536]{1,0:T(8,128)(2,1)S(1)} %get-tuple-element.221), channel_id=1, source_target_pairs={{0,56},{4,60},{8,0},{12,4},{16,8},{20,12},{24,16},{28,20},{32,24},... | collective-permute-start | bytes 1032200 | tf_op jit(solution)/shard_map/ppermute | solution.py:24
  391.7 19.5 %collective-permute-start.43 = (bf16[2,112,1536]{2,1,0:T(8,128)(2,1)S(1)}, bf16[2,112,1536]{2,1,0:T(8,128)(2,1)S(1)}, u32[]{:S(2)}, u32[]{:S(2)}) collective-permute-start(bf16[2,112,1536]{2,1,0:T(8,128)(2,1)S(1)} %pad_maximum_fusion.1), channel_id=1, source_target_pairs={{0,8},{4,12},{8,16},{12,20},{16,24},{20,28},{24,32},{28,36},{32,40... | collective-permute-start | bytes 2064392 | tf_op jit(solution)/shard_map/ppermute | solution.py:24
  391.9 19.2 %collective-permute-start.47 = (bf16[2,112,1536]{2,1,0:T(8,128)(2,1)S(1)}, bf16[2,112,1536]{2,1,0:T(8,128)(2,1)S(1)}, u32[]{:S(2)}, u32[]{:S(2)}) collective-permute-start(bf16[2,112,1536]{2,1,0:T(8,128)(2,1)S(1)} %pad_maximum_fusion.2), channel_id=1, source_target_pairs={{0,56},{4,60},{8,0},{12,4},{16,8},{20,12},{24,16},{28,20},{32,24},... | collective-permute-start | bytes 2064392 | tf_op jit(solution)/shard_map/ppermute | solution.py:24
  411.5 18.2 %collective-permute-start.44 = (bf16[2,112,1536]{2,1,0:T(8,128)(2,1)S(1)}, bf16[2,112,1536]{2,1,0:T(8,128)(2,1)S(1)}, u32[]{:S(2)}, u32[]{:S(2)}) collective-permute-start(bf16[2,112,1536]{2,1,0:T(8,128)(2,1)S(1)} %get-tuple-element.204), channel_id=1, source_target_pairs={{0,8},{4,12},{8,16},{12,20},{16,24},{20,28},{24,32},{28,36},{32,40... | collective-permute-start | bytes 2064392 | tf_op jit(solution)/shard_map/ppermute | solution.py:24
  411.6 18.1 %collective-permute-start.48 = (bf16[2,112,1536]{2,1,0:T(8,128)(2,1)S(1)}, bf16[2,112,1536]{2,1,0:T(8,128)(2,1)S(1)}, u32[]{:S(2)}, u32[]{:S(2)}) collective-permute-start(bf16[2,112,1536]{2,1,0:T(8,128)(2,1)S(1)} %get-tuple-element.205), channel_id=1, source_target_pairs={{0,56},{4,60},{8,0},{12,4},{16,8},{20,12},{24,16},{28,20},{32,24},... | collective-permute-start | bytes 2064392 | tf_op jit(solution)/shard_map/ppermute | solution.py:24
  430.1 11.5 %collective-permute-start.49 = (bf16[2,112,1536]{2,1,0:T(8,128)(2,1)S(1)}, bf16[2,112,1536]{2,1,0:T(8,128)(2,1)S(1)}, u32[]{:S(2)}, u32[]{:S(2)}) collective-permute-start(bf16[2,112,1536]{2,1,0:T(8,128)(2,1)S(1)} %get-tuple-element.203), channel_id=1, source_target_pairs={{0,56},{4,60},{8,0},{12,4},{16,8},{20,12},{24,16},{28,20},{32,24},... | collective-permute-start | bytes 2064392 | tf_op jit(solution)/shard_map/ppermute | solution.py:24
  433.2 12.1 %collective-permute-start.45 = (bf16[2,112,1536]{2,1,0:T(8,128)(2,1)S(1)}, bf16[2,112,1536]{2,1,0:T(8,128)(2,1)S(1)}, u32[]{:S(2)}, u32[]{:S(2)}) collective-permute-start(bf16[2,112,1536]{2,1,0:T(8,128)(2,1)S(1)} %get-tuple-element.202), channel_id=1, source_target_pairs={{0,8},{4,12},{8,16},{12,20},{16,24},{20,28},{24,32},{28,36},{32,40... | collective-permute-start | bytes 2064392 | tf_op jit(solution)/shard_map/ppermute | solution.py:24
  446.7 7.3 %collective-permute-start.50 = (bf16[112,1536]{1,0:T(8,128)(2,1)S(1)}, bf16[112,1536]{1,0:T(8,128)(2,1)S(1)}, u32[]{:S(2)}, u32[]{:S(2)}) collective-permute-start(bf16[112,1536]{1,0:T(8,128)(2,1)S(1)} %fusion.28), channel_id=1, source_target_pairs={{0,4},{4,0},{8,12},{12,8},{16,20},{20,16},{24,28},{28,24},{32,36},... | collective-permute-start | bytes 1032200 | tf_op jit(solution)/shard_map/ppermute | solution.py:29
  454.2 17.0 %collective-permute-start.53 = (bf16[112,1536]{1,0:T(8,128)(2,1)S(1)}, bf16[112,1536]{1,0:T(8,128)(2,1)S(1)}, u32[]{:S(2)}, u32[]{:S(2)}) collective-permute-start(bf16[112,1536]{1,0:T(8,128)(2,1)S(1)} %fusion.19), channel_id=1, source_target_pairs={{0,3},{1,0},{2,1},{3,2},{4,7},{5,4},{6,5},{7,6},{8,11},{9,8},{10,9... | collective-permute-start | bytes 1032200 | tf_op jit(solution)/shard_map/ppermute | solution.py:24
  456.0 18.2 %collective-permute-start.52 = (bf16[112,1536]{1,0:T(8,128)(2,1)S(1)}, bf16[112,1536]{1,0:T(8,128)(2,1)S(1)}, u32[]{:S(2)}, u32[]{:S(2)}) collective-permute-start(bf16[112,1536]{1,0:T(8,128)(2,1)S(1)} %fusion.19), channel_id=1, source_target_pairs={{0,1},{1,2},{2,3},{3,0},{4,5},{5,6},{6,7},{7,4},{8,9},{9,10},{10,1... | collective-permute-start | bytes 1032200 | tf_op jit(solution)/shard_map/ppermute | solution.py:24
  456.3 23.5 %collective-permute-start.51 = (bf16[112,1536]{1,0:T(8,128)(2,1)S(1)}, bf16[112,1536]{1,0:T(8,128)(2,1)S(1)}, u32[]{:S(2)}, u32[]{:S(2)}) collective-permute-start(bf16[112,1536]{1,0:T(8,128)(2,1)S(1)} %fusion.19), channel_id=1, source_target_pairs={{0,2},{1,3},{2,0},{3,1},{4,6},{5,7},{6,4},{7,5},{8,10},{9,11},{10,... | collective-permute-start | bytes 1032200 | tf_op jit(solution)/shard_map/ppermute | solution.py:24
  479.9 3.9 collective-permute-start.54
  483.8 5.9 %collective-permute-start.55 = (f32[2,3,1536]{2,1,0:T(4,128)S(1)}, f32[2,3,1536]{2,1,0:T(4,128)S(1)}, u32[]{:S(2)}, u32[]{:S(2)}) collective-permute-start(f32[2,3,1536]{2,1,0:T(4,128)S(1)} %maximum_select_fusion.5), channel_id=1, source_target_pairs={{0,8},{4,12},{8,16},{12,20},{16,24},{20,28},{24,32},{28,36},{32,40... | collective-permute-start | bytes 110600 | tf_op jit(solution)/shard_map/ppermute | solution.py:24
  485.5 4.3 collective-permute-start.56
  489.7 5.3 collective-permute-start.57
  489.7 5.3 collective-permute-start.58
  495.0 24.0 %collective-permute-start.59 = (f32[2,3,1536]{2,1,0:T(4,128)S(1)}, f32[2,3,1536]{2,1,0:T(4,128)S(1)}, u32[]{:S(2)}, u32[]{:S(2)}) collective-permute-start(f32[2,3,1536]{2,1,0:T(4,128)S(1)} %collective-permute-done.57), channel_id=1, source_target_pairs={{0,8},{4,12},{8,16},{12,20},{16,24},{20,28},{24,32},{28,36},{32,40... | collective-permute-start | bytes 110600 | tf_op jit(solution)/shard_map/ppermute | solution.py:24
  495.0 13.6 %collective-permute-start.60 = (f32[2,3,1536]{2,1,0:T(4,128)S(1)}, f32[2,3,1536]{2,1,0:T(4,128)S(1)}, u32[]{:S(2)}, u32[]{:S(2)}) collective-permute-start(f32[2,3,1536]{2,1,0:T(4,128)S(1)} %collective-permute-done.58), channel_id=1, source_target_pairs={{0,56},{4,60},{8,0},{12,4},{16,8},{20,12},{24,16},{28,20},{32,24},... | collective-permute-start | bytes 110600 | tf_op jit(solution)/shard_map/ppermute | solution.py:24
  500.2 7.0 %collective-permute-start.30 = (bf16[96,768]{1,0:T(8,128)(2,1)S(1)}, bf16[96,768]{1,0:T(8,128)(2,1)S(1)}, u32[]{:S(2)}, u32[]{:S(2)}) collective-permute-start(bf16[96,768]{1,0:T(8,128)(2,1)S(1)} %get-tuple-element.213), channel_id=1, source_target_pairs={{0,8},{4,12},{8,16},{12,20},{16,24},{20,28},{24,32},{28,36},{32,40... | collective-permute-start | bytes 442376 | tf_op jit(solution)/shard_map/ppermute | solution.py:24
  500.3 7.0 %collective-permute-start.34 = (bf16[96,768]{1,0:T(8,128)(2,1)S(1)}, bf16[96,768]{1,0:T(8,128)(2,1)S(1)}, u32[]{:S(2)}, u32[]{:S(2)}) collective-permute-start(bf16[96,768]{1,0:T(8,128)(2,1)S(1)} %get-tuple-element.215), channel_id=1, source_target_pairs={{0,56},{4,60},{8,0},{12,4},{16,8},{20,12},{24,16},{28,20},{32,24},... | collective-permute-start | bytes 442376 | tf_op jit(solution)/shard_map/ppermute | solution.py:24
  508.3 10.5 %collective-permute-start.31 = (bf16[2,96,768]{2,1,0:T(8,128)(2,1)S(1)}, bf16[2,96,768]{2,1,0:T(8,128)(2,1)S(1)}, u32[]{:S(2)}, u32[]{:S(2)}) collective-permute-start(bf16[2,96,768]{2,1,0:T(8,128)(2,1)S(1)} %pad_maximum_fusion.4), channel_id=1, source_target_pairs={{0,8},{4,12},{8,16},{12,20},{16,24},{20,28},{24,32},{28,36},{32,40... | collective-permute-start | bytes 884744 | tf_op jit(solution)/shard_map/ppermute | solution.py:24
  508.6 27.3 %collective-permute-start.62 = (f32[3,1536]{1,0:T(4,128)S(1)}, f32[3,1536]{1,0:T(4,128)S(1)}, u32[]{:S(2)}, u32[]{:S(2)}) collective-permute-start(f32[3,1536]{1,0:T(4,128)S(1)} %slice_bitcast_fusion.11), channel_id=1, source_target_pairs={{0,56},{4,60},{8,0},{12,4},{16,8},{20,12},{24,16},{28,20},{32,24},... | collective-permute-start | bytes 55304 | tf_op jit(solution)/shard_map/ppermute | solution.py:24
  511.7 9.6 %collective-permute-start.35 = (bf16[2,96,768]{2,1,0:T(8,128)(2,1)S(1)}, bf16[2,96,768]{2,1,0:T(8,128)(2,1)S(1)}, u32[]{:S(2)}, u32[]{:S(2)}) collective-permute-start(bf16[2,96,768]{2,1,0:T(8,128)(2,1)S(1)} %pad_maximum_fusion.5), channel_id=1, source_target_pairs={{0,56},{4,60},{8,0},{12,4},{16,8},{20,12},{24,16},{28,20},{32,24},... | collective-permute-start | bytes 884744 | tf_op jit(solution)/shard_map/ppermute | solution.py:24
  518.9 8.0 %collective-permute-start.32 = (bf16[2,96,768]{2,1,0:T(8,128)(2,1)S(1)}, bf16[2,96,768]{2,1,0:T(8,128)(2,1)S(1)}, u32[]{:S(2)}, u32[]{:S(2)}) collective-permute-start(bf16[2,96,768]{2,1,0:T(8,128)(2,1)S(1)} %fusion.25), channel_id=1, source_target_pairs={{0,8},{4,12},{8,16},{12,20},{16,24},{20,28},{24,32},{28,36},{32,40... | collective-permute-start | bytes 884744 | tf_op jit(solution)/shard_map/ppermute | solution.py:24
  519.1 16.9 %collective-permute-start.61 = (f32[3,1536]{1,0:T(4,128)S(1)}, f32[3,1536]{1,0:T(4,128)S(1)}, u32[]{:S(2)}, u32[]{:S(2)}) collective-permute-start(f32[3,1536]{1,0:T(4,128)S(1)} %slice_bitcast_fusion.12), channel_id=1, source_target_pairs={{0,8},{4,12},{8,16},{12,20},{16,24},{20,28},{24,32},{28,36},{32,40... | collective-permute-start | bytes 55304 | tf_op jit(solution)/shard_map/ppermute | solution.py:24
  527.8 6.7 %collective-permute-start.36 = (bf16[2,96,768]{2,1,0:T(8,128)(2,1)S(1)}, bf16[2,96,768]{2,1,0:T(8,128)(2,1)S(1)}, u32[]{:S(2)}, u32[]{:S(2)}) collective-permute-start(bf16[2,96,768]{2,1,0:T(8,128)(2,1)S(1)} %get-tuple-element.210), channel_id=1, source_target_pairs={{0,56},{4,60},{8,0},{12,4},{16,8},{20,12},{24,16},{28,20},{32,24},... | collective-permute-start | bytes 884744 | tf_op jit(solution)/shard_map/ppermute | solution.py:24
  527.8 8.3 %collective-permute-start.33 = (bf16[2,96,768]{2,1,0:T(8,128)(2,1)}, bf16[2,96,768]{2,1,0:T(8,128)(2,1)}, u32[]{:S(2)}, u32[]{:S(2)}) collective-permute-start(bf16[2,96,768]{2,1,0:T(8,128)(2,1)} %get-tuple-element.209), channel_id=1, source_target_pairs={{0,8},{4,12},{8,16},{12,20},{16,24},{20,28},{24,32},{28,36},{32,40... | collective-permute-start | bytes 884744 | tf_op jit(solution)/shard_map/ppermute | solution.py:24
  534.6 6.9 %collective-permute-start.37 = (bf16[2,96,768]{2,1,0:T(8,128)(2,1)S(1)}, bf16[2,96,768]{2,1,0:T(8,128)(2,1)}, u32[]{:S(2)}, u32[]{:S(2)}) collective-permute-start(bf16[2,96,768]{2,1,0:T(8,128)(2,1)S(1)} %fusion.24), channel_id=1, source_target_pairs={{0,56},{4,60},{8,0},{12,4},{16,8},{20,12},{24,16},{28,20},{32,24},... | collective-permute-start | bytes 884744 | tf_op jit(solution)/shard_map/ppermute | solution.py:24
  542.7 5.2 collective-permute-start.38
  548.0 5.2 collective-permute-start.41
  549.2 6.8 %collective-permute-start.40 = (bf16[96,768]{1,0:T(8,128)(2,1)S(1)}, bf16[96,768]{1,0:T(8,128)(2,1)S(1)}, u32[]{:S(2)}, u32[]{:S(2)}) collective-permute-start(bf16[96,768]{1,0:T(8,128)(2,1)S(1)} %fusion.42), channel_id=1, source_target_pairs={{0,2},{1,3},{2,0},{3,1},{4,6},{5,7},{6,4},{7,5},{8,10},{9,11},{10,... | collective-permute-start | bytes 442376 | tf_op jit(solution)/shard_map/ppermute | solution.py:24
  549.4 8.0 %collective-permute-start.39 = (bf16[96,768]{1,0:T(8,128)(2,1)S(1)}, bf16[96,768]{1,0:T(8,128)(2,1)S(1)}, u32[]{:S(2)}, u32[]{:S(2)}) collective-permute-start(bf16[96,768]{1,0:T(8,128)(2,1)S(1)} %fusion.42), channel_id=1, source_target_pairs={{0,1},{1,2},{2,3},{3,0},{4,5},{5,6},{6,7},{7,4},{8,9},{9,10},{10,1... | collective-permute-start | bytes 442376 | tf_op jit(solution)/shard_map/ppermute | solution.py:24
  (14 other events, 130.4 us)
Sparse Core Ops, SparseCore 0:
  53.7 94.4 all-gather.1
  375.1 103.2 reduce-scatter.1

commit v3 on v2

--- a/solution.py
+++ b/solution.py
@@ -15,6 +15,7 @@
 GAIN_A = 32
 GAIN_B = 40
 PARAM_ROWS = 48
+SKEW = 2
 VMEM_LIMIT = 64 * 1024 * 1024 - 64 * 1024
 PAIR = 2
 
@@ -124,8 +125,12 @@
 
 def write_shifts(shifts, padded):
     span = shifts.shape[1]
-    for by in range(SUBLANES):
-        shifts[by] = padded[pl.ds(by, span), :]
+
+    def shift(lanes):
+        for by in range(SUBLANES):
+            shifts[by, :, lanes] = padded[pl.ds(by, span), lanes]
+
+    each_lane_block(padded.shape[1], shift)
 
 
 def clear_margins(padded, length):
@@ -134,12 +139,16 @@
     padded[pl.ds(MARGIN + length, MARGIN), :] = zeros
 
 
+def each_block(width, size, body):
+    def step(block, carry):
+        body(block, pl.ds(pl.multiple_of(block * size, size), size))
+        return carry
+
+    lax.fori_loop(0, width // size, step, 0)
+
+
 def each_lane_block(width, body):
-    def step(block, carry):
-        body(pl.ds(pl.multiple_of(block * LANES, LANES), LANES))
-        return carry
-
-    lax.fori_loop(0, width // LANES, step, 0)
+    each_block(width, LANES, lambda block, lanes: body(lanes))
 
 
 def shifted(shifts, offset, length, lanes):
@@ -199,15 +208,18 @@
         proj_v[...] = (normed_in * params_v[pl.ds(GAIN_A, 1), :]).astype(jnp.bfloat16)
         save(proj_v, proj_all.at[slot])
         part_width = w_in_v.shape[2]
-        for part in range(parts):
-            w_in_copies[part].wait()
-            out = rows_by(proj_v[...], w_in_v[part])
-            place = part % (parts // 2)
-            lanes = pl.ds(place * part_width, part_width)
-            if part < parts // 2:
-                value_v[:, lanes] = out
-            else:
-                gate_v[:, lanes] = jax.nn.sigmoid(out)
+
+        def into_value(part, lanes):
+            pltpu.make_async_copy(w_in.at[part], w_in_v.at[part], in_sems.at[2 + part]).wait()
+            value_v[:, lanes] = rows_by(proj_v[...], w_in_v[part])
+
+        def into_gate(block, lanes):
+            part = block + parts // 2
+            pltpu.make_async_copy(w_in.at[part], w_in_v.at[part], in_sems.at[2 + part]).wait()
+            gate_v[:, lanes] = jax.nn.sigmoid(rows_by(proj_v[...], w_in_v[part]))
+
+        each_block(width, part_width, into_value)
+        each_block(width, part_width, into_gate)
         save(value_v, value_all.at[slot])
         save(gate_v, gate_all.at[slot])
         rows = lax.broadcasted_iota(jnp.int32, (length, width), 0)
@@ -232,8 +244,14 @@
         swish_v[...] = (scaled_mid * jax.nn.sigmoid(scaled_mid)).astype(jnp.bfloat16)
         save(swish_v, swish_all.at[slot])
         w_out_copy.wait()
-        source = x_v[...].astype(jnp.float32)
-        out_v[...] = (source + rows_by(swish_v[...], w_out_v[...])).astype(jnp.bfloat16)
+
+        def into_out(block, lanes):
+            source = x_v[:, lanes].astype(jnp.float32)
+            out_v[:, lanes] = (source + rows_by(swish_v[...], w_out_v[:, lanes])).astype(
+                jnp.bfloat16
+            )
+
+        each_block(width, part_width, into_out)
         save(out_v, outgoing)
         for copy in saves:
             copy.wait()
@@ -305,7 +323,13 @@
         u_copy.wait()
         save(u_v, up_all.at[slot])
         w_out_copy.wait()
-        swish_grad = rows_back(u_v[...], w_out_v[...])
+        part_width = w_in_v.shape[2]
+
+        def into_swish(block, lanes):
+            conv_v[:, lanes] = rows_back(u_v[...], w_out_v[lanes, :])
+
+        each_block(width, part_width, into_swish)
+        swish_grad = conv_v[...]
         normed_mid = mid_v[...]
         gain_b = params_v[pl.ds(GAIN_B, 1), :]
         scaled_mid = normed_mid * gain_b
@@ -341,12 +365,14 @@
             gated_grad * value_v[...] * glu_gate * (1.0 - glu_gate)
         ).astype(jnp.bfloat16)
         save(grad_v, grad_all.at[slot])
-        part_width = w_in_v.shape[2]
-        input_side = jnp.zeros((length, width), jnp.float32)
-        for part in range(parts):
-            w_in_copies[part].wait()
-            lanes = pl.ds(part * part_width, part_width)
-            input_side = input_side + rows_back(grad_v[:, lanes], w_in_v[part])
+        conv_v[...] = jnp.zeros_like(conv_v)
+
+        def into_input(part, lanes):
+            pltpu.make_async_copy(w_in.at[part], w_in_v.at[part], in_sems.at[8 + part]).wait()
+            conv_v[...] += rows_back(grad_v[:, lanes], w_in_v[part])
+
+        each_block(2 * width, part_width, into_input)
+        input_side = conv_v[...]
         normed_in, inv_in = layer_stats(x_v[...].astype(jnp.float32))
         small_v[pl.ds(GAIN_A, 1), :] = jnp.sum(input_side * normed_in, axis=0, keepdims=True)
         save(small_v, small_all.at[slot])
@@ -478,7 +504,7 @@
     return scale * grad_in.astype(jnp.float32), grad_out, small_sum
 
 
-def send_active(x, moment, senders, by):
+def send_active(x, senders, by):
     pairs = [(s, s + by) for s in senders if 0 <= s + by < lax.axis_size("section")]
     return lax.ppermute(x, "section", pairs)
 
@@ -489,7 +515,7 @@
     micro_count = frames.shape[0]
     frames_len = frames.shape[2]
     model_width = frames.shape[3]
-    moments = micro_count + sections - 1
+    slots = micro_count + SKEW * (sections - 1)
     scale = 1.0 / math.sqrt(
         micro_count * frames_len * lax.axis_size("fsdp") * lax.axis_size("batch")
     )
@@ -509,38 +535,38 @@
     frame_rows = frames.reshape(micro_count, frames_len, model_width)
     cotangent_rows = cotangent.reshape(micro_count, frames_len, model_width)
 
-    def info_at(moment, place, first):
-        micro_index = moment - place
+    def info_table(place):
+        micro_index = jnp.arange(slots, dtype=jnp.int32) - SKEW * place
         active = (micro_index >= 0) & (micro_index < micro_count)
         slot = jnp.clip(micro_index, 0, micro_count - 1)
-        return jnp.stack(
-            [slot, active.astype(jnp.int32), first.astype(jnp.int32), lengths[slot, 0]]
-        ).astype(jnp.int32)
-
-    def active_at(moment, flipped):
-        places = [p for p in range(sections) if 0 <= moment - p < micro_count]
+        first = jnp.broadcast_to(place == 0, active.shape)
+        valid = jnp.take(lengths[:, 0], slot)
+        return jnp.stack([slot, active.astype(jnp.int32), first.astype(jnp.int32), valid], axis=1)
+
+    def active_at(slot, flipped):
+        places = [p for p in range(sections) if 0 <= slot - SKEW * p < micro_count]
         return [sections - 1 - p for p in places] if flipped else places
 
-    incoming = jnp.zeros((frames_len, model_width), jnp.bfloat16)
+    blank = jnp.zeros((frames_len, model_width), jnp.bfloat16)
+    pending = [blank] * SKEW
+    table = info_table(section_index)
     saved = None
-    for moment in range(moments):
-        info = info_at(moment, section_index, section_index == 0)
+    for slot in range(slots):
         outgoing, *saved = forward_stage(
-            info, incoming, frame_rows, w_in_full, w_out_full, params, saved, taps
+            table[slot], pending.pop(0), frame_rows, w_in_full, w_out_full, params, saved, taps
         )
-        if moment < moments - 1:
-            incoming = send_active(outgoing, moment, active_at(moment, False), 1)
+        pending.append(send_active(outgoing, active_at(slot, False), 1))
     x_all, proj_all, swish_all, value_all, gate_all, mid_all, inv_all = saved
     kept = (x_all, value_all, gate_all, mid_all, inv_all)
-    place = sections - 1 - section_index
+    pending = [blank] * SKEW
+    table = info_table(sections - 1 - section_index)
     grads = None
-    for moment in range(moments):
-        info = info_at(moment, place, place == 0)
+    for slot in range(slots):
         outgoing, *grads = backward_stage(
-            info, incoming, cotangent_rows, w_in_full, w_out_full, params, kept, grads, taps
+            table[slot], pending.pop(0), cotangent_rows, w_in_full, w_out_full, params, kept,
+            grads, taps,
         )
-        if moment < moments - 1:
-            incoming = send_active(outgoing, moment, active_at(moment, True), -1)
+        pending.append(send_active(outgoing, active_at(slot, True), -1))
     input_all, grad_all, up_all, small_all = grads
     total_rows = micro_count * frames_len
     parts, unused, width = w_in_full.shape

time: 576 us -> 544 us (0.944)
  waiting for transfers between devices: 298 us -> 263 us
  other arithmetic: 32.4 us -> 20.2 us
  Pallas kernels: 86.8 us -> 96.9 us
    ppermute x12 -> x16, waiting for transfers between devices: 88.5 us -> 61.9 us  [send_active(): return lax.ppermute(x, 'section', pairs)]
    another operation x14 -> x4, other arithmetic: 17.3 us -> 2.59 us  [info_table(): jnp.stack([slot, active.astype(jnp.int32), first.astype(jnp.int32), valid...]
    pallas_call x14 -> x20, Pallas kernels: 86.8 us -> 96.9 us  [stage_call(): pl.pallas_call(functools.partial(kernel, taps=taps, length=length, width=...]
    ppermute x12 -> x16, starting transfers between devices: 25.1 us -> 24.1 us  [send_active(): return lax.ppermute(x, 'section', pairs)]
  transfers between devices with their start and end apart: 65 -> 69, of which waited for: 40 -> 38; matrix products, arithmetic and copies ran while one was open for 8% -> 7% of each run, Pallas kernels for 0% -> 14%
where the time goes in v3:
time: 544 us; the launch traced here: 535 us
  waiting for transfers between devices  263 us (48%)
  starting transfers between devices  105 us (19%)
  Pallas kernels  96.9 us (18%)
  local copies, waits for them, and re-layouts  28.2 us (5%)
  other arithmetic  20.2 us (4%)
  between operations  15.4 us (3%)
  matrix products  6.02 us (1%)
    ppermute x46, waiting for transfers between devices, rotate(): return lax.ppermute(x, axis, [(i, (i + by) % peers) for i in range(peers)])  151 us
    pallas_call x20, Pallas kernels, stage_call(): pl.pallas_call(functools.partial(kernel, taps=taps, length=length, width=...  96.9 us
    ppermute x46, starting transfers between devices, rotate(): return lax.ppermute(x, axis, [(i, (i + by) % peers) for i in range(peers)])  76.2 us
    ppermute x16, waiting for transfers between devices, send_active(): return lax.ppermute(x, 'section', pairs)  61.9 us
    all_gather x1, waiting for transfers between devices, gather_weights(): w_in_full = lax.all_gather(mine, 'batch', axis=0, tiled=False)  30 us
    ppermute x16, starting transfers between devices, send_active(): return lax.ppermute(x, 'section', pairs)  24.1 us
    ppermute x5, waiting for transfers between devices, swap_pair(): return lax.ppermute(x, 'fsdp', [(i, i ^ 1) for i in range(peers)])  20.7 us
  transfers between devices with their start and end apart: 69, of which 38 were waited for; matrix products, arithmetic and copies ran while one was open for 7% of the time, Pallas kernels for 14%

profile of v3, /device:TPU:8, one launch (start us, length us, event | category | flops | bytes accessed | tf_op | source)
XLA Modules:
  0.0 535.0 jit_solution(9457977680934318227)
XLA Ops:
  8.1 2.3 collective-permute-start
  11.3 2.5 collective-permute-done
  15.9 4.0 collective-permute-start.2
  21.1 4.8 collective-permute-done.1
  25.9 3.2 collective-permute-start.4
  29.2 5.1 collective-permute-done.3
  34.4 3.2 collective-permute-start.6
  37.7 4.6 collective-permute-done.5
  42.4 3.3 collective-permute-start.8
  45.8 3.0 collective-permute-done.7
  52.6 4.5 collective-permute-done.9
  58.0 3.4 concatenate.67.params
  62.4 3.3 collective-permute-start.11
  65.7 2.7 broadcast_in_dim.102
  71.2 5.3 collective-permute-done.11
  76.5 3.8 collective-permute-start.13
  81.2 3.3 collective-permute-done.12
  86.8 7.0 %collective-permute-done.13 = bf16[2,96,1536]{2,1,0:T(8,128)(2,1)S(1)} collective-permute-done((bf16[2,96,1536]{2,1,0:T(8,128)(2,1)S(1)}, bf16[2,96,1536]{2,1,0:T(8,128)(2,1)S(1)}, u32[]{:S(2)}, u32[]{:S(2)}) %collective-permute-start.13) | collective-permute-done | bytes 589856 | tf_op jit(solution)/shard_map/ppermute | solution.py:25
  96.5 2.3 collective-permute-done.14
  99.0 8.4 %collective-permute-done.15 = bf16[2,96,1536]{2,1,0:T(8,128)(2,1)S(1)} collective-permute-done((bf16[2,96,1536]{2,1,0:T(8,128)(2,1)S(1)}, bf16[2,96,1536]{2,1,0:T(8,128)(2,1)S(1)}, u32[]{:S(2)}, u32[]{:S(2)}) %collective-permute-start.15) | collective-permute-done | bytes 589856 | tf_op jit(solution)/shard_map/ppermute | solution.py:25
  107.4 2.6 collective-permute-start.17
  111.8 2.8 collective-permute-done.17
  115.4 30.0 %all-gather.2.cloned.1.call-done.w_in = bf16[4,1536,768]{2,1,0:T(8,128)(2,1)} async-done(((bf16[1,1536,768]{2,1,0:T(8,128)(2,1)}), bf16[4,1536,768]{2,1,0:T(8,128)(2,1)}) %all-gather.2.cloned.1.call-update) | async-done | bytes 9437200 | tf_op jit(solution)/shard_map/all_gather | solution.py:476
  146.1 8.7 %shard_map.127 = (bf16[48,1536]{1,0:T(8,128)(2,1)}, bf16[4,48,1536]{2,1,0:T(8,128)(2,1)}, bf16[4,48,1536]{2,1,0:T(8,128)(2,1)}, bf16[4,48,1536]{2,1,0:T(8,128)(2...) custom-call(s32[4]{0:T(128)} %get-tuple-element.291.info, ...), custom_call_target="tpu_custom_call" | custom-call | flops 679477248 | bytes 14155776 | tf_op jit(solution)/shard_map/pallas_call | solution.py:399
  156.8 8.7 %shard_map.128 = (bf16[48,1536]{1,0:T(8,128)(2,1)}, bf16[4,48,1536]{2,1,0:T(8,128)(2,1)}, bf16[4,48,1536]{2,1,0:T(8,128)(2,1)}, bf16[4,48,1536]{2,1,0:T(8,128)(2...) custom-call(s32[4]{0:T(128)} %get-tuple-element.292.info, ...), custom_call_target="tpu_custom_call", output_to_operand_aliasing={{1}: (6, {}), {2}: (7, {}), {3}: (8, {}), {4}: (9, {}), {5}... | custom-call | flops 679477248 | bytes 14155776 | tf_op jit(solution)/shard_map/pallas_call | solution.py:399
  169.9 8.7 %shard_map.129 = (bf16[48,1536]{1,0:T(8,128)(2,1)}, bf16[4,48,1536]{2,1,0:T(8,128)(2,1)}, bf16[4,48,1536]{2,1,0:T(8,128)(2,1)}, bf16[4,48,1536]{2,1,0:T(8,128)(2...) custom-call(s32[4]{0:T(128)} %get-tuple-element.290.info, ...), custom_call_target="tpu_custom_call", output_to_operand_aliasing={{1}: (6, {}), {2}: (7, {}), {3}: (8, {}), {4}: (9, {}), {5}... | custom-call | flops 679477248 | bytes 14155776 | tf_op jit(solution)/shard_map/pallas_call | solution.py:399
  180.6 8.7 %shard_map.130 = (bf16[48,1536]{1,0:T(8,128)(2,1)}, bf16[4,48,1536]{2,1,0:T(8,128)(2,1)}, bf16[4,48,1536]{2,1,0:T(8,128)(2,1)}, bf16[4,48,1536]{2,1,0:T(8,128)(2...) custom-call(s32[4]{0:T(128)} %get-tuple-element.293.info, ...), custom_call_target="tpu_custom_call", output_to_operand_aliasing={{1}: (6, {}), {2}: (7, {}), {3}: (8, {}), {4}: (9, {}), {5}... | custom-call | flops 679477248 | bytes 14155776 | tf_op jit(solution)/shard_map/pallas_call | solution.py:399
  220.2 58.8 %collective-permute-done.31.incoming = bf16[48,1536]{1,0:T(8,128)(2,1)} collective-permute-done((bf16[48,1536]{1,0:T(8,128)(2,1)}, bf16[48,1536]{1,0:T(8,128)(2,1)}, u32[]{:S(2)}, u32[]{:S(2)}) %collective-permute-start.31) | collective-permute-done | bytes 147488 | tf_op jit(solution)/shard_map/ppermute | solution.py:509
  279.0 13.0 %shard_map.143 = (bf16[48,1536]{1,0:T(8,128)(2,1)}, bf16[4,48,1536]{2,1,0:T(8,128)(2,1)}, bf16[4,48,3072]{2,1,0:T(8,128)(2,1)}, bf16[4,48,1536]{2,1,0:T(8,128)(2,1)}, f32[4,48,1536]{2,1,0:T(8,128)}) custom-call(s32[4]{0:T(128)} %get-tuple-element.278.info, ...), custom_call_target="tpu_custom_call", output_to_operand_aliasing={{1}: (11, {}), {2}: (12, {}), {3}: (13, {}), {4}: (14, {})} | custom-call | flops 679477248 | bytes 14155776 | tf_op jit(solution)/shard_map/pallas_call | solution.py:399
  294.3 13.0 %shard_map.144 = (bf16[48,1536]{1,0:T(8,128)(2,1)}, bf16[4,48,1536]{2,1,0:T(8,128)(2,1)}, bf16[4,48,3072]{2,1,0:T(8,128)(2,1)}, bf16[4,48,1536]{2,1,0:T(8,128)(2,1)}, f32[4,48,1536]{2,1,0:T(8,128)}) custom-call(s32[4]{0:T(128)} %get-tuple-element.285.info, ...), custom_call_target="tpu_custom_call", output_to_operand_aliasing={{1}: (11, {}), {2}: (12, {}), {3}: (13, {}), {4}: (14, {})} | custom-call | flops 679477248 | bytes 14155776 | tf_op jit(solution)/shard_map/pallas_call | solution.py:399
  308.7 13.0 %shard_map.145 = (bf16[48,1536]{1,0:T(8,128)(2,1)}, bf16[4,48,1536]{2,1,0:T(8,128)(2,1)}, bf16[4,48,3072]{2,1,0:T(8,128)(2,1)}, bf16[4,48,1536]{2,1,0:T(8,128)(2,1)}, f32[4,48,1536]{2,1,0:T(8,128)}) custom-call(s32[4]{0:T(128)} %get-tuple-element.277.info, ...), custom_call_target="tpu_custom_call", output_to_operand_aliasing={{1}: (11, {}), {2}: (12, {}), {3}: (13, {}), {4}: (14, {})} | custom-call | flops 679477248 | bytes 14155776 | tf_op jit(solution)/shard_map/pallas_call | solution.py:399
  323.6 13.1 %shard_map.146 = (bf16[48,1536]{1,0:T(8,128)(2,1)}, bf16[4,48,1536]{2,1,0:T(8,128)(2,1)}, bf16[4,48,3072]{2,1,0:T(8,128)(2,1)}, bf16[4,48,1536]{2,1,0:T(8,128)(2,1)}, f32[4,48,1536]{2,1,0:T(8,128)}) custom-call(s32[4]{0:T(128)} %get-tuple-element.286.info, ...), custom_call_target="tpu_custom_call", output_to_operand_aliasing={{1}: (11, {}), {2}: (12, {}), {3}: (13, {}), {4}: (14, {})} | custom-call | flops 679477248 | bytes 14155776 | tf_op jit(solution)/shard_map/pallas_call | solution.py:399
  336.8 2.1 fusion
  341.4 4.8 pad_maximum_fusion
  350.4 3.4 collective-permute-start.50
  353.9 6.8 %collective-permute-done.50 = bf16[112,1536]{1,0:T(8,128)(2,1)S(1)} collective-permute-done((bf16[112,1536]{1,0:T(8,128)(2,1)S(1)}, bf16[112,1536]{1,0:T(8,128)(2,1)S(1)}, u32[]{:S(2)}, u32[]{:S(2)}) %collective-permute-start.50) | collective-permute-done | bytes 344096 | tf_op jit(solution)/shard_map/ppermute | solution.py:25
  360.9 3.8 collective-permute-start.51
  364.9 14.9 %collective-permute-done.51 = bf16[2,112,1536]{2,1,0:T(8,128)(2,1)S(1)} collective-permute-done((bf16[2,112,1536]{2,1,0:T(8,128)(2,1)S(1)}, bf16[2,112,1536]{2,1,0:T(8,128)(2,1)S(1)}, u32[]{:S(2)}, u32[]{:S(2)}) %collective-permute-start.51) | collective-permute-done | bytes 688160 | tf_op jit(solution)/shard_map/ppermute | solution.py:25
  379.8 2.1 collective-permute-done.47
  382.4 3.2 collective-permute-start.52
  385.6 14.8 %collective-permute-done.48 = bf16[2,112,1536]{2,1,0:T(8,128)(2,1)S(1)} collective-permute-done((bf16[2,112,1536]{2,1,0:T(8,128)(2,1)S(1)}, bf16[2,112,1536]{2,1,0:T(8,128)(2,1)S(1)}, u32[]{:S(2)}, u32[]{:S(2)}) %collective-permute-start.48) | collective-permute-done | bytes 688160 | tf_op jit(solution)/shard_map/ppermute | solution.py:25
  402.1 2.3 collective-permute-start.53
  404.4 8.6 %collective-permute-done.49 = bf16[2,112,1536]{2,1,0:T(8,128)(2,1)S(1)} collective-permute-done((bf16[2,112,1536]{2,1,0:T(8,128)(2,1)S(1)}, bf16[2,112,1536]{2,1,0:T(8,128)(2,1)S(1)}, u32[]{:S(2)}, u32[]{:S(2)}) %collective-permute-start.49) | collective-permute-done | bytes 688160 | tf_op jit(solution)/shard_map/ppermute | solution.py:25
  415.2 6.7 %collective-permute-done.54 = bf16[112,1536]{1,0:T(8,128)(2,1)S(1)} collective-permute-done((bf16[112,1536]{1,0:T(8,128)(2,1)S(1)}, bf16[112,1536]{1,0:T(8,128)(2,1)S(1)}, u32[]{:S(2)}, u32[]{:S(2)}) %collective-permute-start.54) | collective-permute-done | bytes 344096 | tf_op jit(solution)/shard_map/ppermute | solution.py:30
  422.1 2.4 collective-permute-start.55
  424.6 3.1 collective-permute-start.57
  427.7 12.9 %collective-permute-done.55 = bf16[112,1536]{1,0:T(8,128)(2,1)S(1)} collective-permute-done((bf16[112,1536]{1,0:T(8,128)(2,1)S(1)}, bf16[112,1536]{1,0:T(8,128)(2,1)S(1)}, u32[]{:S(2)}, u32[]{:S(2)}) %collective-permute-start.55) | collective-permute-done | bytes 344096 | tf_op jit(solution)/shard_map/ppermute | solution.py:25
  440.6 6.9 %collective-permute-done.56 = bf16[112,1536]{1,0:T(8,128)(2,1)S(1)} collective-permute-done((bf16[112,1536]{1,0:T(8,128)(2,1)S(1)}, bf16[112,1536]{1,0:T(8,128)(2,1)S(1)}, u32[]{:S(2)}, u32[]{:S(2)}) %collective-permute-start.56) | collective-permute-done | bytes 344096 | tf_op jit(solution)/shard_map/ppermute | solution.py:25
  451.1 2.4 collective-permute-done.58
  457.1 2.4 collective-permute-done.59
  459.7 3.1 collective-permute-start.62
  462.8 2.3 collective-permute-done.61
  465.1 3.2 collective-permute-start.64
  469.8 3.2 collective-permute-start.38
  473.1 3.5 collective-permute-done.34
  481.4 7.0 %collective-permute-done.35 = bf16[2,96,768]{2,1,0:T(8,128)(2,1)S(1)} collective-permute-done((bf16[2,96,768]{2,1,0:T(8,128)(2,1)S(1)}, bf16[2,96,768]{2,1,0:T(8,128)(2,1)S(1)}, u32[]{:S(2)}, u32[]{:S(2)}) %collective-permute-start.35) | collective-permute-done | bytes 294944 | tf_op jit(solution)/shard_map/ppermute | solution.py:25
  488.6 3.3 collective-permute-start.66
  491.9 4.6 collective-permute-done.36
  497.4 2.1 collective-permute-start.37
  499.5 4.6 collective-permute-done.40
  505.7 5.4 %collective-permute-done.41 = bf16[2,96,768]{2,1,0:T(8,128)(2,1)} collective-permute-done((bf16[2,96,768]{2,1,0:T(8,128)(2,1)S(1)}, bf16[2,96,768]{2,1,0:T(8,128)(2,1)}, u32[]{:S(2)}, u32[]{:S(2)}) %collective-permute-start.41) | collective-permute-done | bytes 294944 | tf_op jit(solution)/shard_map/ppermute | solution.py:25
  512.9 4.6 collective-permute-done.42
  518.7 2.2 collective-permute-start.45
  522.4 3.2 collective-permute-done.43
  (226 shorter events, 102.4 us)
Async XLA Ops:
  7.2 138.2 %all-gather.2.cloned.1.call-start = ((), (), s32[]{:S(2)}) async-start(), calls=%async_computation.1 | async-start | bytes 11796480 | tf_op jit(solution)/shard_map/all_gather | solution.py:476
  8.1 5.7 %collective-permute-start = (bf16[96,768]{1,0:T(8,128)(2,1)S(1)}, bf16[96,768]{1,0:T(8,128)(2,1)S(1)}, u32[]{:S(2)}, u32[]{:S(2)}) collective-permute-start(bf16[96,768]{1,0:T(8,128)(2,1)S(1)} %fusion.65), channel_id=1, source_target_pairs={{0,4},{4,0},{8,12},{12,8},{16,20},{20,16},{24,28},{28,24},{32,36},... | collective-permute-start | bytes 442376 | tf_op jit(solution)/shard_map/ppermute | solution.py:30
  13.9 12.1 %collective-permute-start.1 = (bf16[2,96,768]{2,1,0:T(8,128)(2,1)S(1)}, bf16[2,96,768]{2,1,0:T(8,128)(2,1)S(1)}, u32[]{:S(2)}, u32[]{:S(2)}) collective-permute-start(bf16[2,96,768]{2,1,0:T(8,128)(2,1)S(1)} %maximum_select_fusion.3), channel_id=1, source_target_pairs={{0,8},{4,12},{8,16},{12,20},{16,24},{20,28},{24,32},{28,36},{32,40... | collective-permute-start | bytes 884744 | tf_op jit(solution)/shard_map/ppermute | solution.py:25
  15.9 10.1 %collective-permute-start.2 = (bf16[2,96,768]{2,1,0:T(8,128)(2,1)S(1)}, bf16[2,96,768]{2,1,0:T(8,128)(2,1)S(1)}, u32[]{:S(2)}, u32[]{:S(2)}) collective-permute-start(bf16[2,96,768]{2,1,0:T(8,128)(2,1)S(1)} %maximum_select_fusion.3), channel_id=1, source_target_pairs={{0,56},{4,60},{8,0},{12,4},{16,8},{20,12},{24,16},{28,20},{32,24},... | collective-permute-start | bytes 884744 | tf_op jit(solution)/shard_map/ppermute | solution.py:25
  25.9 8.4 %collective-permute-start.3 = (bf16[2,96,768]{2,1,0:T(8,128)(2,1)S(1)}, bf16[2,96,768]{2,1,0:T(8,128)(2,1)S(1)}, u32[]{:S(2)}, u32[]{:S(2)}) collective-permute-start(bf16[2,96,768]{2,1,0:T(8,128)(2,1)S(1)} %collective-permute-done.1), channel_id=1, source_target_pairs={{0,8},{4,12},{8,16},{12,20},{16,24},{20,28},{24,32},{28,36},{32,40... | collective-permute-start | bytes 884744 | tf_op jit(solution)/shard_map/ppermute | solution.py:25
  25.9 8.4 %collective-permute-start.4 = (bf16[2,96,768]{2,1,0:T(8,128)(2,1)S(1)}, bf16[2,96,768]{2,1,0:T(8,128)(2,1)S(1)}, u32[]{:S(2)}, u32[]{:S(2)}) collective-permute-start(bf16[2,96,768]{2,1,0:T(8,128)(2,1)S(1)} %collective-permute-done.2), channel_id=1, source_target_pairs={{0,56},{4,60},{8,0},{12,4},{16,8},{20,12},{24,16},{28,20},{32,24},... | collective-permute-start | bytes 884744 | tf_op jit(solution)/shard_map/ppermute | solution.py:25
  34.4 7.9 %collective-permute-start.5 = (bf16[2,96,768]{2,1,0:T(8,128)(2,1)S(1)}, bf16[2,96,768]{2,1,0:T(8,128)(2,1)S(1)}, u32[]{:S(2)}, u32[]{:S(2)}) collective-permute-start(bf16[2,96,768]{2,1,0:T(8,128)(2,1)S(1)} %collective-permute-done.3), channel_id=1, source_target_pairs={{0,8},{4,12},{8,16},{12,20},{16,24},{20,28},{24,32},{28,36},{32,40... | collective-permute-start | bytes 884744 | tf_op jit(solution)/shard_map/ppermute | solution.py:25
  34.4 8.0 %collective-permute-start.6 = (bf16[2,96,768]{2,1,0:T(8,128)(2,1)S(1)}, bf16[2,96,768]{2,1,0:T(8,128)(2,1)S(1)}, u32[]{:S(2)}, u32[]{:S(2)}) collective-permute-start(bf16[2,96,768]{2,1,0:T(8,128)(2,1)S(1)} %collective-permute-done.4), channel_id=1, source_target_pairs={{0,56},{4,60},{8,0},{12,4},{16,8},{20,12},{24,16},{28,20},{32,24},... | collective-permute-start | bytes 884744 | tf_op jit(solution)/shard_map/ppermute | solution.py:25
  42.3 6.4 %collective-permute-start.7 = (bf16[96,768]{1,0:T(8,128)(2,1)S(1)}, bf16[96,768]{1,0:T(8,128)(2,1)S(1)}, u32[]{:S(2)}, u32[]{:S(2)}) collective-permute-start(bf16[96,768]{1,0:T(8,128)(2,1)S(1)} %slice_bitcast_fusion.10), channel_id=1, source_target_pairs={{0,8},{4,12},{8,16},{12,20},{16,24},{20,28},{24,32},{28,36},{32,40... | collective-permute-start | bytes 442376 | tf_op jit(solution)/shard_map/ppermute | solution.py:25
  42.4 6.3 %collective-permute-start.8 = (bf16[96,768]{1,0:T(8,128)(2,1)S(1)}, bf16[96,768]{1,0:T(8,128)(2,1)S(1)}, u32[]{:S(2)}, u32[]{:S(2)}) collective-permute-start(bf16[96,768]{1,0:T(8,128)(2,1)S(1)} %slice_bitcast_fusion.9), channel_id=1, source_target_pairs={{0,56},{4,60},{8,0},{12,4},{16,8},{20,12},{24,16},{28,20},{32,24},... | collective-permute-start | bytes 442376 | tf_op jit(solution)/shard_map/ppermute | solution.py:25
  50.2 418.2 %reduce-scatter.2.cloned.1.call-start = ((), (), s32[]{:S(2)}) async-start(), calls=%async_computation.2 | async-start | bytes 11796480 | tf_op jit(solution)/shard_map/reduce_scatter | solution.py:492
  50.3 6.8 %collective-permute-start.9 = (bf16[96,1536]{1,0:T(8,128)(2,1)S(1)}, bf16[96,1536]{1,0:T(8,128)(2,1)S(1)}, u32[]{:S(2)}, u32[]{:S(2)}) collective-permute-start(bf16[96,1536]{1,0:T(8,128)(2,1)S(1)} %bitcast.260), channel_id=1, source_target_pairs={{0,4},{4,0},{8,12},{12,8},{16,20},{20,16},{24,28},{28,24},{32,36},... | collective-permute-start | bytes 884744 | tf_op jit(solution)/shard_map/ppermute | solution.py:30
  57.2 13.1 %collective-permute-start.10 = (bf16[2,96,1536]{2,1,0:T(8,128)(2,1)S(1)}, bf16[2,96,1536]{2,1,0:T(8,128)(2,1)S(1)}, u32[]{:S(2)}, u32[]{:S(2)}) collective-permute-start(bf16[2,96,1536]{2,1,0:T(8,128)(2,1)S(1)} %maximum_select_fusion.1), channel_id=1, source_target_pairs={{0,8},{4,12},{8,16},{12,20},{16,24},{20,28},{24,32},{28,36},{32,40... | collective-permute-start | bytes 1769480 | tf_op jit(solution)/shard_map/ppermute | solution.py:25
  62.4 14.1 %collective-permute-start.11 = (bf16[2,96,1536]{2,1,0:T(8,128)(2,1)S(1)}, bf16[2,96,1536]{2,1,0:T(8,128)(2,1)S(1)}, u32[]{:S(2)}, u32[]{:S(2)}) collective-permute-start(bf16[2,96,1536]{2,1,0:T(8,128)(2,1)S(1)} %maximum_select_fusion.1), channel_id=1, source_target_pairs={{0,56},{4,60},{8,0},{12,4},{16,8},{20,12},{24,16},{28,20},{32,24},... | collective-permute-start | bytes 1769480 | tf_op jit(solution)/shard_map/ppermute | solution.py:25
  70.3 14.2 %collective-permute-start.12 = (bf16[2,96,1536]{2,1,0:T(8,128)(2,1)S(1)}, bf16[2,96,1536]{2,1,0:T(8,128)(2,1)S(1)}, u32[]{:S(2)}, u32[]{:S(2)}) collective-permute-start(bf16[2,96,1536]{2,1,0:T(8,128)(2,1)S(1)} %collective-permute-done.10), channel_id=1, source_target_pairs={{0,8},{4,12},{8,16},{12,20},{16,24},{20,28},{24,32},{28,36},{32,40... | collective-permute-start | bytes 1769480 | tf_op jit(solution)/shard_map/ppermute | solution.py:25
  76.5 17.2 %collective-permute-start.13 = (bf16[2,96,1536]{2,1,0:T(8,128)(2,1)S(1)}, bf16[2,96,1536]{2,1,0:T(8,128)(2,1)S(1)}, u32[]{:S(2)}, u32[]{:S(2)}) collective-permute-start(bf16[2,96,1536]{2,1,0:T(8,128)(2,1)S(1)} %collective-permute-done.11), channel_id=1, source_target_pairs={{0,56},{4,60},{8,0},{12,4},{16,8},{20,12},{24,16},{28,20},{32,24},... | collective-permute-start | bytes 1769480 | tf_op jit(solution)/shard_map/ppermute | solution.py:25
  84.5 14.3 %collective-permute-start.14 = (bf16[2,96,1536]{2,1,0:T(8,128)(2,1)S(1)}, bf16[2,96,1536]{2,1,0:T(8,128)(2,1)S(1)}, u32[]{:S(2)}, u32[]{:S(2)}) collective-permute-start(bf16[2,96,1536]{2,1,0:T(8,128)(2,1)S(1)} %collective-permute-done.12), channel_id=1, source_target_pairs={{0,8},{4,12},{8,16},{12,20},{16,24},{20,28},{24,32},{28,36},{32,40... | collective-permute-start | bytes 1769480 | tf_op jit(solution)/shard_map/ppermute | solution.py:25
  93.7 13.6 %collective-permute-start.15 = (bf16[2,96,1536]{2,1,0:T(8,128)(2,1)S(1)}, bf16[2,96,1536]{2,1,0:T(8,128)(2,1)S(1)}, u32[]{:S(2)}, u32[]{:S(2)}) collective-permute-start(bf16[2,96,1536]{2,1,0:T(8,128)(2,1)S(1)} %collective-permute-done.13), channel_id=1, source_target_pairs={{0,56},{4,60},{8,0},{12,4},{16,8},{20,12},{24,16},{28,20},{32,24},... | collective-permute-start | bytes 1769480 | tf_op jit(solution)/shard_map/ppermute | solution.py:25
  98.8 13.0 %collective-permute-start.16 = (bf16[96,1536]{1,0:T(8,128)(2,1)S(1)}, bf16[96,1536]{1,0:T(8,128)(2,1)S(1)}, u32[]{:S(2)}, u32[]{:S(2)}) collective-permute-start(bf16[96,1536]{1,0:T(8,128)(2,1)S(1)} %slice_bitcast_fusion.7), channel_id=1, source_target_pairs={{0,8},{4,12},{8,16},{12,20},{16,24},{20,28},{24,32},{28,36},{32,40... | collective-permute-start | bytes 884744 | tf_op jit(solution)/shard_map/ppermute | solution.py:25
  107.4 7.1 %collective-permute-start.17 = (bf16[96,1536]{1,0:T(8,128)(2,1)S(1)}, bf16[96,1536]{1,0:T(8,128)(2,1)S(1)}, u32[]{:S(2)}, u32[]{:S(2)}) collective-permute-start(bf16[96,1536]{1,0:T(8,128)(2,1)S(1)} %slice_bitcast_fusion.6), channel_id=1, source_target_pairs={{0,56},{4,60},{8,0},{12,4},{16,8},{20,12},{24,16},{28,20},{32,24},... | collective-permute-start | bytes 884744 | tf_op jit(solution)/shard_map/ppermute | solution.py:25
  154.8 15.1 %collective-permute-start.19 = (bf16[48,1536]{1,0:T(8,128)(2,1)}, bf16[48,1536]{1,0:T(8,128)(2,1)}, u32[]{:S(2)}, u32[]{:S(2)}) collective-permute-start(bf16[48,1536]{1,0:T(8,128)(2,1)} %get-tuple-element.141), channel_id=1, source_target_pairs={{0,64},{1,65},{2,66},{3,67},{4,68},{5,69},{6,70},{7,71},{8,72},{9,... | collective-permute-start | bytes 442376 | tf_op jit(solution)/shard_map/ppermute | solution.py:509
  165.5 15.1 %collective-permute-start.18 = (bf16[48,1536]{1,0:T(8,128)(2,1)}, bf16[48,1536]{1,0:T(8,128)(2,1)}, u32[]{:S(2)}, u32[]{:S(2)}) collective-permute-start(bf16[48,1536]{1,0:T(8,128)(2,1)} %get-tuple-element.140), channel_id=1, source_target_pairs={{0,64},{1,65},{2,66},{3,67},{4,68},{5,69},{6,70},{7,71},{8,72},{9,... | collective-permute-start | bytes 442376 | tf_op jit(solution)/shard_map/ppermute | solution.py:509
  178.6 14.4 %collective-permute-start.21 = (bf16[48,1536]{1,0:T(8,128)(2,1)}, bf16[48,1536]{1,0:T(8,128)(2,1)}, u32[]{:S(2)}, u32[]{:S(2)}) collective-permute-start(bf16[48,1536]{1,0:T(8,128)(2,1)} %get-tuple-element.157), channel_id=1, source_target_pairs={{0,64},{64,128},{1,65},{65,129},{2,66},{66,130},{3,67},{67,131},{4... | collective-permute-start | bytes 442376 | tf_op jit(solution)/shard_map/ppermute | solution.py:509
  189.3 5.9 %collective-permute-start.20 = (bf16[48,1536]{1,0:T(8,128)(2,1)}, bf16[48,1536]{1,0:T(8,128)(2,1)}, u32[]{:S(2)}, u32[]{:S(2)}) collective-permute-start(bf16[48,1536]{1,0:T(8,128)(2,1)} %get-tuple-element.156), channel_id=1, source_target_pairs={{0,64},{64,128},{1,65},{65,129},{2,66},{66,130},{3,67},{67,131},{4... | collective-permute-start | bytes 442376 | tf_op jit(solution)/shard_map/ppermute | solution.py:509
  193.9 5.0 collective-permute-start.23
  196.2 4.8 collective-permute-start.22
  199.7 5.5 %collective-permute-start.25 = (bf16[48,1536]{1,0:T(8,128)(2,1)}, bf16[48,1536]{1,0:T(8,128)(2,1)}, u32[]{:S(2)}, u32[]{:S(2)}) collective-permute-start(bf16[48,1536]{1,0:T(8,128)(2,1)} %get-tuple-element.189), channel_id=1, source_target_pairs={{128,192},{129,193},{130,194},{131,195},{132,196},{133,197},{134,1... | collective-permute-start | bytes 442376 | tf_op jit(solution)/shard_map/ppermute | solution.py:509
  201.8 4.1 collective-permute-start.24
  216.7 62.3 %collective-permute-start.31 = (bf16[48,1536]{1,0:T(8,128)(2,1)}, bf16[48,1536]{1,0:T(8,128)(2,1)}, u32[]{:S(2)}, u32[]{:S(2)}) collective-permute-start(bf16[48,1536]{1,0:T(8,128)(2,1)} %get-tuple-element.234), channel_id=1, source_target_pairs={{128,64},{64,0},{129,65},{65,1},{130,66},{66,2},{131,67},{67,3},{1... | collective-permute-start | bytes 442376 | tf_op jit(solution)/shard_map/ppermute | solution.py:509
  218.9 75.5 %collective-permute-start.30 = (bf16[48,1536]{1,0:T(8,128)(2,1)}, bf16[48,1536]{1,0:T(8,128)(2,1)}, u32[]{:S(2)}, u32[]{:S(2)}) collective-permute-start(bf16[48,1536]{1,0:T(8,128)(2,1)} %get-tuple-element.233), channel_id=1, source_target_pairs={{128,64},{64,0},{129,65},{65,1},{130,66},{66,2},{131,67},{67,3},{1... | collective-permute-start | bytes 442376 | tf_op jit(solution)/shard_map/ppermute | solution.py:509
  292.0 16.7 %collective-permute-start.33 = (bf16[48,1536]{1,0:T(8,128)(2,1)}, bf16[48,1536]{1,0:T(8,128)(2,1)}, u32[]{:S(2)}, u32[]{:S(2)}) collective-permute-start(bf16[48,1536]{1,0:T(8,128)(2,1)} %get-tuple-element.244), channel_id=1, source_target_pairs={{64,0},{65,1},{66,2},{67,3},{68,4},{69,5},{70,6},{71,7},{72,8},{73... | collective-permute-start | bytes 442376 | tf_op jit(solution)/shard_map/ppermute | solution.py:509
  307.3 16.3 %collective-permute-start.32 = (bf16[48,1536]{1,0:T(8,128)(2,1)}, bf16[48,1536]{1,0:T(8,128)(2,1)}, u32[]{:S(2)}, u32[]{:S(2)}) collective-permute-start(bf16[48,1536]{1,0:T(8,128)(2,1)} %get-tuple-element.243), channel_id=1, source_target_pairs={{64,0},{65,1},{66,2},{67,3},{68,4},{69,5},{70,6},{71,7},{72,8},{73... | collective-permute-start | bytes 442376 | tf_op jit(solution)/shard_map/ppermute | solution.py:509
  350.4 10.3 %collective-permute-start.50 = (bf16[112,1536]{1,0:T(8,128)(2,1)S(1)}, bf16[112,1536]{1,0:T(8,128)(2,1)S(1)}, u32[]{:S(2)}, u32[]{:S(2)}) collective-permute-start(bf16[112,1536]{1,0:T(8,128)(2,1)S(1)} %get-tuple-element.316), channel_id=1, source_target_pairs={{0,56},{4,60},{8,0},{12,4},{16,8},{20,12},{24,16},{28,20},{32,24},... | collective-permute-start | bytes 1032200 | tf_op jit(solution)/shard_map/ppermute | solution.py:25
  353.8 10.8 %collective-permute-start.46 = (bf16[112,1536]{1,0:T(8,128)(2,1)S(1)}, bf16[112,1536]{1,0:T(8,128)(2,1)S(1)}, u32[]{:S(2)}, u32[]{:S(2)}) collective-permute-start(bf16[112,1536]{1,0:T(8,128)(2,1)S(1)} %get-tuple-element.315), channel_id=1, source_target_pairs={{0,8},{4,12},{8,16},{12,20},{16,24},{20,28},{24,32},{28,36},{32,40... | collective-permute-start | bytes 1032200 | tf_op jit(solution)/shard_map/ppermute | solution.py:25
  360.9 18.9 %collective-permute-start.51 = (bf16[2,112,1536]{2,1,0:T(8,128)(2,1)S(1)}, bf16[2,112,1536]{2,1,0:T(8,128)(2,1)S(1)}, u32[]{:S(2)}, u32[]{:S(2)}) collective-permute-start(bf16[2,112,1536]{2,1,0:T(8,128)(2,1)S(1)} %pad_maximum_fusion.2), channel_id=1, source_target_pairs={{0,56},{4,60},{8,0},{12,4},{16,8},{20,12},{24,16},{28,20},{32,24},... | collective-permute-start | bytes 2064392 | tf_op jit(solution)/shard_map/ppermute | solution.py:25
  364.8 17.1 %collective-permute-start.47 = (bf16[2,112,1536]{2,1,0:T(8,128)(2,1)S(1)}, bf16[2,112,1536]{2,1,0:T(8,128)(2,1)S(1)}, u32[]{:S(2)}, u32[]{:S(2)}) collective-permute-start(bf16[2,112,1536]{2,1,0:T(8,128)(2,1)S(1)} %pad_maximum_fusion.1), channel_id=1, source_target_pairs={{0,8},{4,12},{8,16},{12,20},{16,24},{20,28},{24,32},{28,36},{32,40... | collective-permute-start | bytes 2064392 | tf_op jit(solution)/shard_map/ppermute | solution.py:25
  382.3 18.2 %collective-permute-start.48 = (bf16[2,112,1536]{2,1,0:T(8,128)(2,1)S(1)}, bf16[2,112,1536]{2,1,0:T(8,128)(2,1)S(1)}, u32[]{:S(2)}, u32[]{:S(2)}) collective-permute-start(bf16[2,112,1536]{2,1,0:T(8,128)(2,1)S(1)} %get-tuple-element.299), channel_id=1, source_target_pairs={{0,8},{4,12},{8,16},{12,20},{16,24},{20,28},{24,32},{28,36},{32,40... | collective-permute-start | bytes 2064392 | tf_op jit(solution)/shard_map/ppermute | solution.py:25
  382.4 18.1 %collective-permute-start.52 = (bf16[2,112,1536]{2,1,0:T(8,128)(2,1)S(1)}, bf16[2,112,1536]{2,1,0:T(8,128)(2,1)S(1)}, u32[]{:S(2)}, u32[]{:S(2)}) collective-permute-start(bf16[2,112,1536]{2,1,0:T(8,128)(2,1)S(1)} %get-tuple-element.300), channel_id=1, source_target_pairs={{0,56},{4,60},{8,0},{12,4},{16,8},{20,12},{24,16},{28,20},{32,24},... | collective-permute-start | bytes 2064392 | tf_op jit(solution)/shard_map/ppermute | solution.py:25
  400.8 12.2 %collective-permute-start.49 = (bf16[2,112,1536]{2,1,0:T(8,128)(2,1)S(1)}, bf16[2,112,1536]{2,1,0:T(8,128)(2,1)S(1)}, u32[]{:S(2)}, u32[]{:S(2)}) collective-permute-start(bf16[2,112,1536]{2,1,0:T(8,128)(2,1)S(1)} %get-tuple-element.297), channel_id=1, source_target_pairs={{0,8},{4,12},{8,16},{12,20},{16,24},{20,28},{24,32},{28,36},{32,40... | collective-permute-start | bytes 2064392 | tf_op jit(solution)/shard_map/ppermute | solution.py:25
  402.1 11.1 %collective-permute-start.53 = (bf16[2,112,1536]{2,1,0:T(8,128)(2,1)S(1)}, bf16[2,112,1536]{2,1,0:T(8,128)(2,1)S(1)}, u32[]{:S(2)}, u32[]{:S(2)}) collective-permute-start(bf16[2,112,1536]{2,1,0:T(8,128)(2,1)S(1)} %get-tuple-element.298), channel_id=1, source_target_pairs={{0,56},{4,60},{8,0},{12,4},{16,8},{20,12},{24,16},{28,20},{32,24},... | collective-permute-start | bytes 2064392 | tf_op jit(solution)/shard_map/ppermute | solution.py:25
  414.6 7.3 %collective-permute-start.54 = (bf16[112,1536]{1,0:T(8,128)(2,1)S(1)}, bf16[112,1536]{1,0:T(8,128)(2,1)S(1)}, u32[]{:S(2)}, u32[]{:S(2)}) collective-permute-start(bf16[112,1536]{1,0:T(8,128)(2,1)S(1)} %fusion.28), channel_id=1, source_target_pairs={{0,4},{4,0},{8,12},{12,8},{16,20},{20,16},{24,28},{28,24},{32,36},... | collective-permute-start | bytes 1032200 | tf_op jit(solution)/shard_map/ppermute | solution.py:30
  422.1 18.5 %collective-permute-start.55 = (bf16[112,1536]{1,0:T(8,128)(2,1)S(1)}, bf16[112,1536]{1,0:T(8,128)(2,1)S(1)}, u32[]{:S(2)}, u32[]{:S(2)}) collective-permute-start(bf16[112,1536]{1,0:T(8,128)(2,1)S(1)} %fusion.19), channel_id=1, source_target_pairs={{0,2},{1,3},{2,0},{3,1},{4,6},{5,7},{6,4},{7,5},{8,10},{9,11},{10,... | collective-permute-start | bytes 1032200 | tf_op jit(solution)/shard_map/ppermute | solution.py:25
  424.5 23.1 %collective-permute-start.56 = (bf16[112,1536]{1,0:T(8,128)(2,1)S(1)}, bf16[112,1536]{1,0:T(8,128)(2,1)S(1)}, u32[]{:S(2)}, u32[]{:S(2)}) collective-permute-start(bf16[112,1536]{1,0:T(8,128)(2,1)S(1)} %fusion.19), channel_id=1, source_target_pairs={{0,1},{1,2},{2,3},{3,0},{4,5},{5,6},{6,7},{7,4},{8,9},{9,10},{10,1... | collective-permute-start | bytes 1032200 | tf_op jit(solution)/shard_map/ppermute | solution.py:25
  424.6 24.9 %collective-permute-start.57 = (bf16[112,1536]{1,0:T(8,128)(2,1)S(1)}, bf16[112,1536]{1,0:T(8,128)(2,1)S(1)}, u32[]{:S(2)}, u32[]{:S(2)}) collective-permute-start(bf16[112,1536]{1,0:T(8,128)(2,1)S(1)} %fusion.19), channel_id=1, source_target_pairs={{0,3},{1,0},{2,1},{3,2},{4,7},{5,4},{6,5},{7,6},{8,11},{9,8},{10,9... | collective-permute-start | bytes 1032200 | tf_op jit(solution)/shard_map/ppermute | solution.py:25
  453.6 6.0 %collective-permute-start.59 = (f32[2,3,1536]{2,1,0:T(4,128)S(1)}, f32[2,3,1536]{2,1,0:T(4,128)S(1)}, u32[]{:S(2)}, u32[]{:S(2)}) collective-permute-start(f32[2,3,1536]{2,1,0:T(4,128)S(1)} %maximum_select_fusion.5), channel_id=1, source_target_pairs={{0,8},{4,12},{8,16},{12,20},{16,24},{20,28},{24,32},{28,36},{32,40... | collective-permute-start | bytes 110600 | tf_op jit(solution)/shard_map/ppermute | solution.py:25
  455.2 4.4 collective-permute-start.60
  459.6 5.6 %collective-permute-start.61 = (f32[2,3,1536]{2,1,0:T(4,128)S(1)}, f32[2,3,1536]{2,1,0:T(4,128)S(1)}, u32[]{:S(2)}, u32[]{:S(2)}) collective-permute-start(f32[2,3,1536]{2,1,0:T(4,128)S(1)} %collective-permute-done.59), channel_id=1, source_target_pairs={{0,8},{4,12},{8,16},{12,20},{16,24},{20,28},{24,32},{28,36},{32,40... | collective-permute-start | bytes 110600 | tf_op jit(solution)/shard_map/ppermute | solution.py:25
  459.7 5.5 %collective-permute-start.62 = (f32[2,3,1536]{2,1,0:T(4,128)S(1)}, f32[2,3,1536]{2,1,0:T(4,128)S(1)}, u32[]{:S(2)}, u32[]{:S(2)}) collective-permute-start(f32[2,3,1536]{2,1,0:T(4,128)S(1)} %collective-permute-done.60), channel_id=1, source_target_pairs={{0,56},{4,60},{8,0},{12,4},{16,8},{20,12},{24,16},{28,20},{32,24},... | collective-permute-start | bytes 110600 | tf_op jit(solution)/shard_map/ppermute | solution.py:25
  465.1 12.6 %collective-permute-start.63 = (f32[2,3,1536]{2,1,0:T(4,128)S(1)}, f32[2,3,1536]{2,1,0:T(4,128)S(1)}, u32[]{:S(2)}, u32[]{:S(2)}) collective-permute-start(f32[2,3,1536]{2,1,0:T(4,128)S(1)} %collective-permute-done.61), channel_id=1, source_target_pairs={{0,8},{4,12},{8,16},{12,20},{16,24},{20,28},{24,32},{28,36},{32,40... | collective-permute-start | bytes 110600 | tf_op jit(solution)/shard_map/ppermute | solution.py:25
  465.1 23.5 %collective-permute-start.64 = (f32[2,3,1536]{2,1,0:T(4,128)S(1)}, f32[2,3,1536]{2,1,0:T(4,128)S(1)}, u32[]{:S(2)}, u32[]{:S(2)}) collective-permute-start(f32[2,3,1536]{2,1,0:T(4,128)S(1)} %collective-permute-done.62), channel_id=1, source_target_pairs={{0,56},{4,60},{8,0},{12,4},{16,8},{20,12},{24,16},{28,20},{32,24},... | collective-permute-start | bytes 110600 | tf_op jit(solution)/shard_map/ppermute | solution.py:25
  469.7 6.8 %collective-permute-start.34 = (bf16[96,768]{1,0:T(8,128)(2,1)S(1)}, bf16[96,768]{1,0:T(8,128)(2,1)S(1)}, u32[]{:S(2)}, u32[]{:S(2)}) collective-permute-start(bf16[96,768]{1,0:T(8,128)(2,1)S(1)} %get-tuple-element.308), channel_id=1, source_target_pairs={{0,8},{4,12},{8,16},{12,20},{16,24},{20,28},{24,32},{28,36},{32,40... | collective-permute-start | bytes 442376 | tf_op jit(solution)/shard_map/ppermute | solution.py:25
  469.8 6.7 %collective-permute-start.38 = (bf16[96,768]{1,0:T(8,128)(2,1)S(1)}, bf16[96,768]{1,0:T(8,128)(2,1)S(1)}, u32[]{:S(2)}, u32[]{:S(2)}) collective-permute-start(bf16[96,768]{1,0:T(8,128)(2,1)S(1)} %get-tuple-element.310), channel_id=1, source_target_pairs={{0,56},{4,60},{8,0},{12,4},{16,8},{20,12},{24,16},{28,20},{32,24},... | collective-permute-start | bytes 442376 | tf_op jit(solution)/shard_map/ppermute | solution.py:25
  477.6 10.8 %collective-permute-start.35 = (bf16[2,96,768]{2,1,0:T(8,128)(2,1)S(1)}, bf16[2,96,768]{2,1,0:T(8,128)(2,1)S(1)}, u32[]{:S(2)}, u32[]{:S(2)}) collective-permute-start(bf16[2,96,768]{2,1,0:T(8,128)(2,1)S(1)} %pad_maximum_fusion.4), channel_id=1, source_target_pairs={{0,8},{4,12},{8,16},{12,20},{16,24},{20,28},{24,32},{28,36},{32,40... | collective-permute-start | bytes 884744 | tf_op jit(solution)/shard_map/ppermute | solution.py:25
  477.8 27.7 %collective-permute-start.65 = (f32[3,1536]{1,0:T(4,128)S(1)}, f32[3,1536]{1,0:T(4,128)S(1)}, u32[]{:S(2)}, u32[]{:S(2)}) collective-permute-start(f32[3,1536]{1,0:T(4,128)S(1)} %slice_bitcast_fusion.12), channel_id=1, source_target_pairs={{0,8},{4,12},{8,16},{12,20},{16,24},{20,28},{24,32},{28,36},{32,40... | collective-permute-start | bytes 55304 | tf_op jit(solution)/shard_map/ppermute | solution.py:25
  479.8 12.1 %collective-permute-start.39 = (bf16[2,96,768]{2,1,0:T(8,128)(2,1)S(1)}, bf16[2,96,768]{2,1,0:T(8,128)(2,1)S(1)}, u32[]{:S(2)}, u32[]{:S(2)}) collective-permute-start(bf16[2,96,768]{2,1,0:T(8,128)(2,1)S(1)} %pad_maximum_fusion.5), channel_id=1, source_target_pairs={{0,56},{4,60},{8,0},{12,4},{16,8},{20,12},{24,16},{28,20},{32,24},... | collective-permute-start | bytes 884744 | tf_op jit(solution)/shard_map/ppermute | solution.py:25
  488.5 8.0 %collective-permute-start.36 = (bf16[2,96,768]{2,1,0:T(8,128)(2,1)S(1)}, bf16[2,96,768]{2,1,0:T(8,128)(2,1)S(1)}, u32[]{:S(2)}, u32[]{:S(2)}) collective-permute-start(bf16[2,96,768]{2,1,0:T(8,128)(2,1)S(1)} %fusion.25), channel_id=1, source_target_pairs={{0,8},{4,12},{8,16},{12,20},{16,24},{20,28},{24,32},{28,36},{32,40... | collective-permute-start | bytes 884744 | tf_op jit(solution)/shard_map/ppermute | solution.py:25
  488.6 16.9 %collective-permute-start.66 = (f32[3,1536]{1,0:T(4,128)S(1)}, f32[3,1536]{1,0:T(4,128)S(1)}, u32[]{:S(2)}, u32[]{:S(2)}) collective-permute-start(f32[3,1536]{1,0:T(4,128)S(1)} %slice_bitcast_fusion.11), channel_id=1, source_target_pairs={{0,56},{4,60},{8,0},{12,4},{16,8},{20,12},{24,16},{28,20},{32,24},... | collective-permute-start | bytes 55304 | tf_op jit(solution)/shard_map/ppermute | solution.py:25
  497.4 6.7 %collective-permute-start.40 = (bf16[2,96,768]{2,1,0:T(8,128)(2,1)S(1)}, bf16[2,96,768]{2,1,0:T(8,128)(2,1)S(1)}, u32[]{:S(2)}, u32[]{:S(2)}) collective-permute-start(bf16[2,96,768]{2,1,0:T(8,128)(2,1)S(1)} %get-tuple-element.305), channel_id=1, source_target_pairs={{0,56},{4,60},{8,0},{12,4},{16,8},{20,12},{24,16},{28,20},{32,24},... | collective-permute-start | bytes 884744 | tf_op jit(solution)/shard_map/ppermute | solution.py:25
  497.4 8.3 %collective-permute-start.37 = (bf16[2,96,768]{2,1,0:T(8,128)(2,1)}, bf16[2,96,768]{2,1,0:T(8,128)(2,1)}, u32[]{:S(2)}, u32[]{:S(2)}) collective-permute-start(bf16[2,96,768]{2,1,0:T(8,128)(2,1)} %get-tuple-element.304), channel_id=1, source_target_pairs={{0,8},{4,12},{8,16},{12,20},{16,24},{20,28},{24,32},{28,36},{32,40... | collective-permute-start | bytes 884744 | tf_op jit(solution)/shard_map/ppermute | solution.py:25
  504.2 6.9 %collective-permute-start.41 = (bf16[2,96,768]{2,1,0:T(8,128)(2,1)S(1)}, bf16[2,96,768]{2,1,0:T(8,128)(2,1)}, u32[]{:S(2)}, u32[]{:S(2)}) collective-permute-start(bf16[2,96,768]{2,1,0:T(8,128)(2,1)S(1)} %fusion.24), channel_id=1, source_target_pairs={{0,56},{4,60},{8,0},{12,4},{16,8},{20,12},{24,16},{28,20},{32,24},... | collective-permute-start | bytes 884744 | tf_op jit(solution)/shard_map/ppermute | solution.py:25
  512.3 5.2 collective-permute-start.42
  517.6 8.0 %collective-permute-start.43 = (bf16[96,768]{1,0:T(8,128)(2,1)S(1)}, bf16[96,768]{1,0:T(8,128)(2,1)S(1)}, u32[]{:S(2)}, u32[]{:S(2)}) collective-permute-start(bf16[96,768]{1,0:T(8,128)(2,1)S(1)} %fusion.42), channel_id=1, source_target_pairs={{0,1},{1,2},{2,3},{3,0},{4,5},{5,6},{6,7},{7,4},{8,9},{9,10},{10,1... | collective-permute-start | bytes 442376 | tf_op jit(solution)/shard_map/ppermute | solution.py:25
  517.7 7.9 %collective-permute-start.44 = (bf16[96,768]{1,0:T(8,128)(2,1)S(1)}, bf16[96,768]{1,0:T(8,128)(2,1)S(1)}, u32[]{:S(2)}, u32[]{:S(2)}) collective-permute-start(bf16[96,768]{1,0:T(8,128)(2,1)S(1)} %fusion.42), channel_id=1, source_target_pairs={{0,2},{1,3},{2,0},{3,1},{4,6},{5,7},{6,4},{7,5},{8,10},{9,11},{10,... | collective-permute-start | bytes 442376 | tf_op jit(solution)/shard_map/ppermute | solution.py:25
  518.7 7.8 %collective-permute-start.45 = (bf16[96,768]{1,0:T(8,128)(2,1)S(1)}, bf16[96,768]{1,0:T(8,128)(2,1)S(1)}, u32[]{:S(2)}, u32[]{:S(2)}) collective-permute-start(bf16[96,768]{1,0:T(8,128)(2,1)S(1)} %fusion.42), channel_id=1, source_target_pairs={{0,3},{1,0},{2,1},{3,2},{4,7},{5,4},{6,5},{7,6},{8,11},{9,8},{10,9... | collective-permute-start | bytes 442376 | tf_op jit(solution)/shard_map/ppermute | solution.py:25
  (18 other events, 125.7 us)
Sparse Core Ops, SparseCore 0:
  50.3 95.0 all-gather.1
  346.3 105.7 reduce-scatter.1

commit v4 on v3

--- a/solution.py
+++ b/solution.py
@@ -16,6 +16,7 @@
 GAIN_B = 40
 PARAM_ROWS = 48
 SKEW = 2
+IN_PARTS = 6
 VMEM_LIMIT = 64 * 1024 * 1024 - 64 * 1024
 PAIR = 2
 
@@ -25,9 +26,9 @@
     return lax.ppermute(x, axis, [(i, (i + by) % peers) for i in range(peers)])
 
 
-def swap_pair(x):
+def swap_bit(x, bit):
     peers = lax.axis_size("fsdp")
-    return lax.ppermute(x, "fsdp", [(i, i ^ 1) for i in range(peers)])
+    return lax.ppermute(x, "fsdp", [(i, i ^ bit) for i in range(peers)])
 
 
 def ring_position():
@@ -35,67 +36,167 @@
     return index // PAIR, index % PAIR
 
 
-def pick(stacked, index):
-    return lax.dynamic_index_in_dim(stacked, index, 0, keepdims=False)
-
-
-def gather_rows(shard):
+def pick(stacked, index, axis=0):
+    return lax.dynamic_index_in_dim(stacked, index, axis, keepdims=False)
+
+
+def column_parts(x, width):
+    return [x[:, start : start + width] for start in range(0, x.shape[1], width)]
+
+
+def ring_gather(payload, place, far_split):
     ring = lax.axis_size("fsdp") // PAIR
     half = ring // 2
-    at, side = ring_position()
-    other = swap_pair(shard)
-    pair = jnp.where(side == 0, jnp.stack([shard, other]), jnp.stack([other, shard]))
-    whole = jnp.zeros((ring,) + pair.shape, pair.dtype)
-
-    def put(whole, piece, offset):
-        return lax.dynamic_update_slice(whole, piece[None], ((at + offset) % ring, 0, 0, 0))
-
-    whole = put(whole, pair, 0)
-    up, down = pair, pair
+    up, down = payload, payload
     for hop in range(1, half):
         up = rotate(up, "fsdp", PAIR)
         down = rotate(down, "fsdp", -PAIR)
-        whole = put(put(whole, up, ring - hop), down, hop)
-    far_up = rotate(up[0], "fsdp", PAIR)
-    far_down = rotate(down[1], "fsdp", -PAIR)
-    whole = put(whole, jnp.stack([far_up, far_down]), half)
-    return whole.reshape((ring * PAIR,) + shard.shape)
-
-
-def scatter_rows(terms):
+        place(up, ring - hop)
+        place(down, hop)
+    far_up = rotate(up[:far_split], "fsdp", PAIR)
+    far_down = rotate(down[far_split:], "fsdp", -PAIR)
+    place(jnp.concatenate([far_up, far_down], axis=0), half)
+
+
+def gather_weights(w_in, w_out):
+    quarters = lax.axis_size("batch")
+    ring = lax.axis_size("fsdp") // PAIR
+    at, side = ring_position()
+    rows, width = w_in.shape[0], w_in.shape[1] // IN_PARTS
+    out_parts = w_out.shape[1] // width
+    rest = IN_PARTS - quarters
+    mine = lax.dynamic_slice_in_dim(w_in, lax.axis_index("batch") * width, width, 1)
+    first = jnp.stack([mine] + column_parts(w_in, width)[quarters:])
+    other = swap_bit(first, 1)
+    both = jnp.where(side == 0, jnp.stack([first, other], 1), jnp.stack([other, first], 1))
+    shared = jnp.zeros((ring, PAIR, rows, width), w_in.dtype)
+    whole = jnp.zeros((rest, ring, PAIR, rows, width), w_in.dtype)
+    out = jnp.zeros((out_parts, ring, PAIR, rows, width), w_in.dtype)
+
+    def place_shared(piece, offset):
+        nonlocal shared
+        spot = ((at + offset) % ring, 0, 0, 0)
+        shared = lax.dynamic_update_slice(shared, piece[None], spot)
+
+    def place_out(piece, offset, where):
+        nonlocal out
+        spot = (0, (at + offset) % ring, where, 0, 0)
+        out = lax.dynamic_update_slice(out, piece[:, None, None], spot)
+
+    def place_rest(piece, offset):
+        nonlocal whole
+        pair = piece[: rest * PAIR].reshape(rest, 1, PAIR, rows, width)
+        whole = lax.dynamic_update_slice(whole, pair, (0, (at + offset) % ring, 0, 0, 0))
+        own = piece[rest * PAIR :]
+        place_out(own, offset, side)
+        place_out(swap_bit(own, 1), offset, 1 - side)
+
+    place_shared(both[0], 0)
+    ring_gather(both[0], place_shared, 1)
+    payload = jnp.concatenate(
+        [both[1:].reshape(rest * PAIR, rows, width), jnp.stack(column_parts(w_out, width))]
+    )
+    place_rest(payload, 0)
+    ring_gather(payload, place_rest, (rest * PAIR + out_parts) // 2)
+    depth = ring * PAIR * rows
+    shared = lax.all_gather(shared.reshape(depth, width), "batch", axis=0, tiled=False)
+    return shared, whole.reshape(rest, depth, width), out.reshape(out_parts, depth, width)
+
+
+def ring_scatter(term_at, far_split):
     ring = lax.axis_size("fsdp") // PAIR
     half = ring // 2
-    at, side = ring_position()
-    pairs = terms.reshape((ring, PAIR) + terms.shape[1:])
-    far = pick(pairs, (at + half) % ring)
-    up = rotate(far[0], "fsdp", PAIR)
-    down = rotate(far[1], "fsdp", -PAIR)
+    far = term_at(half)
+    kind = far.dtype
+    up = rotate(far[:far_split], "fsdp", PAIR).astype(jnp.float32)
+    down = rotate(far[far_split:], "fsdp", -PAIR).astype(jnp.float32)
     for hop in range(half - 1, 0, -1):
-        mine_up = pick(pairs, (at + hop) % ring).astype(jnp.float32)
-        mine_down = pick(pairs, (at + ring - hop) % ring).astype(jnp.float32)
-        up = up.astype(jnp.float32)
-        down = down.astype(jnp.float32)
+        mine_up = term_at(hop).astype(jnp.float32)
+        mine_down = term_at(ring - hop).astype(jnp.float32)
         if hop == half - 1:
-            up = jnp.stack([mine_up[0] + up, mine_up[1]])
-            down = jnp.stack([mine_down[0], mine_down[1] + down])
+            up = jnp.concatenate([mine_up[:far_split] + up, mine_up[far_split:]])
+            down = jnp.concatenate([mine_down[:far_split], mine_down[far_split:] + down])
         else:
             up = mine_up + up
             down = mine_down + down
-        up = rotate(up.astype(terms.dtype), "fsdp", PAIR)
-        down = rotate(down.astype(terms.dtype), "fsdp", -PAIR)
-    total = pick(pairs, at).astype(jnp.float32) + up.astype(jnp.float32) + down.astype(jnp.float32)
-    mine = jnp.where(side == 0, total[0], total[1])
-    theirs = jnp.where(side == 0, total[1], total[0])
-    return mine + swap_pair(theirs.astype(terms.dtype)).astype(jnp.float32)
+        up = rotate(up.astype(kind), "fsdp", PAIR).astype(jnp.float32)
+        down = rotate(down.astype(kind), "fsdp", -PAIR).astype(jnp.float32)
+    return term_at(0).astype(jnp.float32) + up + down
+
+
+def keep_side(total, kind):
+    side = lax.axis_index("fsdp") % PAIR
+    mine = jnp.where(side == 0, total[:, 0], total[:, 1])
+    theirs = jnp.where(side == 0, total[:, 1], total[:, 0])
+    return mine + swap_bit(theirs.astype(kind), 1).astype(jnp.float32)
 
 
 def batch_copies(x):
     return x, rotate(x, "batch", 1), rotate(x, "batch", 2), rotate(x, "batch", 3)
+
+
+def batch_order(copies):
+    quarters = len(copies)
+    here = lax.axis_index("batch")
+    stacked = jnp.stack(copies)
+    return [pick(stacked, (here + quarters - part) % quarters) for part in range(quarters)]
 
 
 def sum_batch(x):
     own, left, far, right = (part.astype(jnp.float32) for part in batch_copies(x))
     return (own + far) + (left + right)
+
+
+def sum_small(small):
+    quarters = lax.axis_size("batch")
+    here = lax.axis_index("batch")
+    width = small.shape[1] // quarters
+    pieces = jnp.stack(column_parts(small, width))
+    mine = pick(pieces, here)
+    for by in range(1, quarters):
+        mine = mine + rotate(pick(pieces, (here + by) % quarters), "batch", by)
+    bit = 1
+    while bit < lax.axis_size("fsdp"):
+        mine = mine + swap_bit(mine, bit)
+        bit *= 2
+    return jnp.concatenate(batch_order(batch_copies(mine)), axis=1)
+
+
+def reduce_weights(shared, rest, out, small, scale):
+    ring = lax.axis_size("fsdp") // PAIR
+    at, side = ring_position()
+    kind = shared.dtype
+    quarters, depth, width = shared.shape
+    rows = depth // (ring * PAIR)
+    split = (ring, PAIR, rows, width)
+    shared_sum = lax.psum_scatter(shared, "batch", scatter_dimension=0, tiled=False).reshape(split)
+    rest_pairs = rest.reshape((-1,) + split)
+    out_pairs = out.reshape((-1,) + split)
+    rest_parts, out_parts = rest_pairs.shape[0], out_pairs.shape[0]
+    small_total = scale * sum_small(small)
+
+    def out_for(offset, where):
+        spot = pick(out_pairs, (at + offset) % ring, 1)
+        return pick(spot, where, 1)
+
+    def main_term(offset):
+        pair = pick(rest_pairs, (at + offset) % ring, 1).reshape(-1, rows, width)
+        given = swap_bit(out_for(offset, 1 - side), 1).astype(jnp.float32)
+        own = (out_for(offset, side).astype(jnp.float32) + given).astype(kind)
+        return jnp.concatenate([pair, own])
+
+    total = ring_scatter(main_term, (rest_parts * PAIR + out_parts) // 2)
+    rest_share = keep_side(
+        total[: rest_parts * PAIR].reshape(rest_parts, PAIR, rows, width), kind
+    )
+    share = jnp.concatenate([rest_share, total[rest_parts * PAIR :]]).astype(kind)
+    share = sum_batch(share)
+    shared_total = ring_scatter(lambda offset: pick(shared_sum, (at + offset) % ring), 1)
+    shared_share = keep_side(shared_total[None], kind)[0].astype(kind)
+    in_parts = [part.astype(jnp.float32) for part in batch_order(batch_copies(shared_share))]
+    grad_in = jnp.concatenate(in_parts + [share[part] for part in range(rest_parts)], axis=1)
+    grad_out = jnp.concatenate([share[rest_parts + part] for part in range(out_parts)], axis=1)
+    return scale * grad_in, scale * grad_out, small_total
 
 
 def layer_stats(values):
@@ -156,8 +257,19 @@
     return shifts[offset % SUBLANES, pl.ds(start, length), lanes]
 
 
+def part_copy(source, index, target, part, sems, base):
+    return pltpu.make_async_copy(source.at[index], target.at[part], sems.at[base + part])
+
+
+def start_parts(shared, rest, target, sems, base):
+    for part in range(shared.shape[0]):
+        part_copy(shared, part, target, part, sems, base).start()
+    for part in range(rest.shape[0]):
+        part_copy(rest, part, target, shared.shape[0] + part, sems, base).start()
+
+
 def forward_kernel(
-    info, incoming, frames, w_in, w_out, params, *refs, taps, length, width, aliased
+    info, incoming, frames, w_shared, w_rest, w_out, params, *refs, taps, length, width, aliased
 ):
     refs = refs[aliased:]
     outgoing, x_all, proj_all, swish_all, value_all, gate_all, mid_all, inv_all = refs[:8]
@@ -184,12 +296,7 @@
 
         params_copy = pltpu.make_async_copy(params, params_v, in_sems.at[1])
         params_copy.start()
-        w_in_copies = [
-            pltpu.make_async_copy(w_in.at[part], w_in_v.at[part], in_sems.at[2 + part])
-            for part in range(parts)
-        ]
-        for copy in w_in_copies:
-            copy.start()
+        start_parts(w_shared, w_rest, w_in_v, in_sems, 2)
         w_out_copy = pltpu.make_async_copy(w_out, w_out_v, in_sems.at[2 + parts])
         w_out_copy.start()
         saves = []
@@ -210,12 +317,12 @@
         part_width = w_in_v.shape[2]
 
         def into_value(part, lanes):
-            pltpu.make_async_copy(w_in.at[part], w_in_v.at[part], in_sems.at[2 + part]).wait()
+            part_copy(w_shared, 0, w_in_v, part, in_sems, 2).wait()
             value_v[:, lanes] = rows_by(proj_v[...], w_in_v[part])
 
         def into_gate(block, lanes):
             part = block + parts // 2
-            pltpu.make_async_copy(w_in.at[part], w_in_v.at[part], in_sems.at[2 + part]).wait()
+            part_copy(w_shared, 0, w_in_v, part, in_sems, 2).wait()
             gate_v[:, lanes] = jax.nn.sigmoid(rows_by(proj_v[...], w_in_v[part]))
 
         each_block(width, part_width, into_value)
@@ -247,9 +354,7 @@
 
         def into_out(block, lanes):
             source = x_v[:, lanes].astype(jnp.float32)
-            out_v[:, lanes] = (source + rows_by(swish_v[...], w_out_v[:, lanes])).astype(
-                jnp.bfloat16
-            )
+            out_v[:, lanes] = (source + rows_by(swish_v[...], w_out_v[block])).astype(jnp.bfloat16)
 
         each_block(width, part_width, into_out)
         save(out_v, outgoing)
@@ -258,7 +363,7 @@
 
 
 def backward_kernel(
-    info, incoming, cotangent, w_in, w_out, params,
+    info, incoming, cotangent, w_shared, w_rest, w_out, params,
     x_all, value_all, gate_all, mid_all, inv_all, *refs, taps, length, width, aliased
 ):
     refs = refs[aliased:]
@@ -299,12 +404,7 @@
             copy = pltpu.make_async_copy(source, target, in_sems.at[2 + number])
             copy.start()
             loads.append(copy)
-        w_in_copies = [
-            pltpu.make_async_copy(w_in.at[part], w_in_v.at[part], in_sems.at[8 + part])
-            for part in range(parts)
-        ]
-        for copy in w_in_copies:
-            copy.start()
+        start_parts(w_shared, w_rest, w_in_v, in_sems, 8)
         saves = []
 
         def save(source, target):
@@ -324,9 +424,10 @@
         save(u_v, up_all.at[slot])
         w_out_copy.wait()
         part_width = w_in_v.shape[2]
+        conv_v[...] = jnp.zeros_like(conv_v)
 
         def into_swish(block, lanes):
-            conv_v[:, lanes] = rows_back(u_v[...], w_out_v[lanes, :])
+            conv_v[...] += rows_back(u_v[:, lanes], w_out_v[block])
 
         each_block(width, part_width, into_swish)
         swish_grad = conv_v[...]
@@ -368,7 +469,7 @@
         conv_v[...] = jnp.zeros_like(conv_v)
 
         def into_input(part, lanes):
-            pltpu.make_async_copy(w_in.at[part], w_in_v.at[part], in_sems.at[8 + part]).wait()
+            part_copy(w_shared, 0, w_in_v, part, in_sems, 8).wait()
             conv_v[...] += rows_back(grad_v[:, lanes], w_in_v[part])
 
         each_block(2 * width, part_width, into_input)
@@ -421,7 +522,7 @@
     )
 
 
-def forward_stage(info, incoming, frames, w_in, w_out, params, buffers, taps):
+def forward_stage(info, incoming, frames, weights, params, buffers, taps):
     micro, length, width = frames.shape
     f32, bf16 = jnp.float32, jnp.bfloat16
     shape = jax.ShapeDtypeStruct
@@ -431,18 +532,18 @@
     rows = functools.partial(pltpu.VMEM, (length, width))
     span = length + 2 * MARGIN
     scratch = [
-        rows(bf16), pltpu.VMEM(w_in.shape, bf16), pltpu.VMEM(w_out.shape, bf16),
+        rows(bf16), pltpu.VMEM((IN_PARTS,) + weights[2].shape[1:], bf16), pltpu.VMEM(weights[2].shape, bf16),
         pltpu.VMEM(params.shape, f32), rows(bf16), rows(bf16), rows(f32), rows(f32), rows(f32),
         pltpu.VMEM((length, LANES), f32), pltpu.VMEM((span, width), f32),
         pltpu.VMEM((SUBLANES, span - SUBLANES, width), f32), rows(f32), rows(bf16),
     ]
     return stage_call(
-        forward_kernel, scratch, info, (incoming, frames, w_in, w_out, params), outs, buffers,
-        taps, length, width, stage_cost(length, width), (3 + w_in.shape[0], 8),
-    )
-
-
-def backward_stage(info, incoming, cotangent, w_in, w_out, params, saved, buffers, taps):
+        forward_kernel, scratch, info, (incoming, frames, *weights, params), outs, buffers,
+        taps, length, width, stage_cost(length, width), (3 + IN_PARTS, 8),
+    )
+
+
+def backward_stage(info, incoming, cotangent, weights, params, saved, buffers, taps):
     micro, length, width = cotangent.shape
     f32, bf16 = jnp.float32, jnp.bfloat16
     shape = jax.ShapeDtypeStruct
@@ -455,53 +556,16 @@
     span = length + 2 * MARGIN
     lifted = pltpu.VMEM((SUBLANES, span - SUBLANES, width), f32)
     scratch = [
-        rows(bf16), pltpu.VMEM(w_in.shape, bf16), pltpu.VMEM(w_out.shape, bf16),
+        rows(bf16), pltpu.VMEM((IN_PARTS,) + weights[2].shape[1:], bf16), pltpu.VMEM(weights[2].shape, bf16),
         pltpu.VMEM(params.shape, f32), rows(bf16), rows(f32), rows(f32), rows(f32),
         pltpu.VMEM((length, LANES), f32), pltpu.VMEM((span, width), f32), lifted,
         pltpu.VMEM((span, width), f32), lifted, rows(f32),
         pltpu.VMEM((length, 2 * width), bf16), pltpu.VMEM(params.shape, f32), rows(bf16),
     ]
     return stage_call(
-        backward_kernel, scratch, info, (incoming, cotangent, w_in, w_out, params) + tuple(saved),
-        outs, buffers, taps, length, width, stage_cost(length, width), (8 + w_in.shape[0], 5),
-    )
-
-
-def gather_weights(w_in, w_out):
-    quarters = lax.axis_size("batch")
-    width = w_in.shape[1] // quarters
-    mine = lax.dynamic_slice_in_dim(w_in, lax.axis_index("batch") * width, width, 1)
-    mine = gather_rows(mine)
-    mine = mine.reshape(-1, width)
-    w_in_full = lax.all_gather(mine, "batch", axis=0, tiled=False)
-    w_out_full = gather_rows(w_out).reshape(-1, w_out.shape[1])
-    return w_in_full, w_out_full
-
-
-def reduce_weights(term_in, term_out, small, scale):
-    quarters, depth, width = term_in.shape
-    fsdp = lax.axis_size("fsdp")
-    rows = depth // fsdp
-    small_rows = -(-small.shape[0] // fsdp)
-    small_pad = jnp.pad(small, ((0, small_rows * fsdp - small.shape[0]), (0, 0)))
-    extra = jnp.pad(
-        small_pad.reshape(fsdp, small_rows, depth).astype(jnp.bfloat16),
-        ((0, 0), (0, 16 - small_rows), (0, 0)),
-    )
-    out_terms = jnp.concatenate([term_out.reshape(fsdp, rows, depth), extra], axis=1)
-    in_quarter = lax.psum_scatter(term_in, "batch", scatter_dimension=0, tiled=False)
-    out_share = scatter_rows(out_terms)
-    out_sum = sum_batch(out_share.astype(jnp.bfloat16))
-    grad_out = scale * out_sum[:rows]
-    small_sum = gather_rows(scale * out_sum[rows : rows + small_rows])
-    small_sum = small_sum.reshape(fsdp * small_rows, depth)[: small.shape[0]]
-    in_share = scatter_rows(in_quarter.reshape(fsdp, rows, width)).astype(jnp.bfloat16)
-    copies = jnp.stack(batch_copies(in_share))
-    here = lax.axis_index("batch")
-    grad_in = jnp.concatenate(
-        [pick(copies, (here + quarters - part) % quarters) for part in range(quarters)], axis=1
-    )
-    return scale * grad_in.astype(jnp.float32), grad_out, small_sum
+        backward_kernel, scratch, info, (incoming, cotangent, *weights, params) + tuple(saved),
+        outs, buffers, taps, length, width, stage_cost(length, width), (8 + IN_PARTS, 5),
+    )
 
 
 def send_active(x, senders, by):
@@ -519,7 +583,7 @@
     scale = 1.0 / math.sqrt(
         micro_count * frames_len * lax.axis_size("fsdp") * lax.axis_size("batch")
     )
-    w_in_full, w_out_full = gather_weights(w_in[0], w_out[0])
+    weights = gather_weights(w_in[0], w_out[0])
     taps = w_depth.shape[1]
     params = jnp.concatenate(
         [
@@ -553,7 +617,7 @@
     saved = None
     for slot in range(slots):
         outgoing, *saved = forward_stage(
-            table[slot], pending.pop(0), frame_rows, w_in_full, w_out_full, params, saved, taps
+            table[slot], pending.pop(0), frame_rows, weights, params, saved, taps
         )
         pending.append(send_active(outgoing, active_at(slot, False), 1))
     x_all, proj_all, swish_all, value_all, gate_all, mid_all, inv_all = saved
@@ -563,13 +627,14 @@
     grads = None
     for slot in range(slots):
         outgoing, *grads = backward_stage(
-            table[slot], pending.pop(0), cotangent_rows, w_in_full, w_out_full, params, kept,
+            table[slot], pending.pop(0), cotangent_rows, weights, params, kept,
             grads, taps,
         )
         pending.append(send_active(outgoing, active_at(slot, True), -1))
     input_all, grad_all, up_all, small_all = grads
     total_rows = micro_count * frames_len
-    parts, unused, width = w_in_full.shape
+    width = weights[2].shape[2]
+    quarters = weights[0].shape[0]
     proj_rows = proj_all.reshape(total_rows, model_width)
     grad_rows = grad_all.reshape(total_rows, 2 * model_width)
     swish_rows = swish_all.reshape(total_rows, model_width)
@@ -580,10 +645,14 @@
             left, right, (((0,), (0,)), ((), ())), preferred_element_type=jnp.float32
         ).astype(jnp.bfloat16)
 
-    term_in = jnp.stack(
-        [term(proj_rows, grad_rows[:, part * width : (part + 1) * width]) for part in range(parts)]
-    )
-    term_out = term(swish_rows, upstream_rows)
+    def terms(left, right, parts):
+        return jnp.stack(
+            [term(left, right[:, part * width : (part + 1) * width]) for part in parts]
+        )
+
+    shared_terms = terms(proj_rows, grad_rows, range(quarters))
+    rest_terms = terms(proj_rows, grad_rows, range(quarters, IN_PARTS))
+    out_terms = terms(swish_rows, upstream_rows, range(weights[2].shape[0]))
     small_rows = jnp.sum(small_all, axis=0)
     small = jnp.concatenate(
         [
@@ -593,7 +662,9 @@
         ],
         axis=0,
     )
-    grad_in, grad_out, small_total = reduce_weights(term_in, term_out, small, scale)
+    grad_in, grad_out, small_total = reduce_weights(
+        shared_terms, rest_terms, out_terms, small, scale
+    )
     input_grads = input_all.reshape(1, micro_count, 1, frames_len, model_width)
     return (
         input_grads,

time: 544 us -> 514 us (0.945)
  waiting for transfers between devices: 263 us -> 189 us
  starting transfers between devices: 105 us -> 127 us
  local copies, waits for them, and re-layouts: 28.2 us -> 41.8 us
    ppermute x46 -> x44, waiting for transfers between devices: 151 us -> 68.7 us  [rotate(): return lax.ppermute(x, axis, [(i, (i + by) % peers) for i in range(peers)])]
    ppermute x5 -> x23, waiting for transfers between devices: 20.7 us -> 57.6 us  [swap_bit(): return lax.ppermute(x, 'fsdp', [(i, i ^ bit) for i in range(peers)])]
    all_gather x1, waiting for transfers between devices: 30 us -> 0.01 us  [gather_weights(): lax.all_gather(shared.reshape(depth, width), 'batch', axis=0, tiled=False)]
    ppermute x5 -> x23, starting transfers between devices: 4.63 us -> 30.8 us  [swap_bit(): return lax.ppermute(x, 'fsdp', [(i, i ^ bit) for i in range(peers)])]
    dynamic_update_slice x18 -> x29, local copies, waits for them, and re-layouts: 5.43 us -> 17.3 us  [the longest x15 11 us: place_out(): out = lax.dynamic_update_slice(out, piece[:, None, None], spot)]
    convert_element_type x9 -> x11, other arithmetic: 1.95 us -> 7.75 us  [the longest x4 4.44 us: ring_scatter(): up = rotate(up.astype(kind), 'fsdp', PAIR).astype(jnp.float32)]
    ppermute x46 -> x44, starting transfers between devices: 76.2 us -> 71.9 us  [rotate(): return lax.ppermute(x, axis, [(i, (i + by) % peers) for i in range(peers)])]
  transfers between devices with their start and end apart: 69 -> 85, of which waited for: 38 -> 44; matrix products, arithmetic and copies ran while one was open for 7% -> 12% of each run, Pallas kernels for 14% -> 15%
where the time goes in v4:
time: 514 us; the launch traced here: 504 us
  waiting for transfers between devices  189 us (37%)
  starting transfers between devices  127 us (25%)
  Pallas kernels  99 us (19%)
  local copies, waits for them, and re-layouts  41.8 us (8%)
  other arithmetic  24.6 us (5%)
  between operations  15.4 us (3%)
  matrix products  7.72 us (2%)
    pallas_call x20, Pallas kernels, stage_call(): pl.pallas_call(functools.partial(kernel, taps=taps, length=length, width=...  99 us
    ppermute x44, starting transfers between devices, rotate(): return lax.ppermute(x, axis, [(i, (i + by) % peers) for i in range(peers)])  71.9 us
    ppermute x44, waiting for transfers between devices, rotate(): return lax.ppermute(x, axis, [(i, (i + by) % peers) for i in range(peers)])  68.7 us
    ppermute x16, waiting for transfers between devices, send_active(): return lax.ppermute(x, 'section', pairs)  62.7 us
    ppermute x23, waiting for transfers between devices, swap_bit(): return lax.ppermute(x, 'fsdp', [(i, i ^ bit) for i in range(peers)])  57.6 us
    ppermute x23, starting transfers between devices, swap_bit(): return lax.ppermute(x, 'fsdp', [(i, i ^ bit) for i in range(peers)])  30.8 us
    ppermute x16, starting transfers between devices, send_active(): return lax.ppermute(x, 'section', pairs)  23.8 us
    dynamic_update_slice x15, local copies, waits for them, and re-layouts, place_out(): out = lax.dynamic_update_slice(out, piece[:, None, None], spot)  11 us
  transfers between devices with their start and end apart: 85, of which 44 were waited for; matrix products, arithmetic and copies ran while one was open for 12% of the time, Pallas kernels for 15%

profile of v4, /device:TPU:8, one launch (start us, length us, event | category | flops | bytes accessed | tf_op | source)
XLA Modules:
  0.0 504.0 jit_solution(7746172568582053537)
XLA Ops:
  9.1 2.3 collective-permute-start
  11.4 6.6 %collective-permute-done = bf16[3,96,512]{2,1,0:T(8,128)(2,1)S(1)} collective-permute-done((bf16[3,96,512]{2,1,0:T(8,128)(2,1)S(1)}, bf16[3,96,512]{2,1,0:T(8,128)(2,1)S(1)}, u32[]{:S(2)}, u32[]{:S(2)}) %collective-permute-start) | collective-permute-done | bytes 294944 | tf_op jit(solution)/shard_map/ppermute | solution.py:31
  18.2 2.0 collective-permute-start.1
  20.2 4.0 collective-permute-start.2
  24.2 3.9 collective-permute-done.1
  28.2 3.2 collective-permute-start.4
  31.5 3.6 collective-permute-done.3
  35.1 3.2 collective-permute-start.6
  38.4 3.6 collective-permute-done.5
  42.1 3.4 collective-permute-start.8
  45.5 2.3 collective-permute-done.7
  51.1 3.4 concatenate.88.params
  55.9 3.5 collective-permute-start.10
  60.3 2.8 broadcast_in_dim.107
  64.6 2.0 broadcast_in_dim.106
  67.4 2.0 collective-permute-done.9
  73.5 2.4 collective-permute-start.11
  80.1 5.9 %collective-permute-done.11 = bf16[7,96,512]{2,1,0:T(8,128)(2,1)S(1)} collective-permute-done((bf16[7,96,512]{2,1,0:T(8,128)(2,1)S(1)}, bf16[7,96,512]{2,1,0:T(8,128)(2,1)S(1)}, u32[]{:S(2)}, u32[]{:S(2)}) %collective-permute-start.11) | collective-permute-done | bytes 688160 | tf_op jit(solution)/shard_map/ppermute | solution.py:26
  96.8 7.0 %collective-permute-done.13 = bf16[7,96,512]{2,1,0:T(8,128)(2,1)S(1)} collective-permute-done((bf16[7,96,512]{2,1,0:T(8,128)(2,1)S(1)}, bf16[7,96,512]{2,1,0:T(8,128)(2,1)S(1)}, u32[]{:S(2)}, u32[]{:S(2)}) %collective-permute-start.13) | collective-permute-done | bytes 688160 | tf_op jit(solution)/shard_map/ppermute | solution.py:26
  103.8 3.7 collective-permute-start.22
  109.1 3.3 collective-permute-start.16
  122.6 3.5 collective-permute-done.24
  127.5 8.7 %shard_map.127 = (bf16[48,1536]{1,0:T(8,128)(2,1)}, bf16[4,48,1536]{2,1,0:T(8,128)(2,1)}, bf16[4,48,1536]{2,1,0:T(8,128)(2,1)}, bf16[4,48,1536]{2,1,0:T(8,128)(2...) custom-call(s32[4]{0:T(128)} %get-tuple-element.291.info, ...), custom_call_target="tpu_custom_call" | custom-call | flops 679477248 | bytes 14155776 | tf_op jit(solution)/shard_map/pallas_call | solution.py:500
  138.1 8.6 %shard_map.128 = (bf16[48,1536]{1,0:T(8,128)(2,1)}, bf16[4,48,1536]{2,1,0:T(8,128)(2,1)}, bf16[4,48,1536]{2,1,0:T(8,128)(2,1)}, bf16[4,48,1536]{2,1,0:T(8,128)(2...) custom-call(s32[4]{0:T(128)} %get-tuple-element.292.info, ...), custom_call_target="tpu_custom_call", output_to_operand_aliasing={{1}: (7, {}), {2}: (8, {}), {3}: (9, {}), {4}: (10, {}), {5... | custom-call | flops 679477248 | bytes 14155776 | tf_op jit(solution)/shard_map/pallas_call | solution.py:500
  146.8 2.0 collective-permute-start.25
  151.2 8.7 %shard_map.129 = (bf16[48,1536]{1,0:T(8,128)(2,1)}, bf16[4,48,1536]{2,1,0:T(8,128)(2,1)}, bf16[4,48,1536]{2,1,0:T(8,128)(2,1)}, bf16[4,48,1536]{2,1,0:T(8,128)(2...) custom-call(s32[4]{0:T(128)} %get-tuple-element.290.info, ...), custom_call_target="tpu_custom_call", output_to_operand_aliasing={{1}: (7, {}), {2}: (8, {}), {3}: (9, {}), {4}: (10, {}), {5... | custom-call | flops 679477248 | bytes 14155776 | tf_op jit(solution)/shard_map/pallas_call | solution.py:500
  161.8 8.9 %shard_map.130 = (bf16[48,1536]{1,0:T(8,128)(2,1)}, bf16[4,48,1536]{2,1,0:T(8,128)(2,1)}, bf16[4,48,1536]{2,1,0:T(8,128)(2,1)}, bf16[4,48,1536]{2,1,0:T(8,128)(2...) custom-call(s32[4]{0:T(128)} %get-tuple-element.293.info, ...), custom_call_target="tpu_custom_call", output_to_operand_aliasing={{1}: (7, {}), {2}: (8, {}), {3}: (9, {}), {4}: (10, {}), {5... | custom-call | flops 679477248 | bytes 14155776 | tf_op jit(solution)/shard_map/pallas_call | solution.py:500
  170.7 2.0 collective-permute-start.27
  201.7 59.6 %collective-permute-done.38.incoming = bf16[48,1536]{1,0:T(8,128)(2,1)} collective-permute-done((bf16[48,1536]{1,0:T(8,128)(2,1)}, bf16[48,1536]{1,0:T(8,128)(2,1)}, u32[]{:S(2)}, u32[]{:S(2)}) %collective-permute-start.38) | collective-permute-done | bytes 147488 | tf_op jit(solution)/shard_map/ppermute | solution.py:573
  261.2 13.4 %shard_map.143 = (bf16[48,1536]{1,0:T(8,128)(2,1)}, bf16[4,48,1536]{2,1,0:T(8,128)(2,1)}, bf16[4,48,3072]{2,1,0:T(8,128)(2,1)}, bf16[4,48,1536]{2,1,0:T(8,128)(2,1)}, f32[4,48,1536]{2,1,0:T(8,128)}) custom-call(s32[4]{0:T(128)} %get-tuple-element.278.info, ...), custom_call_target="tpu_custom_call", output_to_operand_aliasing={{1}: (12, {}), {2}: (13, {}), {3}: (14, {}), {4}: (15, {})} | custom-call | flops 679477248 | bytes 14155776 | tf_op jit(solution)/shard_map/pallas_call | solution.py:500
  277.0 13.4 %shard_map.144 = (bf16[48,1536]{1,0:T(8,128)(2,1)}, bf16[4,48,1536]{2,1,0:T(8,128)(2,1)}, bf16[4,48,3072]{2,1,0:T(8,128)(2,1)}, bf16[4,48,1536]{2,1,0:T(8,128)(2,1)}, f32[4,48,1536]{2,1,0:T(8,128)}) custom-call(s32[4]{0:T(128)} %get-tuple-element.285.info, ...), custom_call_target="tpu_custom_call", output_to_operand_aliasing={{1}: (12, {}), {2}: (13, {}), {3}: (14, {}), {4}: (15, {})} | custom-call | flops 679477248 | bytes 14155776 | tf_op jit(solution)/shard_map/pallas_call | solution.py:500
  291.7 13.4 %shard_map.145 = (bf16[48,1536]{1,0:T(8,128)(2,1)}, bf16[4,48,1536]{2,1,0:T(8,128)(2,1)}, bf16[4,48,3072]{2,1,0:T(8,128)(2,1)}, bf16[4,48,1536]{2,1,0:T(8,128)(2,1)}, f32[4,48,1536]{2,1,0:T(8,128)}) custom-call(s32[4]{0:T(128)} %get-tuple-element.277.info, ...), custom_call_target="tpu_custom_call", output_to_operand_aliasing={{1}: (12, {}), {2}: (13, {}), {3}: (14, {}), {4}: (15, {})} | custom-call | flops 679477248 | bytes 14155776 | tf_op jit(solution)/shard_map/pallas_call | solution.py:500
  307.1 13.6 %shard_map.146 = (bf16[48,1536]{1,0:T(8,128)(2,1)}, bf16[4,48,1536]{2,1,0:T(8,128)(2,1)}, bf16[4,48,3072]{2,1,0:T(8,128)(2,1)}, bf16[4,48,1536]{2,1,0:T(8,128)(2,1)}, f32[4,48,1536]{2,1,0:T(8,128)}) custom-call(s32[4]{0:T(128)} %get-tuple-element.286.info, ...), custom_call_target="tpu_custom_call", output_to_operand_aliasing={{1}: (12, {}), {2}: (13, {}), {3}: (14, {}), {4}: (15, {})} | custom-call | flops 679477248 | bytes 14155776 | tf_op jit(solution)/shard_map/pallas_call | solution.py:500
  324.4 3.2 pad_maximum_fusion
  345.1 4.6 collective-permute-done.54
  351.4 4.6 collective-permute-done.55
  357.8 3.9 collective-permute-done.57
  362.6 2.4 collective-permute-done.61
  365.0 3.2 collective-permute-done.62
  368.1 3.2 collective-permute-done.63
  371.3 3.2 collective-permute-done.64
  375.3 2.6 collective-permute-start.65
  379.0 7.1 %collective-permute-done.65 = bf16[4,96,512]{2,1,0:T(8,128)(2,1)S(1)} collective-permute-done((bf16[4,96,512]{2,1,0:T(8,128)(2,1)S(1)}, bf16[4,96,512]{2,1,0:T(8,128)(2,1)S(1)}, u32[]{:S(2)}, u32[]{:S(2)}) %collective-permute-start.65) | collective-permute-done | bytes 393248 | tf_op jit(solution)/shard_map/ppermute | solution.py:26
  387.1 3.7 collective-permute-start.66
  392.6 3.1 collective-permute-start.74
  401.8 2.1 add_convert_fusion.3
  405.6 8.3 %collective-permute-done.77 = f32[33,384]{1,0:T(8,128)S(1)} collective-permute-done((f32[33,384]{1,0:T(8,128)S(1)}, f32[33,384]{1,0:T(8,128)S(1)}, u32[]{:S(2)}, u32[]{:S(2)}) %collective-permute-start.77) | collective-permute-done | bytes 50720 | tf_op jit(solution)/shard_map/ppermute | solution.py:31
  415.3 3.8 collective-permute-done.78
  419.1 3.3 collective-permute-start.79
  422.5 2.1 add_convert_fusion.1
  424.6 2.7 collective-permute-start.67
  429.6 2.9 collective-permute-start.81
  436.9 2.1 add_convert_fusion.2
  443.0 2.2 collective-permute-start.45
  446.8 7.7 %collective-permute-done.41 = bf16[1,96,512]{2,1,0:T(8,128)(2,1)S(1)} collective-permute-done((bf16[1,96,512]{2,1,0:T(8,128)(2,1)S(1)}, bf16[1,96,512]{2,1,0:T(8,128)(2,1)S(1)}, u32[]{:S(2)}, u32[]{:S(2)}) %collective-permute-start.41) | collective-permute-done | bytes 98336 | tf_op jit(solution)/shard_map/ppermute | solution.py:26
  455.1 2.9 collective-permute-start.46
  458.1 3.5 collective-permute-done.42
  462.1 6.5 %collective-permute-done.43 = bf16[2,96,512]{2,1,0:T(8,128)(2,1)S(1)} collective-permute-done((bf16[2,96,512]{2,1,0:T(8,128)(2,1)S(1)}, bf16[2,96,512]{2,1,0:T(8,128)(2,1)S(1)}, u32[]{:S(2)}, u32[]{:S(2)}) %collective-permute-start.43) | collective-permute-done | bytes 196640 | tf_op jit(solution)/shard_map/ppermute | solution.py:26
  469.6 2.0 collective-permute-start.44
  471.6 2.8 collective-permute-done.47
  476.0 2.0 collective-permute-start.70
  482.9 3.2 collective-permute-done.49
  489.4 2.3 collective-permute-done.71
  492.7 2.0 collective-permute-done.50
  (306 shorter events, 149.4 us)
Async XLA Ops:
  7.2 119.6 %all-gather.2.cloned.1.call-start = ((), (), s32[]{:S(2)}) async-start(), calls=%async_computation.1 | async-start | bytes 7864320 | tf_op jit(solution)/shard_map/all_gather | solution.py:102
  9.1 8.8 %collective-permute-start = (bf16[3,96,512]{2,1,0:T(8,128)(2,1)S(1)}, bf16[3,96,512]{2,1,0:T(8,128)(2,1)S(1)}, u32[]{:S(2)}, u32[]{:S(2)}) collective-permute-start(bf16[3,96,512]{2,1,0:T(8,128)(2,1)S(1)} %get-tuple-element.347), channel_id=1, source_target_pairs={{0,4},{4,0},{8,12},{12,8},{16,20},{20,16},{24,28},{28,24},{32,36},... | collective-permute-start | bytes 884744 | tf_op jit(solution)/shard_map/ppermute | solution.py:31
  18.2 10.0 %collective-permute-start.1 = (bf16[2,96,512]{2,1,0:T(8,128)(2,1)S(1)}, bf16[2,96,512]{2,1,0:T(8,128)(2,1)S(1)}, u32[]{:S(2)}, u32[]{:S(2)}) collective-permute-start(bf16[2,96,512]{2,1,0:T(8,128)(2,1)S(1)} %get-tuple-element.337), channel_id=1, source_target_pairs={{0,8},{4,12},{8,16},{12,20},{16,24},{20,28},{24,32},{28,36},{32,40... | collective-permute-start | bytes 589832 | tf_op jit(solution)/shard_map/ppermute | solution.py:26
  20.2 8.0 %collective-permute-start.2 = (bf16[2,96,512]{2,1,0:T(8,128)(2,1)S(1)}, bf16[2,96,512]{2,1,0:T(8,128)(2,1)S(1)}, u32[]{:S(2)}, u32[]{:S(2)}) collective-permute-start(bf16[2,96,512]{2,1,0:T(8,128)(2,1)S(1)} %get-tuple-element.337), channel_id=1, source_target_pairs={{0,56},{4,60},{8,0},{12,4},{16,8},{20,12},{24,16},{28,20},{32,24},... | collective-permute-start | bytes 589832 | tf_op jit(solution)/shard_map/ppermute | solution.py:26
  28.2 6.9 %collective-permute-start.3 = (bf16[2,96,512]{2,1,0:T(8,128)(2,1)S(1)}, bf16[2,96,512]{2,1,0:T(8,128)(2,1)S(1)}, u32[]{:S(2)}, u32[]{:S(2)}) collective-permute-start(bf16[2,96,512]{2,1,0:T(8,128)(2,1)S(1)} %collective-permute-done.1), channel_id=1, source_target_pairs={{0,8},{4,12},{8,16},{12,20},{16,24},{20,28},{24,32},{28,36},{32,40... | collective-permute-start | bytes 589832 | tf_op jit(solution)/shard_map/ppermute | solution.py:26
  28.2 6.9 %collective-permute-start.4 = (bf16[2,96,512]{2,1,0:T(8,128)(2,1)S(1)}, bf16[2,96,512]{2,1,0:T(8,128)(2,1)S(1)}, u32[]{:S(2)}, u32[]{:S(2)}) collective-permute-start(bf16[2,96,512]{2,1,0:T(8,128)(2,1)S(1)} %collective-permute-done.2), channel_id=1, source_target_pairs={{0,56},{4,60},{8,0},{12,4},{16,8},{20,12},{24,16},{28,20},{32,24},... | collective-permute-start | bytes 589832 | tf_op jit(solution)/shard_map/ppermute | solution.py:26
  35.1 6.9 %collective-permute-start.5 = (bf16[2,96,512]{2,1,0:T(8,128)(2,1)S(1)}, bf16[2,96,512]{2,1,0:T(8,128)(2,1)S(1)}, u32[]{:S(2)}, u32[]{:S(2)}) collective-permute-start(bf16[2,96,512]{2,1,0:T(8,128)(2,1)S(1)} %collective-permute-done.3), channel_id=1, source_target_pairs={{0,8},{4,12},{8,16},{12,20},{16,24},{20,28},{24,32},{28,36},{32,40... | collective-permute-start | bytes 589832 | tf_op jit(solution)/shard_map/ppermute | solution.py:26
  35.1 7.0 %collective-permute-start.6 = (bf16[2,96,512]{2,1,0:T(8,128)(2,1)S(1)}, bf16[2,96,512]{2,1,0:T(8,128)(2,1)S(1)}, u32[]{:S(2)}, u32[]{:S(2)}) collective-permute-start(bf16[2,96,512]{2,1,0:T(8,128)(2,1)S(1)} %collective-permute-done.4), channel_id=1, source_target_pairs={{0,56},{4,60},{8,0},{12,4},{16,8},{20,12},{24,16},{28,20},{32,24},... | collective-permute-start | bytes 589832 | tf_op jit(solution)/shard_map/ppermute | solution.py:26
  49.1 391.5 %reduce-scatter.2.cloned.1.call-start = ((), (), s32[]{:S(2)}) async-start(), calls=%async_computation.2 | async-start | bytes 7864320 | tf_op jit(solution)/shard_map/reduce_scatter | solution.py:172
  49.2 14.6 %collective-permute-start.17 = (bf16[3,96,512]{2,1,0:T(8,128)(2,1)S(1)}, bf16[3,96,512]{2,1,0:T(8,128)(2,1)S(1)}, u32[]{:S(2)}, u32[]{:S(2)}) collective-permute-start(bf16[3,96,512]{2,1,0:T(8,128)(2,1)S(1)} %pad_maximum_fusion.10), channel_id=1, source_target_pairs={{0,4},{4,0},{8,12},{12,8},{16,20},{20,16},{24,28},{28,24},{32,36},... | collective-permute-start | bytes 884744 | tf_op jit(solution)/shard_map/ppermute | solution.py:31
  55.8 13.6 %collective-permute-start.9 = (bf16[7,96,512]{2,1,0:T(8,128)(2,1)S(1)}, bf16[7,96,512]{2,1,0:T(8,128)(2,1)S(1)}, u32[]{:S(2)}, u32[]{:S(2)}) collective-permute-start(bf16[7,96,512]{2,1,0:T(8,128)(2,1)S(1)} %pad_maximum_fusion.2), channel_id=1, source_target_pairs={{0,8},{4,12},{8,16},{12,20},{16,24},{20,28},{24,32},{28,36},{32,40... | collective-permute-start | bytes 2064392 | tf_op jit(solution)/shard_map/ppermute | solution.py:26
  55.9 15.2 %collective-permute-start.10 = (bf16[7,96,512]{2,1,0:T(8,128)(2,1)S(1)}, bf16[7,96,512]{2,1,0:T(8,128)(2,1)S(1)}, u32[]{:S(2)}, u32[]{:S(2)}) collective-permute-start(bf16[7,96,512]{2,1,0:T(8,128)(2,1)S(1)} %pad_maximum_fusion.2), channel_id=1, source_target_pairs={{0,56},{4,60},{8,0},{12,4},{16,8},{20,12},{24,16},{28,20},{32,24},... | collective-permute-start | bytes 2064392 | tf_op jit(solution)/shard_map/ppermute | solution.py:26
  69.4 8.0 %collective-permute-start.18 = (bf16[3,96,512]{2,1,0:T(8,128)(2,1)S(1)}, bf16[3,96,512]{2,1,0:T(8,128)(2,1)S(1)}, u32[]{:S(2)}, u32[]{:S(2)}) collective-permute-start(bf16[3,96,512]{2,1,0:T(8,128)(2,1)S(1)} %slice.423), channel_id=1, source_target_pairs={{0,4},{4,0},{8,12},{12,8},{16,20},{20,16},{24,28},{28,24},{32,36},... | collective-permute-start | bytes 884744 | tf_op jit(solution)/shard_map/ppermute | solution.py:31
  71.1 8.3 %collective-permute-start.19 = (bf16[3,96,512]{2,1,0:T(8,128)(2,1)S(1)}, bf16[3,96,512]{2,1,0:T(8,128)(2,1)S(1)}, u32[]{:S(2)}, u32[]{:S(2)}) collective-permute-start(bf16[3,96,512]{2,1,0:T(8,128)(2,1)S(1)} %slice.424), channel_id=1, source_target_pairs={{0,4},{4,0},{8,12},{12,8},{16,20},{20,16},{24,28},{28,24},{32,36},... | collective-permute-start | bytes 884744 | tf_op jit(solution)/shard_map/ppermute | solution.py:31
  73.5 12.6 %collective-permute-start.11 = (bf16[7,96,512]{2,1,0:T(8,128)(2,1)S(1)}, bf16[7,96,512]{2,1,0:T(8,128)(2,1)S(1)}, u32[]{:S(2)}, u32[]{:S(2)}) collective-permute-start(bf16[7,96,512]{2,1,0:T(8,128)(2,1)S(1)} %collective-permute-done.9), channel_id=1, source_target_pairs={{0,8},{4,12},{8,16},{12,20},{16,24},{20,28},{24,32},{28,36},{32,40... | collective-permute-start | bytes 2064392 | tf_op jit(solution)/shard_map/ppermute | solution.py:26
  75.9 12.9 %collective-permute-start.12 = (bf16[7,96,512]{2,1,0:T(8,128)(2,1)S(1)}, bf16[7,96,512]{2,1,0:T(8,128)(2,1)S(1)}, u32[]{:S(2)}, u32[]{:S(2)}) collective-permute-start(bf16[7,96,512]{2,1,0:T(8,128)(2,1)S(1)} %collective-permute-done.10), channel_id=1, source_target_pairs={{0,56},{4,60},{8,0},{12,4},{16,8},{20,12},{24,16},{28,20},{32,24},... | collective-permute-start | bytes 2064392 | tf_op jit(solution)/shard_map/ppermute | solution.py:26
  86.1 8.4 %collective-permute-start.20 = (bf16[3,96,512]{2,1,0:T(8,128)(2,1)S(1)}, bf16[3,96,512]{2,1,0:T(8,128)(2,1)S(1)}, u32[]{:S(2)}, u32[]{:S(2)}) collective-permute-start(bf16[3,96,512]{2,1,0:T(8,128)(2,1)S(1)} %slice.425), channel_id=1, source_target_pairs={{0,4},{4,0},{8,12},{12,8},{16,20},{20,16},{24,28},{28,24},{32,36},... | collective-permute-start | bytes 884744 | tf_op jit(solution)/shard_map/ppermute | solution.py:31
  88.8 7.2 %collective-permute-start.21 = (bf16[3,96,512]{2,1,0:T(8,128)(2,1)S(1)}, bf16[3,96,512]{2,1,0:T(8,128)(2,1)S(1)}, u32[]{:S(2)}, u32[]{:S(2)}) collective-permute-start(bf16[3,96,512]{2,1,0:T(8,128)(2,1)S(1)} %slice.426), channel_id=1, source_target_pairs={{0,4},{4,0},{8,12},{12,8},{16,20},{20,16},{24,28},{28,24},{32,36},... | collective-permute-start | bytes 884744 | tf_op jit(solution)/shard_map/ppermute | solution.py:31
  90.5 13.2 %collective-permute-start.13 = (bf16[7,96,512]{2,1,0:T(8,128)(2,1)S(1)}, bf16[7,96,512]{2,1,0:T(8,128)(2,1)S(1)}, u32[]{:S(2)}, u32[]{:S(2)}) collective-permute-start(bf16[7,96,512]{2,1,0:T(8,128)(2,1)S(1)} %collective-permute-done.11), channel_id=1, source_target_pairs={{0,8},{4,12},{8,16},{12,20},{16,24},{20,28},{24,32},{28,36},{32,40... | collective-permute-start | bytes 2064392 | tf_op jit(solution)/shard_map/ppermute | solution.py:26
  92.4 15.2 %collective-permute-start.14 = (bf16[7,96,512]{2,1,0:T(8,128)(2,1)S(1)}, bf16[7,96,512]{2,1,0:T(8,128)(2,1)S(1)}, u32[]{:S(2)}, u32[]{:S(2)}) collective-permute-start(bf16[7,96,512]{2,1,0:T(8,128)(2,1)S(1)} %collective-permute-done.12), channel_id=1, source_target_pairs={{0,56},{4,60},{8,0},{12,4},{16,8},{20,12},{24,16},{28,20},{32,24},... | collective-permute-start | bytes 2064392 | tf_op jit(solution)/shard_map/ppermute | solution.py:26
  103.8 11.2 %collective-permute-start.22 = (bf16[3,96,512]{2,1,0:T(8,128)(2,1)S(1)}, bf16[3,96,512]{2,1,0:T(8,128)(2,1)S(1)}, u32[]{:S(2)}, u32[]{:S(2)}) collective-permute-start(bf16[3,96,512]{2,1,0:T(8,128)(2,1)S(1)} %get-tuple-element.333), channel_id=1, source_target_pairs={{0,4},{4,0},{8,12},{12,8},{16,20},{20,16},{24,28},{28,24},{32,36},... | collective-permute-start | bytes 884744 | tf_op jit(solution)/shard_map/ppermute | solution.py:31
  107.6 10.9 %collective-permute-start.23 = (bf16[3,96,512]{2,1,0:T(8,128)(2,1)S(1)}, bf16[3,96,512]{2,1,0:T(8,128)(2,1)S(1)}, u32[]{:S(2)}, u32[]{:S(2)}) collective-permute-start(bf16[3,96,512]{2,1,0:T(8,128)(2,1)S(1)} %slice.428), channel_id=1, source_target_pairs={{0,4},{4,0},{8,12},{12,8},{16,20},{20,16},{24,28},{28,24},{32,36},... | collective-permute-start | bytes 884744 | tf_op jit(solution)/shard_map/ppermute | solution.py:31
  109.1 10.2 %collective-permute-start.16 = (bf16[4,96,512]{2,1,0:T(8,128)(2,1)S(1)}, bf16[4,96,512]{2,1,0:T(8,128)(2,1)S(1)}, u32[]{:S(2)}, u32[]{:S(2)}) collective-permute-start(bf16[4,96,512]{2,1,0:T(8,128)(2,1)S(1)} %get-tuple-element.335), channel_id=1, source_target_pairs={{0,56},{4,60},{8,0},{12,4},{16,8},{20,12},{24,16},{28,20},{32,24},... | collective-permute-start | bytes 1179656 | tf_op jit(solution)/shard_map/ppermute | solution.py:26
  112.4 8.6 %collective-permute-start.15 = (bf16[3,96,512]{2,1,0:T(8,128)(2,1)S(1)}, bf16[3,96,512]{2,1,0:T(8,128)(2,1)S(1)}, u32[]{:S(2)}, u32[]{:S(2)}) collective-permute-start(bf16[3,96,512]{2,1,0:T(8,128)(2,1)S(1)} %get-tuple-element.334), channel_id=1, source_target_pairs={{0,8},{4,12},{8,16},{12,20},{16,24},{20,28},{24,32},{28,36},{32,40... | collective-permute-start | bytes 884744 | tf_op jit(solution)/shard_map/ppermute | solution.py:26
  119.3 6.8 %collective-permute-start.24 = (bf16[3,96,512]{2,1,0:T(8,128)(2,1)S(1)}, bf16[3,96,512]{2,1,0:T(8,128)(2,1)S(1)}, u32[]{:S(2)}, u32[]{:S(2)}) collective-permute-start(bf16[3,96,512]{2,1,0:T(8,128)(2,1)S(1)} %slice.429), channel_id=1, source_target_pairs={{0,4},{4,0},{8,12},{12,8},{16,20},{20,16},{24,28},{28,24},{32,36},... | collective-permute-start | bytes 884744 | tf_op jit(solution)/shard_map/ppermute | solution.py:31
  136.1 15.1 %collective-permute-start.26 = (bf16[48,1536]{1,0:T(8,128)(2,1)}, bf16[48,1536]{1,0:T(8,128)(2,1)}, u32[]{:S(2)}, u32[]{:S(2)}) collective-permute-start(bf16[48,1536]{1,0:T(8,128)(2,1)} %get-tuple-element.141), channel_id=1, source_target_pairs={{0,64},{1,65},{2,66},{3,67},{4,68},{5,69},{6,70},{7,71},{8,72},{9,... | collective-permute-start | bytes 442376 | tf_op jit(solution)/shard_map/ppermute | solution.py:573
  146.8 15.1 %collective-permute-start.25 = (bf16[48,1536]{1,0:T(8,128)(2,1)}, bf16[48,1536]{1,0:T(8,128)(2,1)}, u32[]{:S(2)}, u32[]{:S(2)}) collective-permute-start(bf16[48,1536]{1,0:T(8,128)(2,1)} %get-tuple-element.140), channel_id=1, source_target_pairs={{0,64},{1,65},{2,66},{3,67},{4,68},{5,69},{6,70},{7,71},{8,72},{9,... | collective-permute-start | bytes 442376 | tf_op jit(solution)/shard_map/ppermute | solution.py:573
  159.9 14.6 %collective-permute-start.28 = (bf16[48,1536]{1,0:T(8,128)(2,1)}, bf16[48,1536]{1,0:T(8,128)(2,1)}, u32[]{:S(2)}, u32[]{:S(2)}) collective-permute-start(bf16[48,1536]{1,0:T(8,128)(2,1)} %get-tuple-element.157), channel_id=1, source_target_pairs={{0,64},{64,128},{1,65},{65,129},{2,66},{66,130},{3,67},{67,131},{4... | collective-permute-start | bytes 442376 | tf_op jit(solution)/shard_map/ppermute | solution.py:573
  198.2 63.0 %collective-permute-start.38 = (bf16[48,1536]{1,0:T(8,128)(2,1)}, bf16[48,1536]{1,0:T(8,128)(2,1)}, u32[]{:S(2)}, u32[]{:S(2)}) collective-permute-start(bf16[48,1536]{1,0:T(8,128)(2,1)} %get-tuple-element.234), channel_id=1, source_target_pairs={{128,64},{64,0},{129,65},{65,1},{130,66},{66,2},{131,67},{67,3},{1... | collective-permute-start | bytes 442376 | tf_op jit(solution)/shard_map/ppermute | solution.py:573
  200.4 76.6 %collective-permute-start.37 = (bf16[48,1536]{1,0:T(8,128)(2,1)}, bf16[48,1536]{1,0:T(8,128)(2,1)}, u32[]{:S(2)}, u32[]{:S(2)}) collective-permute-start(bf16[48,1536]{1,0:T(8,128)(2,1)} %get-tuple-element.233), channel_id=1, source_target_pairs={{128,64},{64,0},{129,65},{65,1},{130,66},{66,2},{131,67},{67,3},{1... | collective-permute-start | bytes 442376 | tf_op jit(solution)/shard_map/ppermute | solution.py:573
  274.6 17.1 %collective-permute-start.40 = (bf16[48,1536]{1,0:T(8,128)(2,1)}, bf16[48,1536]{1,0:T(8,128)(2,1)}, u32[]{:S(2)}, u32[]{:S(2)}) collective-permute-start(bf16[48,1536]{1,0:T(8,128)(2,1)} %get-tuple-element.244), channel_id=1, source_target_pairs={{64,0},{65,1},{66,2},{67,3},{68,4},{69,5},{70,6},{71,7},{72,8},{73... | collective-permute-start | bytes 442376 | tf_op jit(solution)/shard_map/ppermute | solution.py:573
  290.4 16.7 %collective-permute-start.39 = (bf16[48,1536]{1,0:T(8,128)(2,1)}, bf16[48,1536]{1,0:T(8,128)(2,1)}, u32[]{:S(2)}, u32[]{:S(2)}) collective-permute-start(bf16[48,1536]{1,0:T(8,128)(2,1)} %get-tuple-element.243), channel_id=1, source_target_pairs={{64,0},{65,1},{66,2},{67,3},{68,4},{69,5},{70,6},{71,7},{72,8},{73... | collective-permute-start | bytes 442376 | tf_op jit(solution)/shard_map/ppermute | solution.py:573
  333.4 10.0 %collective-permute-start.53 = (bf16[3,96,512]{2,1,0:T(8,128)(2,1)S(1)}, bf16[3,96,512]{2,1,0:T(8,128)(2,1)S(1)}, u32[]{:S(2)}, u32[]{:S(2)}) collective-permute-start(bf16[3,96,512]{2,1,0:T(8,128)(2,1)S(1)} %get-tuple-element.305), channel_id=1, source_target_pairs={{0,4},{4,0},{8,12},{12,8},{16,20},{20,16},{24,28},{28,24},{32,36},... | collective-permute-start | bytes 884744 | tf_op jit(solution)/shard_map/ppermute | solution.py:31
  335.1 14.6 %collective-permute-start.54 = (bf16[3,96,512]{2,1,0:T(8,128)(2,1)S(1)}, bf16[3,96,512]{2,1,0:T(8,128)(2,1)S(1)}, u32[]{:S(2)}, u32[]{:S(2)}) collective-permute-start(bf16[3,96,512]{2,1,0:T(8,128)(2,1)S(1)} %get-tuple-element.312), channel_id=1, source_target_pairs={{0,4},{4,0},{8,12},{12,8},{16,20},{20,16},{24,28},{28,24},{32,36},... | collective-permute-start | bytes 884744 | tf_op jit(solution)/shard_map/ppermute | solution.py:31
  335.5 20.6 %collective-permute-start.55 = (bf16[3,96,512]{2,1,0:T(8,128)(2,1)S(1)}, bf16[3,96,512]{2,1,0:T(8,128)(2,1)S(1)}, u32[]{:S(2)}, u32[]{:S(2)}) collective-permute-start(bf16[3,96,512]{2,1,0:T(8,128)(2,1)S(1)} %get-tuple-element.311), channel_id=1, source_target_pairs={{0,4},{4,0},{8,12},{12,8},{16,20},{20,16},{24,28},{28,24},{32,36},... | collective-permute-start | bytes 884744 | tf_op jit(solution)/shard_map/ppermute | solution.py:31
  337.2 24.6 %collective-permute-start.57 = (bf16[3,96,512]{2,1,0:T(8,128)(2,1)S(1)}, bf16[3,96,512]{2,1,0:T(8,128)(2,1)S(1)}, u32[]{:S(2)}, u32[]{:S(2)}) collective-permute-start(bf16[3,96,512]{2,1,0:T(8,128)(2,1)S(1)} %get-tuple-element.310), channel_id=1, source_target_pairs={{0,4},{4,0},{8,12},{12,8},{16,20},{20,16},{24,28},{28,24},{32,36},... | collective-permute-start | bytes 884744 | tf_op jit(solution)/shard_map/ppermute | solution.py:31
  337.5 27.4 %collective-permute-start.61 = (bf16[3,96,512]{2,1,0:T(8,128)(2,1)S(1)}, bf16[3,96,512]{2,1,0:T(8,128)(2,1)S(1)}, u32[]{:S(2)}, u32[]{:S(2)}) collective-permute-start(bf16[3,96,512]{2,1,0:T(8,128)(2,1)S(1)} %get-tuple-element.309), channel_id=1, source_target_pairs={{0,4},{4,0},{8,12},{12,8},{16,20},{20,16},{24,28},{28,24},{32,36},... | collective-permute-start | bytes 884744 | tf_op jit(solution)/shard_map/ppermute | solution.py:31
  343.4 24.7 %collective-permute-start.62 = (bf16[3,96,512]{2,1,0:T(8,128)(2,1)S(1)}, bf16[3,96,512]{2,1,0:T(8,128)(2,1)S(1)}, u32[]{:S(2)}, u32[]{:S(2)}) collective-permute-start(bf16[3,96,512]{2,1,0:T(8,128)(2,1)S(1)} %get-tuple-element.308), channel_id=1, source_target_pairs={{0,4},{4,0},{8,12},{12,8},{16,20},{20,16},{24,28},{28,24},{32,36},... | collective-permute-start | bytes 884744 | tf_op jit(solution)/shard_map/ppermute | solution.py:31
  349.7 21.5 %collective-permute-start.63 = (bf16[3,96,512]{2,1,0:T(8,128)(2,1)S(1)}, bf16[3,96,512]{2,1,0:T(8,128)(2,1)S(1)}, u32[]{:S(2)}, u32[]{:S(2)}) collective-permute-start(bf16[3,96,512]{2,1,0:T(8,128)(2,1)S(1)} %get-tuple-element.307), channel_id=1, source_target_pairs={{0,4},{4,0},{8,12},{12,8},{16,20},{20,16},{24,28},{28,24},{32,36},... | collective-permute-start | bytes 884744 | tf_op jit(solution)/shard_map/ppermute | solution.py:31
  356.0 18.4 %collective-permute-start.64 = (bf16[3,96,512]{2,1,0:T(8,128)(2,1)S(1)}, bf16[3,96,512]{2,1,0:T(8,128)(2,1)S(1)}, u32[]{:S(2)}, u32[]{:S(2)}) collective-permute-start(bf16[3,96,512]{2,1,0:T(8,128)(2,1)S(1)} %get-tuple-element.306), channel_id=1, source_target_pairs={{0,4},{4,0},{8,12},{12,8},{16,20},{20,16},{24,28},{28,24},{32,36},... | collective-permute-start | bytes 884744 | tf_op jit(solution)/shard_map/ppermute | solution.py:31
  361.8 16.2 %collective-permute-start.56 = (bf16[3,96,512]{2,1,0:T(8,128)(2,1)S(1)}, bf16[3,96,512]{2,1,0:T(8,128)(2,1)S(1)}, u32[]{:S(2)}, u32[]{:S(2)}) collective-permute-start(bf16[3,96,512]{2,1,0:T(8,128)(2,1)S(1)} %slice.442), channel_id=1, source_target_pairs={{0,8},{4,12},{8,16},{12,20},{16,24},{20,28},{24,32},{28,36},{32,40... | collective-permute-start | bytes 884744 | tf_op jit(solution)/shard_map/ppermute | solution.py:26
  375.3 10.8 %collective-permute-start.65 = (bf16[4,96,512]{2,1,0:T(8,128)(2,1)S(1)}, bf16[4,96,512]{2,1,0:T(8,128)(2,1)S(1)}, u32[]{:S(2)}, u32[]{:S(2)}) collective-permute-start(bf16[4,96,512]{2,1,0:T(8,128)(2,1)S(1)} %pad_maximum_fusion.5), channel_id=1, source_target_pairs={{0,56},{4,60},{8,0},{12,4},{16,8},{20,12},{24,16},{28,20},{32,24},... | collective-permute-start | bytes 1179656 | tf_op jit(solution)/shard_map/ppermute | solution.py:26
  379.0 22.8 %collective-permute-start.58 = (bf16[7,96,512]{2,1,0:T(8,128)(2,1)}, bf16[7,96,512]{2,1,0:T(8,128)(2,1)}, u32[]{:S(2)}, u32[]{:S(2)}) collective-permute-start(bf16[7,96,512]{2,1,0:T(8,128)(2,1)} %fusion.6), channel_id=1, source_target_pairs={{0,8},{4,12},{8,16},{12,20},{16,24},{20,28},{24,32},{28,36},{32,40... | collective-permute-start | bytes 2064392 | tf_op jit(solution)/shard_map/ppermute | solution.py:26
  387.1 35.3 %collective-permute-start.66 = (bf16[7,96,512]{2,1,0:T(8,128)(2,1)}, bf16[7,96,512]{2,1,0:T(8,128)(2,1)}, u32[]{:S(2)}, u32[]{:S(2)}) collective-permute-start(bf16[7,96,512]{2,1,0:T(8,128)(2,1)} %pad_maximum_fusion.3), channel_id=1, source_target_pairs={{0,56},{4,60},{8,0},{12,4},{16,8},{20,12},{24,16},{28,20},{32,24},... | collective-permute-start | bytes 2064392 | tf_op jit(solution)/shard_map/ppermute | solution.py:26
  403.9 33.0 %collective-permute-start.59 = (bf16[7,96,512]{2,1,0:T(8,128)(2,1)}, bf16[7,96,512]{2,1,0:T(8,128)(2,1)}, u32[]{:S(2)}, u32[]{:S(2)}) collective-permute-start(bf16[7,96,512]{2,1,0:T(8,128)(2,1)} %add_convert_fusion.3), channel_id=1, source_target_pairs={{0,8},{4,12},{8,16},{12,20},{16,24},{20,28},{24,32},{28,36},{32,40... | collective-permute-start | bytes 2064392 | tf_op jit(solution)/shard_map/ppermute | solution.py:26
  405.5 8.4 %collective-permute-start.77 = (f32[33,384]{1,0:T(8,128)S(1)}, f32[33,384]{1,0:T(8,128)S(1)}, u32[]{:S(2)}, u32[]{:S(2)}) collective-permute-start(f32[33,384]{1,0:T(8,128)S(1)} %add.606), channel_id=1, source_target_pairs={{0,8},{4,12},{8,0},{12,4},{16,24},{20,28},{24,16},{28,20},{32,40},... | collective-permute-start | bytes 152072 | tf_op jit(solution)/shard_map/ppermute | solution.py:31
  419.1 9.2 %collective-permute-start.79 = (f32[33,384]{1,0:T(8,128)S(1)}, f32[33,384]{1,0:T(8,128)S(1)}, u32[]{:S(2)}, u32[]{:S(2)}) collective-permute-start(f32[33,384]{1,0:T(8,128)S(1)} %add.608), channel_id=1, source_target_pairs={{0,32},{4,36},{8,40},{12,44},{16,48},{20,52},{24,56},{28,60},{32,0... | collective-permute-start | bytes 152072 | tf_op jit(solution)/shard_map/ppermute | solution.py:31
  424.6 20.7 %collective-permute-start.67 = (bf16[7,96,512]{2,1,0:T(8,128)(2,1)}, bf16[7,96,512]{2,1,0:T(8,128)(2,1)S(1)}, u32[]{:S(2)}, u32[]{:S(2)}) collective-permute-start(bf16[7,96,512]{2,1,0:T(8,128)(2,1)} %add_convert_fusion.1), channel_id=1, source_target_pairs={{0,56},{4,60},{8,0},{12,4},{16,8},{20,12},{24,16},{28,20},{32,24},... | collective-permute-start | bytes 2064392 | tf_op jit(solution)/shard_map/ppermute | solution.py:26
  439.0 22.7 %collective-permute-start.60 = (bf16[7,96,512]{2,1,0:T(8,128)(2,1)}, bf16[7,96,512]{2,1,0:T(8,128)(2,1)S(1)}, u32[]{:S(2)}, u32[]{:S(2)}) collective-permute-start(bf16[7,96,512]{2,1,0:T(8,128)(2,1)} %add_convert_fusion.2), channel_id=1, source_target_pairs={{0,8},{4,12},{8,16},{12,20},{16,24},{20,28},{24,32},{28,36},{32,40... | collective-permute-start | bytes 2064392 | tf_op jit(solution)/shard_map/ppermute | solution.py:26
  441.8 12.7 %collective-permute-start.41 = (bf16[1,96,512]{2,1,0:T(8,128)(2,1)S(1)}, bf16[1,96,512]{2,1,0:T(8,128)(2,1)S(1)}, u32[]{:S(2)}, u32[]{:S(2)}) collective-permute-start(bf16[1,96,512]{2,1,0:T(8,128)(2,1)S(1)} %get-tuple-element.325), channel_id=1, source_target_pairs={{0,8},{4,12},{8,16},{12,20},{16,24},{20,28},{24,32},{28,36},{32,40... | collective-permute-start | bytes 294920 | tf_op jit(solution)/shard_map/ppermute | solution.py:26
  443.0 11.5 %collective-permute-start.45 = (bf16[1,96,512]{2,1,0:T(8,128)(2,1)S(1)}, bf16[1,96,512]{2,1,0:T(8,128)(2,1)S(1)}, u32[]{:S(2)}, u32[]{:S(2)}) collective-permute-start(bf16[1,96,512]{2,1,0:T(8,128)(2,1)S(1)} %get-tuple-element.327), channel_id=1, source_target_pairs={{0,56},{4,60},{8,0},{12,4},{16,8},{20,12},{24,16},{28,20},{32,24},... | collective-permute-start | bytes 294920 | tf_op jit(solution)/shard_map/ppermute | solution.py:26
  445.5 16.3 %collective-permute-start.68 = (bf16[7,96,512]{2,1,0:T(8,128)(2,1)S(1)}, bf16[7,96,512]{2,1,0:T(8,128)(2,1)S(1)}, u32[]{:S(2)}, u32[]{:S(2)}) collective-permute-start(bf16[7,96,512]{2,1,0:T(8,128)(2,1)S(1)} %add_convert_fusion), channel_id=1, source_target_pairs={{0,56},{4,60},{8,0},{12,4},{16,8},{20,12},{24,16},{28,20},{32,24},... | collective-permute-start | bytes 2064392 | tf_op jit(solution)/shard_map/ppermute | solution.py:26
  454.6 7.0 %collective-permute-start.42 = (bf16[2,96,512]{2,1,0:T(8,128)(2,1)S(1)}, bf16[2,96,512]{2,1,0:T(8,128)(2,1)S(1)}, u32[]{:S(2)}, u32[]{:S(2)}) collective-permute-start(bf16[2,96,512]{2,1,0:T(8,128)(2,1)S(1)} %pad_maximum_fusion.14), channel_id=1, source_target_pairs={{0,8},{4,12},{8,16},{12,20},{16,24},{20,28},{24,32},{28,36},{32,40... | collective-permute-start | bytes 589832 | tf_op jit(solution)/shard_map/ppermute | solution.py:26
  455.1 7.0 %collective-permute-start.46 = (bf16[2,96,512]{2,1,0:T(8,128)(2,1)S(1)}, bf16[2,96,512]{2,1,0:T(8,128)(2,1)S(1)}, u32[]{:S(2)}, u32[]{:S(2)}) collective-permute-start(bf16[2,96,512]{2,1,0:T(8,128)(2,1)S(1)} %pad_maximum_fusion.15), channel_id=1, source_target_pairs={{0,56},{4,60},{8,0},{12,4},{16,8},{20,12},{24,16},{28,20},{32,24},... | collective-permute-start | bytes 589832 | tf_op jit(solution)/shard_map/ppermute | solution.py:26
  461.6 7.0 %collective-permute-start.43 = (bf16[2,96,512]{2,1,0:T(8,128)(2,1)S(1)}, bf16[2,96,512]{2,1,0:T(8,128)(2,1)S(1)}, u32[]{:S(2)}, u32[]{:S(2)}) collective-permute-start(bf16[2,96,512]{2,1,0:T(8,128)(2,1)S(1)} %fusion.25), channel_id=1, source_target_pairs={{0,8},{4,12},{8,16},{12,20},{16,24},{20,28},{24,32},{28,36},{32,40... | collective-permute-start | bytes 589832 | tf_op jit(solution)/shard_map/ppermute | solution.py:26
  468.8 7.0 %collective-permute-start.69 = (bf16[2,96,512]{2,1,0:T(8,128)(2,1)S(1)}, bf16[2,96,512]{2,1,0:T(8,128)(2,1)S(1)}, u32[]{:S(2)}, u32[]{:S(2)}) collective-permute-start(bf16[2,96,512]{2,1,0:T(8,128)(2,1)S(1)} %fusion.30), channel_id=1, source_target_pairs={{0,4},{4,0},{8,12},{12,8},{16,20},{20,16},{24,28},{28,24},{32,36},... | collective-permute-start | bytes 589832 | tf_op jit(solution)/shard_map/ppermute | solution.py:31
  469.6 11.6 %collective-permute-start.44 = (bf16[2,96,512]{2,1,0:T(8,128)(2,1)S(1)}, bf16[2,96,512]{2,1,0:T(8,128)(2,1)S(1)}, u32[]{:S(2)}, u32[]{:S(2)}) collective-permute-start(bf16[2,96,512]{2,1,0:T(8,128)(2,1)S(1)} %get-tuple-element.321), channel_id=1, source_target_pairs={{0,8},{4,12},{8,16},{12,20},{16,24},{20,28},{24,32},{28,36},{32,40... | collective-permute-start | bytes 589832 | tf_op jit(solution)/shard_map/ppermute | solution.py:26
  474.5 6.7 %collective-permute-start.48 = (bf16[2,96,512]{2,1,0:T(8,128)(2,1)S(1)}, bf16[2,96,512]{2,1,0:T(8,128)(2,1)S(1)}, u32[]{:S(2)}, u32[]{:S(2)}) collective-permute-start(bf16[2,96,512]{2,1,0:T(8,128)(2,1)S(1)} %fusion.24), channel_id=1, source_target_pairs={{0,56},{4,60},{8,0},{12,4},{16,8},{20,12},{24,16},{28,20},{32,24},... | collective-permute-start | bytes 589832 | tf_op jit(solution)/shard_map/ppermute | solution.py:26
  476.0 12.2 %collective-permute-start.70 = (bf16[5,96,512]{2,1,0:T(8,128)(2,1)S(1)}, bf16[5,96,512]{2,1,0:T(8,128)(2,1)S(1)}, u32[]{:S(2)}, u32[]{:S(2)}) collective-permute-start(bf16[5,96,512]{2,1,0:T(8,128)(2,1)S(1)} %pad_maximum_fusion.4), channel_id=1, source_target_pairs={{0,2},{1,3},{2,0},{3,1},{4,6},{5,7},{6,4},{7,5},{8,10},{9,11},{10,... | collective-permute-start | bytes 1474568 | tf_op jit(solution)/shard_map/ppermute | solution.py:26
  478.0 13.6 %collective-permute-start.71 = (bf16[5,96,512]{2,1,0:T(8,128)(2,1)S(1)}, bf16[5,96,512]{2,1,0:T(8,128)(2,1)S(1)}, u32[]{:S(2)}, u32[]{:S(2)}) collective-permute-start(bf16[5,96,512]{2,1,0:T(8,128)(2,1)S(1)} %pad_maximum_fusion.4), channel_id=1, source_target_pairs={{0,1},{1,2},{2,3},{3,0},{4,5},{5,6},{6,7},{7,4},{8,9},{9,10},{10,1... | collective-permute-start | bytes 1474568 | tf_op jit(solution)/shard_map/ppermute | solution.py:26
  479.6 12.1 %collective-permute-start.72 = (bf16[5,96,512]{2,1,0:T(8,128)(2,1)S(1)}, bf16[5,96,512]{2,1,0:T(8,128)(2,1)S(1)}, u32[]{:S(2)}, u32[]{:S(2)}) collective-permute-start(bf16[5,96,512]{2,1,0:T(8,128)(2,1)S(1)} %pad_maximum_fusion.4), channel_id=1, source_target_pairs={{0,3},{1,0},{2,1},{3,2},{4,7},{5,4},{6,5},{7,6},{8,11},{9,8},{10,9... | collective-permute-start | bytes 1474568 | tf_op jit(solution)/shard_map/ppermute | solution.py:26
  486.1 6.6 %collective-permute-start.52 = (bf16[96,512]{1,0:T(8,128)(2,1)S(1)}, bf16[96,512]{1,0:T(8,128)(2,1)S(1)}, u32[]{:S(2)}, u32[]{:S(2)}) collective-permute-start(bf16[96,512]{1,0:T(8,128)(2,1)S(1)} %bitcast.399), channel_id=1, source_target_pairs={{0,3},{1,0},{2,1},{3,2},{4,7},{5,4},{6,5},{7,6},{8,11},{9,8},{10,9... | collective-permute-start | bytes 294920 | tf_op jit(solution)/shard_map/ppermute | solution.py:26
  487.9 6.9 %collective-permute-start.50 = (bf16[96,512]{1,0:T(8,128)(2,1)S(1)}, bf16[96,512]{1,0:T(8,128)(2,1)S(1)}, u32[]{:S(2)}, u32[]{:S(2)}) collective-permute-start(bf16[96,512]{1,0:T(8,128)(2,1)S(1)} %bitcast.400), channel_id=1, source_target_pairs={{0,1},{1,2},{2,3},{3,0},{4,5},{5,6},{6,7},{7,4},{8,9},{9,10},{10,1... | collective-permute-start | bytes 294920 | tf_op jit(solution)/shard_map/ppermute | solution.py:26
  488.2 6.5 %collective-permute-start.51 = (bf16[96,512]{1,0:T(8,128)(2,1)S(1)}, bf16[96,512]{1,0:T(8,128)(2,1)S(1)}, u32[]{:S(2)}, u32[]{:S(2)}) collective-permute-start(bf16[96,512]{1,0:T(8,128)(2,1)S(1)} %bitcast.401), channel_id=1, source_target_pairs={{0,2},{1,3},{2,0},{3,1},{4,6},{5,7},{6,4},{7,5},{8,10},{9,11},{10,... | collective-permute-start | bytes 294920 | tf_op jit(solution)/shard_map/ppermute | solution.py:26
  (36 other events, 165.8 us)
Sparse Core Ops, SparseCore 0:
  49.2 69.2 all-gather.1
  327.8 65.7 reduce-scatter.1

commit v5 on v4

--- a/solution.py
+++ b/solution.py
@@ -17,6 +17,9 @@
 PARAM_ROWS = 48
 SKEW = 2
 IN_PARTS = 6
+SMALL_A = 0
+SMALL_B = 8
+LARGEST = 3.0e38
 VMEM_LIMIT = 64 * 1024 * 1024 - 64 * 1024
 PAIR = 2
 
@@ -38,6 +41,11 @@
 
 def pick(stacked, index, axis=0):
     return lax.dynamic_index_in_dim(stacked, index, axis, keepdims=False)
+
+
+def after(x):
+    value = jnp.abs(x.reshape(-1)[0].astype(jnp.float32))
+    return jnp.where(value <= LARGEST, 0, 1).astype(jnp.int32)
 
 
 def column_parts(x, width):
@@ -103,11 +111,12 @@
     return shared, whole.reshape(rest, depth, width), out.reshape(out_parts, depth, width)
 
 
-def ring_scatter(term_at, far_split):
+def ring_scatter(term_at, far_split, prepare=lambda hop, tie: None):
     ring = lax.axis_size("fsdp") // PAIR
     half = ring // 2
     far = term_at(half)
     kind = far.dtype
+    prepare(half - 1, far)
     up = rotate(far[:far_split], "fsdp", PAIR).astype(jnp.float32)
     down = rotate(far[far_split:], "fsdp", -PAIR).astype(jnp.float32)
     for hop in range(half - 1, 0, -1):
@@ -119,8 +128,11 @@
         else:
             up = mine_up + up
             down = mine_down + down
-        up = rotate(up.astype(kind), "fsdp", PAIR).astype(jnp.float32)
-        down = rotate(down.astype(kind), "fsdp", -PAIR).astype(jnp.float32)
+        up = up.astype(kind)
+        down = down.astype(kind)
+        prepare(hop - 1, up)
+        up = rotate(up, "fsdp", PAIR).astype(jnp.float32)
+        down = rotate(down, "fsdp", -PAIR).astype(jnp.float32)
     return term_at(0).astype(jnp.float32) + up + down
 
 
@@ -147,19 +159,23 @@
     return (own + far) + (left + right)
 
 
-def sum_small(small):
+def small_steps(small):
     quarters = lax.axis_size("batch")
     here = lax.axis_index("batch")
     width = small.shape[1] // quarters
     pieces = jnp.stack(column_parts(small, width))
+    tie = yield None
     mine = pick(pieces, here)
     for by in range(1, quarters):
-        mine = mine + rotate(pick(pieces, (here + by) % quarters), "batch", by)
+        mine = mine + rotate(pick(pieces, (here + by) % quarters + tie), "batch", by)
     bit = 1
     while bit < lax.axis_size("fsdp"):
-        mine = mine + swap_bit(mine, bit)
+        tie = yield None
+        mine = mine + swap_bit(mine + tie.astype(jnp.float32), bit)
         bit *= 2
-    return jnp.concatenate(batch_order(batch_copies(mine)), axis=1)
+    tie = yield None
+    mine = mine + tie.astype(jnp.float32)
+    yield jnp.concatenate(batch_order(batch_copies(mine)), axis=1)
 
 
 def reduce_weights(shared, rest, out, small, scale):
@@ -173,23 +189,39 @@
     rest_pairs = rest.reshape((-1,) + split)
     out_pairs = out.reshape((-1,) + split)
     rest_parts, out_parts = rest_pairs.shape[0], out_pairs.shape[0]
-    small_total = scale * sum_small(small)
+    steps = small_steps(small)
+    next(steps)
+    given = {}
 
     def out_for(offset, where):
         spot = pick(out_pairs, (at + offset) % ring, 1)
         return pick(spot, where, 1)
 
+    def exchange(offsets, tie):
+        theirs = jnp.concatenate([out_for(offset + tie, 1 - side) for offset in offsets])
+        arrived = swap_bit(theirs, 1)
+        for number, offset in enumerate(offsets):
+            given[offset] = arrived[number * out_parts : (number + 1) * out_parts]
+
     def main_term(offset):
         pair = pick(rest_pairs, (at + offset) % ring, 1).reshape(-1, rows, width)
-        given = swap_bit(out_for(offset, 1 - side), 1).astype(jnp.float32)
-        own = (out_for(offset, side).astype(jnp.float32) + given).astype(kind)
+        extra = given[offset].astype(jnp.float32)
+        own = (out_for(offset, side).astype(jnp.float32) + extra).astype(kind)
         return jnp.concatenate([pair, own])
 
-    total = ring_scatter(main_term, (rest_parts * PAIR + out_parts) // 2)
+    def prepare(hop, ready):
+        tie = after(ready)
+        exchange([hop, ring - hop] if hop else [0], tie)
+        steps.send(tie)
+
+    exchange([ring // 2], 0)
+    total = ring_scatter(main_term, (rest_parts * PAIR + out_parts) // 2, prepare)
+    steps.send(after(total))
     rest_share = keep_side(
         total[: rest_parts * PAIR].reshape(rest_parts, PAIR, rows, width), kind
     )
     share = jnp.concatenate([rest_share, total[rest_parts * PAIR :]]).astype(kind)
+    small_total = scale * steps.send(after(share))
     share = sum_batch(share)
     shared_total = ring_scatter(lambda offset: pick(shared_sum, (at + offset) % ring), 1)
     shared_share = keep_side(shared_total[None], kind)[0].astype(kind)
@@ -367,12 +399,12 @@
     x_all, value_all, gate_all, mid_all, inv_all, *refs, taps, length, width, aliased
 ):
     refs = refs[aliased:]
-    outgoing, input_all, grad_all, up_all, small_all = refs[:5]
+    outgoing, input_all, grad_all, up_all, small_all, conv_all = refs[:6]
     (
         u_v, w_in_v, w_out_v, params_v, x_v, value_v, gate_v, mid_v, inv_v,
-        padded, shifts, padded_grad, shifts_grad, conv_v, grad_v, small_v, out_v,
+        padded_grad, shifts_grad, conv_v, grad_v, small_v, out_v,
         in_sems, out_sems,
-    ) = refs[5:]
+    ) = refs[6:]
     slot, active, first, valid = info[0], info[1], info[2], info[3]
     parts = w_in_v.shape[0]
     half = taps // 2
@@ -412,14 +444,12 @@
             copy.start()
             saves.append(copy)
 
-        clear_margins(padded, length)
         clear_margins(padded_grad, length)
+        small_v[...] = jnp.zeros_like(small_v)
         for copy in loads:
             copy.wait()
         rows = lax.broadcasted_iota(jnp.int32, (length, width), 0)
         mask = (rows < valid).astype(jnp.float32)
-        padded[pl.ds(MARGIN, length), :] = value_v[...] * gate_v[...] * mask
-        write_shifts(shifts, padded)
         u_copy.wait()
         save(u_v, up_all.at[slot])
         w_out_copy.wait()
@@ -438,9 +468,10 @@
         scaled_grad = swish_grad * (
             sigmoid_mid + scaled_mid * sigmoid_mid * (1.0 - sigmoid_mid)
         )
-        small_v[pl.ds(GAIN_B, 1), :] = jnp.sum(scaled_grad * normed_mid, axis=0, keepdims=True)
+        small_v[pl.ds(SMALL_B, 1), :] = jnp.sum(scaled_grad * normed_mid, axis=0, keepdims=True)
         conv_grad = norm_grad(scaled_grad * gain_b, normed_mid, inv_v[:, :1])
         padded_grad[pl.ds(MARGIN, length), :] = conv_grad
+        save(padded_grad.at[pl.ds(MARGIN, length), :], conv_all.at[slot])
         write_shifts(shifts_grad, padded_grad)
 
         def convolve(lanes):
@@ -452,13 +483,6 @@
 
         each_lane_block(width, convolve)
 
-        def correlate(lanes):
-            given = padded_grad[pl.ds(MARGIN, length), lanes]
-            for tap in range(taps):
-                product = given * shifted(shifts, tap + MARGIN - half, length, lanes)
-                small_v[pl.ds(tap, 1), lanes] = jnp.sum(product, axis=0, keepdims=True)
-
-        each_lane_block(width, correlate)
         gated_grad = conv_v[...] * mask
         glu_gate = gate_v[...]
         grad_v[:, :width] = (gated_grad * glu_gate).astype(jnp.bfloat16)
@@ -475,7 +499,7 @@
         each_block(2 * width, part_width, into_input)
         input_side = conv_v[...]
         normed_in, inv_in = layer_stats(x_v[...].astype(jnp.float32))
-        small_v[pl.ds(GAIN_A, 1), :] = jnp.sum(input_side * normed_in, axis=0, keepdims=True)
+        small_v[pl.ds(SMALL_A, 1), :] = jnp.sum(input_side * normed_in, axis=0, keepdims=True)
         save(small_v, small_all.at[slot])
         gain_a = params_v[pl.ds(GAIN_A, 1), :]
         out_v[...] = (
@@ -485,6 +509,54 @@
         save(out_v, input_all.at[slot])
         for copy in saves:
             copy.wait()
+
+
+def taps_kernel(valid, grads, values, gates, out, padded, shifts, *, taps, length, width):
+    micro = pl.program_id(0)
+
+    @pl.when(micro == 0)
+    def clear():
+        out[...] = jnp.zeros_like(out)
+        clear_margins(padded, length)
+
+    rows = lax.broadcasted_iota(jnp.int32, (length, width), 0)
+    mask = (rows < valid[micro]).astype(jnp.float32)
+    padded[pl.ds(MARGIN, length), :] = values[0] * gates[0] * mask
+    write_shifts(shifts, padded)
+
+    def correlate(lanes):
+        given = grads[0, :, lanes]
+        for tap in range(taps):
+            product = given * shifted(shifts, tap + MARGIN - taps // 2, length, lanes)
+            out[pl.ds(tap, 1), lanes] += jnp.sum(product, axis=0, keepdims=True)
+
+    each_lane_block(width, correlate)
+
+
+def taps_sums(valid, grads, values, gates, taps):
+    micro, length, width = grads.shape
+    span = length + 2 * MARGIN
+    block = pl.BlockSpec((1, length, width), lambda index, valid: (index, 0, 0))
+    return pl.pallas_call(
+        functools.partial(taps_kernel, taps=taps, length=length, width=width),
+        grid_spec=pltpu.PrefetchScalarGridSpec(
+            num_scalar_prefetch=1,
+            grid=(micro,),
+            in_specs=[block] * 3,
+            out_specs=pl.BlockSpec((GAIN_A, width), lambda index, valid: (0, 0)),
+            scratch_shapes=[
+                pltpu.VMEM((span, width), jnp.float32),
+                pltpu.VMEM((SUBLANES, span - SUBLANES, width), jnp.float32),
+            ],
+        ),
+        out_shape=jax.ShapeDtypeStruct((GAIN_A, width), jnp.float32),
+        compiler_params=pltpu.CompilerParams(vmem_limit_bytes=32 * 1024 * 1024),
+        cost_estimate=pl.CostEstimate(
+            flops=2 * taps * micro * length * width,
+            transcendentals=0,
+            bytes_accessed=12 * micro * length * width,
+        ),
+    )(valid, grads, values, gates)
 
 
 def stage_call(kernel, scratch, info, inputs, out_shapes, buffers, taps, length, width, cost, sems):
@@ -550,7 +622,7 @@
     outs = [
         shape((length, width), bf16), shape((micro, length, width), bf16),
         shape((micro, length, 2 * width), bf16), shape((micro, length, width), bf16),
-        shape((micro,) + params.shape, f32),
+        shape((micro, 2 * SUBLANES, width), f32), shape((micro, length, width), f32),
     ]
     rows = functools.partial(pltpu.VMEM, (length, width))
     span = length + 2 * MARGIN
@@ -558,13 +630,13 @@
     scratch = [
         rows(bf16), pltpu.VMEM((IN_PARTS,) + weights[2].shape[1:], bf16), pltpu.VMEM(weights[2].shape, bf16),
         pltpu.VMEM(params.shape, f32), rows(bf16), rows(f32), rows(f32), rows(f32),
-        pltpu.VMEM((length, LANES), f32), pltpu.VMEM((span, width), f32), lifted,
-        pltpu.VMEM((span, width), f32), lifted, rows(f32),
-        pltpu.VMEM((length, 2 * width), bf16), pltpu.VMEM(params.shape, f32), rows(bf16),
+        pltpu.VMEM((length, LANES), f32), pltpu.VMEM((span, width), f32), lifted, rows(f32),
+        pltpu.VMEM((length, 2 * width), bf16), pltpu.VMEM((2 * SUBLANES, width), f32),
+        rows(bf16),
     ]
     return stage_call(
         backward_kernel, scratch, info, (incoming, cotangent, *weights, params) + tuple(saved),
-        outs, buffers, taps, length, width, stage_cost(length, width), (8 + IN_PARTS, 5),
+        outs, buffers, taps, length, width, stage_cost(length, width), (8 + IN_PARTS, 6),
     )
 
 
@@ -631,7 +703,7 @@
             grads, taps,
         )
         pending.append(send_active(outgoing, active_at(slot, True), -1))
-    input_all, grad_all, up_all, small_all = grads
+    input_all, grad_all, up_all, small_all, conv_all = grads
     total_rows = micro_count * frames_len
     width = weights[2].shape[2]
     quarters = weights[0].shape[0]
@@ -654,11 +726,12 @@
     rest_terms = terms(proj_rows, grad_rows, range(quarters, IN_PARTS))
     out_terms = terms(swish_rows, upstream_rows, range(weights[2].shape[0]))
     small_rows = jnp.sum(small_all, axis=0)
+    tap_rows = taps_sums(lengths[:, 0], conv_all, value_all, gate_all, taps)
     small = jnp.concatenate(
         [
-            small_rows[GAIN_A : GAIN_A + 1],
-            small_rows[GAIN_B : GAIN_B + 1],
-            small_rows[:taps],
+            small_rows[SMALL_A : SMALL_A + 1],
+            small_rows[SMALL_B : SMALL_B + 1],
+            tap_rows[:taps],
         ],
         axis=0,
     )

time: 514 us -> 501 us (0.975)
  the two profiles are of different devices: /device:TPU:8 before, /device:TPU:6 now
where the time goes in v5:
time: 501 us; the launch traced here: 491 us
  waiting for transfers between devices  155 us (31%)
  starting transfers between devices  119 us (24%)
  Pallas kernels  99.9 us (20%)
  local copies, waits for them, and re-layouts  53.1 us (11%)
  other arithmetic  34.8 us (7%)
  between operations  19.8 us (4%)
  matrix products  9.1 us (2%)
    pallas_call x20, Pallas kernels, stage_call(): pl.pallas_call(functools.partial(kernel, taps=taps, length=length, width=...  92.7 us
    ppermute x44, starting transfers between devices, rotate(): return lax.ppermute(x, axis, [(i, (i + by) % peers) for i in range(peers)])  71.6 us
    ppermute x44, waiting for transfers between devices, rotate(): return lax.ppermute(x, axis, [(i, (i + by) % peers) for i in range(peers)])  60.4 us
    ppermute x16, waiting for transfers between devices, send_active(): return lax.ppermute(x, 'section', pairs)  57.9 us
    ppermute x20, waiting for transfers between devices, swap_bit(): return lax.ppermute(x, 'fsdp', [(i, i ^ bit) for i in range(peers)])  37 us
    ppermute x20, starting transfers between devices, swap_bit(): return lax.ppermute(x, 'fsdp', [(i, i ^ bit) for i in range(peers)])  23.8 us
    ppermute x16, starting transfers between devices, send_active(): return lax.ppermute(x, 'section', pairs)  23.7 us
    dynamic_update_slice x15, local copies, waits for them, and re-layouts, place_out(): out = lax.dynamic_update_slice(out, piece[:, None, None], spot)  11 us
  transfers between devices with their start and end apart: 82, of which 34 were waited for; matrix products, arithmetic and copies ran while one was open for 17% of the time, Pallas kernels for 16%

profile of v5, /device:TPU:6, one launch (start us, length us, event | category | flops | bytes accessed | tf_op | source)
XLA Modules:
  0.0 491.3 jit_solution(1489871549373744223)
XLA Ops:
  10.8 7.2 %collective-permute-done = bf16[3,96,512]{2,1,0:T(8,128)(2,1)S(1)} collective-permute-done((bf16[3,96,512]{2,1,0:T(8,128)(2,1)S(1)}, bf16[3,96,512]{2,1,0:T(8,128)(2,1)S(1)}, u32[]{:S(2)}, u32[]{:S(2)}) %collective-permute-start) | collective-permute-done | bytes 294944 | tf_op jit(solution)/shard_map/ppermute | solution.py:34
  18.2 2.0 collective-permute-start.1
  20.2 4.0 collective-permute-start.2
  24.2 3.9 collective-permute-done.1
  28.2 3.2 collective-permute-start.4
  31.5 3.6 collective-permute-done.3
  35.1 3.2 collective-permute-start.6
  38.4 3.6 collective-permute-done.5
  42.1 3.4 collective-permute-start.8
  45.5 2.3 collective-permute-done.7
  52.2 3.4 concatenate.95.params
  57.0 3.5 collective-permute-start.10
  61.4 2.8 broadcast_in_dim.107
  65.7 2.0 broadcast_in_dim.106
  68.4 2.0 collective-permute-done.9
  75.4 2.3 collective-permute-start.12
  81.2 5.8 %collective-permute-done.11 = bf16[7,96,512]{2,1,0:T(8,128)(2,1)S(1)} collective-permute-done((bf16[7,96,512]{2,1,0:T(8,128)(2,1)S(1)}, bf16[7,96,512]{2,1,0:T(8,128)(2,1)S(1)}, u32[]{:S(2)}, u32[]{:S(2)}) %collective-permute-start.11) | collective-permute-done | bytes 688160 | tf_op jit(solution)/shard_map/ppermute | solution.py:29
  87.8 2.7 collective-permute-start.21
  93.1 2.3 collective-permute-start.14
  98.3 8.7 %collective-permute-done.13 = bf16[7,96,512]{2,1,0:T(8,128)(2,1)S(1)} collective-permute-done((bf16[7,96,512]{2,1,0:T(8,128)(2,1)S(1)}, bf16[7,96,512]{2,1,0:T(8,128)(2,1)S(1)}, u32[]{:S(2)}, u32[]{:S(2)}) %collective-permute-start.13) | collective-permute-done | bytes 688160 | tf_op jit(solution)/shard_map/ppermute | solution.py:29
  109.4 2.6 collective-permute-start.16
  114.4 2.1 collective-permute-done.22
  122.6 4.7 collective-permute-done.24
  128.6 8.7 %shard_map.127 = (bf16[48,1536]{1,0:T(8,128)(2,1)}, bf16[4,48,1536]{2,1,0:T(8,128)(2,1)}, bf16[4,48,1536]{2,1,0:T(8,128)(2,1)}, bf16[4,48,1536]{2,1,0:T(8,128)(2...) custom-call(s32[4]{0:T(128)} %get-tuple-element.311.info, ...), custom_call_target="tpu_custom_call" | custom-call | flops 679477248 | bytes 14155776 | tf_op jit(solution)/shard_map/pallas_call | solution.py:572
  137.3 2.0 collective-permute-start.26
  139.3 8.6 %shard_map.128 = (bf16[48,1536]{1,0:T(8,128)(2,1)}, bf16[4,48,1536]{2,1,0:T(8,128)(2,1)}, bf16[4,48,1536]{2,1,0:T(8,128)(2,1)}, bf16[4,48,1536]{2,1,0:T(8,128)(2...) custom-call(s32[4]{0:T(128)} %get-tuple-element.312.info, ...), custom_call_target="tpu_custom_call", output_to_operand_aliasing={{1}: (7, {}), {2}: (8, {}), {3}: (9, {}), {4}: (10, {}), {5... | custom-call | flops 679477248 | bytes 14155776 | tf_op jit(solution)/shard_map/pallas_call | solution.py:572
  147.9 2.0 collective-permute-start.25
  152.4 8.7 %shard_map.129 = (bf16[48,1536]{1,0:T(8,128)(2,1)}, bf16[4,48,1536]{2,1,0:T(8,128)(2,1)}, bf16[4,48,1536]{2,1,0:T(8,128)(2,1)}, bf16[4,48,1536]{2,1,0:T(8,128)(2...) custom-call(s32[4]{0:T(128)} %get-tuple-element.310.info, ...), custom_call_target="tpu_custom_call", output_to_operand_aliasing={{1}: (7, {}), {2}: (8, {}), {3}: (9, {}), {4}: (10, {}), {5... | custom-call | flops 679477248 | bytes 14155776 | tf_op jit(solution)/shard_map/pallas_call | solution.py:572
  161.0 2.0 collective-permute-start.28
  163.0 8.9 %shard_map.130 = (bf16[48,1536]{1,0:T(8,128)(2,1)}, bf16[4,48,1536]{2,1,0:T(8,128)(2,1)}, bf16[4,48,1536]{2,1,0:T(8,128)(2,1)}, bf16[4,48,1536]{2,1,0:T(8,128)(2...) custom-call(s32[4]{0:T(128)} %get-tuple-element.313.info, ...), custom_call_target="tpu_custom_call", output_to_operand_aliasing={{1}: (7, {}), {2}: (8, {}), {3}: (9, {}), {4}: (10, {}), {5... | custom-call | flops 679477248 | bytes 14155776 | tf_op jit(solution)/shard_map/pallas_call | solution.py:572
  171.9 2.0 collective-permute-start.27
  202.8 54.8 %collective-permute-done.38.incoming = bf16[48,1536]{1,0:T(8,128)(2,1)} collective-permute-done((bf16[48,1536]{1,0:T(8,128)(2,1)}, bf16[48,1536]{1,0:T(8,128)(2,1)}, u32[]{:S(2)}, u32[]{:S(2)}) %collective-permute-start.38) | collective-permute-done | bytes 147488 | tf_op jit(solution)/shard_map/ppermute | solution.py:645
  257.6 11.8 %shard_map.143 = (bf16[48,1536]{1,0:T(8,128)(2,1)}, bf16[4,48,1536]{2,1,0:T(8,128)(2,1)}, bf16[4,48,3072]{2,1,0:T(8,128)(2,1)}, bf16[4,48,1536]{2,1,0:T(8,128)(2...) custom-call(s32[4]{0:T(128)} %get-tuple-element.298.info, ...), custom_call_target="tpu_custom_call", output_to_operand_aliasing={{1}: (12, {}), {2}: (13, {}), {3}: (14, {}), {4}: (15, {}),... | custom-call | flops 679477248 | bytes 14155776 | tf_op jit(solution)/shard_map/pallas_call | solution.py:572
  271.8 11.8 %shard_map.144 = (bf16[48,1536]{1,0:T(8,128)(2,1)}, bf16[4,48,1536]{2,1,0:T(8,128)(2,1)}, bf16[4,48,3072]{2,1,0:T(8,128)(2,1)}, bf16[4,48,1536]{2,1,0:T(8,128)(2...) custom-call(s32[4]{0:T(128)} %get-tuple-element.305.info, ...), custom_call_target="tpu_custom_call", output_to_operand_aliasing={{1}: (12, {}), {2}: (13, {}), {3}: (14, {}), {4}: (15, {}),... | custom-call | flops 679477248 | bytes 14155776 | tf_op jit(solution)/shard_map/pallas_call | solution.py:572
  284.9 11.8 %shard_map.145 = (bf16[48,1536]{1,0:T(8,128)(2,1)}, bf16[4,48,1536]{2,1,0:T(8,128)(2,1)}, bf16[4,48,3072]{2,1,0:T(8,128)(2,1)}, bf16[4,48,1536]{2,1,0:T(8,128)(2...) custom-call(s32[4]{0:T(128)} %get-tuple-element.297.info, ...), custom_call_target="tpu_custom_call", output_to_operand_aliasing={{1}: (12, {}), {2}: (13, {}), {3}: (14, {}), {4}: (15, {}),... | custom-call | flops 679477248 | bytes 14155776 | tf_op jit(solution)/shard_map/pallas_call | solution.py:572
  296.7 2.0 collective-permute-done.39.incoming
  298.7 12.0 %shard_map.146 = (bf16[48,1536]{1,0:T(8,128)(2,1)}, bf16[4,48,1536]{2,1,0:T(8,128)(2,1)}, bf16[4,48,3072]{2,1,0:T(8,128)(2,1)}, bf16[4,48,1536]{2,1,0:T(8,128)(2...) custom-call(s32[4]{0:T(128)} %get-tuple-element.306.info, ...), custom_call_target="tpu_custom_call", output_to_operand_aliasing={{1}: (12, {}), {2}: (13, {}), {3}: (14, {}), {4}: (15, {}),... | custom-call | flops 679477248 | bytes 14155776 | tf_op jit(solution)/shard_map/pallas_call | solution.py:572
  314.4 3.2 pad_maximum_fusion
  326.2 3.5 fusion.13
  338.4 7.3 %shard_map.147 = f32[32,1536]{1,0:T(8,128)S(1)} custom-call(s32[4]{0:T(128)S(1)} %bitcast.346, f32[4,48,1536]{2,1,0:T(8,128)S(1)} %copy-done.4, f32[4,48,1536]{2,1,0:T(8,128)S(1)} %copy-done.2, f32[4,48,1536]{2,1,0:T(8,128)S(1)} %copy-done.3), custom_call_target="tpu_custom_call" | custom-call | flops 18284544 | bytes 3538944 | tf_op jit(solution)/shard_map/pallas_call | solution.py:540
  347.2 2.3 collective-permute-start.62
  361.0 3.7 collective-permute-start.63
  364.7 5.2 %collective-permute-done.56 = bf16[6,96,512]{2,1,0:T(8,128)(2,1)} collective-permute-done((bf16[6,96,512]{2,1,0:T(8,128)(2,1)}, bf16[6,96,512]{2,1,0:T(8,128)(2,1)}, u32[]{:S(2)}, u32[]{:S(2)}) %collective-permute-start.56) | collective-permute-done | bytes 589856 | tf_op jit(solution)/shard_map/ppermute | solution.py:34
  371.3 3.7 collective-permute-done.57
  379.6 2.2 collective-permute-start.71
  389.3 2.8 collective-permute-done.58
  393.3 6.2 %collective-permute-done.59 = bf16[7,96,512]{2,1,0:T(8,128)(2,1)S(1)} collective-permute-done((bf16[7,96,512]{2,1,0:T(8,128)(2,1)S(1)}, bf16[7,96,512]{2,1,0:T(8,128)(2,1)S(1)}, u32[]{:S(2)}, u32[]{:S(2)}) %collective-permute-start.59) | collective-permute-done | bytes 688160 | tf_op jit(solution)/shard_map/ppermute | solution.py:29
  404.8 3.3 collective-permute-start.65
  409.6 9.3 %collective-permute-done.74 = f32[33,384]{1,0:T(8,128)S(1)} collective-permute-done((f32[33,384]{1,0:T(8,128)}, f32[33,384]{1,0:T(8,128)S(1)}, u32[]{:S(2)}, u32[]{:S(2)}) %collective-permute-start.74) | collective-permute-done | bytes 50720 | tf_op jit(solution)/shard_map/ppermute | solution.py:34
  426.4 2.8 collective-permute-start.76
  430.5 3.2 collective-permute-start.45
  433.8 2.5 collective-permute-done.41
  439.2 3.0 collective-permute-start.46
  442.2 3.3 collective-permute-done.42
  447.8 4.1 collective-permute-start.67
  452.7 2.1 collective-permute-start.69
  454.8 2.6 collective-permute-start.47
  457.5 4.4 collective-permute-start.44
  462.0 2.5 collective-permute-start.48
  465.1 2.6 collective-permute-done.48
  469.8 2.7 collective-permute-done.49
  472.7 3.2 collective-permute-start.50
  476.2 2.3 collective-permute-done.52
  479.1 2.9 collective-permute-done.51
  (362 shorter events, 146.3 us)
Async XLA Ops:
  7.2 120.8 %all-gather.2.cloned.1.call-start = ((), (), s32[]{:S(2)}) async-start(), calls=%async_computation.1 | async-start | bytes 7864320 | tf_op jit(solution)/shard_map/all_gather | solution.py:110
  9.1 8.8 %collective-permute-start = (bf16[3,96,512]{2,1,0:T(8,128)(2,1)S(1)}, bf16[3,96,512]{2,1,0:T(8,128)(2,1)S(1)}, u32[]{:S(2)}, u32[]{:S(2)}) collective-permute-start(bf16[3,96,512]{2,1,0:T(8,128)(2,1)S(1)} %get-tuple-element.369), channel_id=1, source_target_pairs={{0,4},{4,0},{8,12},{12,8},{16,20},{20,16},{24,28},{28,24},{32,36},... | collective-permute-start | bytes 884744 | tf_op jit(solution)/shard_map/ppermute | solution.py:34
  18.2 10.0 %collective-permute-start.1 = (bf16[2,96,512]{2,1,0:T(8,128)(2,1)S(1)}, bf16[2,96,512]{2,1,0:T(8,128)(2,1)S(1)}, u32[]{:S(2)}, u32[]{:S(2)}) collective-permute-start(bf16[2,96,512]{2,1,0:T(8,128)(2,1)S(1)} %get-tuple-element.361), channel_id=1, source_target_pairs={{0,8},{4,12},{8,16},{12,20},{16,24},{20,28},{24,32},{28,36},{32,40... | collective-permute-start | bytes 589832 | tf_op jit(solution)/shard_map/ppermute | solution.py:29
  20.2 8.0 %collective-permute-start.2 = (bf16[2,96,512]{2,1,0:T(8,128)(2,1)S(1)}, bf16[2,96,512]{2,1,0:T(8,128)(2,1)S(1)}, u32[]{:S(2)}, u32[]{:S(2)}) collective-permute-start(bf16[2,96,512]{2,1,0:T(8,128)(2,1)S(1)} %get-tuple-element.361), channel_id=1, source_target_pairs={{0,56},{4,60},{8,0},{12,4},{16,8},{20,12},{24,16},{28,20},{32,24},... | collective-permute-start | bytes 589832 | tf_op jit(solution)/shard_map/ppermute | solution.py:29
  28.2 6.9 %collective-permute-start.3 = (bf16[2,96,512]{2,1,0:T(8,128)(2,1)S(1)}, bf16[2,96,512]{2,1,0:T(8,128)(2,1)S(1)}, u32[]{:S(2)}, u32[]{:S(2)}) collective-permute-start(bf16[2,96,512]{2,1,0:T(8,128)(2,1)S(1)} %collective-permute-done.1), channel_id=1, source_target_pairs={{0,8},{4,12},{8,16},{12,20},{16,24},{20,28},{24,32},{28,36},{32,40... | collective-permute-start | bytes 589832 | tf_op jit(solution)/shard_map/ppermute | solution.py:29
  28.2 6.9 %collective-permute-start.4 = (bf16[2,96,512]{2,1,0:T(8,128)(2,1)S(1)}, bf16[2,96,512]{2,1,0:T(8,128)(2,1)S(1)}, u32[]{:S(2)}, u32[]{:S(2)}) collective-permute-start(bf16[2,96,512]{2,1,0:T(8,128)(2,1)S(1)} %collective-permute-done.2), channel_id=1, source_target_pairs={{0,56},{4,60},{8,0},{12,4},{16,8},{20,12},{24,16},{28,20},{32,24},... | collective-permute-start | bytes 589832 | tf_op jit(solution)/shard_map/ppermute | solution.py:29
  35.1 6.9 %collective-permute-start.5 = (bf16[2,96,512]{2,1,0:T(8,128)(2,1)S(1)}, bf16[2,96,512]{2,1,0:T(8,128)(2,1)S(1)}, u32[]{:S(2)}, u32[]{:S(2)}) collective-permute-start(bf16[2,96,512]{2,1,0:T(8,128)(2,1)S(1)} %collective-permute-done.3), channel_id=1, source_target_pairs={{0,8},{4,12},{8,16},{12,20},{16,24},{20,28},{24,32},{28,36},{32,40... | collective-permute-start | bytes 589832 | tf_op jit(solution)/shard_map/ppermute | solution.py:29
  35.1 7.0 %collective-permute-start.6 = (bf16[2,96,512]{2,1,0:T(8,128)(2,1)S(1)}, bf16[2,96,512]{2,1,0:T(8,128)(2,1)S(1)}, u32[]{:S(2)}, u32[]{:S(2)}) collective-permute-start(bf16[2,96,512]{2,1,0:T(8,128)(2,1)S(1)} %collective-permute-done.4), channel_id=1, source_target_pairs={{0,56},{4,60},{8,0},{12,4},{16,8},{20,12},{24,16},{28,20},{32,24},... | collective-permute-start | bytes 589832 | tf_op jit(solution)/shard_map/ppermute | solution.py:29
  49.1 380.1 %reduce-scatter.2.cloned.1.call-start = ((), (), s32[]{:S(2)}) async-start(), calls=%async_computation.2 | async-start | bytes 7864320 | tf_op jit(solution)/shard_map/reduce_scatter | solution.py:188
  49.2 15.7 %collective-permute-start.17 = (bf16[3,96,512]{2,1,0:T(8,128)(2,1)S(1)}, bf16[3,96,512]{2,1,0:T(8,128)(2,1)S(1)}, u32[]{:S(2)}, u32[]{:S(2)}) collective-permute-start(bf16[3,96,512]{2,1,0:T(8,128)(2,1)S(1)} %pad_maximum_fusion.13), channel_id=1, source_target_pairs={{0,4},{4,0},{8,12},{12,8},{16,20},{20,16},{24,28},{28,24},{32,36},... | collective-permute-start | bytes 884744 | tf_op jit(solution)/shard_map/ppermute | solution.py:34
  56.9 13.6 %collective-permute-start.9 = (bf16[7,96,512]{2,1,0:T(8,128)(2,1)S(1)}, bf16[7,96,512]{2,1,0:T(8,128)(2,1)S(1)}, u32[]{:S(2)}, u32[]{:S(2)}) collective-permute-start(bf16[7,96,512]{2,1,0:T(8,128)(2,1)S(1)} %pad_maximum_fusion.3), channel_id=1, source_target_pairs={{0,8},{4,12},{8,16},{12,20},{16,24},{20,28},{24,32},{28,36},{32,40... | collective-permute-start | bytes 2064392 | tf_op jit(solution)/shard_map/ppermute | solution.py:29
  57.0 14.0 %collective-permute-start.10 = (bf16[7,96,512]{2,1,0:T(8,128)(2,1)S(1)}, bf16[7,96,512]{2,1,0:T(8,128)(2,1)S(1)}, u32[]{:S(2)}, u32[]{:S(2)}) collective-permute-start(bf16[7,96,512]{2,1,0:T(8,128)(2,1)S(1)} %pad_maximum_fusion.3), channel_id=1, source_target_pairs={{0,56},{4,60},{8,0},{12,4},{16,8},{20,12},{24,16},{28,20},{32,24},... | collective-permute-start | bytes 2064392 | tf_op jit(solution)/shard_map/ppermute | solution.py:29
  70.5 8.0 %collective-permute-start.18 = (bf16[3,96,512]{2,1,0:T(8,128)(2,1)S(1)}, bf16[3,96,512]{2,1,0:T(8,128)(2,1)S(1)}, u32[]{:S(2)}, u32[]{:S(2)}) collective-permute-start(bf16[3,96,512]{2,1,0:T(8,128)(2,1)S(1)} %slice.464), channel_id=1, source_target_pairs={{0,4},{4,0},{8,12},{12,8},{16,20},{20,16},{24,28},{28,24},{32,36},... | collective-permute-start | bytes 884744 | tf_op jit(solution)/shard_map/ppermute | solution.py:34
  71.1 9.4 %collective-permute-start.19 = (bf16[3,96,512]{2,1,0:T(8,128)(2,1)S(1)}, bf16[3,96,512]{2,1,0:T(8,128)(2,1)S(1)}, u32[]{:S(2)}, u32[]{:S(2)}) collective-permute-start(bf16[3,96,512]{2,1,0:T(8,128)(2,1)S(1)} %slice.465), channel_id=1, source_target_pairs={{0,4},{4,0},{8,12},{12,8},{16,20},{20,16},{24,28},{28,24},{32,36},... | collective-permute-start | bytes 884744 | tf_op jit(solution)/shard_map/ppermute | solution.py:34
  74.5 12.4 %collective-permute-start.11 = (bf16[7,96,512]{2,1,0:T(8,128)(2,1)S(1)}, bf16[7,96,512]{2,1,0:T(8,128)(2,1)S(1)}, u32[]{:S(2)}, u32[]{:S(2)}) collective-permute-start(bf16[7,96,512]{2,1,0:T(8,128)(2,1)S(1)} %collective-permute-done.9), channel_id=1, source_target_pairs={{0,8},{4,12},{8,16},{12,20},{16,24},{20,28},{24,32},{28,36},{32,40... | collective-permute-start | bytes 2064392 | tf_op jit(solution)/shard_map/ppermute | solution.py:29
  75.4 12.3 %collective-permute-start.12 = (bf16[7,96,512]{2,1,0:T(8,128)(2,1)S(1)}, bf16[7,96,512]{2,1,0:T(8,128)(2,1)S(1)}, u32[]{:S(2)}, u32[]{:S(2)}) collective-permute-start(bf16[7,96,512]{2,1,0:T(8,128)(2,1)S(1)} %collective-permute-done.10), channel_id=1, source_target_pairs={{0,56},{4,60},{8,0},{12,4},{16,8},{20,12},{24,16},{28,20},{32,24},... | collective-permute-start | bytes 2064392 | tf_op jit(solution)/shard_map/ppermute | solution.py:29
  87.0 9.1 %collective-permute-start.20 = (bf16[3,96,512]{2,1,0:T(8,128)(2,1)S(1)}, bf16[3,96,512]{2,1,0:T(8,128)(2,1)S(1)}, u32[]{:S(2)}, u32[]{:S(2)}) collective-permute-start(bf16[3,96,512]{2,1,0:T(8,128)(2,1)S(1)} %slice.466), channel_id=1, source_target_pairs={{0,4},{4,0},{8,12},{12,8},{16,20},{20,16},{24,28},{28,24},{32,36},... | collective-permute-start | bytes 884744 | tf_op jit(solution)/shard_map/ppermute | solution.py:34
  87.8 9.8 %collective-permute-start.21 = (bf16[3,96,512]{2,1,0:T(8,128)(2,1)S(1)}, bf16[3,96,512]{2,1,0:T(8,128)(2,1)S(1)}, u32[]{:S(2)}, u32[]{:S(2)}) collective-permute-start(bf16[3,96,512]{2,1,0:T(8,128)(2,1)S(1)} %slice.467), channel_id=1, source_target_pairs={{0,4},{4,0},{8,12},{12,8},{16,20},{20,16},{24,28},{28,24},{32,36},... | collective-permute-start | bytes 884744 | tf_op jit(solution)/shard_map/ppermute | solution.py:34
  92.1 14.9 %collective-permute-start.13 = (bf16[7,96,512]{2,1,0:T(8,128)(2,1)S(1)}, bf16[7,96,512]{2,1,0:T(8,128)(2,1)S(1)}, u32[]{:S(2)}, u32[]{:S(2)}) collective-permute-start(bf16[7,96,512]{2,1,0:T(8,128)(2,1)S(1)} %collective-permute-done.11), channel_id=1, source_target_pairs={{0,8},{4,12},{8,16},{12,20},{16,24},{20,28},{24,32},{28,36},{32,40... | collective-permute-start | bytes 2064392 | tf_op jit(solution)/shard_map/ppermute | solution.py:29
  93.1 15.2 %collective-permute-start.14 = (bf16[7,96,512]{2,1,0:T(8,128)(2,1)S(1)}, bf16[7,96,512]{2,1,0:T(8,128)(2,1)S(1)}, u32[]{:S(2)}, u32[]{:S(2)}) collective-permute-start(bf16[7,96,512]{2,1,0:T(8,128)(2,1)S(1)} %collective-permute-done.12), channel_id=1, source_target_pairs={{0,56},{4,60},{8,0},{12,4},{16,8},{20,12},{24,16},{28,20},{32,24},... | collective-permute-start | bytes 2064392 | tf_op jit(solution)/shard_map/ppermute | solution.py:29
  107.1 9.4 %collective-permute-start.22 = (bf16[3,96,512]{2,1,0:T(8,128)(2,1)S(1)}, bf16[3,96,512]{2,1,0:T(8,128)(2,1)S(1)}, u32[]{:S(2)}, u32[]{:S(2)}) collective-permute-start(bf16[3,96,512]{2,1,0:T(8,128)(2,1)S(1)} %get-tuple-element.357), channel_id=1, source_target_pairs={{0,4},{4,0},{8,12},{12,8},{16,20},{20,16},{24,28},{28,24},{32,36},... | collective-permute-start | bytes 884744 | tf_op jit(solution)/shard_map/ppermute | solution.py:34
  108.3 11.4 %collective-permute-start.23 = (bf16[3,96,512]{2,1,0:T(8,128)(2,1)S(1)}, bf16[3,96,512]{2,1,0:T(8,128)(2,1)S(1)}, u32[]{:S(2)}, u32[]{:S(2)}) collective-permute-start(bf16[3,96,512]{2,1,0:T(8,128)(2,1)S(1)} %slice.469), channel_id=1, source_target_pairs={{0,4},{4,0},{8,12},{12,8},{16,20},{20,16},{24,28},{28,24},{32,36},... | collective-permute-start | bytes 884744 | tf_op jit(solution)/shard_map/ppermute | solution.py:34
  109.4 11.1 %collective-permute-start.16 = (bf16[4,96,512]{2,1,0:T(8,128)(2,1)S(1)}, bf16[4,96,512]{2,1,0:T(8,128)(2,1)S(1)}, u32[]{:S(2)}, u32[]{:S(2)}) collective-permute-start(bf16[4,96,512]{2,1,0:T(8,128)(2,1)S(1)} %get-tuple-element.359), channel_id=1, source_target_pairs={{0,56},{4,60},{8,0},{12,4},{16,8},{20,12},{24,16},{28,20},{32,24},... | collective-permute-start | bytes 1179656 | tf_op jit(solution)/shard_map/ppermute | solution.py:29
  112.0 9.1 %collective-permute-start.15 = (bf16[3,96,512]{2,1,0:T(8,128)(2,1)S(1)}, bf16[3,96,512]{2,1,0:T(8,128)(2,1)S(1)}, u32[]{:S(2)}, u32[]{:S(2)}) collective-permute-start(bf16[3,96,512]{2,1,0:T(8,128)(2,1)S(1)} %get-tuple-element.358), channel_id=1, source_target_pairs={{0,8},{4,12},{8,16},{12,20},{16,24},{20,28},{24,32},{28,36},{32,40... | collective-permute-start | bytes 884744 | tf_op jit(solution)/shard_map/ppermute | solution.py:29
  120.4 6.8 %collective-permute-start.24 = (bf16[3,96,512]{2,1,0:T(8,128)(2,1)S(1)}, bf16[3,96,512]{2,1,0:T(8,128)(2,1)S(1)}, u32[]{:S(2)}, u32[]{:S(2)}) collective-permute-start(bf16[3,96,512]{2,1,0:T(8,128)(2,1)S(1)} %slice.470), channel_id=1, source_target_pairs={{0,4},{4,0},{8,12},{12,8},{16,20},{20,16},{24,28},{28,24},{32,36},... | collective-permute-start | bytes 884744 | tf_op jit(solution)/shard_map/ppermute | solution.py:34
  137.3 15.1 %collective-permute-start.26 = (bf16[48,1536]{1,0:T(8,128)(2,1)}, bf16[48,1536]{1,0:T(8,128)(2,1)}, u32[]{:S(2)}, u32[]{:S(2)}) collective-permute-start(bf16[48,1536]{1,0:T(8,128)(2,1)} %get-tuple-element.151), channel_id=1, source_target_pairs={{0,64},{1,65},{2,66},{3,67},{4,68},{5,69},{6,70},{7,71},{8,72},{9,... | collective-permute-start | bytes 442376 | tf_op jit(solution)/shard_map/ppermute | solution.py:645
  147.9 15.1 %collective-permute-start.25 = (bf16[48,1536]{1,0:T(8,128)(2,1)}, bf16[48,1536]{1,0:T(8,128)(2,1)}, u32[]{:S(2)}, u32[]{:S(2)}) collective-permute-start(bf16[48,1536]{1,0:T(8,128)(2,1)} %get-tuple-element.150), channel_id=1, source_target_pairs={{0,64},{1,65},{2,66},{3,67},{4,68},{5,69},{6,70},{7,71},{8,72},{9,... | collective-permute-start | bytes 442376 | tf_op jit(solution)/shard_map/ppermute | solution.py:645
  161.0 14.6 %collective-permute-start.28 = (bf16[48,1536]{1,0:T(8,128)(2,1)}, bf16[48,1536]{1,0:T(8,128)(2,1)}, u32[]{:S(2)}, u32[]{:S(2)}) collective-permute-start(bf16[48,1536]{1,0:T(8,128)(2,1)} %get-tuple-element.167), channel_id=1, source_target_pairs={{0,64},{64,128},{1,65},{65,129},{2,66},{66,130},{3,67},{67,131},{4... | collective-permute-start | bytes 442376 | tf_op jit(solution)/shard_map/ppermute | solution.py:645
  199.3 58.3 %collective-permute-start.38 = (bf16[48,1536]{1,0:T(8,128)(2,1)}, bf16[48,1536]{1,0:T(8,128)(2,1)}, u32[]{:S(2)}, u32[]{:S(2)}) collective-permute-start(bf16[48,1536]{1,0:T(8,128)(2,1)} %get-tuple-element.249), channel_id=1, source_target_pairs={{128,64},{64,0},{129,65},{65,1},{130,66},{66,2},{131,67},{67,3},{1... | collective-permute-start | bytes 442376 | tf_op jit(solution)/shard_map/ppermute | solution.py:645
  201.5 70.3 %collective-permute-start.37 = (bf16[48,1536]{1,0:T(8,128)(2,1)}, bf16[48,1536]{1,0:T(8,128)(2,1)}, u32[]{:S(2)}, u32[]{:S(2)}) collective-permute-start(bf16[48,1536]{1,0:T(8,128)(2,1)} %get-tuple-element.248), channel_id=1, source_target_pairs={{128,64},{64,0},{129,65},{65,1},{130,66},{66,2},{131,67},{67,3},{1... | collective-permute-start | bytes 442376 | tf_op jit(solution)/shard_map/ppermute | solution.py:645
  269.4 15.5 %collective-permute-start.40 = (bf16[48,1536]{1,0:T(8,128)(2,1)}, bf16[48,1536]{1,0:T(8,128)(2,1)}, u32[]{:S(2)}, u32[]{:S(2)}) collective-permute-start(bf16[48,1536]{1,0:T(8,128)(2,1)} %get-tuple-element.261), channel_id=1, source_target_pairs={{64,0},{65,1},{66,2},{67,3},{68,4},{69,5},{70,6},{71,7},{72,8},{73... | collective-permute-start | bytes 442376 | tf_op jit(solution)/shard_map/ppermute | solution.py:645
  283.6 15.1 %collective-permute-start.39 = (bf16[48,1536]{1,0:T(8,128)(2,1)}, bf16[48,1536]{1,0:T(8,128)(2,1)}, u32[]{:S(2)}, u32[]{:S(2)}) collective-permute-start(bf16[48,1536]{1,0:T(8,128)(2,1)} %get-tuple-element.260), channel_id=1, source_target_pairs={{64,0},{65,1},{66,2},{67,3},{68,4},{69,5},{70,6},{71,7},{72,8},{73... | collective-permute-start | bytes 442376 | tf_op jit(solution)/shard_map/ppermute | solution.py:645
  321.3 9.3 %collective-permute-start.53 = (bf16[3,96,512]{2,1,0:T(8,128)(2,1)S(1)}, bf16[3,96,512]{2,1,0:T(8,128)(2,1)S(1)}, u32[]{:S(2)}, u32[]{:S(2)}) collective-permute-start(bf16[3,96,512]{2,1,0:T(8,128)(2,1)S(1)} %dynamic-slice_bitcast_fusion.7), channel_id=1, source_target_pairs={{0,4},{4,0},{8,12},{12,8},{16,20},{20,16},{24,28},{28,24},{32,36},... | collective-permute-start | bytes 884744 | tf_op jit(solution)/shard_map/ppermute | solution.py:34
  334.8 14.8 %collective-permute-start.54 = (bf16[6,96,512]{2,1,0:T(8,128)(2,1)S(1)}, bf16[6,96,512]{2,1,0:T(8,128)(2,1)S(1)}, u32[]{:S(2)}, u32[]{:S(2)}) collective-permute-start(bf16[6,96,512]{2,1,0:T(8,128)(2,1)S(1)} %pad_maximum_fusion.5), channel_id=1, source_target_pairs={{0,4},{4,0},{8,12},{12,8},{16,20},{20,16},{24,28},{28,24},{32,36},... | collective-permute-start | bytes 1769480 | tf_op jit(solution)/shard_map/ppermute | solution.py:34
  337.4 14.2 %collective-permute-start.55 = (bf16[3,96,512]{2,1,0:T(8,128)(2,1)S(1)}, bf16[3,96,512]{2,1,0:T(8,128)(2,1)S(1)}, u32[]{:S(2)}, u32[]{:S(2)}) collective-permute-start(bf16[3,96,512]{2,1,0:T(8,128)(2,1)S(1)} %slice.484), channel_id=1, source_target_pairs={{0,8},{4,12},{8,16},{12,20},{16,24},{20,28},{24,32},{28,36},{32,40... | collective-permute-start | bytes 884744 | tf_op jit(solution)/shard_map/ppermute | solution.py:29
  347.2 12.5 %collective-permute-start.62 = (bf16[4,96,512]{2,1,0:T(8,128)(2,1)}, bf16[4,96,512]{2,1,0:T(8,128)(2,1)}, u32[]{:S(2)}, u32[]{:S(2)}) collective-permute-start(bf16[4,96,512]{2,1,0:T(8,128)(2,1)} %fusion.20), channel_id=1, source_target_pairs={{0,56},{4,60},{8,0},{12,4},{16,8},{20,12},{24,16},{28,20},{32,24},... | collective-permute-start | bytes 1179656 | tf_op jit(solution)/shard_map/ppermute | solution.py:29
  357.3 12.6 %collective-permute-start.56 = (bf16[6,96,512]{2,1,0:T(8,128)(2,1)}, bf16[6,96,512]{2,1,0:T(8,128)(2,1)}, u32[]{:S(2)}, u32[]{:S(2)}) collective-permute-start(bf16[6,96,512]{2,1,0:T(8,128)(2,1)} %pad_maximum_fusion.6), channel_id=1, source_target_pairs={{0,4},{4,0},{8,12},{12,8},{16,20},{20,16},{24,28},{28,24},{32,36},... | collective-permute-start | bytes 1769480 | tf_op jit(solution)/shard_map/ppermute | solution.py:34
  359.6 15.5 %collective-permute-start.57 = (bf16[7,96,512]{2,1,0:T(8,128)(2,1)}, bf16[7,96,512]{2,1,0:T(8,128)(2,1)}, u32[]{:S(2)}, u32[]{:S(2)}) collective-permute-start(bf16[7,96,512]{2,1,0:T(8,128)(2,1)} %maximum_convert_fusion), channel_id=1, source_target_pairs={{0,8},{4,12},{8,16},{12,20},{16,24},{20,28},{24,32},{28,36},{32,40... | collective-permute-start | bytes 2064392 | tf_op jit(solution)/shard_map/ppermute | solution.py:29
  361.0 20.8 %collective-permute-start.63 = (bf16[7,96,512]{2,1,0:T(8,128)(2,1)S(1)}, bf16[7,96,512]{2,1,0:T(8,128)(2,1)S(1)}, u32[]{:S(2)}, u32[]{:S(2)}) collective-permute-start(bf16[7,96,512]{2,1,0:T(8,128)(2,1)S(1)} %pad_maximum_fusion.4), channel_id=1, source_target_pairs={{0,56},{4,60},{8,0},{12,4},{16,8},{20,12},{24,16},{28,20},{32,24},... | collective-permute-start | bytes 2064392 | tf_op jit(solution)/shard_map/ppermute | solution.py:29
  379.0 13.1 %collective-permute-start.58 = (bf16[6,96,512]{2,1,0:T(8,128)(2,1)S(1)}, bf16[6,96,512]{2,1,0:T(8,128)(2,1)S(1)}, u32[]{:S(2)}, u32[]{:S(2)}) collective-permute-start(bf16[6,96,512]{2,1,0:T(8,128)(2,1)S(1)} %pad_maximum_fusion.7), channel_id=1, source_target_pairs={{0,4},{4,0},{8,12},{12,8},{16,20},{20,16},{24,28},{28,24},{32,36},... | collective-permute-start | bytes 1769480 | tf_op jit(solution)/shard_map/ppermute | solution.py:34
  381.9 17.6 %collective-permute-start.59 = (bf16[7,96,512]{2,1,0:T(8,128)(2,1)S(1)}, bf16[7,96,512]{2,1,0:T(8,128)(2,1)S(1)}, u32[]{:S(2)}, u32[]{:S(2)}) collective-permute-start(bf16[7,96,512]{2,1,0:T(8,128)(2,1)S(1)} %add_convert_fusion.3), channel_id=1, source_target_pairs={{0,8},{4,12},{8,16},{12,20},{16,24},{20,28},{24,32},{28,36},{32,40... | collective-permute-start | bytes 2064392 | tf_op jit(solution)/shard_map/ppermute | solution.py:29
  383.9 19.6 %collective-permute-start.64 = (bf16[7,96,512]{2,1,0:T(8,128)(2,1)S(1)}, bf16[7,96,512]{2,1,0:T(8,128)(2,1)}, u32[]{:S(2)}, u32[]{:S(2)}) collective-permute-start(bf16[7,96,512]{2,1,0:T(8,128)(2,1)S(1)} %add_convert_fusion.1), channel_id=1, source_target_pairs={{0,56},{4,60},{8,0},{12,4},{16,8},{20,12},{24,16},{28,20},{32,24},... | collective-permute-start | bytes 2064392 | tf_op jit(solution)/shard_map/ppermute | solution.py:29
  388.0 20.1 %collective-permute-start.73 = (f32[33,384]{1,0:T(8,128)}, f32[33,384]{1,0:T(8,128)}, u32[]{:S(2)}, u32[]{:S(2)}) collective-permute-start(f32[33,384]{1,0:T(8,128)} %get-tuple-element.323), channel_id=1, source_target_pairs={{0,4},{4,0},{8,12},{12,8},{16,20},{20,16},{24,28},{28,24},{32,36},... | collective-permute-start | bytes 152072 | tf_op jit(solution)/shard_map/ppermute | solution.py:34
  401.2 21.5 %collective-permute-start.61 = (bf16[7,96,512]{2,1,0:T(8,128)(2,1)S(1)}, bf16[7,96,512]{2,1,0:T(8,128)(2,1)S(1)}, u32[]{:S(2)}, u32[]{:S(2)}) collective-permute-start(bf16[7,96,512]{2,1,0:T(8,128)(2,1)S(1)} %add_convert_fusion.2), channel_id=1, source_target_pairs={{0,8},{4,12},{8,16},{12,20},{16,24},{20,28},{24,32},{28,36},{32,40... | collective-permute-start | bytes 2064392 | tf_op jit(solution)/shard_map/ppermute | solution.py:29
  402.3 19.3 %collective-permute-start.60 = (bf16[3,96,512]{2,1,0:T(8,128)(2,1)S(1)}, bf16[3,96,512]{2,1,0:T(8,128)(2,1)}, u32[]{:S(2)}, u32[]{:S(2)}) collective-permute-start(bf16[3,96,512]{2,1,0:T(8,128)(2,1)S(1)} %dynamic-slice_bitcast_fusion), channel_id=1, source_target_pairs={{0,4},{4,0},{8,12},{12,8},{16,20},{20,16},{24,28},{28,24},{32,36},... | collective-permute-start | bytes 884744 | tf_op jit(solution)/shard_map/ppermute | solution.py:34
  404.8 17.9 %collective-permute-start.65 = (bf16[7,96,512]{2,1,0:T(8,128)(2,1)S(1)}, bf16[7,96,512]{2,1,0:T(8,128)(2,1)S(1)}, u32[]{:S(2)}, u32[]{:S(2)}) collective-permute-start(bf16[7,96,512]{2,1,0:T(8,128)(2,1)S(1)} %add_convert_fusion), channel_id=1, source_target_pairs={{0,56},{4,60},{8,0},{12,4},{16,8},{20,12},{24,16},{28,20},{32,24},... | collective-permute-start | bytes 2064392 | tf_op jit(solution)/shard_map/ppermute | solution.py:29
  409.6 9.3 %collective-permute-start.74 = (f32[33,384]{1,0:T(8,128)}, f32[33,384]{1,0:T(8,128)S(1)}, u32[]{:S(2)}, u32[]{:S(2)}) collective-permute-start(f32[33,384]{1,0:T(8,128)} %get-tuple-element.321), channel_id=1, source_target_pairs={{0,8},{4,12},{8,0},{12,4},{16,24},{20,28},{24,16},{28,20},{32,40},... | collective-permute-start | bytes 152072 | tf_op jit(solution)/shard_map/ppermute | solution.py:34
  419.7 6.7 %collective-permute-start.75 = (f32[33,384]{1,0:T(8,128)S(1)}, f32[33,384]{1,0:T(8,128)S(1)}, u32[]{:S(2)}, u32[]{:S(2)}) collective-permute-start(f32[33,384]{1,0:T(8,128)S(1)} %get-tuple-element.319), channel_id=1, source_target_pairs={{0,16},{4,20},{8,24},{12,28},{16,0},{20,4},{24,8},{28,12},{32,48},... | collective-permute-start | bytes 152072 | tf_op jit(solution)/shard_map/ppermute | solution.py:34
  424.6 9.1 %collective-permute-start.66 = (bf16[2,96,512]{2,1,0:T(8,128)(2,1)S(1)}, bf16[2,96,512]{2,1,0:T(8,128)(2,1)S(1)}, u32[]{:S(2)}, u32[]{:S(2)}) collective-permute-start(bf16[2,96,512]{2,1,0:T(8,128)(2,1)S(1)} %fusion.28), channel_id=1, source_target_pairs={{0,4},{4,0},{8,12},{12,8},{16,20},{20,16},{24,28},{28,24},{32,36},... | collective-permute-start | bytes 589832 | tf_op jit(solution)/shard_map/ppermute | solution.py:34
  426.4 19.3 %collective-permute-start.76 = (f32[33,384]{1,0:T(8,128)S(1)}, f32[33,384]{1,0:T(8,128)S(1)}, u32[]{:S(2)}, u32[]{:S(2)}) collective-permute-start(f32[33,384]{1,0:T(8,128)S(1)} %get-tuple-element.317), channel_id=1, source_target_pairs={{0,32},{4,36},{8,40},{12,44},{16,48},{20,52},{24,56},{28,60},{32,0... | collective-permute-start | bytes 152072 | tf_op jit(solution)/shard_map/ppermute | solution.py:34
  430.5 6.3 %collective-permute-start.45 = (bf16[1,96,512]{2,1,0:T(8,128)(2,1)S(1)}, bf16[1,96,512]{2,1,0:T(8,128)(2,1)S(1)}, u32[]{:S(2)}, u32[]{:S(2)}) collective-permute-start(bf16[1,96,512]{2,1,0:T(8,128)(2,1)S(1)} %get-tuple-element.351), channel_id=1, source_target_pairs={{0,56},{4,60},{8,0},{12,4},{16,8},{20,12},{24,16},{28,20},{32,24},... | collective-permute-start | bytes 294920 | tf_op jit(solution)/shard_map/ppermute | solution.py:29
  436.9 8.6 %collective-permute-start.42 = (bf16[2,96,512]{2,1,0:T(8,128)(2,1)S(1)}, bf16[2,96,512]{2,1,0:T(8,128)(2,1)S(1)}, u32[]{:S(2)}, u32[]{:S(2)}) collective-permute-start(bf16[2,96,512]{2,1,0:T(8,128)(2,1)S(1)} %pad_maximum_fusion.17), channel_id=1, source_target_pairs={{0,8},{4,12},{8,16},{12,20},{16,24},{20,28},{24,32},{28,36},{32,40... | collective-permute-start | bytes 589832 | tf_op jit(solution)/shard_map/ppermute | solution.py:29
  439.2 8.6 %collective-permute-start.46 = (bf16[2,96,512]{2,1,0:T(8,128)(2,1)S(1)}, bf16[2,96,512]{2,1,0:T(8,128)(2,1)S(1)}, u32[]{:S(2)}, u32[]{:S(2)}) collective-permute-start(bf16[2,96,512]{2,1,0:T(8,128)(2,1)S(1)} %pad_maximum_fusion.18), channel_id=1, source_target_pairs={{0,56},{4,60},{8,0},{12,4},{16,8},{20,12},{24,16},{28,20},{32,24},... | collective-permute-start | bytes 589832 | tf_op jit(solution)/shard_map/ppermute | solution.py:29
  445.6 7.0 %collective-permute-start.43 = (bf16[2,96,512]{2,1,0:T(8,128)(2,1)S(1)}, bf16[2,96,512]{2,1,0:T(8,128)(2,1)S(1)}, u32[]{:S(2)}, u32[]{:S(2)}) collective-permute-start(bf16[2,96,512]{2,1,0:T(8,128)(2,1)S(1)} %fusion.24), channel_id=1, source_target_pairs={{0,8},{4,12},{8,16},{12,20},{16,24},{20,28},{24,32},{28,36},{32,40... | collective-permute-start | bytes 589832 | tf_op jit(solution)/shard_map/ppermute | solution.py:29
  445.7 7.0 %collective-permute-start.77 = (f32[33,384]{1,0:T(8,128)S(1)}, f32[33,384]{1,0:T(8,128)S(1)}, u32[]{:S(2)}, u32[]{:S(2)}) collective-permute-start(f32[33,384]{1,0:T(8,128)S(1)} %add_add_fusion.1), channel_id=1, source_target_pairs={{0,1},{1,2},{2,3},{3,0},{4,5},{5,6},{6,7},{7,4},{8,9},{9,10},{10,1... | collective-permute-start | bytes 152072 | tf_op jit(solution)/shard_map/ppermute | solution.py:29
  445.9 8.9 %collective-permute-start.78 = (f32[33,384]{1,0:T(8,128)S(1)}, f32[33,384]{1,0:T(8,128)S(1)}, u32[]{:S(2)}, u32[]{:S(2)}) collective-permute-start(f32[33,384]{1,0:T(8,128)S(1)} %add_add_fusion.1), channel_id=1, source_target_pairs={{0,2},{1,3},{2,0},{3,1},{4,6},{5,7},{6,4},{7,5},{8,10},{9,11},{10,... | collective-permute-start | bytes 152072 | tf_op jit(solution)/shard_map/ppermute | solution.py:29
  447.2 10.2 %collective-permute-start.79 = (f32[33,384]{1,0:T(8,128)S(1)}, f32[33,384]{1,0:T(8,128)S(1)}, u32[]{:S(2)}, u32[]{:S(2)}) collective-permute-start(f32[33,384]{1,0:T(8,128)S(1)} %add_add_fusion.1), channel_id=1, source_target_pairs={{0,3},{1,0},{2,1},{3,2},{4,7},{5,4},{6,5},{7,6},{8,11},{9,8},{10,9... | collective-permute-start | bytes 152072 | tf_op jit(solution)/shard_map/ppermute | solution.py:29
  447.8 28.0 %collective-permute-start.67 = (bf16[5,96,512]{2,1,0:T(8,128)(2,1)S(1)}, bf16[5,96,512]{2,1,0:T(8,128)(2,1)S(1)}, u32[]{:S(2)}, u32[]{:S(2)}) collective-permute-start(bf16[5,96,512]{2,1,0:T(8,128)(2,1)S(1)} %maximum_convert_fusion.1), channel_id=1, source_target_pairs={{0,2},{1,3},{2,0},{3,1},{4,6},{5,7},{6,4},{7,5},{8,10},{9,11},{10,... | collective-permute-start | bytes 1474568 | tf_op jit(solution)/shard_map/ppermute | solution.py:29
  452.6 23.3 %collective-permute-start.68 = (bf16[5,96,512]{2,1,0:T(8,128)(2,1)S(1)}, bf16[5,96,512]{2,1,0:T(8,128)(2,1)S(1)}, u32[]{:S(2)}, u32[]{:S(2)}) collective-permute-start(bf16[5,96,512]{2,1,0:T(8,128)(2,1)S(1)} %maximum_convert_fusion.1), channel_id=1, source_target_pairs={{0,1},{1,2},{2,3},{3,0},{4,5},{5,6},{6,7},{7,4},{8,9},{9,10},{10,1... | collective-permute-start | bytes 1474568 | tf_op jit(solution)/shard_map/ppermute | solution.py:29
  452.7 23.2 %collective-permute-start.69 = (bf16[5,96,512]{2,1,0:T(8,128)(2,1)S(1)}, bf16[5,96,512]{2,1,0:T(8,128)(2,1)S(1)}, u32[]{:S(2)}, u32[]{:S(2)}) collective-permute-start(bf16[5,96,512]{2,1,0:T(8,128)(2,1)S(1)} %maximum_convert_fusion.1), channel_id=1, source_target_pairs={{0,3},{1,0},{2,1},{3,2},{4,7},{5,4},{6,5},{7,6},{8,11},{9,8},{10,9... | collective-permute-start | bytes 1474568 | tf_op jit(solution)/shard_map/ppermute | solution.py:29
  454.8 7.1 %collective-permute-start.47 = (bf16[2,96,512]{2,1,0:T(8,128)(2,1)S(1)}, bf16[2,96,512]{2,1,0:T(8,128)(2,1)S(1)}, u32[]{:S(2)}, u32[]{:S(2)}) collective-permute-start(bf16[2,96,512]{2,1,0:T(8,128)(2,1)S(1)} %get-tuple-element.346), channel_id=1, source_target_pairs={{0,56},{4,60},{8,0},{12,4},{16,8},{20,12},{24,16},{28,20},{32,24},... | collective-permute-start | bytes 589832 | tf_op jit(solution)/shard_map/ppermute | solution.py:29
  457.5 7.6 %collective-permute-start.44 = (bf16[2,96,512]{2,1,0:T(8,128)(2,1)S(1)}, bf16[2,96,512]{2,1,0:T(8,128)(2,1)S(1)}, u32[]{:S(2)}, u32[]{:S(2)}) collective-permute-start(bf16[2,96,512]{2,1,0:T(8,128)(2,1)S(1)} %get-tuple-element.345), channel_id=1, source_target_pairs={{0,8},{4,12},{8,16},{12,20},{16,24},{20,28},{24,32},{28,36},{32,40... | collective-permute-start | bytes 589832 | tf_op jit(solution)/shard_map/ppermute | solution.py:29
  472.7 6.4 %collective-permute-start.50 = (bf16[96,512]{1,0:T(8,128)(2,1)S(1)}, bf16[96,512]{1,0:T(8,128)(2,1)S(1)}, u32[]{:S(2)}, u32[]{:S(2)}) collective-permute-start(bf16[96,512]{1,0:T(8,128)(2,1)S(1)} %bitcast.436), channel_id=1, source_target_pairs={{0,1},{1,2},{2,3},{3,0},{4,5},{5,6},{6,7},{7,4},{8,9},{9,10},{10,1... | collective-permute-start | bytes 294920 | tf_op jit(solution)/shard_map/ppermute | solution.py:29
  475.9 6.1 %collective-permute-start.51 = (bf16[96,512]{1,0:T(8,128)(2,1)S(1)}, bf16[96,512]{1,0:T(8,128)(2,1)S(1)}, u32[]{:S(2)}, u32[]{:S(2)}) collective-permute-start(bf16[96,512]{1,0:T(8,128)(2,1)S(1)} %bitcast.437), channel_id=1, source_target_pairs={{0,2},{1,3},{2,0},{3,1},{4,6},{5,7},{6,4},{7,5},{8,10},{9,11},{10,... | collective-permute-start | bytes 294920 | tf_op jit(solution)/shard_map/ppermute | solution.py:29
  (51 other events, 270.8 us)
Sparse Core Ops, SparseCore 0:
  49.2 67.7 all-gather.1
  317.8 62.7 reduce-scatter.1

commit v6 on v5

--- a/solution.py
+++ b/solution.py
@@ -211,19 +211,29 @@
 
     def prepare(hop, ready):
         tie = after(ready)
+        if hop == 0:
+            tie = tie + after(shared_sum)
         exchange([hop, ring - hop] if hop else [0], tie)
         steps.send(tie)
 
+    late = []
+
+    def note(hop, ready):
+        if hop == 1:
+            late.append(after(ready))
+
     exchange([ring // 2], 0)
+    steps.send(jnp.int32(0))
     total = ring_scatter(main_term, (rest_parts * PAIR + out_parts) // 2, prepare)
-    steps.send(after(total))
+    small_total = scale * steps.send(after(total))
     rest_share = keep_side(
         total[: rest_parts * PAIR].reshape(rest_parts, PAIR, rows, width), kind
     )
-    share = jnp.concatenate([rest_share, total[rest_parts * PAIR :]]).astype(kind)
-    small_total = scale * steps.send(after(share))
-    share = sum_batch(share)
-    shared_total = ring_scatter(lambda offset: pick(shared_sum, (at + offset) % ring), 1)
+    shared_total = ring_scatter(
+        lambda offset: pick(shared_sum, (at + offset) % ring), 1, note
+    )
+    share = jnp.concatenate([rest_share, total[rest_parts * PAIR :]])
+    share = sum_batch((share + late[0].astype(jnp.float32)).astype(kind))
     shared_share = keep_side(shared_total[None], kind)[0].astype(kind)
     in_parts = [part.astype(jnp.float32) for part in batch_order(batch_copies(shared_share))]
     grad_in = jnp.concatenate(in_parts + [share[part] for part in range(rest_parts)], axis=1)

time: 501 us -> 492 us (0.982)
  the two profiles are of different devices: /device:TPU:6 before, /device:TPU:8 now
where the time goes in v6:
time: 492 us; the launch traced here: 483 us
  waiting for transfers between devices  154 us (31%)
  starting transfers between devices  121 us (25%)
  Pallas kernels  99.9 us (20%)
  local copies, waits for them, and re-layouts  54.8 us (11%)
  other arithmetic  26 us (5%)
  between operations  20.5 us (4%)
  matrix products  6.69 us (1%)
    pallas_call x20, Pallas kernels, stage_call(): pl.pallas_call(functools.partial(kernel, taps=taps, length=length, width=...  92.7 us
    ppermute x44, starting transfers between devices, rotate(): return lax.ppermute(x, axis, [(i, (i + by) % peers) for i in range(peers)])  71 us
    ppermute x44, waiting for transfers between devices, rotate(): return lax.ppermute(x, axis, [(i, (i + by) % peers) for i in range(peers)])  63.4 us
    ppermute x16, waiting for transfers between devices, send_active(): return lax.ppermute(x, 'section', pairs)  57.9 us
    ppermute x20, waiting for transfers between devices, swap_bit(): return lax.ppermute(x, 'fsdp', [(i, i ^ bit) for i in range(peers)])  32.6 us
    ppermute x20, starting transfers between devices, swap_bit(): return lax.ppermute(x, 'fsdp', [(i, i ^ bit) for i in range(peers)])  26.1 us
    ppermute x16, starting transfers between devices, send_active(): return lax.ppermute(x, 'section', pairs)  23.7 us
    dynamic_update_slice x15, local copies, waits for them, and re-layouts, place_out(): out = lax.dynamic_update_slice(out, piece[:, None, None], spot)  11 us
  transfers between devices with their start and end apart: 82, of which 35 were waited for; matrix products, arithmetic and copies ran while one was open for 15% of the time, Pallas kernels for 16%

profile of v6, /device:TPU:8, one launch (start us, length us, event | category | flops | bytes accessed | tf_op | source)
XLA Modules:
  0.0 482.8 jit_solution(12824744746663131754)
XLA Ops:
  9.1 2.3 collective-permute-start
  11.4 6.6 %collective-permute-done = bf16[3,96,512]{2,1,0:T(8,128)(2,1)S(1)} collective-permute-done((bf16[3,96,512]{2,1,0:T(8,128)(2,1)S(1)}, bf16[3,96,512]{2,1,0:T(8,128)(2,1)S(1)}, u32[]{:S(2)}, u32[]{:S(2)}) %collective-permute-start) | collective-permute-done | bytes 294944 | tf_op jit(solution)/shard_map/ppermute | solution.py:34
  18.2 2.0 collective-permute-start.1
  20.2 4.0 collective-permute-start.2
  24.2 3.9 collective-permute-done.1
  28.2 3.2 collective-permute-start.4
  31.5 3.6 collective-permute-done.3
  35.1 3.2 collective-permute-start.6
  38.4 3.6 collective-permute-done.5
  42.1 3.4 collective-permute-start.8
  45.5 2.3 collective-permute-done.7
  51.1 3.4 concatenate.95.params
  55.9 3.5 collective-permute-start.10
  60.3 2.7 broadcast_in_dim.107
  64.5 2.0 broadcast_in_dim.106
  67.3 2.1 collective-permute-done.9
  73.4 2.5 collective-permute-start.11
  80.1 6.0 %collective-permute-done.11 = bf16[7,96,512]{2,1,0:T(8,128)(2,1)S(1)} collective-permute-done((bf16[7,96,512]{2,1,0:T(8,128)(2,1)S(1)}, bf16[7,96,512]{2,1,0:T(8,128)(2,1)S(1)}, u32[]{:S(2)}, u32[]{:S(2)}) %collective-permute-start.11) | collective-permute-done | bytes 688160 | tf_op jit(solution)/shard_map/ppermute | solution.py:29
  96.9 7.1 %collective-permute-done.13 = bf16[7,96,512]{2,1,0:T(8,128)(2,1)S(1)} collective-permute-done((bf16[7,96,512]{2,1,0:T(8,128)(2,1)S(1)}, bf16[7,96,512]{2,1,0:T(8,128)(2,1)S(1)}, u32[]{:S(2)}, u32[]{:S(2)}) %collective-permute-start.13) | collective-permute-done | bytes 688160 | tf_op jit(solution)/shard_map/ppermute | solution.py:29
  104.0 3.7 collective-permute-start.22
  109.0 3.4 collective-permute-start.16
  122.5 3.7 collective-permute-done.24
  127.7 8.7 %shard_map.127 = (bf16[48,1536]{1,0:T(8,128)(2,1)}, bf16[4,48,1536]{2,1,0:T(8,128)(2,1)}, bf16[4,48,1536]{2,1,0:T(8,128)(2,1)}, bf16[4,48,1536]{2,1,0:T(8,128)(2...) custom-call(s32[4]{0:T(128)} %get-tuple-element.311.info, ...), custom_call_target="tpu_custom_call" | custom-call | flops 679477248 | bytes 14155776 | tf_op jit(solution)/shard_map/pallas_call | solution.py:582
  136.3 2.0 collective-permute-start.26
  138.3 8.6 %shard_map.128 = (bf16[48,1536]{1,0:T(8,128)(2,1)}, bf16[4,48,1536]{2,1,0:T(8,128)(2,1)}, bf16[4,48,1536]{2,1,0:T(8,128)(2,1)}, bf16[4,48,1536]{2,1,0:T(8,128)(2...) custom-call(s32[4]{0:T(128)} %get-tuple-element.312.info, ...), custom_call_target="tpu_custom_call", output_to_operand_aliasing={{1}: (7, {}), {2}: (8, {}), {3}: (9, {}), {4}: (10, {}), {5... | custom-call | flops 679477248 | bytes 14155776 | tf_op jit(solution)/shard_map/pallas_call | solution.py:582
  146.9 2.0 collective-permute-start.25
  151.4 8.7 %shard_map.129 = (bf16[48,1536]{1,0:T(8,128)(2,1)}, bf16[4,48,1536]{2,1,0:T(8,128)(2,1)}, bf16[4,48,1536]{2,1,0:T(8,128)(2,1)}, bf16[4,48,1536]{2,1,0:T(8,128)(2...) custom-call(s32[4]{0:T(128)} %get-tuple-element.310.info, ...), custom_call_target="tpu_custom_call", output_to_operand_aliasing={{1}: (7, {}), {2}: (8, {}), {3}: (9, {}), {4}: (10, {}), {5... | custom-call | flops 679477248 | bytes 14155776 | tf_op jit(solution)/shard_map/pallas_call | solution.py:582
  160.1 2.0 collective-permute-start.28
  162.0 8.9 %shard_map.130 = (bf16[48,1536]{1,0:T(8,128)(2,1)}, bf16[4,48,1536]{2,1,0:T(8,128)(2,1)}, bf16[4,48,1536]{2,1,0:T(8,128)(2,1)}, bf16[4,48,1536]{2,1,0:T(8,128)(2...) custom-call(s32[4]{0:T(128)} %get-tuple-element.313.info, ...), custom_call_target="tpu_custom_call", output_to_operand_aliasing={{1}: (7, {}), {2}: (8, {}), {3}: (9, {}), {4}: (10, {}), {5... | custom-call | flops 679477248 | bytes 14155776 | tf_op jit(solution)/shard_map/pallas_call | solution.py:582
  170.9 2.0 collective-permute-start.27
  201.8 54.8 %collective-permute-done.38.incoming = bf16[48,1536]{1,0:T(8,128)(2,1)} collective-permute-done((bf16[48,1536]{1,0:T(8,128)(2,1)}, bf16[48,1536]{1,0:T(8,128)(2,1)}, u32[]{:S(2)}, u32[]{:S(2)}) %collective-permute-start.38) | collective-permute-done | bytes 147488 | tf_op jit(solution)/shard_map/ppermute | solution.py:655
  256.6 11.8 %shard_map.143 = (bf16[48,1536]{1,0:T(8,128)(2,1)}, bf16[4,48,1536]{2,1,0:T(8,128)(2,1)}, bf16[4,48,3072]{2,1,0:T(8,128)(2,1)}, bf16[4,48,1536]{2,1,0:T(8,128)(2...) custom-call(s32[4]{0:T(128)} %get-tuple-element.298.info, ...), custom_call_target="tpu_custom_call", output_to_operand_aliasing={{1}: (12, {}), {2}: (13, {}), {3}: (14, {}), {4}: (15, {}),... | custom-call | flops 679477248 | bytes 14155776 | tf_op jit(solution)/shard_map/pallas_call | solution.py:582
  270.8 11.8 %shard_map.144 = (bf16[48,1536]{1,0:T(8,128)(2,1)}, bf16[4,48,1536]{2,1,0:T(8,128)(2,1)}, bf16[4,48,3072]{2,1,0:T(8,128)(2,1)}, bf16[4,48,1536]{2,1,0:T(8,128)(2...) custom-call(s32[4]{0:T(128)} %get-tuple-element.305.info, ...), custom_call_target="tpu_custom_call", output_to_operand_aliasing={{1}: (12, {}), {2}: (13, {}), {3}: (14, {}), {4}: (15, {}),... | custom-call | flops 679477248 | bytes 14155776 | tf_op jit(solution)/shard_map/pallas_call | solution.py:582
  284.0 11.8 %shard_map.145 = (bf16[48,1536]{1,0:T(8,128)(2,1)}, bf16[4,48,1536]{2,1,0:T(8,128)(2,1)}, bf16[4,48,3072]{2,1,0:T(8,128)(2,1)}, bf16[4,48,1536]{2,1,0:T(8,128)(2...) custom-call(s32[4]{0:T(128)} %get-tuple-element.297.info, ...), custom_call_target="tpu_custom_call", output_to_operand_aliasing={{1}: (12, {}), {2}: (13, {}), {3}: (14, {}), {4}: (15, {}),... | custom-call | flops 679477248 | bytes 14155776 | tf_op jit(solution)/shard_map/pallas_call | solution.py:582
  295.8 2.0 collective-permute-done.39.incoming
  297.7 12.0 %shard_map.146 = (bf16[48,1536]{1,0:T(8,128)(2,1)}, bf16[4,48,1536]{2,1,0:T(8,128)(2,1)}, bf16[4,48,3072]{2,1,0:T(8,128)(2,1)}, bf16[4,48,1536]{2,1,0:T(8,128)(2...) custom-call(s32[4]{0:T(128)} %get-tuple-element.306.info, ...), custom_call_target="tpu_custom_call", output_to_operand_aliasing={{1}: (12, {}), {2}: (13, {}), {3}: (14, {}), {4}: (15, {}),... | custom-call | flops 679477248 | bytes 14155776 | tf_op jit(solution)/shard_map/pallas_call | solution.py:582
  313.4 3.3 pad_maximum_fusion
  326.9 7.3 %shard_map.147 = f32[32,1536]{1,0:T(8,128)S(1)} custom-call(s32[4]{0:T(128)S(1)} %bitcast.350, f32[4,48,1536]{2,1,0:T(8,128)S(1)} %copy-done.4, f32[4,48,1536]{2,1,0:T(8,128)S(1)} %copy-done.2, f32[4,48,1536]{2,1,0:T(8,128)S(1)} %copy-done.3), custom_call_target="tpu_custom_call" | custom-call | flops 18284544 | bytes 3538944 | tf_op jit(solution)/shard_map/pallas_call | solution.py:550
  341.2 3.2 collective-permute-start.71
  350.9 5.7 %collective-permute-done.55 = bf16[3,96,512]{2,1,0:T(8,128)(2,1)S(1)} collective-permute-done((bf16[3,96,512]{2,1,0:T(8,128)(2,1)S(1)}, bf16[3,96,512]{2,1,0:T(8,128)(2,1)S(1)}, u32[]{:S(2)}, u32[]{:S(2)}) %collective-permute-start.55) | collective-permute-done | bytes 294944 | tf_op jit(solution)/shard_map/ppermute | solution.py:29
  363.2 3.3 collective-permute-start.63
  366.5 9.0 %collective-permute-done.56 = bf16[6,96,512]{2,1,0:T(8,128)(2,1)S(1)} collective-permute-done((bf16[6,96,512]{2,1,0:T(8,128)(2,1)S(1)}, bf16[6,96,512]{2,1,0:T(8,128)(2,1)S(1)}, u32[]{:S(2)}, u32[]{:S(2)}) %collective-permute-start.56) | collective-permute-done | bytes 589856 | tf_op jit(solution)/shard_map/ppermute | solution.py:34
  380.7 2.0 collective-permute-start.58
  382.9 2.0 collective-permute-start.59
  387.8 2.8 collective-permute-done.58
  391.9 7.7 %collective-permute-done.59 = bf16[7,96,512]{2,1,0:T(8,128)(2,1)S(1)} collective-permute-done((bf16[7,96,512]{2,1,0:T(8,128)(2,1)S(1)}, bf16[7,96,512]{2,1,0:T(8,128)(2,1)S(1)}, u32[]{:S(2)}, u32[]{:S(2)}) %collective-permute-start.59) | collective-permute-done | bytes 688160 | tf_op jit(solution)/shard_map/ppermute | solution.py:29
  399.9 4.9 %collective-permute-done.64 = bf16[7,96,512]{2,1,0:T(8,128)(2,1)S(1)} collective-permute-done((bf16[7,96,512]{2,1,0:T(8,128)(2,1)S(1)}, bf16[7,96,512]{2,1,0:T(8,128)(2,1)S(1)}, u32[]{:S(2)}, u32[]{:S(2)}) %collective-permute-start.64) | collective-permute-done | bytes 688160 | tf_op jit(solution)/shard_map/ppermute | solution.py:29
  407.3 2.1 collective-permute-start.65
  409.4 2.3 copy.219
  413.0 4.0 collective-permute-start.76
  417.1 3.4 collective-permute-start.45
  423.7 3.8 collective-permute-start.46
  427.5 2.5 collective-permute-done.60
  435.2 2.1 collective-permute-start.79
  442.5 2.0 collective-permute-done.43
  444.6 2.1 collective-permute-start.47
  446.8 3.5 collective-permute-done.47
  450.4 3.3 collective-permute-start.48
  453.9 3.0 collective-permute-start.67
  456.9 3.2 collective-permute-start.69
  462.0 3.1 collective-permute-done.49
  465.3 2.0 collective-permute-start.50
  467.3 2.2 collective-permute-done.68
  471.2 2.2 collective-permute-done.51
  (348 shorter events, 139.0 us)
Async XLA Ops:
  7.2 119.8 %all-gather.2.cloned.1.call-start = ((), (), s32[]{:S(2)}) async-start(), calls=%async_computation.1 | async-start | bytes 7864320 | tf_op jit(solution)/shard_map/all_gather | solution.py:110
  9.1 8.8 %collective-permute-start = (bf16[3,96,512]{2,1,0:T(8,128)(2,1)S(1)}, bf16[3,96,512]{2,1,0:T(8,128)(2,1)S(1)}, u32[]{:S(2)}, u32[]{:S(2)}) collective-permute-start(bf16[3,96,512]{2,1,0:T(8,128)(2,1)S(1)} %get-tuple-element.369), channel_id=1, source_target_pairs={{0,4},{4,0},{8,12},{12,8},{16,20},{20,16},{24,28},{28,24},{32,36},... | collective-permute-start | bytes 884744 | tf_op jit(solution)/shard_map/ppermute | solution.py:34
  18.2 10.0 %collective-permute-start.1 = (bf16[2,96,512]{2,1,0:T(8,128)(2,1)S(1)}, bf16[2,96,512]{2,1,0:T(8,128)(2,1)S(1)}, u32[]{:S(2)}, u32[]{:S(2)}) collective-permute-start(bf16[2,96,512]{2,1,0:T(8,128)(2,1)S(1)} %get-tuple-element.361), channel_id=1, source_target_pairs={{0,8},{4,12},{8,16},{12,20},{16,24},{20,28},{24,32},{28,36},{32,40... | collective-permute-start | bytes 589832 | tf_op jit(solution)/shard_map/ppermute | solution.py:29
  20.2 8.0 %collective-permute-start.2 = (bf16[2,96,512]{2,1,0:T(8,128)(2,1)S(1)}, bf16[2,96,512]{2,1,0:T(8,128)(2,1)S(1)}, u32[]{:S(2)}, u32[]{:S(2)}) collective-permute-start(bf16[2,96,512]{2,1,0:T(8,128)(2,1)S(1)} %get-tuple-element.361), channel_id=1, source_target_pairs={{0,56},{4,60},{8,0},{12,4},{16,8},{20,12},{24,16},{28,20},{32,24},... | collective-permute-start | bytes 589832 | tf_op jit(solution)/shard_map/ppermute | solution.py:29
  28.2 6.9 %collective-permute-start.3 = (bf16[2,96,512]{2,1,0:T(8,128)(2,1)S(1)}, bf16[2,96,512]{2,1,0:T(8,128)(2,1)S(1)}, u32[]{:S(2)}, u32[]{:S(2)}) collective-permute-start(bf16[2,96,512]{2,1,0:T(8,128)(2,1)S(1)} %collective-permute-done.1), channel_id=1, source_target_pairs={{0,8},{4,12},{8,16},{12,20},{16,24},{20,28},{24,32},{28,36},{32,40... | collective-permute-start | bytes 589832 | tf_op jit(solution)/shard_map/ppermute | solution.py:29
  28.2 6.9 %collective-permute-start.4 = (bf16[2,96,512]{2,1,0:T(8,128)(2,1)S(1)}, bf16[2,96,512]{2,1,0:T(8,128)(2,1)S(1)}, u32[]{:S(2)}, u32[]{:S(2)}) collective-permute-start(bf16[2,96,512]{2,1,0:T(8,128)(2,1)S(1)} %collective-permute-done.2), channel_id=1, source_target_pairs={{0,56},{4,60},{8,0},{12,4},{16,8},{20,12},{24,16},{28,20},{32,24},... | collective-permute-start | bytes 589832 | tf_op jit(solution)/shard_map/ppermute | solution.py:29
  35.1 6.9 %collective-permute-start.5 = (bf16[2,96,512]{2,1,0:T(8,128)(2,1)S(1)}, bf16[2,96,512]{2,1,0:T(8,128)(2,1)S(1)}, u32[]{:S(2)}, u32[]{:S(2)}) collective-permute-start(bf16[2,96,512]{2,1,0:T(8,128)(2,1)S(1)} %collective-permute-done.3), channel_id=1, source_target_pairs={{0,8},{4,12},{8,16},{12,20},{16,24},{20,28},{24,32},{28,36},{32,40... | collective-permute-start | bytes 589832 | tf_op jit(solution)/shard_map/ppermute | solution.py:29
  35.1 7.0 %collective-permute-start.6 = (bf16[2,96,512]{2,1,0:T(8,128)(2,1)S(1)}, bf16[2,96,512]{2,1,0:T(8,128)(2,1)S(1)}, u32[]{:S(2)}, u32[]{:S(2)}) collective-permute-start(bf16[2,96,512]{2,1,0:T(8,128)(2,1)S(1)} %collective-permute-done.4), channel_id=1, source_target_pairs={{0,56},{4,60},{8,0},{12,4},{16,8},{20,12},{24,16},{28,20},{32,24},... | collective-permute-start | bytes 589832 | tf_op jit(solution)/shard_map/ppermute | solution.py:29
  49.1 360.3 %reduce-scatter.2.cloned.1.call-start = ((), (), s32[]{:S(2)}) async-start(), calls=%async_computation.2 | async-start | bytes 7864320 | tf_op jit(solution)/shard_map/reduce_scatter | solution.py:188
  49.2 14.5 %collective-permute-start.17 = (bf16[3,96,512]{2,1,0:T(8,128)(2,1)S(1)}, bf16[3,96,512]{2,1,0:T(8,128)(2,1)S(1)}, u32[]{:S(2)}, u32[]{:S(2)}) collective-permute-start(bf16[3,96,512]{2,1,0:T(8,128)(2,1)S(1)} %pad_maximum_fusion.13), channel_id=1, source_target_pairs={{0,4},{4,0},{8,12},{12,8},{16,20},{20,16},{24,28},{28,24},{32,36},... | collective-permute-start | bytes 884744 | tf_op jit(solution)/shard_map/ppermute | solution.py:34
  55.8 13.6 %collective-permute-start.9 = (bf16[7,96,512]{2,1,0:T(8,128)(2,1)S(1)}, bf16[7,96,512]{2,1,0:T(8,128)(2,1)S(1)}, u32[]{:S(2)}, u32[]{:S(2)}) collective-permute-start(bf16[7,96,512]{2,1,0:T(8,128)(2,1)S(1)} %pad_maximum_fusion.3), channel_id=1, source_target_pairs={{0,8},{4,12},{8,16},{12,20},{16,24},{20,28},{24,32},{28,36},{32,40... | collective-permute-start | bytes 2064392 | tf_op jit(solution)/shard_map/ppermute | solution.py:29
  55.9 15.2 %collective-permute-start.10 = (bf16[7,96,512]{2,1,0:T(8,128)(2,1)S(1)}, bf16[7,96,512]{2,1,0:T(8,128)(2,1)S(1)}, u32[]{:S(2)}, u32[]{:S(2)}) collective-permute-start(bf16[7,96,512]{2,1,0:T(8,128)(2,1)S(1)} %pad_maximum_fusion.3), channel_id=1, source_target_pairs={{0,56},{4,60},{8,0},{12,4},{16,8},{20,12},{24,16},{28,20},{32,24},... | collective-permute-start | bytes 2064392 | tf_op jit(solution)/shard_map/ppermute | solution.py:29
  69.4 8.0 %collective-permute-start.18 = (bf16[3,96,512]{2,1,0:T(8,128)(2,1)S(1)}, bf16[3,96,512]{2,1,0:T(8,128)(2,1)S(1)}, u32[]{:S(2)}, u32[]{:S(2)}) collective-permute-start(bf16[3,96,512]{2,1,0:T(8,128)(2,1)S(1)} %slice.468), channel_id=1, source_target_pairs={{0,4},{4,0},{8,12},{12,8},{16,20},{20,16},{24,28},{28,24},{32,36},... | collective-permute-start | bytes 884744 | tf_op jit(solution)/shard_map/ppermute | solution.py:34
  71.1 8.3 %collective-permute-start.19 = (bf16[3,96,512]{2,1,0:T(8,128)(2,1)S(1)}, bf16[3,96,512]{2,1,0:T(8,128)(2,1)S(1)}, u32[]{:S(2)}, u32[]{:S(2)}) collective-permute-start(bf16[3,96,512]{2,1,0:T(8,128)(2,1)S(1)} %slice.469), channel_id=1, source_target_pairs={{0,4},{4,0},{8,12},{12,8},{16,20},{20,16},{24,28},{28,24},{32,36},... | collective-permute-start | bytes 884744 | tf_op jit(solution)/shard_map/ppermute | solution.py:34
  73.4 12.6 %collective-permute-start.11 = (bf16[7,96,512]{2,1,0:T(8,128)(2,1)S(1)}, bf16[7,96,512]{2,1,0:T(8,128)(2,1)S(1)}, u32[]{:S(2)}, u32[]{:S(2)}) collective-permute-start(bf16[7,96,512]{2,1,0:T(8,128)(2,1)S(1)} %collective-permute-done.9), channel_id=1, source_target_pairs={{0,8},{4,12},{8,16},{12,20},{16,24},{20,28},{24,32},{28,36},{32,40... | collective-permute-start | bytes 2064392 | tf_op jit(solution)/shard_map/ppermute | solution.py:29
  75.9 12.9 %collective-permute-start.12 = (bf16[7,96,512]{2,1,0:T(8,128)(2,1)S(1)}, bf16[7,96,512]{2,1,0:T(8,128)(2,1)S(1)}, u32[]{:S(2)}, u32[]{:S(2)}) collective-permute-start(bf16[7,96,512]{2,1,0:T(8,128)(2,1)S(1)} %collective-permute-done.10), channel_id=1, source_target_pairs={{0,56},{4,60},{8,0},{12,4},{16,8},{20,12},{24,16},{28,20},{32,24},... | collective-permute-start | bytes 2064392 | tf_op jit(solution)/shard_map/ppermute | solution.py:29
  86.1 8.5 %collective-permute-start.20 = (bf16[3,96,512]{2,1,0:T(8,128)(2,1)S(1)}, bf16[3,96,512]{2,1,0:T(8,128)(2,1)S(1)}, u32[]{:S(2)}, u32[]{:S(2)}) collective-permute-start(bf16[3,96,512]{2,1,0:T(8,128)(2,1)S(1)} %slice.470), channel_id=1, source_target_pairs={{0,4},{4,0},{8,12},{12,8},{16,20},{20,16},{24,28},{28,24},{32,36},... | collective-permute-start | bytes 884744 | tf_op jit(solution)/shard_map/ppermute | solution.py:34
  88.8 7.3 %collective-permute-start.21 = (bf16[3,96,512]{2,1,0:T(8,128)(2,1)S(1)}, bf16[3,96,512]{2,1,0:T(8,128)(2,1)S(1)}, u32[]{:S(2)}, u32[]{:S(2)}) collective-permute-start(bf16[3,96,512]{2,1,0:T(8,128)(2,1)S(1)} %slice.471), channel_id=1, source_target_pairs={{0,4},{4,0},{8,12},{12,8},{16,20},{20,16},{24,28},{28,24},{32,36},... | collective-permute-start | bytes 884744 | tf_op jit(solution)/shard_map/ppermute | solution.py:34
  90.6 13.3 %collective-permute-start.13 = (bf16[7,96,512]{2,1,0:T(8,128)(2,1)S(1)}, bf16[7,96,512]{2,1,0:T(8,128)(2,1)S(1)}, u32[]{:S(2)}, u32[]{:S(2)}) collective-permute-start(bf16[7,96,512]{2,1,0:T(8,128)(2,1)S(1)} %collective-permute-done.11), channel_id=1, source_target_pairs={{0,8},{4,12},{8,16},{12,20},{16,24},{20,28},{24,32},{28,36},{32,40... | collective-permute-start | bytes 2064392 | tf_op jit(solution)/shard_map/ppermute | solution.py:29
  92.4 15.2 %collective-permute-start.14 = (bf16[7,96,512]{2,1,0:T(8,128)(2,1)S(1)}, bf16[7,96,512]{2,1,0:T(8,128)(2,1)S(1)}, u32[]{:S(2)}, u32[]{:S(2)}) collective-permute-start(bf16[7,96,512]{2,1,0:T(8,128)(2,1)S(1)} %collective-permute-done.12), channel_id=1, source_target_pairs={{0,56},{4,60},{8,0},{12,4},{16,8},{20,12},{24,16},{28,20},{32,24},... | collective-permute-start | bytes 2064392 | tf_op jit(solution)/shard_map/ppermute | solution.py:29
  104.0 11.3 %collective-permute-start.22 = (bf16[3,96,512]{2,1,0:T(8,128)(2,1)S(1)}, bf16[3,96,512]{2,1,0:T(8,128)(2,1)S(1)}, u32[]{:S(2)}, u32[]{:S(2)}) collective-permute-start(bf16[3,96,512]{2,1,0:T(8,128)(2,1)S(1)} %get-tuple-element.357), channel_id=1, source_target_pairs={{0,4},{4,0},{8,12},{12,8},{16,20},{20,16},{24,28},{28,24},{32,36},... | collective-permute-start | bytes 884744 | tf_op jit(solution)/shard_map/ppermute | solution.py:34
  107.7 11.0 %collective-permute-start.23 = (bf16[3,96,512]{2,1,0:T(8,128)(2,1)S(1)}, bf16[3,96,512]{2,1,0:T(8,128)(2,1)S(1)}, u32[]{:S(2)}, u32[]{:S(2)}) collective-permute-start(bf16[3,96,512]{2,1,0:T(8,128)(2,1)S(1)} %slice.473), channel_id=1, source_target_pairs={{0,4},{4,0},{8,12},{12,8},{16,20},{20,16},{24,28},{28,24},{32,36},... | collective-permute-start | bytes 884744 | tf_op jit(solution)/shard_map/ppermute | solution.py:34
  109.0 10.3 %collective-permute-start.16 = (bf16[4,96,512]{2,1,0:T(8,128)(2,1)S(1)}, bf16[4,96,512]{2,1,0:T(8,128)(2,1)S(1)}, u32[]{:S(2)}, u32[]{:S(2)}) collective-permute-start(bf16[4,96,512]{2,1,0:T(8,128)(2,1)S(1)} %get-tuple-element.359), channel_id=1, source_target_pairs={{0,56},{4,60},{8,0},{12,4},{16,8},{20,12},{24,16},{28,20},{32,24},... | collective-permute-start | bytes 1179656 | tf_op jit(solution)/shard_map/ppermute | solution.py:29
  112.4 8.5 %collective-permute-start.15 = (bf16[3,96,512]{2,1,0:T(8,128)(2,1)S(1)}, bf16[3,96,512]{2,1,0:T(8,128)(2,1)S(1)}, u32[]{:S(2)}, u32[]{:S(2)}) collective-permute-start(bf16[3,96,512]{2,1,0:T(8,128)(2,1)S(1)} %get-tuple-element.358), channel_id=1, source_target_pairs={{0,8},{4,12},{8,16},{12,20},{16,24},{20,28},{24,32},{28,36},{32,40... | collective-permute-start | bytes 884744 | tf_op jit(solution)/shard_map/ppermute | solution.py:29
  119.4 6.8 %collective-permute-start.24 = (bf16[3,96,512]{2,1,0:T(8,128)(2,1)S(1)}, bf16[3,96,512]{2,1,0:T(8,128)(2,1)S(1)}, u32[]{:S(2)}, u32[]{:S(2)}) collective-permute-start(bf16[3,96,512]{2,1,0:T(8,128)(2,1)S(1)} %slice.474), channel_id=1, source_target_pairs={{0,4},{4,0},{8,12},{12,8},{16,20},{20,16},{24,28},{28,24},{32,36},... | collective-permute-start | bytes 884744 | tf_op jit(solution)/shard_map/ppermute | solution.py:34
  136.3 15.1 %collective-permute-start.26 = (bf16[48,1536]{1,0:T(8,128)(2,1)}, bf16[48,1536]{1,0:T(8,128)(2,1)}, u32[]{:S(2)}, u32[]{:S(2)}) collective-permute-start(bf16[48,1536]{1,0:T(8,128)(2,1)} %get-tuple-element.151), channel_id=1, source_target_pairs={{0,64},{1,65},{2,66},{3,67},{4,68},{5,69},{6,70},{7,71},{8,72},{9,... | collective-permute-start | bytes 442376 | tf_op jit(solution)/shard_map/ppermute | solution.py:655
  146.9 15.1 %collective-permute-start.25 = (bf16[48,1536]{1,0:T(8,128)(2,1)}, bf16[48,1536]{1,0:T(8,128)(2,1)}, u32[]{:S(2)}, u32[]{:S(2)}) collective-permute-start(bf16[48,1536]{1,0:T(8,128)(2,1)} %get-tuple-element.150), channel_id=1, source_target_pairs={{0,64},{1,65},{2,66},{3,67},{4,68},{5,69},{6,70},{7,71},{8,72},{9,... | collective-permute-start | bytes 442376 | tf_op jit(solution)/shard_map/ppermute | solution.py:655
  160.1 14.6 %collective-permute-start.28 = (bf16[48,1536]{1,0:T(8,128)(2,1)}, bf16[48,1536]{1,0:T(8,128)(2,1)}, u32[]{:S(2)}, u32[]{:S(2)}) collective-permute-start(bf16[48,1536]{1,0:T(8,128)(2,1)} %get-tuple-element.167), channel_id=1, source_target_pairs={{0,64},{64,128},{1,65},{65,129},{2,66},{66,130},{3,67},{67,131},{4... | collective-permute-start | bytes 442376 | tf_op jit(solution)/shard_map/ppermute | solution.py:655
  198.4 58.3 %collective-permute-start.38 = (bf16[48,1536]{1,0:T(8,128)(2,1)}, bf16[48,1536]{1,0:T(8,128)(2,1)}, u32[]{:S(2)}, u32[]{:S(2)}) collective-permute-start(bf16[48,1536]{1,0:T(8,128)(2,1)} %get-tuple-element.249), channel_id=1, source_target_pairs={{128,64},{64,0},{129,65},{65,1},{130,66},{66,2},{131,67},{67,3},{1... | collective-permute-start | bytes 442376 | tf_op jit(solution)/shard_map/ppermute | solution.py:655
  200.5 70.3 %collective-permute-start.37 = (bf16[48,1536]{1,0:T(8,128)(2,1)}, bf16[48,1536]{1,0:T(8,128)(2,1)}, u32[]{:S(2)}, u32[]{:S(2)}) collective-permute-start(bf16[48,1536]{1,0:T(8,128)(2,1)} %get-tuple-element.248), channel_id=1, source_target_pairs={{128,64},{64,0},{129,65},{65,1},{130,66},{66,2},{131,67},{67,3},{1... | collective-permute-start | bytes 442376 | tf_op jit(solution)/shard_map/ppermute | solution.py:655
  268.5 15.5 %collective-permute-start.40 = (bf16[48,1536]{1,0:T(8,128)(2,1)}, bf16[48,1536]{1,0:T(8,128)(2,1)}, u32[]{:S(2)}, u32[]{:S(2)}) collective-permute-start(bf16[48,1536]{1,0:T(8,128)(2,1)} %get-tuple-element.261), channel_id=1, source_target_pairs={{64,0},{65,1},{66,2},{67,3},{68,4},{69,5},{70,6},{71,7},{72,8},{73... | collective-permute-start | bytes 442376 | tf_op jit(solution)/shard_map/ppermute | solution.py:655
  282.6 15.1 %collective-permute-start.39 = (bf16[48,1536]{1,0:T(8,128)(2,1)}, bf16[48,1536]{1,0:T(8,128)(2,1)}, u32[]{:S(2)}, u32[]{:S(2)}) collective-permute-start(bf16[48,1536]{1,0:T(8,128)(2,1)} %get-tuple-element.260), channel_id=1, source_target_pairs={{64,0},{65,1},{66,2},{67,3},{68,4},{69,5},{70,6},{71,7},{72,8},{73... | collective-permute-start | bytes 442376 | tf_op jit(solution)/shard_map/ppermute | solution.py:655
  320.5 14.4 %collective-permute-start.53 = (bf16[3,96,512]{2,1,0:T(8,128)(2,1)S(1)}, bf16[3,96,512]{2,1,0:T(8,128)(2,1)S(1)}, u32[]{:S(2)}, u32[]{:S(2)}) collective-permute-start(bf16[3,96,512]{2,1,0:T(8,128)(2,1)S(1)} %dynamic-slice_bitcast_fusion.7), channel_id=1, source_target_pairs={{0,4},{4,0},{8,12},{12,8},{16,20},{20,16},{24,28},{28,24},{32,36},... | collective-permute-start | bytes 884744 | tf_op jit(solution)/shard_map/ppermute | solution.py:34
  337.8 10.7 %collective-permute-start.54 = (bf16[6,96,512]{2,1,0:T(8,128)(2,1)S(1)}, bf16[6,96,512]{2,1,0:T(8,128)(2,1)S(1)}, u32[]{:S(2)}, u32[]{:S(2)}) collective-permute-start(bf16[6,96,512]{2,1,0:T(8,128)(2,1)S(1)} %pad_maximum_fusion.5), channel_id=1, source_target_pairs={{0,4},{4,0},{8,12},{12,8},{16,20},{20,16},{24,28},{28,24},{32,36},... | collective-permute-start | bytes 1769480 | tf_op jit(solution)/shard_map/ppermute | solution.py:34
  339.9 20.0 %collective-permute-start.70 = (f32[33,384]{1,0:T(8,128)}, f32[33,384]{1,0:T(8,128)S(1)}, u32[]{:S(2)}, u32[]{:S(2)}) collective-permute-start(f32[33,384]{1,0:T(8,128)} %get-tuple-element.376), channel_id=1, source_target_pairs={{0,1},{1,2},{2,3},{3,0},{4,5},{5,6},{6,7},{7,4},{8,9},{9,10},{10,1... | collective-permute-start | bytes 152072 | tf_op jit(solution)/shard_map/ppermute | solution.py:29
  341.2 20.3 %collective-permute-start.71 = (f32[33,384]{1,0:T(8,128)}, f32[33,384]{1,0:T(8,128)S(1)}, u32[]{:S(2)}, u32[]{:S(2)}) collective-permute-start(f32[33,384]{1,0:T(8,128)} %get-tuple-element.378), channel_id=1, source_target_pairs={{0,2},{1,3},{2,0},{3,1},{4,6},{5,7},{6,4},{7,5},{8,10},{9,11},{10,... | collective-permute-start | bytes 152072 | tf_op jit(solution)/shard_map/ppermute | solution.py:29
  344.4 17.1 %collective-permute-start.72 = (f32[33,384]{1,0:T(8,128)S(1)}, f32[33,384]{1,0:T(8,128)}, u32[]{:S(2)}, u32[]{:S(2)}) collective-permute-start(f32[33,384]{1,0:T(8,128)S(1)} %get-tuple-element.377), channel_id=1, source_target_pairs={{0,3},{1,0},{2,1},{3,2},{4,7},{5,4},{6,5},{7,6},{8,11},{9,8},{10,9... | collective-permute-start | bytes 152072 | tf_op jit(solution)/shard_map/ppermute | solution.py:29
  345.4 11.2 %collective-permute-start.55 = (bf16[3,96,512]{2,1,0:T(8,128)(2,1)S(1)}, bf16[3,96,512]{2,1,0:T(8,128)(2,1)S(1)}, u32[]{:S(2)}, u32[]{:S(2)}) collective-permute-start(bf16[3,96,512]{2,1,0:T(8,128)(2,1)S(1)} %slice.488), channel_id=1, source_target_pairs={{0,8},{4,12},{8,16},{12,20},{16,24},{20,28},{24,32},{28,36},{32,40... | collective-permute-start | bytes 884744 | tf_op jit(solution)/shard_map/ppermute | solution.py:29
  348.5 14.5 %collective-permute-start.62 = (bf16[4,96,512]{2,1,0:T(8,128)(2,1)S(1)}, bf16[4,96,512]{2,1,0:T(8,128)(2,1)S(1)}, u32[]{:S(2)}, u32[]{:S(2)}) collective-permute-start(bf16[4,96,512]{2,1,0:T(8,128)(2,1)S(1)} %fusion.21), channel_id=1, source_target_pairs={{0,56},{4,60},{8,0},{12,4},{16,8},{20,12},{24,16},{28,20},{32,24},... | collective-permute-start | bytes 1179656 | tf_op jit(solution)/shard_map/ppermute | solution.py:29
  358.2 18.5 %collective-permute-start.57 = (bf16[7,96,512]{2,1,0:T(8,128)(2,1)S(1)}, bf16[7,96,512]{2,1,0:T(8,128)(2,1)}, u32[]{:S(2)}, u32[]{:S(2)}) collective-permute-start(bf16[7,96,512]{2,1,0:T(8,128)(2,1)S(1)} %maximum_convert_fusion), channel_id=1, source_target_pairs={{0,8},{4,12},{8,16},{12,20},{16,24},{20,28},{24,32},{28,36},{32,40... | collective-permute-start | bytes 2064392 | tf_op jit(solution)/shard_map/ppermute | solution.py:29
  359.9 15.6 %collective-permute-start.56 = (bf16[6,96,512]{2,1,0:T(8,128)(2,1)S(1)}, bf16[6,96,512]{2,1,0:T(8,128)(2,1)S(1)}, u32[]{:S(2)}, u32[]{:S(2)}) collective-permute-start(bf16[6,96,512]{2,1,0:T(8,128)(2,1)S(1)} %pad_maximum_fusion.6), channel_id=1, source_target_pairs={{0,4},{4,0},{8,12},{12,8},{16,20},{20,16},{24,28},{28,24},{32,36},... | collective-permute-start | bytes 1769480 | tf_op jit(solution)/shard_map/ppermute | solution.py:34
  362.4 20.4 %collective-permute-start.73 = (f32[33,384]{1,0:T(8,128)S(1)}, f32[33,384]{1,0:T(8,128)S(1)}, u32[]{:S(2)}, u32[]{:S(2)}) collective-permute-start(f32[33,384]{1,0:T(8,128)S(1)} %get-tuple-element.323), channel_id=1, source_target_pairs={{0,4},{4,0},{8,12},{12,8},{16,20},{20,16},{24,28},{28,24},{32,36},... | collective-permute-start | bytes 152072 | tf_op jit(solution)/shard_map/ppermute | solution.py:34
  363.2 21.7 %collective-permute-start.63 = (bf16[7,96,512]{2,1,0:T(8,128)(2,1)S(1)}, bf16[7,96,512]{2,1,0:T(8,128)(2,1)S(1)}, u32[]{:S(2)}, u32[]{:S(2)}) collective-permute-start(bf16[7,96,512]{2,1,0:T(8,128)(2,1)S(1)} %pad_maximum_fusion.4), channel_id=1, source_target_pairs={{0,56},{4,60},{8,0},{12,4},{16,8},{20,12},{24,16},{28,20},{32,24},... | collective-permute-start | bytes 2064392 | tf_op jit(solution)/shard_map/ppermute | solution.py:29
  380.7 10.0 %collective-permute-start.58 = (bf16[6,96,512]{2,1,0:T(8,128)(2,1)S(1)}, bf16[6,96,512]{2,1,0:T(8,128)(2,1)S(1)}, u32[]{:S(2)}, u32[]{:S(2)}) collective-permute-start(bf16[6,96,512]{2,1,0:T(8,128)(2,1)S(1)} %pad_maximum_fusion.7), channel_id=1, source_target_pairs={{0,4},{4,0},{8,12},{12,8},{16,20},{20,16},{24,28},{28,24},{32,36},... | collective-permute-start | bytes 1769480 | tf_op jit(solution)/shard_map/ppermute | solution.py:34
  382.9 16.7 %collective-permute-start.59 = (bf16[7,96,512]{2,1,0:T(8,128)(2,1)S(1)}, bf16[7,96,512]{2,1,0:T(8,128)(2,1)S(1)}, u32[]{:S(2)}, u32[]{:S(2)}) collective-permute-start(bf16[7,96,512]{2,1,0:T(8,128)(2,1)S(1)} %add_convert_fusion.3), channel_id=1, source_target_pairs={{0,8},{4,12},{8,16},{12,20},{16,24},{20,28},{24,32},{28,36},{32,40... | collective-permute-start | bytes 2064392 | tf_op jit(solution)/shard_map/ppermute | solution.py:29
  385.1 19.7 %collective-permute-start.64 = (bf16[7,96,512]{2,1,0:T(8,128)(2,1)S(1)}, bf16[7,96,512]{2,1,0:T(8,128)(2,1)S(1)}, u32[]{:S(2)}, u32[]{:S(2)}) collective-permute-start(bf16[7,96,512]{2,1,0:T(8,128)(2,1)S(1)} %add_convert_fusion.1), channel_id=1, source_target_pairs={{0,56},{4,60},{8,0},{12,4},{16,8},{20,12},{24,16},{28,20},{32,24},... | collective-permute-start | bytes 2064392 | tf_op jit(solution)/shard_map/ppermute | solution.py:29
  387.1 25.8 %collective-permute-start.75 = (f32[33,384]{1,0:T(8,128)S(1)}, f32[33,384]{1,0:T(8,128)S(1)}, u32[]{:S(2)}, u32[]{:S(2)}) collective-permute-start(f32[33,384]{1,0:T(8,128)S(1)} %get-tuple-element.319), channel_id=1, source_target_pairs={{0,16},{4,20},{8,24},{12,28},{16,0},{20,4},{24,8},{28,12},{32,48},... | collective-permute-start | bytes 152072 | tf_op jit(solution)/shard_map/ppermute | solution.py:34
  399.8 31.2 %collective-permute-start.61 = (bf16[7,96,512]{2,1,0:T(8,128)(2,1)S(1)}, bf16[7,96,512]{2,1,0:T(8,128)(2,1)S(1)}, u32[]{:S(2)}, u32[]{:S(2)}) collective-permute-start(bf16[7,96,512]{2,1,0:T(8,128)(2,1)S(1)} %add_convert_fusion.2), channel_id=1, source_target_pairs={{0,8},{4,12},{8,16},{12,20},{16,24},{20,28},{24,32},{28,36},{32,40... | collective-permute-start | bytes 2064392 | tf_op jit(solution)/shard_map/ppermute | solution.py:29
  407.3 23.8 %collective-permute-start.65 = (bf16[7,96,512]{2,1,0:T(8,128)(2,1)}, bf16[7,96,512]{2,1,0:T(8,128)(2,1)}, u32[]{:S(2)}, u32[]{:S(2)}) collective-permute-start(bf16[7,96,512]{2,1,0:T(8,128)(2,1)} %add_convert_fusion), channel_id=1, source_target_pairs={{0,56},{4,60},{8,0},{12,4},{16,8},{20,12},{24,16},{28,20},{32,24},... | collective-permute-start | bytes 2064392 | tf_op jit(solution)/shard_map/ppermute | solution.py:29
  413.0 21.0 %collective-permute-start.76 = (f32[33,384]{1,0:T(8,128)S(1)}, f32[33,384]{1,0:T(8,128)S(1)}, u32[]{:S(2)}, u32[]{:S(2)}) collective-permute-start(f32[33,384]{1,0:T(8,128)S(1)} %get-tuple-element.317), channel_id=1, source_target_pairs={{0,32},{4,36},{8,40},{12,44},{16,48},{20,52},{24,56},{28,60},{32,0... | collective-permute-start | bytes 152072 | tf_op jit(solution)/shard_map/ppermute | solution.py:34
  417.1 6.5 %collective-permute-start.45 = (bf16[1,96,512]{2,1,0:T(8,128)(2,1)S(1)}, bf16[1,96,512]{2,1,0:T(8,128)(2,1)S(1)}, u32[]{:S(2)}, u32[]{:S(2)}) collective-permute-start(bf16[1,96,512]{2,1,0:T(8,128)(2,1)S(1)} %get-tuple-element.351), channel_id=1, source_target_pairs={{0,56},{4,60},{8,0},{12,4},{16,8},{20,12},{24,16},{28,20},{32,24},... | collective-permute-start | bytes 294920 | tf_op jit(solution)/shard_map/ppermute | solution.py:29
  423.3 6.7 %collective-permute-start.60 = (bf16[3,96,512]{2,1,0:T(8,128)(2,1)S(1)}, bf16[3,96,512]{2,1,0:T(8,128)(2,1)S(1)}, u32[]{:S(2)}, u32[]{:S(2)}) collective-permute-start(bf16[3,96,512]{2,1,0:T(8,128)(2,1)S(1)} %dynamic-slice_bitcast_fusion), channel_id=1, source_target_pairs={{0,4},{4,0},{8,12},{12,8},{16,20},{20,16},{24,28},{28,24},{32,36},... | collective-permute-start | bytes 884744 | tf_op jit(solution)/shard_map/ppermute | solution.py:34
  423.7 18.8 %collective-permute-start.46 = (bf16[2,96,512]{2,1,0:T(8,128)(2,1)S(1)}, bf16[2,96,512]{2,1,0:T(8,128)(2,1)S(1)}, u32[]{:S(2)}, u32[]{:S(2)}) collective-permute-start(bf16[2,96,512]{2,1,0:T(8,128)(2,1)S(1)} %pad_maximum_fusion.18), channel_id=1, source_target_pairs={{0,56},{4,60},{8,0},{12,4},{16,8},{20,12},{24,16},{28,20},{32,24},... | collective-permute-start | bytes 589832 | tf_op jit(solution)/shard_map/ppermute | solution.py:29
  430.0 7.4 %collective-permute-start.42 = (bf16[2,96,512]{2,1,0:T(8,128)(2,1)S(1)}, bf16[2,96,512]{2,1,0:T(8,128)(2,1)S(1)}, u32[]{:S(2)}, u32[]{:S(2)}) collective-permute-start(bf16[2,96,512]{2,1,0:T(8,128)(2,1)S(1)} %pad_maximum_fusion.17), channel_id=1, source_target_pairs={{0,8},{4,12},{8,16},{12,20},{16,24},{20,28},{24,32},{28,36},{32,40... | collective-permute-start | bytes 589832 | tf_op jit(solution)/shard_map/ppermute | solution.py:29
  434.0 6.9 %collective-permute-start.77 = (f32[33,384]{1,0:T(8,128)S(1)}, f32[33,384]{1,0:T(8,128)S(1)}, u32[]{:S(2)}, u32[]{:S(2)}) collective-permute-start(f32[33,384]{1,0:T(8,128)S(1)} %add_add_fusion.1), channel_id=1, source_target_pairs={{0,1},{1,2},{2,3},{3,0},{4,5},{5,6},{6,7},{7,4},{8,9},{9,10},{10,1... | collective-permute-start | bytes 152072 | tf_op jit(solution)/shard_map/ppermute | solution.py:29
  434.1 8.3 %collective-permute-start.78 = (f32[33,384]{1,0:T(8,128)S(1)}, f32[33,384]{1,0:T(8,128)S(1)}, u32[]{:S(2)}, u32[]{:S(2)}) collective-permute-start(f32[33,384]{1,0:T(8,128)S(1)} %add_add_fusion.1), channel_id=1, source_target_pairs={{0,2},{1,3},{2,0},{3,1},{4,6},{5,7},{6,4},{7,5},{8,10},{9,11},{10,... | collective-permute-start | bytes 152072 | tf_op jit(solution)/shard_map/ppermute | solution.py:29
  435.2 7.2 %collective-permute-start.79 = (f32[33,384]{1,0:T(8,128)S(1)}, f32[33,384]{1,0:T(8,128)S(1)}, u32[]{:S(2)}, u32[]{:S(2)}) collective-permute-start(f32[33,384]{1,0:T(8,128)S(1)} %add_add_fusion.1), channel_id=1, source_target_pairs={{0,3},{1,0},{2,1},{3,2},{4,7},{5,4},{6,5},{7,6},{8,11},{9,8},{10,9... | collective-permute-start | bytes 152072 | tf_op jit(solution)/shard_map/ppermute | solution.py:29
  437.5 7.0 %collective-permute-start.43 = (bf16[2,96,512]{2,1,0:T(8,128)(2,1)S(1)}, bf16[2,96,512]{2,1,0:T(8,128)(2,1)S(1)}, u32[]{:S(2)}, u32[]{:S(2)}) collective-permute-start(bf16[2,96,512]{2,1,0:T(8,128)(2,1)S(1)} %fusion.25), channel_id=1, source_target_pairs={{0,8},{4,12},{8,16},{12,20},{16,24},{20,28},{24,32},{28,36},{32,40... | collective-permute-start | bytes 589832 | tf_op jit(solution)/shard_map/ppermute | solution.py:29
  440.9 12.8 %collective-permute-start.66 = (bf16[2,96,512]{2,1,0:T(8,128)(2,1)S(1)}, bf16[2,96,512]{2,1,0:T(8,128)(2,1)S(1)}, u32[]{:S(2)}, u32[]{:S(2)}) collective-permute-start(bf16[2,96,512]{2,1,0:T(8,128)(2,1)S(1)} %fusion.29), channel_id=1, source_target_pairs={{0,4},{4,0},{8,12},{12,8},{16,20},{20,16},{24,28},{28,24},{32,36},... | collective-permute-start | bytes 589832 | tf_op jit(solution)/shard_map/ppermute | solution.py:34
  446.7 13.5 %collective-permute-start.44 = (bf16[2,96,512]{2,1,0:T(8,128)(2,1)S(1)}, bf16[2,96,512]{2,1,0:T(8,128)(2,1)S(1)}, u32[]{:S(2)}, u32[]{:S(2)}) collective-permute-start(bf16[2,96,512]{2,1,0:T(8,128)(2,1)S(1)} %get-tuple-element.345), channel_id=1, source_target_pairs={{0,8},{4,12},{8,16},{12,20},{16,24},{20,28},{24,32},{28,36},{32,40... | collective-permute-start | bytes 589832 | tf_op jit(solution)/shard_map/ppermute | solution.py:29
  450.4 9.8 %collective-permute-start.48 = (bf16[2,96,512]{2,1,0:T(8,128)(2,1)S(1)}, bf16[2,96,512]{2,1,0:T(8,128)(2,1)S(1)}, u32[]{:S(2)}, u32[]{:S(2)}) collective-permute-start(bf16[2,96,512]{2,1,0:T(8,128)(2,1)S(1)} %fusion.24), channel_id=1, source_target_pairs={{0,56},{4,60},{8,0},{12,4},{16,8},{20,12},{24,16},{28,20},{32,24},... | collective-permute-start | bytes 589832 | tf_op jit(solution)/shard_map/ppermute | solution.py:29
  453.9 13.4 %collective-permute-start.67 = (bf16[5,96,512]{2,1,0:T(8,128)(2,1)S(1)}, bf16[5,96,512]{2,1,0:T(8,128)(2,1)S(1)}, u32[]{:S(2)}, u32[]{:S(2)}) collective-permute-start(bf16[5,96,512]{2,1,0:T(8,128)(2,1)S(1)} %fusion.4), channel_id=1, source_target_pairs={{0,2},{1,3},{2,0},{3,1},{4,6},{5,7},{6,4},{7,5},{8,10},{9,11},{10,... | collective-permute-start | bytes 1474568 | tf_op jit(solution)/shard_map/ppermute | solution.py:29
  456.9 12.7 %collective-permute-start.68 = (bf16[5,96,512]{2,1,0:T(8,128)(2,1)S(1)}, bf16[5,96,512]{2,1,0:T(8,128)(2,1)S(1)}, u32[]{:S(2)}, u32[]{:S(2)}) collective-permute-start(bf16[5,96,512]{2,1,0:T(8,128)(2,1)S(1)} %fusion.4), channel_id=1, source_target_pairs={{0,1},{1,2},{2,3},{3,0},{4,5},{5,6},{6,7},{7,4},{8,9},{9,10},{10,1... | collective-permute-start | bytes 1474568 | tf_op jit(solution)/shard_map/ppermute | solution.py:29
  456.9 12.7 %collective-permute-start.69 = (bf16[5,96,512]{2,1,0:T(8,128)(2,1)S(1)}, bf16[5,96,512]{2,1,0:T(8,128)(2,1)S(1)}, u32[]{:S(2)}, u32[]{:S(2)}) collective-permute-start(bf16[5,96,512]{2,1,0:T(8,128)(2,1)S(1)} %fusion.4), channel_id=1, source_target_pairs={{0,3},{1,0},{2,1},{3,2},{4,7},{5,4},{6,5},{7,6},{8,11},{9,8},{10,9... | collective-permute-start | bytes 1474568 | tf_op jit(solution)/shard_map/ppermute | solution.py:29
  (43 other events, 237.1 us)
Sparse Core Ops, SparseCore 0:
  49.2 69.2 all-gather.1
  316.9 66.8 reduce-scatter.1

commit v7 on v6

--- a/solution.py
+++ b/solution.py
@@ -223,9 +223,8 @@
             late.append(after(ready))
 
     exchange([ring // 2], 0)
-    steps.send(jnp.int32(0))
     total = ring_scatter(main_term, (rest_parts * PAIR + out_parts) // 2, prepare)
-    small_total = scale * steps.send(after(total))
+    steps.send(after(total))
     rest_share = keep_side(
         total[: rest_parts * PAIR].reshape(rest_parts, PAIR, rows, width), kind
     )
@@ -233,6 +232,7 @@
         lambda offset: pick(shared_sum, (at + offset) % ring), 1, note
     )
     share = jnp.concatenate([rest_share, total[rest_parts * PAIR :]])
+    small_total = scale * steps.send(late[0])
     share = sum_batch((share + late[0].astype(jnp.float32)).astype(kind))
     shared_share = keep_side(shared_total[None], kind)[0].astype(kind)
     in_parts = [part.astype(jnp.float32) for part in batch_order(batch_copies(shared_share))]

time: 492 us -> 494 us (level)
  starting transfers between devices: 121 us -> 128 us
  waiting for transfers between devices: 154 us -> 147 us
    ppermute x44, waiting for transfers between devices: 63.4 us -> 51.5 us  [rotate(): return lax.ppermute(x, axis, [(i, (i + by) % peers) for i in range(peers)])]
    ppermute x44, starting transfers between devices: 71 us -> 78.1 us  [rotate(): return lax.ppermute(x, axis, [(i, (i + by) % peers) for i in range(peers)])]
where the time goes in v7:
time: 494 us; the launch traced here: 485 us
  waiting for transfers between devices  147 us (30%)
  starting transfers between devices  128 us (26%)
  Pallas kernels  100 us (20%)
  local copies, waits for them, and re-layouts  55.6 us (11%)
  other arithmetic  26.6 us (5%)
  between operations  20.7 us (4%)
  matrix products  6.71 us (1%)
    pallas_call x20, Pallas kernels, stage_call(): pl.pallas_call(functools.partial(kernel, taps=taps, length=length, width=...  92.7 us
    ppermute x44, starting transfers between devices, rotate(): return lax.ppermute(x, axis, [(i, (i + by) % peers) for i in range(peers)])  78.1 us
    ppermute x16, waiting for transfers between devices, send_active(): return lax.ppermute(x, 'section', pairs)  58 us
    ppermute x44, waiting for transfers between devices, rotate(): return lax.ppermute(x, axis, [(i, (i + by) % peers) for i in range(peers)])  51.5 us
    ppermute x20, waiting for transfers between devices, swap_bit(): return lax.ppermute(x, 'fsdp', [(i, i ^ bit) for i in range(peers)])  37.1 us
    ppermute x20, starting transfers between devices, swap_bit(): return lax.ppermute(x, 'fsdp', [(i, i ^ bit) for i in range(peers)])  26.6 us
    ppermute x16, starting transfers between devices, send_active(): return lax.ppermute(x, 'section', pairs)  23.6 us
    dynamic_update_slice x15, local copies, waits for them, and re-layouts, place_out(): out = lax.dynamic_update_slice(out, piece[:, None, None], spot)  11.1 us
  transfers between devices with their start and end apart: 82, of which 35 were waited for; matrix products, arithmetic and copies ran while one was open for 15% of the time, Pallas kernels for 16%

profile of v7, /device:TPU:8, one launch (start us, length us, event | category | flops | bytes accessed | tf_op | source)
XLA Modules:
  0.0 484.6 jit_solution(7088315422577540382)
XLA Ops:
  9.1 2.3 collective-permute-start
  11.4 6.6 %collective-permute-done = bf16[3,96,512]{2,1,0:T(8,128)(2,1)S(1)} collective-permute-done((bf16[3,96,512]{2,1,0:T(8,128)(2,1)S(1)}, bf16[3,96,512]{2,1,0:T(8,128)(2,1)S(1)}, u32[]{:S(2)}, u32[]{:S(2)}) %collective-permute-start) | collective-permute-done | bytes 294944 | tf_op jit(solution)/shard_map/ppermute | solution.py:34
  18.2 2.0 collective-permute-start.1
  20.2 4.0 collective-permute-start.2
  24.2 3.9 collective-permute-done.1
  28.2 3.2 collective-permute-start.4
  31.5 3.6 collective-permute-done.3
  35.1 3.2 collective-permute-start.6
  38.4 3.6 collective-permute-done.5
  42.1 3.4 collective-permute-start.8
  45.5 2.3 collective-permute-done.7
  51.1 3.4 concatenate.95.params
  55.9 3.5 collective-permute-start.10
  60.3 2.8 broadcast_in_dim.107
  64.5 2.0 broadcast_in_dim.106
  67.3 2.1 collective-permute-done.9
  73.5 2.5 collective-permute-start.11
  80.1 6.0 %collective-permute-done.11 = bf16[7,96,512]{2,1,0:T(8,128)(2,1)S(1)} collective-permute-done((bf16[7,96,512]{2,1,0:T(8,128)(2,1)S(1)}, bf16[7,96,512]{2,1,0:T(8,128)(2,1)S(1)}, u32[]{:S(2)}, u32[]{:S(2)}) %collective-permute-start.11) | collective-permute-done | bytes 688160 | tf_op jit(solution)/shard_map/ppermute | solution.py:29
  96.9 7.0 %collective-permute-done.13 = bf16[7,96,512]{2,1,0:T(8,128)(2,1)S(1)} collective-permute-done((bf16[7,96,512]{2,1,0:T(8,128)(2,1)S(1)}, bf16[7,96,512]{2,1,0:T(8,128)(2,1)S(1)}, u32[]{:S(2)}, u32[]{:S(2)}) %collective-permute-start.13) | collective-permute-done | bytes 688160 | tf_op jit(solution)/shard_map/ppermute | solution.py:29
  103.9 3.7 collective-permute-start.22
  109.0 3.5 collective-permute-start.16
  122.6 3.6 collective-permute-done.24
  127.6 8.7 %shard_map.127 = (bf16[48,1536]{1,0:T(8,128)(2,1)}, bf16[4,48,1536]{2,1,0:T(8,128)(2,1)}, bf16[4,48,1536]{2,1,0:T(8,128)(2,1)}, bf16[4,48,1536]{2,1,0:T(8,128)(2...) custom-call(s32[4]{0:T(128)} %get-tuple-element.311.info, ...), custom_call_target="tpu_custom_call" | custom-call | flops 679477248 | bytes 14155776 | tf_op jit(solution)/shard_map/pallas_call | solution.py:582
  136.3 2.0 collective-permute-start.26
  138.2 8.7 %shard_map.128 = (bf16[48,1536]{1,0:T(8,128)(2,1)}, bf16[4,48,1536]{2,1,0:T(8,128)(2,1)}, bf16[4,48,1536]{2,1,0:T(8,128)(2,1)}, bf16[4,48,1536]{2,1,0:T(8,128)(2...) custom-call(s32[4]{0:T(128)} %get-tuple-element.312.info, ...), custom_call_target="tpu_custom_call", output_to_operand_aliasing={{1}: (7, {}), {2}: (8, {}), {3}: (9, {}), {4}: (10, {}), {5... | custom-call | flops 679477248 | bytes 14155776 | tf_op jit(solution)/shard_map/pallas_call | solution.py:582
  146.9 2.0 collective-permute-start.25
  151.3 8.7 %shard_map.129 = (bf16[48,1536]{1,0:T(8,128)(2,1)}, bf16[4,48,1536]{2,1,0:T(8,128)(2,1)}, bf16[4,48,1536]{2,1,0:T(8,128)(2,1)}, bf16[4,48,1536]{2,1,0:T(8,128)(2...) custom-call(s32[4]{0:T(128)} %get-tuple-element.310.info, ...), custom_call_target="tpu_custom_call", output_to_operand_aliasing={{1}: (7, {}), {2}: (8, {}), {3}: (9, {}), {4}: (10, {}), {5... | custom-call | flops 679477248 | bytes 14155776 | tf_op jit(solution)/shard_map/pallas_call | solution.py:582
  160.0 2.0 collective-permute-start.28
  161.9 8.9 %shard_map.130 = (bf16[48,1536]{1,0:T(8,128)(2,1)}, bf16[4,48,1536]{2,1,0:T(8,128)(2,1)}, bf16[4,48,1536]{2,1,0:T(8,128)(2,1)}, bf16[4,48,1536]{2,1,0:T(8,128)(2...) custom-call(s32[4]{0:T(128)} %get-tuple-element.313.info, ...), custom_call_target="tpu_custom_call", output_to_operand_aliasing={{1}: (7, {}), {2}: (8, {}), {3}: (9, {}), {4}: (10, {}), {5... | custom-call | flops 679477248 | bytes 14155776 | tf_op jit(solution)/shard_map/pallas_call | solution.py:582
  201.6 54.9 %collective-permute-done.38.incoming = bf16[48,1536]{1,0:T(8,128)(2,1)} collective-permute-done((bf16[48,1536]{1,0:T(8,128)(2,1)}, bf16[48,1536]{1,0:T(8,128)(2,1)}, u32[]{:S(2)}, u32[]{:S(2)}) %collective-permute-start.38) | collective-permute-done | bytes 147488 | tf_op jit(solution)/shard_map/ppermute | solution.py:655
  256.5 11.8 %shard_map.143 = (bf16[48,1536]{1,0:T(8,128)(2,1)}, bf16[4,48,1536]{2,1,0:T(8,128)(2,1)}, bf16[4,48,3072]{2,1,0:T(8,128)(2,1)}, bf16[4,48,1536]{2,1,0:T(8,128)(2...) custom-call(s32[4]{0:T(128)} %get-tuple-element.298.info, ...), custom_call_target="tpu_custom_call", output_to_operand_aliasing={{1}: (12, {}), {2}: (13, {}), {3}: (14, {}), {4}: (15, {}),... | custom-call | flops 679477248 | bytes 14155776 | tf_op jit(solution)/shard_map/pallas_call | solution.py:582
  270.7 11.8 %shard_map.144 = (bf16[48,1536]{1,0:T(8,128)(2,1)}, bf16[4,48,1536]{2,1,0:T(8,128)(2,1)}, bf16[4,48,3072]{2,1,0:T(8,128)(2,1)}, bf16[4,48,1536]{2,1,0:T(8,128)(2...) custom-call(s32[4]{0:T(128)} %get-tuple-element.305.info, ...), custom_call_target="tpu_custom_call", output_to_operand_aliasing={{1}: (12, {}), {2}: (13, {}), {3}: (14, {}), {4}: (15, {}),... | custom-call | flops 679477248 | bytes 14155776 | tf_op jit(solution)/shard_map/pallas_call | solution.py:582
  283.9 11.8 %shard_map.145 = (bf16[48,1536]{1,0:T(8,128)(2,1)}, bf16[4,48,1536]{2,1,0:T(8,128)(2,1)}, bf16[4,48,3072]{2,1,0:T(8,128)(2,1)}, bf16[4,48,1536]{2,1,0:T(8,128)(2...) custom-call(s32[4]{0:T(128)} %get-tuple-element.297.info, ...), custom_call_target="tpu_custom_call", output_to_operand_aliasing={{1}: (12, {}), {2}: (13, {}), {3}: (14, {}), {4}: (15, {}),... | custom-call | flops 679477248 | bytes 14155776 | tf_op jit(solution)/shard_map/pallas_call | solution.py:582
  295.7 2.0 collective-permute-done.39.incoming
  297.6 12.0 %shard_map.146 = (bf16[48,1536]{1,0:T(8,128)(2,1)}, bf16[4,48,1536]{2,1,0:T(8,128)(2,1)}, bf16[4,48,3072]{2,1,0:T(8,128)(2,1)}, bf16[4,48,1536]{2,1,0:T(8,128)(2...) custom-call(s32[4]{0:T(128)} %get-tuple-element.306.info, ...), custom_call_target="tpu_custom_call", output_to_operand_aliasing={{1}: (12, {}), {2}: (13, {}), {3}: (14, {}), {4}: (15, {}),... | custom-call | flops 679477248 | bytes 14155776 | tf_op jit(solution)/shard_map/pallas_call | solution.py:582
  313.3 3.2 pad_maximum_fusion
  320.2 2.1 copy-done.10
  327.7 5.6 %collective-permute-done.53 = bf16[3,96,512]{2,1,0:T(8,128)(2,1)} collective-permute-done((bf16[3,96,512]{2,1,0:T(8,128)(2,1)}, bf16[3,96,512]{2,1,0:T(8,128)(2,1)}, u32[]{:S(2)}, u32[]{:S(2)}) %collective-permute-start.53) | collective-permute-done | bytes 294944 | tf_op jit(solution)/shard_map/ppermute | solution.py:34
  341.7 7.3 %shard_map.147 = f32[32,1536]{1,0:T(8,128)S(1)} custom-call(s32[4]{0:T(128)S(1)} %bitcast.348, f32[4,48,1536]{2,1,0:T(8,128)S(1)} %copy-done.4, f32[4,48,1536]{2,1,0:T(8,128)S(1)} %copy-done.2, f32[4,48,1536]{2,1,0:T(8,128)S(1)} %copy-done.3), custom_call_target="tpu_custom_call" | custom-call | flops 18284544 | bytes 3538944 | tf_op jit(solution)/shard_map/pallas_call | solution.py:550
  357.2 2.0 collective-permute-start.56
  360.6 2.4 collective-permute-start.70
  362.9 2.3 collective-permute-start.71
  368.3 4.2 collective-permute-done.56
  372.5 3.3 collective-permute-start.63
  381.2 2.1 collective-permute-start.73
  384.5 3.8 collective-permute-start.64
  388.3 2.5 collective-permute-done.73
  392.2 6.7 %collective-permute-done.59 = bf16[7,96,512]{2,1,0:T(8,128)(2,1)S(1)} collective-permute-done((bf16[7,96,512]{2,1,0:T(8,128)(2,1)S(1)}, bf16[7,96,512]{2,1,0:T(8,128)(2,1)S(1)}, u32[]{:S(2)}, u32[]{:S(2)}) %collective-permute-start.59) | collective-permute-done | bytes 688160 | tf_op jit(solution)/shard_map/ppermute | solution.py:29
  399.2 2.0 collective-permute-done.64
  403.7 3.6 collective-permute-start.65
  407.2 2.3 copy.219
  418.3 2.1 collective-permute-start.42
  420.4 5.2 %collective-permute-done.60 = bf16[3,96,512]{2,1,0:T(8,128)(2,1)S(1)} collective-permute-done((bf16[3,96,512]{2,1,0:T(8,128)(2,1)S(1)}, bf16[3,96,512]{2,1,0:T(8,128)(2,1)S(1)}, u32[]{:S(2)}, u32[]{:S(2)}) %collective-permute-start.60) | collective-permute-done | bytes 294944 | tf_op jit(solution)/shard_map/ppermute | solution.py:34
  430.3 3.2 collective-permute-start.76
  436.4 2.3 collective-permute-done.76
  438.7 3.1 collective-permute-start.77
  443.5 2.5 collective-permute-start.79
  450.3 3.5 collective-permute-done.47
  453.9 2.9 collective-permute-start.48
  458.0 2.0 collective-permute-start.68
  463.9 2.4 collective-permute-done.49
  466.3 2.0 collective-permute-start.52
  469.9 2.7 collective-permute-done.68
  473.2 2.0 collective-permute-done.50
  (360 shorter events, 149.5 us)
Async XLA Ops:
  7.2 119.8 %all-gather.2.cloned.1.call-start = ((), (), s32[]{:S(2)}) async-start(), calls=%async_computation.1 | async-start | bytes 7864320 | tf_op jit(solution)/shard_map/all_gather | solution.py:110
  9.1 8.8 %collective-permute-start = (bf16[3,96,512]{2,1,0:T(8,128)(2,1)S(1)}, bf16[3,96,512]{2,1,0:T(8,128)(2,1)S(1)}, u32[]{:S(2)}, u32[]{:S(2)}) collective-permute-start(bf16[3,96,512]{2,1,0:T(8,128)(2,1)S(1)} %get-tuple-element.369), channel_id=1, source_target_pairs={{0,4},{4,0},{8,12},{12,8},{16,20},{20,16},{24,28},{28,24},{32,36},... | collective-permute-start | bytes 884744 | tf_op jit(solution)/shard_map/ppermute | solution.py:34
  18.2 10.0 %collective-permute-start.1 = (bf16[2,96,512]{2,1,0:T(8,128)(2,1)S(1)}, bf16[2,96,512]{2,1,0:T(8,128)(2,1)S(1)}, u32[]{:S(2)}, u32[]{:S(2)}) collective-permute-start(bf16[2,96,512]{2,1,0:T(8,128)(2,1)S(1)} %get-tuple-element.361), channel_id=1, source_target_pairs={{0,8},{4,12},{8,16},{12,20},{16,24},{20,28},{24,32},{28,36},{32,40... | collective-permute-start | bytes 589832 | tf_op jit(solution)/shard_map/ppermute | solution.py:29
  20.2 8.0 %collective-permute-start.2 = (bf16[2,96,512]{2,1,0:T(8,128)(2,1)S(1)}, bf16[2,96,512]{2,1,0:T(8,128)(2,1)S(1)}, u32[]{:S(2)}, u32[]{:S(2)}) collective-permute-start(bf16[2,96,512]{2,1,0:T(8,128)(2,1)S(1)} %get-tuple-element.361), channel_id=1, source_target_pairs={{0,56},{4,60},{8,0},{12,4},{16,8},{20,12},{24,16},{28,20},{32,24},... | collective-permute-start | bytes 589832 | tf_op jit(solution)/shard_map/ppermute | solution.py:29
  28.2 6.9 %collective-permute-start.3 = (bf16[2,96,512]{2,1,0:T(8,128)(2,1)S(1)}, bf16[2,96,512]{2,1,0:T(8,128)(2,1)S(1)}, u32[]{:S(2)}, u32[]{:S(2)}) collective-permute-start(bf16[2,96,512]{2,1,0:T(8,128)(2,1)S(1)} %collective-permute-done.1), channel_id=1, source_target_pairs={{0,8},{4,12},{8,16},{12,20},{16,24},{20,28},{24,32},{28,36},{32,40... | collective-permute-start | bytes 589832 | tf_op jit(solution)/shard_map/ppermute | solution.py:29
  28.2 6.9 %collective-permute-start.4 = (bf16[2,96,512]{2,1,0:T(8,128)(2,1)S(1)}, bf16[2,96,512]{2,1,0:T(8,128)(2,1)S(1)}, u32[]{:S(2)}, u32[]{:S(2)}) collective-permute-start(bf16[2,96,512]{2,1,0:T(8,128)(2,1)S(1)} %collective-permute-done.2), channel_id=1, source_target_pairs={{0,56},{4,60},{8,0},{12,4},{16,8},{20,12},{24,16},{28,20},{32,24},... | collective-permute-start | bytes 589832 | tf_op jit(solution)/shard_map/ppermute | solution.py:29
  35.1 6.9 %collective-permute-start.5 = (bf16[2,96,512]{2,1,0:T(8,128)(2,1)S(1)}, bf16[2,96,512]{2,1,0:T(8,128)(2,1)S(1)}, u32[]{:S(2)}, u32[]{:S(2)}) collective-permute-start(bf16[2,96,512]{2,1,0:T(8,128)(2,1)S(1)} %collective-permute-done.3), channel_id=1, source_target_pairs={{0,8},{4,12},{8,16},{12,20},{16,24},{20,28},{24,32},{28,36},{32,40... | collective-permute-start | bytes 589832 | tf_op jit(solution)/shard_map/ppermute | solution.py:29
  35.1 7.0 %collective-permute-start.6 = (bf16[2,96,512]{2,1,0:T(8,128)(2,1)S(1)}, bf16[2,96,512]{2,1,0:T(8,128)(2,1)S(1)}, u32[]{:S(2)}, u32[]{:S(2)}) collective-permute-start(bf16[2,96,512]{2,1,0:T(8,128)(2,1)S(1)} %collective-permute-done.4), channel_id=1, source_target_pairs={{0,56},{4,60},{8,0},{12,4},{16,8},{20,12},{24,16},{28,20},{32,24},... | collective-permute-start | bytes 589832 | tf_op jit(solution)/shard_map/ppermute | solution.py:29
  49.1 358.2 %reduce-scatter.2.cloned.1.call-start = ((), (), s32[]{:S(2)}) async-start(), calls=%async_computation.2 | async-start | bytes 7864320 | tf_op jit(solution)/shard_map/reduce_scatter | solution.py:188
  49.2 14.6 %collective-permute-start.17 = (bf16[3,96,512]{2,1,0:T(8,128)(2,1)S(1)}, bf16[3,96,512]{2,1,0:T(8,128)(2,1)S(1)}, u32[]{:S(2)}, u32[]{:S(2)}) collective-permute-start(bf16[3,96,512]{2,1,0:T(8,128)(2,1)S(1)} %pad_maximum_fusion.13), channel_id=1, source_target_pairs={{0,4},{4,0},{8,12},{12,8},{16,20},{20,16},{24,28},{28,24},{32,36},... | collective-permute-start | bytes 884744 | tf_op jit(solution)/shard_map/ppermute | solution.py:34
  55.8 13.6 %collective-permute-start.9 = (bf16[7,96,512]{2,1,0:T(8,128)(2,1)S(1)}, bf16[7,96,512]{2,1,0:T(8,128)(2,1)S(1)}, u32[]{:S(2)}, u32[]{:S(2)}) collective-permute-start(bf16[7,96,512]{2,1,0:T(8,128)(2,1)S(1)} %pad_maximum_fusion.3), channel_id=1, source_target_pairs={{0,8},{4,12},{8,16},{12,20},{16,24},{20,28},{24,32},{28,36},{32,40... | collective-permute-start | bytes 2064392 | tf_op jit(solution)/shard_map/ppermute | solution.py:29
  55.9 15.2 %collective-permute-start.10 = (bf16[7,96,512]{2,1,0:T(8,128)(2,1)S(1)}, bf16[7,96,512]{2,1,0:T(8,128)(2,1)S(1)}, u32[]{:S(2)}, u32[]{:S(2)}) collective-permute-start(bf16[7,96,512]{2,1,0:T(8,128)(2,1)S(1)} %pad_maximum_fusion.3), channel_id=1, source_target_pairs={{0,56},{4,60},{8,0},{12,4},{16,8},{20,12},{24,16},{28,20},{32,24},... | collective-permute-start | bytes 2064392 | tf_op jit(solution)/shard_map/ppermute | solution.py:29
  69.4 8.0 %collective-permute-start.18 = (bf16[3,96,512]{2,1,0:T(8,128)(2,1)S(1)}, bf16[3,96,512]{2,1,0:T(8,128)(2,1)S(1)}, u32[]{:S(2)}, u32[]{:S(2)}) collective-permute-start(bf16[3,96,512]{2,1,0:T(8,128)(2,1)S(1)} %slice.468), channel_id=1, source_target_pairs={{0,4},{4,0},{8,12},{12,8},{16,20},{20,16},{24,28},{28,24},{32,36},... | collective-permute-start | bytes 884744 | tf_op jit(solution)/shard_map/ppermute | solution.py:34
  71.1 8.3 %collective-permute-start.19 = (bf16[3,96,512]{2,1,0:T(8,128)(2,1)S(1)}, bf16[3,96,512]{2,1,0:T(8,128)(2,1)S(1)}, u32[]{:S(2)}, u32[]{:S(2)}) collective-permute-start(bf16[3,96,512]{2,1,0:T(8,128)(2,1)S(1)} %slice.469), channel_id=1, source_target_pairs={{0,4},{4,0},{8,12},{12,8},{16,20},{20,16},{24,28},{28,24},{32,36},... | collective-permute-start | bytes 884744 | tf_op jit(solution)/shard_map/ppermute | solution.py:34
  73.5 12.6 %collective-permute-start.11 = (bf16[7,96,512]{2,1,0:T(8,128)(2,1)S(1)}, bf16[7,96,512]{2,1,0:T(8,128)(2,1)S(1)}, u32[]{:S(2)}, u32[]{:S(2)}) collective-permute-start(bf16[7,96,512]{2,1,0:T(8,128)(2,1)S(1)} %collective-permute-done.9), channel_id=1, source_target_pairs={{0,8},{4,12},{8,16},{12,20},{16,24},{20,28},{24,32},{28,36},{32,40... | collective-permute-start | bytes 2064392 | tf_op jit(solution)/shard_map/ppermute | solution.py:29
  75.9 12.9 %collective-permute-start.12 = (bf16[7,96,512]{2,1,0:T(8,128)(2,1)S(1)}, bf16[7,96,512]{2,1,0:T(8,128)(2,1)S(1)}, u32[]{:S(2)}, u32[]{:S(2)}) collective-permute-start(bf16[7,96,512]{2,1,0:T(8,128)(2,1)S(1)} %collective-permute-done.10), channel_id=1, source_target_pairs={{0,56},{4,60},{8,0},{12,4},{16,8},{20,12},{24,16},{28,20},{32,24},... | collective-permute-start | bytes 2064392 | tf_op jit(solution)/shard_map/ppermute | solution.py:29
  86.1 8.5 %collective-permute-start.20 = (bf16[3,96,512]{2,1,0:T(8,128)(2,1)S(1)}, bf16[3,96,512]{2,1,0:T(8,128)(2,1)S(1)}, u32[]{:S(2)}, u32[]{:S(2)}) collective-permute-start(bf16[3,96,512]{2,1,0:T(8,128)(2,1)S(1)} %slice.470), channel_id=1, source_target_pairs={{0,4},{4,0},{8,12},{12,8},{16,20},{20,16},{24,28},{28,24},{32,36},... | collective-permute-start | bytes 884744 | tf_op jit(solution)/shard_map/ppermute | solution.py:34
  88.9 7.3 %collective-permute-start.21 = (bf16[3,96,512]{2,1,0:T(8,128)(2,1)S(1)}, bf16[3,96,512]{2,1,0:T(8,128)(2,1)S(1)}, u32[]{:S(2)}, u32[]{:S(2)}) collective-permute-start(bf16[3,96,512]{2,1,0:T(8,128)(2,1)S(1)} %slice.471), channel_id=1, source_target_pairs={{0,4},{4,0},{8,12},{12,8},{16,20},{20,16},{24,28},{28,24},{32,36},... | collective-permute-start | bytes 884744 | tf_op jit(solution)/shard_map/ppermute | solution.py:34
  90.6 13.3 %collective-permute-start.13 = (bf16[7,96,512]{2,1,0:T(8,128)(2,1)S(1)}, bf16[7,96,512]{2,1,0:T(8,128)(2,1)S(1)}, u32[]{:S(2)}, u32[]{:S(2)}) collective-permute-start(bf16[7,96,512]{2,1,0:T(8,128)(2,1)S(1)} %collective-permute-done.11), channel_id=1, source_target_pairs={{0,8},{4,12},{8,16},{12,20},{16,24},{20,28},{24,32},{28,36},{32,40... | collective-permute-start | bytes 2064392 | tf_op jit(solution)/shard_map/ppermute | solution.py:29
  92.5 15.2 %collective-permute-start.14 = (bf16[7,96,512]{2,1,0:T(8,128)(2,1)S(1)}, bf16[7,96,512]{2,1,0:T(8,128)(2,1)S(1)}, u32[]{:S(2)}, u32[]{:S(2)}) collective-permute-start(bf16[7,96,512]{2,1,0:T(8,128)(2,1)S(1)} %collective-permute-done.12), channel_id=1, source_target_pairs={{0,56},{4,60},{8,0},{12,4},{16,8},{20,12},{24,16},{28,20},{32,24},... | collective-permute-start | bytes 2064392 | tf_op jit(solution)/shard_map/ppermute | solution.py:29
  103.9 11.3 %collective-permute-start.22 = (bf16[3,96,512]{2,1,0:T(8,128)(2,1)S(1)}, bf16[3,96,512]{2,1,0:T(8,128)(2,1)S(1)}, u32[]{:S(2)}, u32[]{:S(2)}) collective-permute-start(bf16[3,96,512]{2,1,0:T(8,128)(2,1)S(1)} %get-tuple-element.357), channel_id=1, source_target_pairs={{0,4},{4,0},{8,12},{12,8},{16,20},{20,16},{24,28},{28,24},{32,36},... | collective-permute-start | bytes 884744 | tf_op jit(solution)/shard_map/ppermute | solution.py:34
  107.6 11.0 %collective-permute-start.23 = (bf16[3,96,512]{2,1,0:T(8,128)(2,1)S(1)}, bf16[3,96,512]{2,1,0:T(8,128)(2,1)S(1)}, u32[]{:S(2)}, u32[]{:S(2)}) collective-permute-start(bf16[3,96,512]{2,1,0:T(8,128)(2,1)S(1)} %slice.473), channel_id=1, source_target_pairs={{0,4},{4,0},{8,12},{12,8},{16,20},{20,16},{24,28},{28,24},{32,36},... | collective-permute-start | bytes 884744 | tf_op jit(solution)/shard_map/ppermute | solution.py:34
  109.0 10.4 %collective-permute-start.16 = (bf16[4,96,512]{2,1,0:T(8,128)(2,1)S(1)}, bf16[4,96,512]{2,1,0:T(8,128)(2,1)S(1)}, u32[]{:S(2)}, u32[]{:S(2)}) collective-permute-start(bf16[4,96,512]{2,1,0:T(8,128)(2,1)S(1)} %get-tuple-element.359), channel_id=1, source_target_pairs={{0,56},{4,60},{8,0},{12,4},{16,8},{20,12},{24,16},{28,20},{32,24},... | collective-permute-start | bytes 1179656 | tf_op jit(solution)/shard_map/ppermute | solution.py:29
  112.5 8.6 %collective-permute-start.15 = (bf16[3,96,512]{2,1,0:T(8,128)(2,1)S(1)}, bf16[3,96,512]{2,1,0:T(8,128)(2,1)S(1)}, u32[]{:S(2)}, u32[]{:S(2)}) collective-permute-start(bf16[3,96,512]{2,1,0:T(8,128)(2,1)S(1)} %get-tuple-element.358), channel_id=1, source_target_pairs={{0,8},{4,12},{8,16},{12,20},{16,24},{20,28},{24,32},{28,36},{32,40... | collective-permute-start | bytes 884744 | tf_op jit(solution)/shard_map/ppermute | solution.py:29
  136.3 15.1 %collective-permute-start.26 = (bf16[48,1536]{1,0:T(8,128)(2,1)}, bf16[48,1536]{1,0:T(8,128)(2,1)}, u32[]{:S(2)}, u32[]{:S(2)}) collective-permute-start(bf16[48,1536]{1,0:T(8,128)(2,1)} %get-tuple-element.151), channel_id=1, source_target_pairs={{0,64},{1,65},{2,66},{3,67},{4,68},{5,69},{6,70},{7,71},{8,72},{9,... | collective-permute-start | bytes 442376 | tf_op jit(solution)/shard_map/ppermute | solution.py:655
  146.9 15.1 %collective-permute-start.25 = (bf16[48,1536]{1,0:T(8,128)(2,1)}, bf16[48,1536]{1,0:T(8,128)(2,1)}, u32[]{:S(2)}, u32[]{:S(2)}) collective-permute-start(bf16[48,1536]{1,0:T(8,128)(2,1)} %get-tuple-element.150), channel_id=1, source_target_pairs={{0,64},{1,65},{2,66},{3,67},{4,68},{5,69},{6,70},{7,71},{8,72},{9,... | collective-permute-start | bytes 442376 | tf_op jit(solution)/shard_map/ppermute | solution.py:655
  160.0 14.6 %collective-permute-start.28 = (bf16[48,1536]{1,0:T(8,128)(2,1)}, bf16[48,1536]{1,0:T(8,128)(2,1)}, u32[]{:S(2)}, u32[]{:S(2)}) collective-permute-start(bf16[48,1536]{1,0:T(8,128)(2,1)} %get-tuple-element.167), channel_id=1, source_target_pairs={{0,64},{64,128},{1,65},{65,129},{2,66},{66,130},{3,67},{67,131},{4... | collective-permute-start | bytes 442376 | tf_op jit(solution)/shard_map/ppermute | solution.py:655
  198.1 58.4 %collective-permute-start.38 = (bf16[48,1536]{1,0:T(8,128)(2,1)}, bf16[48,1536]{1,0:T(8,128)(2,1)}, u32[]{:S(2)}, u32[]{:S(2)}) collective-permute-start(bf16[48,1536]{1,0:T(8,128)(2,1)} %get-tuple-element.249), channel_id=1, source_target_pairs={{128,64},{64,0},{129,65},{65,1},{130,66},{66,2},{131,67},{67,3},{1... | collective-permute-start | bytes 442376 | tf_op jit(solution)/shard_map/ppermute | solution.py:655
  200.3 70.4 %collective-permute-start.37 = (bf16[48,1536]{1,0:T(8,128)(2,1)}, bf16[48,1536]{1,0:T(8,128)(2,1)}, u32[]{:S(2)}, u32[]{:S(2)}) collective-permute-start(bf16[48,1536]{1,0:T(8,128)(2,1)} %get-tuple-element.248), channel_id=1, source_target_pairs={{128,64},{64,0},{129,65},{65,1},{130,66},{66,2},{131,67},{67,3},{1... | collective-permute-start | bytes 442376 | tf_op jit(solution)/shard_map/ppermute | solution.py:655
  268.4 15.5 %collective-permute-start.40 = (bf16[48,1536]{1,0:T(8,128)(2,1)}, bf16[48,1536]{1,0:T(8,128)(2,1)}, u32[]{:S(2)}, u32[]{:S(2)}) collective-permute-start(bf16[48,1536]{1,0:T(8,128)(2,1)} %get-tuple-element.261), channel_id=1, source_target_pairs={{64,0},{65,1},{66,2},{67,3},{68,4},{69,5},{70,6},{71,7},{72,8},{73... | collective-permute-start | bytes 442376 | tf_op jit(solution)/shard_map/ppermute | solution.py:655
  282.5 15.1 %collective-permute-start.39 = (bf16[48,1536]{1,0:T(8,128)(2,1)}, bf16[48,1536]{1,0:T(8,128)(2,1)}, u32[]{:S(2)}, u32[]{:S(2)}) collective-permute-start(bf16[48,1536]{1,0:T(8,128)(2,1)} %get-tuple-element.260), channel_id=1, source_target_pairs={{64,0},{65,1},{66,2},{67,3},{68,4},{69,5},{70,6},{71,7},{72,8},{73... | collective-permute-start | bytes 442376 | tf_op jit(solution)/shard_map/ppermute | solution.py:655
  323.0 10.3 %collective-permute-start.53 = (bf16[3,96,512]{2,1,0:T(8,128)(2,1)}, bf16[3,96,512]{2,1,0:T(8,128)(2,1)}, u32[]{:S(2)}, u32[]{:S(2)}) collective-permute-start(bf16[3,96,512]{2,1,0:T(8,128)(2,1)} %dynamic-slice_bitcast_fusion.7), channel_id=1, source_target_pairs={{0,4},{4,0},{8,12},{12,8},{16,20},{20,16},{24,28},{28,24},{32,36},... | collective-permute-start | bytes 884744 | tf_op jit(solution)/shard_map/ppermute | solution.py:34
  337.6 15.4 %collective-permute-start.54 = (bf16[6,96,512]{2,1,0:T(8,128)(2,1)S(1)}, bf16[6,96,512]{2,1,0:T(8,128)(2,1)S(1)}, u32[]{:S(2)}, u32[]{:S(2)}) collective-permute-start(bf16[6,96,512]{2,1,0:T(8,128)(2,1)S(1)} %pad_maximum_fusion.5), channel_id=1, source_target_pairs={{0,4},{4,0},{8,12},{12,8},{16,20},{20,16},{24,28},{28,24},{32,36},... | collective-permute-start | bytes 1769480 | tf_op jit(solution)/shard_map/ppermute | solution.py:34
  340.1 14.2 %collective-permute-start.55 = (bf16[3,96,512]{2,1,0:T(8,128)(2,1)S(1)}, bf16[3,96,512]{2,1,0:T(8,128)(2,1)S(1)}, u32[]{:S(2)}, u32[]{:S(2)}) collective-permute-start(bf16[3,96,512]{2,1,0:T(8,128)(2,1)S(1)} %slice.488), channel_id=1, source_target_pairs={{0,8},{4,12},{8,16},{12,20},{16,24},{20,28},{24,32},{28,36},{32,40... | collective-permute-start | bytes 884744 | tf_op jit(solution)/shard_map/ppermute | solution.py:29
  349.1 16.1 %collective-permute-start.62 = (bf16[4,96,512]{2,1,0:T(8,128)(2,1)S(1)}, bf16[4,96,512]{2,1,0:T(8,128)(2,1)}, u32[]{:S(2)}, u32[]{:S(2)}) collective-permute-start(bf16[4,96,512]{2,1,0:T(8,128)(2,1)S(1)} %fusion.21), channel_id=1, source_target_pairs={{0,56},{4,60},{8,0},{12,4},{16,8},{20,12},{24,16},{28,20},{32,24},... | collective-permute-start | bytes 1179656 | tf_op jit(solution)/shard_map/ppermute | solution.py:29
  357.2 15.4 %collective-permute-start.56 = (bf16[6,96,512]{2,1,0:T(8,128)(2,1)S(1)}, bf16[6,96,512]{2,1,0:T(8,128)(2,1)}, u32[]{:S(2)}, u32[]{:S(2)}) collective-permute-start(bf16[6,96,512]{2,1,0:T(8,128)(2,1)S(1)} %pad_maximum_fusion.6), channel_id=1, source_target_pairs={{0,4},{4,0},{8,12},{12,8},{16,20},{20,16},{24,28},{28,24},{32,36},... | collective-permute-start | bytes 1769480 | tf_op jit(solution)/shard_map/ppermute | solution.py:34
  359.2 18.0 %collective-permute-start.57 = (bf16[7,96,512]{2,1,0:T(8,128)(2,1)S(1)}, bf16[7,96,512]{2,1,0:T(8,128)(2,1)S(1)}, u32[]{:S(2)}, u32[]{:S(2)}) collective-permute-start(bf16[7,96,512]{2,1,0:T(8,128)(2,1)S(1)} %maximum_convert_fusion), channel_id=1, source_target_pairs={{0,8},{4,12},{8,16},{12,20},{16,24},{20,28},{24,32},{28,36},{32,40... | collective-permute-start | bytes 2064392 | tf_op jit(solution)/shard_map/ppermute | solution.py:29
  360.6 19.7 %collective-permute-start.70 = (f32[33,384]{1,0:T(8,128)}, f32[33,384]{1,0:T(8,128)S(1)}, u32[]{:S(2)}, u32[]{:S(2)}) collective-permute-start(f32[33,384]{1,0:T(8,128)} %get-tuple-element.376), channel_id=1, source_target_pairs={{0,1},{1,2},{2,3},{3,0},{4,5},{5,6},{6,7},{7,4},{8,9},{9,10},{10,1... | collective-permute-start | bytes 152072 | tf_op jit(solution)/shard_map/ppermute | solution.py:29
  362.9 17.4 %collective-permute-start.71 = (f32[33,384]{1,0:T(8,128)}, f32[33,384]{1,0:T(8,128)}, u32[]{:S(2)}, u32[]{:S(2)}) collective-permute-start(f32[33,384]{1,0:T(8,128)} %get-tuple-element.378), channel_id=1, source_target_pairs={{0,2},{1,3},{2,0},{3,1},{4,6},{5,7},{6,4},{7,5},{8,10},{9,11},{10,... | collective-permute-start | bytes 152072 | tf_op jit(solution)/shard_map/ppermute | solution.py:29
  365.3 15.1 %collective-permute-start.72 = (f32[33,384]{1,0:T(8,128)S(1)}, f32[33,384]{1,0:T(8,128)}, u32[]{:S(2)}, u32[]{:S(2)}) collective-permute-start(f32[33,384]{1,0:T(8,128)S(1)} %get-tuple-element.377), channel_id=1, source_target_pairs={{0,3},{1,0},{2,1},{3,2},{4,7},{5,4},{6,5},{7,6},{8,11},{9,8},{10,9... | collective-permute-start | bytes 152072 | tf_op jit(solution)/shard_map/ppermute | solution.py:29
  372.5 11.8 %collective-permute-start.63 = (bf16[7,96,512]{2,1,0:T(8,128)(2,1)S(1)}, bf16[7,96,512]{2,1,0:T(8,128)(2,1)S(1)}, u32[]{:S(2)}, u32[]{:S(2)}) collective-permute-start(bf16[7,96,512]{2,1,0:T(8,128)(2,1)S(1)} %pad_maximum_fusion.4), channel_id=1, source_target_pairs={{0,56},{4,60},{8,0},{12,4},{16,8},{20,12},{24,16},{28,20},{32,24},... | collective-permute-start | bytes 2064392 | tf_op jit(solution)/shard_map/ppermute | solution.py:29
  380.2 10.8 %collective-permute-start.58 = (bf16[6,96,512]{2,1,0:T(8,128)(2,1)S(1)}, bf16[6,96,512]{2,1,0:T(8,128)(2,1)S(1)}, u32[]{:S(2)}, u32[]{:S(2)}) collective-permute-start(bf16[6,96,512]{2,1,0:T(8,128)(2,1)S(1)} %pad_maximum_fusion.7), channel_id=1, source_target_pairs={{0,4},{4,0},{8,12},{12,8},{16,20},{20,16},{24,28},{28,24},{32,36},... | collective-permute-start | bytes 1769480 | tf_op jit(solution)/shard_map/ppermute | solution.py:34
  381.2 9.6 %collective-permute-start.73 = (f32[33,384]{1,0:T(8,128)S(1)}, f32[33,384]{1,0:T(8,128)S(1)}, u32[]{:S(2)}, u32[]{:S(2)}) collective-permute-start(f32[33,384]{1,0:T(8,128)S(1)} %get-tuple-element.323), channel_id=1, source_target_pairs={{0,4},{4,0},{8,12},{12,8},{16,20},{20,16},{24,28},{28,24},{32,36},... | collective-permute-start | bytes 152072 | tf_op jit(solution)/shard_map/ppermute | solution.py:34
  383.3 15.6 %collective-permute-start.59 = (bf16[7,96,512]{2,1,0:T(8,128)(2,1)S(1)}, bf16[7,96,512]{2,1,0:T(8,128)(2,1)S(1)}, u32[]{:S(2)}, u32[]{:S(2)}) collective-permute-start(bf16[7,96,512]{2,1,0:T(8,128)(2,1)S(1)} %add_convert_fusion.3), channel_id=1, source_target_pairs={{0,8},{4,12},{8,16},{12,20},{16,24},{20,28},{24,32},{28,36},{32,40... | collective-permute-start | bytes 2064392 | tf_op jit(solution)/shard_map/ppermute | solution.py:29
  384.5 16.6 %collective-permute-start.64 = (bf16[7,96,512]{2,1,0:T(8,128)(2,1)S(1)}, bf16[7,96,512]{2,1,0:T(8,128)(2,1)S(1)}, u32[]{:S(2)}, u32[]{:S(2)}) collective-permute-start(bf16[7,96,512]{2,1,0:T(8,128)(2,1)S(1)} %add_convert_fusion.1), channel_id=1, source_target_pairs={{0,56},{4,60},{8,0},{12,4},{16,8},{20,12},{24,16},{28,20},{32,24},... | collective-permute-start | bytes 2064392 | tf_op jit(solution)/shard_map/ppermute | solution.py:29
  390.9 19.9 %collective-permute-start.74 = (f32[33,384]{1,0:T(8,128)S(1)}, f32[33,384]{1,0:T(8,128)S(1)}, u32[]{:S(2)}, u32[]{:S(2)}) collective-permute-start(f32[33,384]{1,0:T(8,128)S(1)} %get-tuple-element.321), channel_id=1, source_target_pairs={{0,8},{4,12},{8,0},{12,4},{16,24},{20,28},{24,16},{28,20},{32,40},... | collective-permute-start | bytes 152072 | tf_op jit(solution)/shard_map/ppermute | solution.py:34
  399.1 28.3 %collective-permute-start.61 = (bf16[7,96,512]{2,1,0:T(8,128)(2,1)S(1)}, bf16[7,96,512]{2,1,0:T(8,128)(2,1)S(1)}, u32[]{:S(2)}, u32[]{:S(2)}) collective-permute-start(bf16[7,96,512]{2,1,0:T(8,128)(2,1)S(1)} %add_convert_fusion.2), channel_id=1, source_target_pairs={{0,8},{4,12},{8,16},{12,20},{16,24},{20,28},{24,32},{28,36},{32,40... | collective-permute-start | bytes 2064392 | tf_op jit(solution)/shard_map/ppermute | solution.py:29
  403.7 23.7 %collective-permute-start.65 = (bf16[7,96,512]{2,1,0:T(8,128)(2,1)}, bf16[7,96,512]{2,1,0:T(8,128)(2,1)}, u32[]{:S(2)}, u32[]{:S(2)}) collective-permute-start(bf16[7,96,512]{2,1,0:T(8,128)(2,1)} %add_convert_fusion), channel_id=1, source_target_pairs={{0,56},{4,60},{8,0},{12,4},{16,8},{20,12},{24,16},{28,20},{32,24},... | collective-permute-start | bytes 2064392 | tf_op jit(solution)/shard_map/ppermute | solution.py:29
  410.8 19.5 %collective-permute-start.75 = (f32[33,384]{1,0:T(8,128)S(1)}, f32[33,384]{1,0:T(8,128)S(1)}, u32[]{:S(2)}, u32[]{:S(2)}) collective-permute-start(f32[33,384]{1,0:T(8,128)S(1)} %get-tuple-element.319), channel_id=1, source_target_pairs={{0,16},{4,20},{8,24},{12,28},{16,0},{20,4},{24,8},{28,12},{32,48},... | collective-permute-start | bytes 152072 | tf_op jit(solution)/shard_map/ppermute | solution.py:34
  417.1 8.5 %collective-permute-start.60 = (bf16[3,96,512]{2,1,0:T(8,128)(2,1)S(1)}, bf16[3,96,512]{2,1,0:T(8,128)(2,1)S(1)}, u32[]{:S(2)}, u32[]{:S(2)}) collective-permute-start(bf16[3,96,512]{2,1,0:T(8,128)(2,1)S(1)} %dynamic-slice_bitcast_fusion), channel_id=1, source_target_pairs={{0,4},{4,0},{8,12},{12,8},{16,20},{20,16},{24,28},{28,24},{32,36},... | collective-permute-start | bytes 884744 | tf_op jit(solution)/shard_map/ppermute | solution.py:34
  418.3 15.2 %collective-permute-start.42 = (bf16[2,96,512]{2,1,0:T(8,128)(2,1)S(1)}, bf16[2,96,512]{2,1,0:T(8,128)(2,1)S(1)}, u32[]{:S(2)}, u32[]{:S(2)}) collective-permute-start(bf16[2,96,512]{2,1,0:T(8,128)(2,1)S(1)} %pad_maximum_fusion.17), channel_id=1, source_target_pairs={{0,8},{4,12},{8,16},{12,20},{16,24},{20,28},{24,32},{28,36},{32,40... | collective-permute-start | bytes 589832 | tf_op jit(solution)/shard_map/ppermute | solution.py:29
  425.6 22.4 %collective-permute-start.46 = (bf16[2,96,512]{2,1,0:T(8,128)(2,1)S(1)}, bf16[2,96,512]{2,1,0:T(8,128)(2,1)S(1)}, u32[]{:S(2)}, u32[]{:S(2)}) collective-permute-start(bf16[2,96,512]{2,1,0:T(8,128)(2,1)S(1)} %pad_maximum_fusion.18), channel_id=1, source_target_pairs={{0,56},{4,60},{8,0},{12,4},{16,8},{20,12},{24,16},{28,20},{32,24},... | collective-permute-start | bytes 589832 | tf_op jit(solution)/shard_map/ppermute | solution.py:29
  430.3 8.3 %collective-permute-start.76 = (f32[33,384]{1,0:T(8,128)S(1)}, f32[33,384]{1,0:T(8,128)S(1)}, u32[]{:S(2)}, u32[]{:S(2)}) collective-permute-start(f32[33,384]{1,0:T(8,128)S(1)} %get-tuple-element.317), channel_id=1, source_target_pairs={{0,32},{4,36},{8,40},{12,44},{16,48},{20,52},{24,56},{28,60},{32,0... | collective-permute-start | bytes 152072 | tf_op jit(solution)/shard_map/ppermute | solution.py:34
  433.6 14.3 %collective-permute-start.43 = (bf16[2,96,512]{2,1,0:T(8,128)(2,1)S(1)}, bf16[2,96,512]{2,1,0:T(8,128)(2,1)S(1)}, u32[]{:S(2)}, u32[]{:S(2)}) collective-permute-start(bf16[2,96,512]{2,1,0:T(8,128)(2,1)S(1)} %fusion.25), channel_id=1, source_target_pairs={{0,8},{4,12},{8,16},{12,20},{16,24},{20,28},{24,32},{28,36},{32,40... | collective-permute-start | bytes 589832 | tf_op jit(solution)/shard_map/ppermute | solution.py:29
  438.7 7.4 %collective-permute-start.77 = (f32[33,384]{1,0:T(8,128)S(1)}, f32[33,384]{1,0:T(8,128)S(1)}, u32[]{:S(2)}, u32[]{:S(2)}) collective-permute-start(f32[33,384]{1,0:T(8,128)S(1)} %add_add_fusion.1), channel_id=1, source_target_pairs={{0,1},{1,2},{2,3},{3,0},{4,5},{5,6},{6,7},{7,4},{8,9},{9,10},{10,1... | collective-permute-start | bytes 152072 | tf_op jit(solution)/shard_map/ppermute | solution.py:29
  446.1 10.6 %collective-permute-start.66 = (bf16[2,96,512]{2,1,0:T(8,128)(2,1)S(1)}, bf16[2,96,512]{2,1,0:T(8,128)(2,1)S(1)}, u32[]{:S(2)}, u32[]{:S(2)}) collective-permute-start(bf16[2,96,512]{2,1,0:T(8,128)(2,1)S(1)} %fusion.29), channel_id=1, source_target_pairs={{0,4},{4,0},{8,12},{12,8},{16,20},{20,16},{24,28},{28,24},{32,36},... | collective-permute-start | bytes 589832 | tf_op jit(solution)/shard_map/ppermute | solution.py:34
  449.8 11.5 %collective-permute-start.44 = (bf16[2,96,512]{2,1,0:T(8,128)(2,1)S(1)}, bf16[2,96,512]{2,1,0:T(8,128)(2,1)S(1)}, u32[]{:S(2)}, u32[]{:S(2)}) collective-permute-start(bf16[2,96,512]{2,1,0:T(8,128)(2,1)S(1)} %get-tuple-element.345), channel_id=1, source_target_pairs={{0,8},{4,12},{8,16},{12,20},{16,24},{20,28},{24,32},{28,36},{32,40... | collective-permute-start | bytes 589832 | tf_op jit(solution)/shard_map/ppermute | solution.py:29
  453.9 7.3 %collective-permute-start.48 = (bf16[2,96,512]{2,1,0:T(8,128)(2,1)S(1)}, bf16[2,96,512]{2,1,0:T(8,128)(2,1)S(1)}, u32[]{:S(2)}, u32[]{:S(2)}) collective-permute-start(bf16[2,96,512]{2,1,0:T(8,128)(2,1)S(1)} %fusion.24), channel_id=1, source_target_pairs={{0,56},{4,60},{8,0},{12,4},{16,8},{20,12},{24,16},{28,20},{32,24},... | collective-permute-start | bytes 589832 | tf_op jit(solution)/shard_map/ppermute | solution.py:29
  457.0 11.4 %collective-permute-start.67 = (bf16[5,96,512]{2,1,0:T(8,128)(2,1)S(1)}, bf16[5,96,512]{2,1,0:T(8,128)(2,1)S(1)}, u32[]{:S(2)}, u32[]{:S(2)}) collective-permute-start(bf16[5,96,512]{2,1,0:T(8,128)(2,1)S(1)} %fusion.4), channel_id=1, source_target_pairs={{0,2},{1,3},{2,0},{3,1},{4,6},{5,7},{6,4},{7,5},{8,10},{9,11},{10,... | collective-permute-start | bytes 1474568 | tf_op jit(solution)/shard_map/ppermute | solution.py:29
  458.0 14.7 %collective-permute-start.68 = (bf16[5,96,512]{2,1,0:T(8,128)(2,1)S(1)}, bf16[5,96,512]{2,1,0:T(8,128)(2,1)S(1)}, u32[]{:S(2)}, u32[]{:S(2)}) collective-permute-start(bf16[5,96,512]{2,1,0:T(8,128)(2,1)S(1)} %fusion.4), channel_id=1, source_target_pairs={{0,1},{1,2},{2,3},{3,0},{4,5},{5,6},{6,7},{7,4},{8,9},{9,10},{10,1... | collective-permute-start | bytes 1474568 | tf_op jit(solution)/shard_map/ppermute | solution.py:29
  460.1 12.6 %collective-permute-start.69 = (bf16[5,96,512]{2,1,0:T(8,128)(2,1)S(1)}, bf16[5,96,512]{2,1,0:T(8,128)(2,1)S(1)}, u32[]{:S(2)}, u32[]{:S(2)}) collective-permute-start(bf16[5,96,512]{2,1,0:T(8,128)(2,1)S(1)} %fusion.4), channel_id=1, source_target_pairs={{0,3},{1,0},{2,1},{3,2},{4,7},{5,4},{6,5},{7,6},{8,11},{9,8},{10,9... | collective-permute-start | bytes 1474568 | tf_op jit(solution)/shard_map/ppermute | solution.py:29
  466.3 6.9 %collective-permute-start.52 = (bf16[96,512]{1,0:T(8,128)(2,1)S(1)}, bf16[96,512]{1,0:T(8,128)(2,1)S(1)}, u32[]{:S(2)}, u32[]{:S(2)}) collective-permute-start(bf16[96,512]{1,0:T(8,128)(2,1)S(1)} %bitcast.439), channel_id=1, source_target_pairs={{0,3},{1,0},{2,1},{3,2},{4,7},{5,4},{6,5},{7,6},{8,11},{9,8},{10,9... | collective-permute-start | bytes 294920 | tf_op jit(solution)/shard_map/ppermute | solution.py:29
  468.4 6.9 %collective-permute-start.50 = (bf16[96,512]{1,0:T(8,128)(2,1)S(1)}, bf16[96,512]{1,0:T(8,128)(2,1)S(1)}, u32[]{:S(2)}, u32[]{:S(2)}) collective-permute-start(bf16[96,512]{1,0:T(8,128)(2,1)S(1)} %bitcast.440), channel_id=1, source_target_pairs={{0,1},{1,2},{2,3},{3,0},{4,5},{5,6},{6,7},{7,4},{8,9},{9,10},{10,1... | collective-permute-start | bytes 294920 | tf_op jit(solution)/shard_map/ppermute | solution.py:29
  468.4 6.8 %collective-permute-start.51 = (bf16[96,512]{1,0:T(8,128)(2,1)S(1)}, bf16[96,512]{1,0:T(8,128)(2,1)S(1)}, u32[]{:S(2)}, u32[]{:S(2)}) collective-permute-start(bf16[96,512]{1,0:T(8,128)(2,1)S(1)} %bitcast.441), channel_id=1, source_target_pairs={{0,2},{1,3},{2,0},{3,1},{4,6},{5,7},{6,4},{7,5},{8,10},{9,11},{10,... | collective-permute-start | bytes 294920 | tf_op jit(solution)/shard_map/ppermute | solution.py:29
  (49 other events, 239.2 us)
Sparse Core Ops, SparseCore 0:
  49.2 69.2 all-gather.1
  316.7 67.0 reduce-scatter.1
